TPU v7x, 32 devices: a whole 2x2x4 slice. The times are simulated.
32 devices in a mesh: group: 4 (over y, x), dp: 8 (over z, core).
Axes of the slice: x: 2, y: 2, z: 4, core: 2. Of those that a mesh axis runs over, the one named last changes fastest.
Arguments:
- layer_input: bfloat16 [3, 32, 320, 1024], P(None, ('group', 'dp')), may hold values from -6 to 6
- lengths: int32 [3, 32], P(None, ('group', 'dp')), may hold values from 256 to 320, as said below
- attend_gain: bfloat16 [1024], P('dp'), may hold values from 0.5 to 1.5
- attend_bias: bfloat16 [1024], P('dp'), may hold values from -1.75 to 1.75
- project_weight: bfloat16 [1024, 3072], P('dp'), may hold values from -0.1875 to 0.1875
- project_bias: bfloat16 [2048], P('dp'), may hold values from -0.625 to 0.625
- output_weight: bfloat16 [1024, 1024], P('dp'), may hold values from -2 to 2
- output_bias: bfloat16 [1024], P('dp'), may hold values from -3 to 3
- feed_gain: bfloat16 [1024], P('dp'), may hold values from 0.5 to 1.5
- feed_bias: bfloat16 [1024], P('dp'), may hold values from -1.75 to 1.75
- expand_weight: bfloat16 [1024, 4096], P('dp'), may hold values from -0.1875 to 0.1875
- expand_bias: bfloat16 [4096], P('dp'), may hold values from -3 to 3
- reduce_weight: bfloat16 [4096, 1024], P('dp'), may hold values from -0.09375 to 0.09375
- reduce_bias: bfloat16 [1024], P('dp'), may hold values from -3 to 3
- cotangent: bfloat16 [3, 32, 320, 1024], P(None, ('group', 'dp')), may hold values from -6 to 6
Outputs:
- layer_output: float32 [3, 32, 320, 1024], P(None, ('group', 'dp'))
- input_grad: float32 [3, 32, 320, 1024], P(None, ('group', 'dp'))
- attend_gain_grad: float32 [1024], P('dp')
- attend_bias_grad: float32 [1024], P('dp')
- project_weight_grad: float32 [1024, 3072], P('dp')
- project_bias_grad: float32 [2048], P('dp')
- output_weight_grad: float32 [1024, 1024], P('dp')
- output_bias_grad: float32 [1024], P('dp')
- feed_gain_grad: float32 [1024], P('dp')
- feed_bias_grad: float32 [1024], P('dp')
- expand_weight_grad: float32 [1024, 4096], P('dp')
- expand_bias_grad: float32 [4096], P('dp')
- reduce_weight_grad: float32 [4096, 1024], P('dp')
- reduce_bias_grad: float32 [1024], P('dp')
Inputs may be any that keep to these rules, and one draw needn't show every extreme that they name: Sequence b of micro-batch m uses its first lengths[m, b] slots (64 buffer slots and the kept image tokens); the other slots are padding. Some sequence of every micro-batch uses all 320 slots and some uses 256.
All inputs are finite; a program needn't handle non-finite values.
Results may differ from a plain program's by a relative error of at most 0.019.
Values may be sent and summed in bfloat16 or wider, within the bound.
No kernel may reach another device: no remote copies, remote signals or barrier semaphores. Data moves between devices by JAX's collectives and lax.ppermute only.
A program may use at most 256 MiB of HBM per device.

v0:
```python
import jax
import jax.numpy as jnp
from jax import lax
from jax.sharding import PartitionSpec as P

H = 16
E = 64


EPS = 1e-06


def as_sent(array):

    def short(part):
        return part.astype(jnp.bfloat16) if part.dtype == jnp.float32 else part

    return jax.tree.map(short, array)


def layer_norm(values, gain_vec, bias_vec):
    row_mean = jnp.mean(values, -1, keepdims=True)
    centred = values - row_mean
    spread = jnp.mean(centred * centred, -1, keepdims=True)
    return centred * lax.rsqrt(spread + EPS) * gain_vec + bias_vec


def exact_gelu(values):
    return jax.nn.gelu(values, approximate=False)


def dot_rows(former, latter):
    return jnp.dot(former, latter, preferred_element_type=jnp.float32)


def dot_left(former, latter):
    return lax.dot_general(
        former, latter, (((0,), (0,)), ((), ())), preferred_element_type=jnp.float32
    )


def dot_right(former, latter):
    return lax.dot_general(
        former, latter, (((1,), (1,)), ((), ())), preferred_element_type=jnp.float32
    )


def fetch_weights(shards):
    return (
        lax.all_gather(shards[0], "dp", axis=0, tiled=True),
        lax.all_gather(shards[1], "dp", axis=0, tiled=True),
        lax.all_gather(shards[2], "dp", axis=0, tiled=True),
        lax.all_gather(shards[3], "dp", axis=0, tiled=True),
        lax.all_gather(shards[4], "dp", axis=0, tiled=True),
        lax.all_gather(shards[5], "dp", axis=0, tiled=True),
        lax.all_gather(shards[6], "dp", axis=0, tiled=True),
        lax.all_gather(shards[7], "dp", axis=0, tiled=True),
        lax.all_gather(shards[8], "dp", axis=0, tiled=True),
        lax.all_gather(shards[9], "dp", axis=0, tiled=True),
        lax.all_gather(shards[10], "dp", axis=0, tiled=True),
        lax.all_gather(shards[11], "dp", axis=0, tiled=True),
    )


def reduce_grads(grads):
    return (
        lax.psum_scatter(
            grads[0].astype(jnp.bfloat16), "dp", scatter_dimension=0, tiled=True
        ).astype(jnp.float32),
        lax.psum_scatter(
            grads[1].astype(jnp.bfloat16), "dp", scatter_dimension=0, tiled=True
        ).astype(jnp.float32),
        lax.psum_scatter(
            grads[2].astype(jnp.bfloat16), "dp", scatter_dimension=0, tiled=True
        ).astype(jnp.float32),
        lax.psum_scatter(
            grads[3].astype(jnp.bfloat16), "dp", scatter_dimension=0, tiled=True
        ).astype(jnp.float32),
        lax.psum_scatter(
            grads[4].astype(jnp.bfloat16), "dp", scatter_dimension=0, tiled=True
        ).astype(jnp.float32),
        lax.psum_scatter(
            grads[5].astype(jnp.bfloat16), "dp", scatter_dimension=0, tiled=True
        ).astype(jnp.float32),
        lax.psum_scatter(
            grads[6].astype(jnp.bfloat16), "dp", scatter_dimension=0, tiled=True
        ).astype(jnp.float32),
        lax.psum_scatter(
            grads[7].astype(jnp.bfloat16), "dp", scatter_dimension=0, tiled=True
        ).astype(jnp.float32),
        lax.psum_scatter(
            grads[8].astype(jnp.bfloat16), "dp", scatter_dimension=0, tiled=True
        ).astype(jnp.float32),
        lax.psum_scatter(
            grads[9].astype(jnp.bfloat16), "dp", scatter_dimension=0, tiled=True
        ).astype(jnp.float32),
        lax.psum_scatter(
            grads[10].astype(jnp.bfloat16), "dp", scatter_dimension=0, tiled=True
        ).astype(jnp.float32),
        lax.psum_scatter(
            grads[11].astype(jnp.bfloat16), "dp", scatter_dimension=0, tiled=True
        ).astype(jnp.float32),
    )


def masked_scores(queries, keys, key_valid):
    scores = jnp.einsum(
        "sqhe,skhe->shqk", queries, keys, preferred_element_type=jnp.float32
    ) * E ** (-0.5)
    return jnp.where(key_valid, scores, -1e30)


def attend_forward(queries, keys, key_valid):
    scores = masked_scores(queries, keys, key_valid)
    row_max = jnp.max(scores, -1, keepdims=True)
    weights = jnp.exp(scores - row_max)
    row_total = jnp.sum(weights, -1, keepdims=True)
    return (weights / row_total, row_max + jnp.log(row_total))


def attend_backward(queries, keys, values, log_sum, key_valid, grad_mixed):
    probs = jnp.exp(masked_scores(queries, keys, key_valid) - log_sum)
    probs_low = probs.astype(jnp.bfloat16)
    grad_probs = jnp.einsum(
        "sqhe,skhe->shqk", grad_mixed, values, preferred_element_type=jnp.float32
    )
    grad_values = jnp.einsum(
        "shqk,sqhe->skhe", probs_low, grad_mixed, preferred_element_type=jnp.float32
    )
    inner = jnp.sum(grad_probs * probs, -1, keepdims=True)
    grad_scores = (probs * (grad_probs - inner)).astype(jnp.bfloat16)
    scale = E ** (-0.5)
    grad_queries = (
        jnp.einsum("shqk,skhe->sqhe", grad_scores, keys, preferred_element_type=jnp.float32) * scale
    )
    grad_keys = (
        jnp.einsum("shqk,sqhe->skhe", grad_scores, queries, preferred_element_type=jnp.float32)
        * scale
    )
    return (grad_queries, grad_keys, grad_values)


def local(
    layer_input,
    lengths,
    attend_gain,
    attend_bias,
    project_weight,
    project_bias,
    output_weight,
    output_bias,
    feed_gain,
    feed_bias,
    expand_weight,
    expand_bias,
    reduce_weight,
    reduce_bias,
    cotangent,
):
    shards = (
        attend_gain,
        attend_bias,
        project_weight,
        project_bias,
        output_weight,
        output_bias,
        feed_gain,
        feed_bias,
        expand_weight,
        expand_bias,
        reduce_weight,
        reduce_bias,
    )
    micro_count, seq_count, slot_count, width = layer_input.shape
    row_count = seq_count * slot_count
    running = None
    outputs = []
    input_grads = []
    slot_ids = jnp.arange(slot_count, dtype=jnp.int32)
    for micro_idx in range(micro_count):
        gathered = fetch_weights(shards)
        valid_grid = (slot_ids[None, :] < lengths[micro_idx][:, None]).astype(jnp.float32)
        row_valid = valid_grid.reshape(row_count, 1)
        key_valid = valid_grid[:, None, None, :] > 0
        masked = layer_input[micro_idx].reshape(row_count, width).astype(jnp.float32) * row_valid
        normed, norm_one_back = jax.vjp(
            layer_norm, masked, gathered[0].astype(jnp.float32), gathered[1].astype(jnp.float32)
        )
        normed = normed.astype(jnp.bfloat16)
        bias_pair = gathered[3].astype(jnp.float32)
        full_bias = jnp.concatenate(
            [bias_pair[:width], jnp.zeros((width,), jnp.float32), bias_pair[width:]]
        )
        packed = (dot_rows(normed, gathered[2]) + full_bias).astype(jnp.bfloat16)
        packed = packed.reshape(seq_count, slot_count, 3, H, E)
        queries = packed[:, :, 0]
        keys = packed[:, :, 1]
        values = packed[:, :, 2]
        probs, log_sum = attend_forward(queries, keys, key_valid)
        mixed = jnp.einsum(
            "shqk,skhe->sqhe",
            probs.astype(jnp.bfloat16),
            values,
            preferred_element_type=jnp.float32,
        )
        mixed = mixed.reshape(row_count, width).astype(jnp.bfloat16)
        resid = masked + dot_rows(mixed, gathered[4]) + gathered[5].astype(jnp.float32)
        normed_two, norm_two_back = jax.vjp(
            layer_norm, resid, gathered[6].astype(jnp.float32), gathered[7].astype(jnp.float32)
        )
        normed_two = normed_two.astype(jnp.bfloat16)
        hidden = dot_rows(normed_two, gathered[8]) + gathered[9].astype(jnp.float32)
        activated, gelu_back = jax.vjp(exact_gelu, hidden)
        activated = activated.astype(jnp.bfloat16)
        result = (
            resid + dot_rows(activated, gathered[10]) + gathered[11].astype(jnp.float32)
        ) * row_valid
        outputs.append(result.reshape(seq_count, slot_count, width))
        back_weights = (
            lax.all_gather(shards[0], "dp", axis=0, tiled=True),
            lax.all_gather(shards[1], "dp", axis=0, tiled=True),
            lax.all_gather(shards[2], "dp", axis=0, tiled=True),
            lax.all_gather(shards[3], "dp", axis=0, tiled=True),
            lax.all_gather(shards[4], "dp", axis=0, tiled=True),
            lax.all_gather(shards[5], "dp", axis=0, tiled=True),
            lax.all_gather(shards[6], "dp", axis=0, tiled=True),
            lax.all_gather(shards[7], "dp", axis=0, tiled=True),
            lax.all_gather(shards[8], "dp", axis=0, tiled=True),
            lax.all_gather(shards[9], "dp", axis=0, tiled=True),
            lax.all_gather(shards[10], "dp", axis=0, tiled=True),
            lax.all_gather(shards[11], "dp", axis=0, tiled=True),
        )
        upstream = cotangent[micro_idx].reshape(row_count, width).astype(jnp.float32) * row_valid
        up_low = upstream.astype(jnp.bfloat16)
        grad_reduce_w = dot_left(activated, up_low)
        grad_reduce_b = jnp.sum(up_low, 0, dtype=jnp.float32)
        (grad_hidden,) = gelu_back(dot_right(up_low, back_weights[10]))
        hidden_low = grad_hidden.astype(jnp.bfloat16)
        grad_expand_w = dot_left(normed_two, hidden_low)
        grad_expand_b = jnp.sum(hidden_low, 0, dtype=jnp.float32)
        grad_resid_norm, grad_feed_gain, grad_feed_bias = norm_two_back(
            dot_right(hidden_low, back_weights[8])
        )
        grad_resid = upstream + grad_resid_norm
        branch_low = grad_resid.astype(jnp.bfloat16)
        grad_output_w = dot_left(mixed, branch_low)
        grad_output_b = jnp.sum(branch_low, 0, dtype=jnp.float32)
        grad_mixed = dot_right(branch_low, back_weights[4]).astype(jnp.bfloat16)
        grad_mixed = grad_mixed.reshape(seq_count, slot_count, H, E)
        grad_queries, grad_keys, grad_values = attend_backward(
            queries, keys, values, log_sum, key_valid, grad_mixed
        )
        grad_packed = jnp.stack([grad_queries, grad_keys, grad_values], 2).astype(jnp.bfloat16)
        grad_packed = grad_packed.reshape(row_count, 3 * width)
        grad_project_w = dot_left(normed, grad_packed)
        column_sums = jnp.sum(grad_packed, 0, dtype=jnp.float32)
        grad_project_b = jnp.concatenate([column_sums[:width], column_sums[2 * width :]])
        grad_in_norm, grad_attend_gain, grad_attend_bias = norm_one_back(
            dot_right(grad_packed, back_weights[2])
        )
        input_grads.append(
            ((grad_resid + grad_in_norm) * row_valid).reshape(seq_count, slot_count, width)
        )
        grads = (
            grad_attend_gain,
            grad_attend_bias,
            grad_project_w,
            grad_project_b,
            grad_output_w,
            grad_output_b,
            grad_feed_gain,
            grad_feed_bias,
            grad_expand_w,
            grad_expand_b,
            grad_reduce_w,
            grad_reduce_b,
        )
        grads = reduce_grads(grads)
        running = grads if running is None else jax.tree.map(jnp.add, running, grads)
    summed = jax.tree.map(
        lambda part: part.astype(jnp.float32), lax.psum(as_sent(running), "group")
    )
    return (
        jnp.stack(outputs),
        jnp.stack(input_grads),
        summed[0],
        summed[1],
        summed[2],
        summed[3],
        summed[4],
        summed[5],
        summed[6],
        summed[7],
        summed[8],
        summed[9],
        summed[10],
        summed[11],
    )


def solution(mesh):
    return jax.shard_map(
        local,
        mesh=mesh,
        in_specs=(
            P(None, ("group", "dp"), None, None),
            P(None, ("group", "dp")),
            P("dp"),
            P("dp"),
            P("dp", None),
            P("dp"),
            P("dp", None),
            P("dp"),
            P("dp"),
            P("dp"),
            P("dp", None),
            P("dp"),
            P("dp", None),
            P("dp"),
            P(None, ("group", "dp"), None, None),
        ),
        out_specs=(
            P(None, ("group", "dp"), None, None),
            P(None, ("group", "dp"), None, None),
            P("dp"),
            P("dp"),
            P("dp", None),
            P("dp"),
            P("dp", None),
            P("dp"),
            P("dp"),
            P("dp"),
            P("dp", None),
            P("dp"),
            P("dp", None),
            P("dp"),
        ),
        check_vma=False,
    )
```

profile of v0, /device:TPU:0, one launch (start us, length us, event | category | flops | bytes accessed | tf_op | source)
XLA Modules:
  0.0 1389.3 jit_solution(1911880560296571932)
XLA Ops:
  14.7 13.4 all-gather
  28.1 8.8 all-gather.1
  37.0 10.4 all-gather.3
  47.4 8.8 all-gather.4
  56.2 10.0 all-gather.5
  68.3 8.8 all-gather.2
  77.2 13.0 all-gather.6
  149.8 40.2 %all-gather.17.cloned.1.call-done = bf16[1024,4096]{1,0:T(8,128)(2,1)} async-done(((bf16[128,4096]{1,0:T(8,128)(2,1)}), bf16[1024,4096]{1,0:T(8,128)(2,1)}) %all-gather.17.cloned.1.call-update) | async-done | bytes 8388624 | tf_op jit(solution)/shard_map/all_gather | solution.py:58
  190.0 18.3 %multiply_convert_fusion.4 = (bf16[320,4096]{1,0:T(8,128)(2,1)}, f32[320,4096]{1,0:T(8,128)}, f32[320,4096]{1,0:T(8,128)}) fusion(f32[4096]{0:T(1024)S(1)} %bitcast.447, bf16[1024,4096]{1,0:T(8,128)(2,1)} %all-gather.17.cloned.1.call-done, f32[320,1024]{1,0:T(8,128)} %copy-done.20, f32[320]{0:T(512)S(1)} %fusion.183, f32[320]{0:T(512)S(1)} %broadcast_multiply_fusion.2, ...), kind=kOutput, calls=%fused_computation.58 | convolution fusion | flops 2772500480 | bytes 22833664 | tf_op jit(solution)/shard_map/dot_general | solution.py:33
  208.3 18.9 %multiply_convert_fusion.3 = (bf16[320,4096]{1,0:T(8,128)(2,1)}, f32[320,4096]{1,0:T(8,128)}, f32[320,4096]{1,0:T(8,128)}) fusion(f32[4096]{0:T(1024)S(1)} %bitcast.448, bf16[1024,4096]{1,0:T(8,128)(2,1)S(1)} %copy-done.129, f32[320,1024]{1,0:T(8,128)S(1)} %copy-done.17, f32[320]{0:T(512)S(1)} %fusion.185, f32[320]{0:T(512)S(1)} %broadcast_multiply_fusion, ...), kind=kOutput, calls=%fused_computation.45 | convolution fusion | flops 2772500480 | bytes 22833664 | tf_op jit(solution)/shard_map/dot_general | solution.py:33
  227.2 44.8 %all-gather.19.cloned.1.call-done = bf16[4096,1024]{1,0:T(8,128)(2,1)} async-done(((bf16[512,1024]{1,0:T(8,128)(2,1)}), bf16[4096,1024]{1,0:T(8,128)(2,1)}) %all-gather.19.cloned.1.call-update) | async-done | bytes 8388624 | tf_op jit(solution)/shard_map/all_gather | solution.py:60
  272.1 11.8 fusion.251
  290.6 18.7 %multiply_convert_fusion.5 = (bf16[320,4096]{1,0:T(8,128)(2,1)}, f32[320,4096]{1,0:T(8,128)}, f32[320,4096]{1,0:T(8,128)}) fusion(f32[4096]{0:T(1024)S(1)} %bitcast.449, bf16[1024,4096]{1,0:T(8,128)(2,1)S(1)} %copy-done.130, f32[320,1024]{1,0:T(8,128)S(1)} %get-tuple-element.156, f32[1024]{0:T(1024)S(1)} %bitcast.454, f32[1024]{0:T(1024)S(1)} %bitcast.441, ...), kind=kOutput, calls=%fused_computation.71 | convolution fusion | flops 2772500480 | bytes 22833664 | tf_op jit(solution)/shard_map/dot_general | solution.py:33
  309.4 14.0 %fusion.253 = (bf16[4096]{0:T(1024)(128)(2,1)}, bf16[320,4096]{1,0:T(8,128)(2,1)}) fusion(f32[320,4096]{1,0:T(8,128)} %get-tuple-element.103, f32[320,4096]{1,0:T(8,128)} %get-tuple-element.157, bf16[4096,1024]{1,0:T(8,128)(2,1)} %all-gather.19.cloned.1.call-done, f32[320]{0:T(512)S(1)} %copy-done.59, bf16[3,1,320,1024]{3,2,1,0:T(8,128)(2,1)S(1)} %copy-done.29), kind=kOutput, calls=%fused_computation.409 | convolution fusion | flops 2704994304 | bytes 22161408 | tf_op jit(solution)/shard_map/dot_general | solution.py:43
  329.6 14.2 %fusion.252 = (bf16[4096]{0:T(1024)(128)(2,1)}, bf16[320,4096]{1,0:T(8,128)(2,1)}) fusion(f32[320,4096]{1,0:T(8,128)} %get-tuple-element.105, f32[320,4096]{1,0:T(8,128)} %get-tuple-element.152, bf16[4096,1024]{1,0:T(8,128)(2,1)} %all-gather.19.cloned.1.call-done, f32[320]{0:T(512)S(1)} %fusion.178, bf16[3,1,320,1024]{3,2,1,0:T(8,128)(2,1)S(1)} %copy-done.29), kind=kOutput, calls=%fused_computation.408 | convolution fusion | flops 2704994304 | bytes 22161408 | tf_op jit(solution)/shard_map/dot_general | solution.py:43
  474.9 8.9 convolution_convert_fusion.4
  485.1 8.8 convolution_convert_fusion.3
  495.3 8.8 convolution_convert_fusion.5
  504.2 9.8 convolution_convert_fusion.1
  514.2 9.8 convolution_convert_fusion
  524.1 9.8 convolution_convert_fusion.2
  587.7 23.3 %reduce-scatter.13.cloned.1.call-done = bf16[128,3072]{1,0:T(8,128)(2,1)} async-done(((bf16[1024,3072]{1,0:T(8,128)(2,1)}), bf16[128,3072]{1,0:T(8,128)(2,1)}) %reduce-scatter.13.cloned.1.call-update) | async-done | bytes 786448 | tf_op jit(solution)/shard_map/reduce_scatter | solution.py:73
  611.0 70.4 %reduce-scatter.17.cloned.1.call-done = bf16[128,3072]{1,0:T(8,128)(2,1)} async-done(((bf16[1024,3072]{1,0:T(8,128)(2,1)}), bf16[128,3072]{1,0:T(8,128)(2,1)}) %reduce-scatter.17.cloned.1.call-update) | async-done | bytes 786448 | tf_op jit(solution)/shard_map/reduce_scatter | solution.py:73
  684.2 87.5 %reduce-scatter.27.cloned.1.call-done = bf16[128,4096]{1,0:T(8,128)(2,1)} async-done(((bf16[1024,4096]{1,0:T(8,128)(2,1)}), bf16[128,4096]{1,0:T(8,128)(2,1)}) %reduce-scatter.27.cloned.1.call-update) | async-done | bytes 1048592 | tf_op jit(solution)/shard_map/reduce_scatter | solution.py:91
  771.7 90.1 %reduce-scatter.29.cloned.1.call-done = bf16[128,4096]{1,0:T(8,128)(2,1)} async-done(((bf16[1024,4096]{1,0:T(8,128)(2,1)}), bf16[128,4096]{1,0:T(8,128)(2,1)}) %reduce-scatter.29.cloned.1.call-update) | async-done | bytes 1048592 | tf_op jit(solution)/shard_map/reduce_scatter | solution.py:91
  861.8 90.3 %reduce-scatter.25.cloned.1.call-done = bf16[128,4096]{1,0:T(8,128)(2,1)} async-done(((bf16[1024,4096]{1,0:T(8,128)(2,1)}), bf16[128,4096]{1,0:T(8,128)(2,1)}) %reduce-scatter.25.cloned.1.call-update) | async-done | bytes 1048592 | tf_op jit(solution)/shard_map/reduce_scatter | solution.py:91
  955.4 86.8 %reduce-scatter.33.cloned.1.call-done = bf16[512,1024]{1,0:T(8,128)(2,1)} async-done(((bf16[4096,1024]{1,0:T(8,128)(2,1)}), bf16[512,1024]{1,0:T(8,128)(2,1)}) %reduce-scatter.33.cloned.1.call-update) | async-done | bytes 1048592 | tf_op jit(solution)/shard_map/reduce_scatter | solution.py:97
  1042.2 90.1 %reduce-scatter.35.cloned.1.call-done = bf16[512,1024]{1,0:T(8,128)(2,1)} async-done(((bf16[4096,1024]{1,0:T(8,128)(2,1)}), bf16[512,1024]{1,0:T(8,128)(2,1)}) %reduce-scatter.35.cloned.1.call-update) | async-done | bytes 1048592 | tf_op jit(solution)/shard_map/reduce_scatter | solution.py:97
  1132.3 90.1 %reduce-scatter.31.cloned.1.call-done = bf16[512,1024]{1,0:T(8,128)(2,1)} async-done(((bf16[4096,1024]{1,0:T(8,128)(2,1)}), bf16[512,1024]{1,0:T(8,128)(2,1)}) %reduce-scatter.31.cloned.1.call-update) | async-done | bytes 1048592 | tf_op jit(solution)/shard_map/reduce_scatter | solution.py:97
  1241.2 38.7 %all-reduce.30.cloned.1.call-done = (bf16[1024]{0:T(1024)(128)(2,1)}, bf16[1024]{0:T(1024)(128)(2,1)}, bf16[1024]{0:T(1024)(128)(2,1)}, bf16[1024]{0:T(1024)(128...) async-done(((bf16[1024]{0:T(1024)(128)(2,1)}, ...) | async-done | bytes 73744
  1286.0 10.1 all-reduce.25
  1300.3 74.4 %all-reduce.32.cloned.1.call-done = (bf16[128,3072]{1,0:T(8,128)(2,1)}, bf16[128,1024]{1,0:T(8,128)(2,1)}, bf16[128,4096]{1,0:T(8,128)(2,1)}, bf16[512,1024]{1,0:T(8,128)(2,1)}) async-done(((bf16[128,3072]{1,0:T(8,128)(2,1)}, bf16[128,1024]{1,0:T(8,128)(2,1)}, bf16[128,4096]{1,0:T(8,128)(2,1)}, bf16[512,1024]{1,0:T(8,128)(2,1)}), (bf16[128,3072]{1,0:T(8,128)(2,1)}, bf16[128,1024]{1,0:T(8,128)(2,1)}, ...) | async-done | bytes 3145744 | tf_op jit(solution)/shard_map/psum | solution.py:281
  (489 shorter events, 309.1 us)
Async XLA Ops:
  7.3 59.0 %copy-start.6 = (bf16[3,1,320,1024]{3,2,1,0:T(8,128)(2,1)S(1)}, bf16[3,1,320,1024]{3,2,1,0:T(8,128)(2,1)}, u32[]{:S(2)}) copy-start(bf16[3,1,320,1024]{3,2,1,0:T(8,128)(2,1)} %param.15) | copy-start | bytes 5898244
  7.3 82.9 %all-gather.13.cloned.1.call-start = ((), (), s32[]{:S(2)}) async-start(), calls=%async_computation.12 | async-start | bytes 7077888 | tf_op jit(solution)/shard_map/all_gather | solution.py:52
  8.0 119.9 %all-gather.15.cloned.1.call-start = ((), (), s32[]{:S(2)}) async-start(), calls=%async_computation.13 | async-start | bytes 2359296 | tf_op jit(solution)/shard_map/all_gather | solution.py:54
  8.8 181.2 %all-gather.17.cloned.1.call-start = ((), (), s32[]{:S(2)}) async-start(), calls=%async_computation.14 | async-start | bytes 9437184 | tf_op jit(solution)/shard_map/all_gather | solution.py:58
  9.5 262.6 %all-gather.19.cloned.1.call-start = ((), (), s32[]{:S(2)}) async-start(), calls=%async_computation.15 | async-start | bytes 9437184 | tf_op jit(solution)/shard_map/all_gather | solution.py:60
  10.1 575.7 %reduce-scatter.21.cloned.1.call-start = ((), (), s32[]{:S(2)}) async-start(), calls=%async_computation.20 | async-start | bytes 2359296 | tf_op jit(solution)/shard_map/reduce_scatter | solution.py:79
  13.3 114.6 %copy-start.58 = (f32[320]{0:T(512)}, f32[320]{0:T(512)S(1)}, u32[]{:S(2)}) copy-start(f32[320]{0:T(512)S(1)} %fusion.177) | copy-start | bytes 3844
  28.1 87.6 %copy-start.70 = (f32[8,1,128]{2,1,0:T(1,128)}, f32[8,1,128]{2,1,0:T(1,128)S(1)}, u32[]{:S(2)}) copy-start(f32[8,1,128]{2,1,0:T(1,128)S(1)} %convert_element_type.843) | copy-start | bytes 12292
  37.0 78.7 %copy-start.119 = (f32[8,1,128]{2,1,0:T(1,128)}, f32[8,1,128]{2,1,0:T(1,128)S(1)}, u32[]{:S(2)}) copy-start(f32[8,1,128]{2,1,0:T(1,128)S(1)} %convert_element_type.844) | copy-start | bytes 12292
  56.2 296.3 %copy-start.100 = (f32[8,1,128]{2,1,0:T(1,128)}, f32[8,1,128]{2,1,0:T(1,128)S(1)}, u32[]{:S(2)}) copy-start(f32[8,1,128]{2,1,0:T(1,128)S(1)} %convert_element_type.847) | copy-start | bytes 12292
  66.2 223.9 %copy-start.117 = (f32[8,1,128]{2,1,0:T(1,128)}, f32[8,1,128]{2,1,0:T(1,128)S(1)}, u32[]{:S(2)}) copy-start(f32[8,1,128]{2,1,0:T(1,128)S(1)} %convert_element_type.848) | copy-start | bytes 12292
  131.0 221.6 %copy-start.14 = (f32[320,1024]{1,0:T(8,128)}, f32[320,1024]{1,0:T(8,128)S(1)}, u32[]{:S(2)}) copy-start(f32[320,1024]{1,0:T(8,128)S(1)} %get-tuple-element.156) | copy-start | bytes 3932164
  139.1 213.4 %copy-start.80 = (f32[320]{0:T(512)}, f32[320]{0:T(512)S(1)}, u32[]{:S(2)}) copy-start(f32[320]{0:T(512)S(1)} %broadcast_multiply_fusion) | copy-start | bytes 3844
  148.3 204.2 %copy-start.82 = (f32[320]{0:T(512)}, f32[320]{0:T(512)S(1)}, u32[]{:S(2)}) copy-start(f32[320]{0:T(512)S(1)} %broadcast_multiply_fusion.2) | copy-start | bytes 3844
  149.7 58.6 %copy-start.96 = (f32[320]{0:T(512)}, f32[320]{0:T(512)S(1)}, u32[]{:S(2)}) copy-start(f32[320]{0:T(512)S(1)} %multiply_reduce_fusion.10) | copy-start | bytes 3844
  149.7 202.9 %copy-start.108 = (f32[320]{0:T(512)}, f32[320]{0:T(512)S(1)}, u32[]{:S(2)}) copy-start(f32[320]{0:T(512)S(1)} %fusion.181) | copy-start | bytes 3844
  149.7 202.8 %copy-start.110 = (f32[320]{0:T(512)}, f32[320]{0:T(512)S(1)}, u32[]{:S(2)}) copy-start(f32[320]{0:T(512)S(1)} %fusion.185) | copy-start | bytes 3844
  149.8 202.8 %copy-start.112 = (f32[320]{0:T(512)}, f32[320]{0:T(512)S(1)}, u32[]{:S(2)}) copy-start(f32[320]{0:T(512)S(1)} %fusion.183) | copy-start | bytes 3844
  290.6 53.1 %copy-start.41 = (f32[320,1024]{1,0:T(8,128)}, f32[320,1024]{1,0:T(8,128)S(1)}, u32[]{:S(2)}) copy-start(f32[320,1024]{1,0:T(8,128)S(1)} %fusion.257) | copy-start | bytes 3932164
  361.4 224.3 %reduce-scatter.19.cloned.1.call-start = ((), (), s32[]{:S(2)}) async-start(), calls=%async_computation.19 | async-start | bytes 2359296 | tf_op jit(solution)/shard_map/reduce_scatter | solution.py:79
  364.1 221.7 %reduce-scatter.23.cloned.1.call-start = ((), (), s32[]{:S(2)}) async-start(), calls=%async_computation.21 | async-start | bytes 2359296 | tf_op jit(solution)/shard_map/reduce_scatter | solution.py:79
  366.8 220.9 %reduce-scatter.15.cloned.1.call-start = ((), (), s32[]{:S(2)}) async-start(), calls=%async_computation.17 | async-start | bytes 7077888 | tf_op jit(solution)/shard_map/reduce_scatter | solution.py:73
  403.0 208.0 %reduce-scatter.13.cloned.1.call-start = ((), (), s32[]{:S(2)}) async-start(), calls=%async_computation.16 | async-start | bytes 7077888 | tf_op jit(solution)/shard_map/reduce_scatter | solution.py:73
  438.8 242.5 %reduce-scatter.17.cloned.1.call-start = ((), (), s32[]{:S(2)}) async-start(), calls=%async_computation.18 | async-start | bytes 7077888 | tf_op jit(solution)/shard_map/reduce_scatter | solution.py:73
  473.7 298.0 %reduce-scatter.27.cloned.1.call-start = ((), (), s32[]{:S(2)}) async-start(), calls=%async_computation.23 | async-start | bytes 9437184 | tf_op jit(solution)/shard_map/reduce_scatter | solution.py:91
  483.9 377.9 %reduce-scatter.29.cloned.1.call-start = ((), (), s32[]{:S(2)}) async-start(), calls=%async_computation.24 | async-start | bytes 9437184 | tf_op jit(solution)/shard_map/reduce_scatter | solution.py:91
  494.0 458.1 %reduce-scatter.25.cloned.1.call-start = ((), (), s32[]{:S(2)}) async-start(), calls=%async_computation.22 | async-start | bytes 9437184 | tf_op jit(solution)/shard_map/reduce_scatter | solution.py:91
  504.1 538.1 %reduce-scatter.33.cloned.1.call-start = ((), (), s32[]{:S(2)}) async-start(), calls=%async_computation.26 | async-start | bytes 9437184 | tf_op jit(solution)/shard_map/reduce_scatter | solution.py:97
  514.0 618.4 %reduce-scatter.35.cloned.1.call-start = ((), (), s32[]{:S(2)}) async-start(), calls=%async_computation.27 | async-start | bytes 9437184 | tf_op jit(solution)/shard_map/reduce_scatter | solution.py:97
  524.0 698.5 %reduce-scatter.31.cloned.1.call-start = ((), (), s32[]{:S(2)}) async-start(), calls=%async_computation.25 | async-start | bytes 9437184 | tf_op jit(solution)/shard_map/reduce_scatter | solution.py:97
  533.9 746.0 %all-reduce.30.cloned.1.call-start = ((), (), s32[]{:S(2)}) async-start(), calls=%async_computation.28 | async-start | bytes 147456
  569.3 805.3 %all-reduce.32.cloned.1.call-start = ((), (), s32[]{:S(2)}) async-start(), calls=%async_computation.29 | async-start | bytes 6291456 | tf_op jit(solution)/shard_map/psum | solution.py:281
  (131 other events, 927.3 us)
Sparse Core Ops, SparseCore 0:
  9.8 67.5 all-gather.12
  79.0 27.8 all-gather.14
  108.5 81.4 all-gather.16
  191.4 80.5 all-gather.18
  361.5 34.3 reduce-scatter.20
  398.0 34.4 reduce-scatter.18
  435.4 34.3 reduce-scatter.22
  472.1 68.3 reduce-scatter.14
  542.7 68.1 reduce-scatter.12
  613.1 68.1 reduce-scatter.16
  683.6 87.9 reduce-scatter.26
  773.8 87.9 reduce-scatter.28
  864.1 87.9 reduce-scatter.24
  954.2 87.9 reduce-scatter.32
  1044.4 87.9 reduce-scatter.34
  1134.5 87.9 reduce-scatter.30
  1227.1 52.7 all-reduce.29
  1284.6 89.9 all-reduce.31
where the time goes:
time: 1390 us
  waiting for transfers between devices  830 us (60%)
  matrix products  326 us (23%)
  blocking collectives  92.1 us (7%)
  other arithmetic  79.2 us (6%)
  local copies, waits for them, and re-layouts  42.1 us (3%)
  between operations  18.2 us (1%)
    reduce_scatter x3, waiting for transfers between devices, reduce_grads(): lax.psum_scatter(grads[8].astype(jnp.bfloat16), 'dp', scatter_dimension=0...  268 us
    reduce_scatter x3, waiting for transfers between devices, reduce_grads(): lax.psum_scatter(grads[10].astype(jnp.bfloat16), 'dp', scatter_dimension=...  267 us
    dot_general x12, matrix products, dot_rows(): return jnp.dot(former, latter, preferred_element_type=jnp.float32)  97.5 us
    reduce_scatter x3, waiting for transfers between devices, reduce_grads(): lax.psum_scatter(grads[2].astype(jnp.bfloat16), 'dp', scatter_dimension=0...  93.6 us
    dot_general x12, matrix products, dot_left(): lax.dot_general(former, latter, (((0,), (0,)), ((), ())), preferred_eleme...  84.1 us
    dot_general x12, matrix products, dot_right(): lax.dot_general(former, latter, (((1,), (1,)), ((), ())), preferred_eleme...  82.8 us
    psum x1, waiting for transfers between devices, local(): lax.psum(as_sent(running), 'group')  74.4 us
    all_gather x1, waiting for transfers between devices, fetch_weights(): lax.all_gather(shards[10], 'dp', axis=0, tiled=True)  44.8 us
  transfers between devices with their start and end apart: 18, of which 12 were waited for; matrix products, arithmetic and copies ran while one was open for 24% of the time, Pallas kernels for 0%

commit v1 on v0

--- a/solution.py
+++ b/solution.py
@@ -172,117 +172,98 @@
         reduce_bias,
     )
     micro_count, seq_count, slot_count, width = layer_input.shape
-    row_count = seq_count * slot_count
-    running = None
-    outputs = []
-    input_grads = []
+    row_count = micro_count * seq_count * slot_count
+    seq_total = micro_count * seq_count
     slot_ids = jnp.arange(slot_count, dtype=jnp.int32)
-    for micro_idx in range(micro_count):
-        gathered = fetch_weights(shards)
-        valid_grid = (slot_ids[None, :] < lengths[micro_idx][:, None]).astype(jnp.float32)
-        row_valid = valid_grid.reshape(row_count, 1)
-        key_valid = valid_grid[:, None, None, :] > 0
-        masked = layer_input[micro_idx].reshape(row_count, width).astype(jnp.float32) * row_valid
-        normed, norm_one_back = jax.vjp(
-            layer_norm, masked, gathered[0].astype(jnp.float32), gathered[1].astype(jnp.float32)
-        )
-        normed = normed.astype(jnp.bfloat16)
-        bias_pair = gathered[3].astype(jnp.float32)
-        full_bias = jnp.concatenate(
-            [bias_pair[:width], jnp.zeros((width,), jnp.float32), bias_pair[width:]]
-        )
-        packed = (dot_rows(normed, gathered[2]) + full_bias).astype(jnp.bfloat16)
-        packed = packed.reshape(seq_count, slot_count, 3, H, E)
-        queries = packed[:, :, 0]
-        keys = packed[:, :, 1]
-        values = packed[:, :, 2]
-        probs, log_sum = attend_forward(queries, keys, key_valid)
-        mixed = jnp.einsum(
-            "shqk,skhe->sqhe",
-            probs.astype(jnp.bfloat16),
-            values,
-            preferred_element_type=jnp.float32,
-        )
-        mixed = mixed.reshape(row_count, width).astype(jnp.bfloat16)
-        resid = masked + dot_rows(mixed, gathered[4]) + gathered[5].astype(jnp.float32)
-        normed_two, norm_two_back = jax.vjp(
-            layer_norm, resid, gathered[6].astype(jnp.float32), gathered[7].astype(jnp.float32)
-        )
-        normed_two = normed_two.astype(jnp.bfloat16)
-        hidden = dot_rows(normed_two, gathered[8]) + gathered[9].astype(jnp.float32)
-        activated, gelu_back = jax.vjp(exact_gelu, hidden)
-        activated = activated.astype(jnp.bfloat16)
-        result = (
-            resid + dot_rows(activated, gathered[10]) + gathered[11].astype(jnp.float32)
-        ) * row_valid
-        outputs.append(result.reshape(seq_count, slot_count, width))
-        back_weights = (
-            lax.all_gather(shards[0], "dp", axis=0, tiled=True),
-            lax.all_gather(shards[1], "dp", axis=0, tiled=True),
-            lax.all_gather(shards[2], "dp", axis=0, tiled=True),
-            lax.all_gather(shards[3], "dp", axis=0, tiled=True),
-            lax.all_gather(shards[4], "dp", axis=0, tiled=True),
-            lax.all_gather(shards[5], "dp", axis=0, tiled=True),
-            lax.all_gather(shards[6], "dp", axis=0, tiled=True),
-            lax.all_gather(shards[7], "dp", axis=0, tiled=True),
-            lax.all_gather(shards[8], "dp", axis=0, tiled=True),
-            lax.all_gather(shards[9], "dp", axis=0, tiled=True),
-            lax.all_gather(shards[10], "dp", axis=0, tiled=True),
-            lax.all_gather(shards[11], "dp", axis=0, tiled=True),
-        )
-        upstream = cotangent[micro_idx].reshape(row_count, width).astype(jnp.float32) * row_valid
-        up_low = upstream.astype(jnp.bfloat16)
-        grad_reduce_w = dot_left(activated, up_low)
-        grad_reduce_b = jnp.sum(up_low, 0, dtype=jnp.float32)
-        (grad_hidden,) = gelu_back(dot_right(up_low, back_weights[10]))
-        hidden_low = grad_hidden.astype(jnp.bfloat16)
-        grad_expand_w = dot_left(normed_two, hidden_low)
-        grad_expand_b = jnp.sum(hidden_low, 0, dtype=jnp.float32)
-        grad_resid_norm, grad_feed_gain, grad_feed_bias = norm_two_back(
-            dot_right(hidden_low, back_weights[8])
-        )
-        grad_resid = upstream + grad_resid_norm
-        branch_low = grad_resid.astype(jnp.bfloat16)
-        grad_output_w = dot_left(mixed, branch_low)
-        grad_output_b = jnp.sum(branch_low, 0, dtype=jnp.float32)
-        grad_mixed = dot_right(branch_low, back_weights[4]).astype(jnp.bfloat16)
-        grad_mixed = grad_mixed.reshape(seq_count, slot_count, H, E)
-        grad_queries, grad_keys, grad_values = attend_backward(
-            queries, keys, values, log_sum, key_valid, grad_mixed
-        )
-        grad_packed = jnp.stack([grad_queries, grad_keys, grad_values], 2).astype(jnp.bfloat16)
-        grad_packed = grad_packed.reshape(row_count, 3 * width)
-        grad_project_w = dot_left(normed, grad_packed)
-        column_sums = jnp.sum(grad_packed, 0, dtype=jnp.float32)
-        grad_project_b = jnp.concatenate([column_sums[:width], column_sums[2 * width :]])
-        grad_in_norm, grad_attend_gain, grad_attend_bias = norm_one_back(
-            dot_right(grad_packed, back_weights[2])
-        )
-        input_grads.append(
-            ((grad_resid + grad_in_norm) * row_valid).reshape(seq_count, slot_count, width)
-        )
-        grads = (
-            grad_attend_gain,
-            grad_attend_bias,
-            grad_project_w,
-            grad_project_b,
-            grad_output_w,
-            grad_output_b,
-            grad_feed_gain,
-            grad_feed_bias,
-            grad_expand_w,
-            grad_expand_b,
-            grad_reduce_w,
-            grad_reduce_b,
-        )
-        grads = reduce_grads(grads)
-        running = grads if running is None else jax.tree.map(jnp.add, running, grads)
+    gathered = fetch_weights(shards)
+    valid_grid = (slot_ids[None, :] < lengths.reshape(-1)[:, None]).astype(jnp.float32)
+    row_valid = valid_grid.reshape(row_count, 1)
+    key_valid = valid_grid[:, None, None, :] > 0
+    masked = layer_input.reshape(row_count, width).astype(jnp.float32) * row_valid
+    normed, norm_one_back = jax.vjp(
+        layer_norm, masked, gathered[0].astype(jnp.float32), gathered[1].astype(jnp.float32)
+    )
+    normed = normed.astype(jnp.bfloat16)
+    bias_pair = gathered[3].astype(jnp.float32)
+    full_bias = jnp.concatenate(
+        [bias_pair[:width], jnp.zeros((width,), jnp.float32), bias_pair[width:]]
+    )
+    packed = (dot_rows(normed, gathered[2]) + full_bias).astype(jnp.bfloat16)
+    packed = packed.reshape(seq_total, slot_count, 3, H, E)
+    queries = packed[:, :, 0]
+    keys = packed[:, :, 1]
+    values = packed[:, :, 2]
+    probs, log_sum = attend_forward(queries, keys, key_valid)
+    mixed = jnp.einsum(
+        "shqk,skhe->sqhe",
+        probs.astype(jnp.bfloat16),
+        values,
+        preferred_element_type=jnp.float32,
+    )
+    mixed = mixed.reshape(row_count, width).astype(jnp.bfloat16)
+    resid = masked + dot_rows(mixed, gathered[4]) + gathered[5].astype(jnp.float32)
+    normed_two, norm_two_back = jax.vjp(
+        layer_norm, resid, gathered[6].astype(jnp.float32), gathered[7].astype(jnp.float32)
+    )
+    normed_two = normed_two.astype(jnp.bfloat16)
+    hidden = dot_rows(normed_two, gathered[8]) + gathered[9].astype(jnp.float32)
+    activated, gelu_back = jax.vjp(exact_gelu, hidden)
+    activated = activated.astype(jnp.bfloat16)
+    result = (
+        resid + dot_rows(activated, gathered[10]) + gathered[11].astype(jnp.float32)
+    ) * row_valid
+    layer_output = result.reshape(layer_input.shape)
+    back_weights = gathered
+    upstream = cotangent.reshape(row_count, width).astype(jnp.float32) * row_valid
+    up_low = upstream.astype(jnp.bfloat16)
+    grad_reduce_w = dot_left(activated, up_low)
+    grad_reduce_b = jnp.sum(up_low, 0, dtype=jnp.float32)
+    (grad_hidden,) = gelu_back(dot_right(up_low, back_weights[10]))
+    hidden_low = grad_hidden.astype(jnp.bfloat16)
+    grad_expand_w = dot_left(normed_two, hidden_low)
+    grad_expand_b = jnp.sum(hidden_low, 0, dtype=jnp.float32)
+    grad_resid_norm, grad_feed_gain, grad_feed_bias = norm_two_back(
+        dot_right(hidden_low, back_weights[8])
+    )
+    grad_resid = upstream + grad_resid_norm
+    branch_low = grad_resid.astype(jnp.bfloat16)
+    grad_output_w = dot_left(mixed, branch_low)
+    grad_output_b = jnp.sum(branch_low, 0, dtype=jnp.float32)
+    grad_mixed = dot_right(branch_low, back_weights[4]).astype(jnp.bfloat16)
+    grad_mixed = grad_mixed.reshape(seq_total, slot_count, H, E)
+    grad_queries, grad_keys, grad_values = attend_backward(
+        queries, keys, values, log_sum, key_valid, grad_mixed
+    )
+    grad_packed = jnp.stack([grad_queries, grad_keys, grad_values], 2).astype(jnp.bfloat16)
+    grad_packed = grad_packed.reshape(row_count, 3 * width)
+    grad_project_w = dot_left(normed, grad_packed)
+    column_sums = jnp.sum(grad_packed, 0, dtype=jnp.float32)
+    grad_project_b = jnp.concatenate([column_sums[:width], column_sums[2 * width :]])
+    grad_in_norm, grad_attend_gain, grad_attend_bias = norm_one_back(
+        dot_right(grad_packed, back_weights[2])
+    )
+    input_grad = ((grad_resid + grad_in_norm) * row_valid).reshape(layer_input.shape)
+    grads = (
+        grad_attend_gain,
+        grad_attend_bias,
+        grad_project_w,
+        grad_project_b,
+        grad_output_w,
+        grad_output_b,
+        grad_feed_gain,
+        grad_feed_bias,
+        grad_expand_w,
+        grad_expand_b,
+        grad_reduce_w,
+        grad_reduce_b,
+    )
+    running = reduce_grads(grads)
     summed = jax.tree.map(
         lambda part: part.astype(jnp.float32), lax.psum(as_sent(running), "group")
     )
     return (
-        jnp.stack(outputs),
-        jnp.stack(input_grads),
+        layer_output,
+        input_grad,
         summed[0],
         summed[1],
         summed[2],

time: 1390 us -> 830 us (0.60)
  waiting for transfers between devices: 830 us -> 260 us
  matrix products: 326 us -> 244 us
  local copies, waits for them, and re-layouts: 42.1 us -> 97.4 us
  blocking collectives: 92.1 us -> 120 us
    reduce_scatter x3 -> x1, waiting for transfers between devices: 268 us -> 85.4 us  [reduce_grads(): lax.psum_scatter(grads[8].astype(jnp.bfloat16), 'dp', scatter_dimension=0...]
    reduce_scatter x3 -> x1, waiting for transfers between devices: 267 us -> 90.3 us  [reduce_grads(): lax.psum_scatter(grads[10].astype(jnp.bfloat16), 'dp', scatter_dimension=...]
    reduce_scatter x3 -> x1, waiting for transfers between devices: 93.6 us -> 0.01 us  [reduce_grads(): lax.psum_scatter(grads[2].astype(jnp.bfloat16), 'dp', scatter_dimension=0...]
    psum x1, waiting for transfers between devices: 74.4 us -> 24.8 us  [local(): lax.psum(as_sent(running), 'group')]
    dot_general x12 -> x4, matrix products: 97.5 us -> 48.8 us  [dot_rows(): return jnp.dot(former, latter, preferred_element_type=jnp.float32)]
    dot_general x12 -> x4, matrix products: 84.1 us -> 42.1 us  [dot_left(): lax.dot_general(former, latter, (((0,), (0,)), ((), ())), preferred_eleme...]
    all_gather x1, waiting for transfers between devices: 40.2 us -> 0.01 us  [fetch_weights(): lax.all_gather(shards[8], 'dp', axis=0, tiled=True)]
    unnamed x19 -> x9, waiting for transfers between devices: 41.5 us -> 2.66 us
  transfers between devices with their start and end apart: 18 -> 9, of which waited for: 12 -> 4; matrix products, arithmetic and copies ran while one was open for 24% -> 41% of each run, Pallas kernels for 0% -> 0%
where the time goes in v1:
time: 830 us; the launch traced here: 824 us
  waiting for transfers between devices  260 us (31%)
  matrix products  244 us (29%)
  blocking collectives  120 us (14%)
  local copies, waits for them, and re-layouts  97.4 us (12%)
  other arithmetic  85.1 us (10%)
  between operations  16.7 us (2%)
    reduce_scatter x1, waiting for transfers between devices, reduce_grads(): lax.psum_scatter(grads[10].astype(jnp.bfloat16), 'dp', scatter_dimension=...  90.3 us
    reduce_scatter x1, waiting for transfers between devices, reduce_grads(): lax.psum_scatter(grads[8].astype(jnp.bfloat16), 'dp', scatter_dimension=0...  85.4 us
    dot_general x4, matrix products, dot_right(): lax.dot_general(former, latter, (((1,), (1,)), ((), ())), preferred_eleme...  80.3 us
    all_gather x1, waiting for transfers between devices, fetch_weights(): lax.all_gather(shards[10], 'dp', axis=0, tiled=True)  57.3 us
    dot_general x4, matrix products, dot_rows(): return jnp.dot(former, latter, preferred_element_type=jnp.float32)  48.8 us
    dot_general x4, matrix products, dot_left(): lax.dot_general(former, latter, (((0,), (0,)), ((), ())), preferred_eleme...  42.1 us
    convert_element_type x2, local copies, waits for them, and re-layouts, local(): jnp.stack([grad_queries, grad_keys, grad_values], 2).astype(jnp.bfloat16)  27.5 us
    unnamed x132, local copies, waits for them, and re-layouts  27.3 us
  transfers between devices with their start and end apart: 9, of which 4 were waited for; matrix products, arithmetic and copies ran while one was open for 41% of the time, Pallas kernels for 0%

profile of v1, /device:TPU:0, one launch (start us, length us, event | category | flops | bytes accessed | tf_op | source)
XLA Modules:
  0.0 824.4 jit_solution(13261429398778242166)
XLA Ops:
  10.7 13.5 %all-gather = bf16[8,1,128]{2,1,0:T(2,128)(2,1)S(1)} all-gather(bf16[1,1,128]{2,1,0:T(2,128)(2,1)} %bitcast.131), channel_id=1, replica_groups=mesh['group'=4,'dp'=8] {'dp'}, dimensions={0}, use_global_device_ids=true | all-gather | bytes 2304 | tf_op jit(solution)/shard_map/all_gather | solution.py:50
  33.2 10.2 %all-gather.2 = bf16[8,1,256]{2,1,0:T(2,128)(2,1)S(1)} all-gather(bf16[1,1,256]{2,1,0:T(2,128)(2,1)S(1)} %reshape.268), channel_id=1, replica_groups=mesh['group'=4,'dp'=8] {'dp'}, dimensions={0}, use_global_device_ids=true | all-gather | bytes 4608 | tf_op jit(solution)/shard_map/all_gather | solution.py:53
  47.8 9.6 %all-gather.3 = bf16[8,1,128]{2,1,0:T(2,128)(2,1)S(1)} all-gather(bf16[1,1,128]{2,1,0:T(2,128)(2,1)S(1)} %bitcast.134), channel_id=1, replica_groups=mesh['group'=4,'dp'=8] {'dp'}, dimensions={0}, use_global_device_ids=true | all-gather | bytes 2304 | tf_op jit(solution)/shard_map/all_gather | solution.py:55
  57.4 11.1 %all-gather.4 = bf16[8,1,128]{2,1,0:T(2,128)(2,1)S(1)} all-gather(bf16[1,1,128]{2,1,0:T(2,128)(2,1)S(1)} %bitcast.135), channel_id=1, replica_groups=mesh['group'=4,'dp'=8] {'dp'}, dimensions={0}, use_global_device_ids=true | all-gather | bytes 2304 | tf_op jit(solution)/shard_map/all_gather | solution.py:56
  77.3 12.8 %all-gather.6 = bf16[8,1,512]{2,1,0:T(2,128)(2,1)S(1)} all-gather(bf16[1,1,512]{2,1,0:T(2,128)(2,1)S(1)} %reshape.276), channel_id=1, replica_groups=mesh['group'=4,'dp'=8] {'dp'}, dimensions={0}, use_global_device_ids=true | all-gather | bytes 9216 | tf_op jit(solution)/shard_map/all_gather | solution.py:59
  95.0 12.0 %add_convert_fusion.1 = bf16[960,3072]{1,0:T(8,128)(2,1)} fusion(f32[3072]{0:T(1024)S(1)} %pad_maximum_fusion, bf16[1024,3072]{1,0:T(8,128)(2,1)} %all-gather.13.cloned.1.call-done, f32[960,1024]{1,0:T(8,128)} %get-tuple-element.101, f32[1024]{0:T(1024)S(1)} %bitcast.124, f32[1024]{0:T(1024)S(1)} %bitcast.116, f32[960]{0:T(1024)S(1)} %rsqrt.23, ...), kind=kOutput, calls=%fused_computation.28 | convolution fusion | flops 6050611200 | bytes 16150016 | tf_op jit(solution)/shard_map/dot_general | solution.py:33
  107.0 15.2 %reshape.298 = bf16[3,320,3,16,64]{4,3,2,1,0:T(8,128)(2,1)} reshape(bf16[960,3072]{1,0:T(8,128)(2,1)} %add_convert_fusion.1) | data formatting | bytes 11796480 | tf_op jit(solution)/shard_map/reshape | solution.py:192
  148.0 12.9 %fusion.12 = (f32[3,16,320]{2,1,0:T(8,128)S(1)}, f32[3,16,320,320]{2,3,1,0:T(8,128)}) fusion(pred[3,320]{1,0:T(4,128)(4,1)S(1)} %get-tuple-element.102, bf16[3,320,1,16,64]{1,4,3,0,2:T(8,128)(2,1)} %copy.80, bf16[3,320,1,16,64]{1,4,3,0,2:T(8,128)(2,1)S(1)} %copy.79), kind=kOutput, calls=%fused_computation.30 | convolution fusion | flops 643875840 | bytes 23655360 | tf_op jit(solution)/shard_map/sqhe,skhe->shqk/dot_general | solution.py:107
  160.9 11.1 %fusion = f32[3,16,320]{2,1,0:T(8,128)S(1)} fusion(f32[3,16,320]{2,1,0:T(8,128)S(1)} %get-tuple-element.104, f32[3,16,320,320]{2,3,1,0:T(8,128)} %get-tuple-element.105, pred[3,320]{1,0:T(4,128)(4,1)S(1)} %get-tuple-element.102), kind=kLoop, calls=%fused_computation.7 | loop fusion | flops 19645440 | bytes 19784640 | tf_op jit(solution)/shard_map/reduce_sum | solution.py:117
  172.0 11.4 %convert_bitcast_fusion = bf16[3,320,16,64]{1,3,2,0:T(8,128)(2,1)S(1)} fusion(f32[3,16,320]{2,1,0:T(8,128)S(1)} %fusion, f32[3,16,320]{2,1,0:T(8,128)S(1)} %get-tuple-element.104, f32[3,16,320,320]{2,3,1,0:T(8,128)} %get-tuple-element.105, pred[3,320]{1,0:T(4,128)(4,1)S(1)} %get-tuple-element.102, bf16[3,320,1,16,64]{1,4,3,0,2:T(8,128)(2,1)S(1)} %copy-done.12), kind=kOutput, calls=%fused_computation.66 | convolution fusion | flops 654704640 | bytes 23716800 | tf_op jit(solution)/shard_map/shqk,skhe->sqhe/dot_general | solution.py:197
  198.8 15.8 %fusion.46 = f32[960,4096]{1,0:T(8,128)} fusion(bf16[1024,4096]{1,0:T(8,128)(2,1)} %all-gather.17.cloned.1.call-done, f32[960,1024]{1,0:T(8,128)} %copy-done.8, f32[1024]{0:T(1024)S(1)} %bitcast.127, f32[1024]{0:T(1024)S(1)} %bitcast.119, f32[960]{0:T(1024)S(1)} %fusion.40, f32[960]{0:T(1024)S(1)} %broadcast_multiply_fusion.1), kind=kOutput, calls=%fused_computation.96 | convolution fusion | flops 8057978880 | bytes 28065280 | tf_op jit(solution)/shard_map/dot_general | solution.py:33
  214.7 57.3 %all-gather.19.cloned.1.call-done = bf16[4096,1024]{1,0:T(8,128)(2,1)} async-done(((bf16[512,1024]{1,0:T(8,128)(2,1)}), bf16[4096,1024]{1,0:T(8,128)(2,1)}) %all-gather.19.cloned.1.call-update) | async-done | bytes 8388624 | tf_op jit(solution)/shard_map/all_gather | solution.py:60
  272.0 49.3 %fusion.47 = (bf16[4096]{0:T(1024)(128)(2,1)}, bf16[960,4096]{1,0:T(8,128)(2,1)}, f32[960,4096]{1,0:T(8,128)}) fusion(f32[960,4096]{1,0:T(8,128)} %fusion.46, f32[4096]{0:T(1024)S(1)} %bitcast.113, bf16[960,1024]{1,0:T(8,128)(2,1)S(1)} %copy-done.18, bf16[4096,1024]{1,0:T(8,128)(2,1)} %all-gather.19.cloned.1.call-done), kind=kOutput, calls=%fused_computation.97 | convolution fusion | flops 8344039424 | bytes 49700864 | tf_op jit(solution)/shard_map/dot_general | solution.py:43
  321.3 13.0 %multiply_reduce_fusion.1 = (bf16[1024]{0:T(1024)(128)(2,1)}, f32[960]{0:T(1024)S(1)}, bf16[1024]{0:T(1024)(128)(2,1)}, f32[960,1024]{1,0:T(8,128)S(1)}) fusion(f32[960,1024]{1,0:T(8,128)S(1)} %copy-done.9, f32[960]{0:T(1024)S(1)} %copy-done.45, f32[960]{0:T(1024)S(1)} %copy-done.35, f32[1024]{0:T(1024)S(1)} %bitcast.120, ...), kind=kOutput, calls=%fused_computation.41 | convolution fusion | flops 8060924928 | bytes 24136960 | tf_op jit(solution)/shard_map/dot_general | solution.py:43
  360.5 21.4 %multiply_reduce_fusion = (f32[3,16,320]{2,1,0:T(8,128)S(1)}, f32[3,16,320,320]{2,3,1,0:T(8,128)}) fusion(f32[3,16,320]{2,1,0:T(8,128)S(1)} %copy-done.21, f32[3,16,320,320]{2,3,1,0:T(8,128)} %get-tuple-element.105, pred[3,320]{1,0:T(4,128)(4,1)S(1)} %copy-done.25, bf16[3,320,16,64]{1,3,2,0:T(8,128)(2,1)} %copy.62, ...), kind=kOutput, calls=%fused_computation.1 | convolution fusion | flops 653706240 | bytes 43377600 | tf_op jit(solution)/shard_map/sqhe,skhe->shqk/dot_general | solution.py:124
  381.8 20.5 %multiply_convert_fusion = bf16[3,16,320,320]{2,3,1,0:T(8,128)(2,1)} fusion(f32[3,16,320,320]{2,3,1,0:T(8,128)} %get-tuple-element.110, f32[3,16,320]{2,1,0:T(8,128)S(1)} %get-tuple-element.109, f32[3,16,320]{2,1,0:T(8,128)S(1)} %copy-done.21, f32[3,16,320,320]{2,3,1,0:T(8,128)} %get-tuple-element.105, pred[3,320]{1,0:T(4,128)(4,1)S(1)} %copy-done.25), kind=kLoop, calls=%fused_computation | loop fusion | flops 29491200 | bytes 49275840 | tf_op jit(solution)/shard_map/convert_element_type | solution.py:131
  402.4 9.7 %multiply_bitcast_fusion = bf16[3,320,1,16,64]{1,4,3,0,2:T(8,128)(2,1)} fusion(bf16[3,16,320,320]{2,3,1,0:T(8,128)(2,1)} %multiply_convert_fusion, bf16[3,320,1,16,64]{1,4,3,0,2:T(8,128)(2,1)S(1)} %copy-done.6), kind=kOutput, calls=%fused_computation.36 | convolution fusion | flops 631111680 | bytes 13762560 | tf_op jit(solution)/shard_map/shqk,sqhe->skhe/dot_general | solution.py:137
  418.9 10.8 %fusion.28 = bf16[3,320,1,16,64]{1,4,3,0,2:T(8,128)(2,1)S(1)} fusion(bf16[3,320,16,64]{1,3,2,0:T(8,128)(2,1)S(1)} %copy-done.14, f32[3,16,320]{2,1,0:T(8,128)S(1)} %copy-done.21, f32[3,16,320,320]{2,3,1,0:T(8,128)} %get-tuple-element.105, pred[3,320]{1,0:T(4,128)(4,1)S(1)} %copy-done.25), kind=kOutput, calls=%fused_computation.67 | convolution fusion | flops 648806400 | bytes 23655360 | tf_op jit(solution)/shard_map/shqk,sqhe->skhe/dot_general | solution.py:127
  431.4 9.2 %copy.67 = bf16[3,320,3,16,64]{1,0,4,3,2:T(4,128)(2,1)} copy(bf16[3,320,3,16,64]{1,4,3,0,2:T(8,128)(2,1)S(1)} %get-tuple-element.88) | data formatting | bytes 11796480 | tf_op jit(solution)/shard_map/convert_element_type | solution.py:237
  440.6 18.3 %convert_element_type.252 = bf16[960,3072]{0,1:T(8,128)(2,1)} reshape(bf16[3,320,3,16,64]{1,0,4,3,2:T(4,128)(2,1)} %copy.67) | data formatting | bytes 11796480 | tf_op jit(solution)/shard_map/convert_element_type | solution.py:237
  458.9 11.4 %convolution_convert_fusion.2 = bf16[1024,3072]{1,0:T(8,128)(2,1)} fusion(bf16[960,1024]{1,0:T(8,128)(2,1)S(1)} %bitcast.112, bf16[960,3072]{0,1:T(8,128)(2,1)} %convert_element_type.252), kind=kOutput, calls=%fused_computation.35 | convolution fusion | flops 6042943488 | bytes 14155776 | tf_op jit(solution)/shard_map/dot_general | solution.py:37
  471.1 15.6 %convolution_convert_fusion.1 = bf16[1024,4096]{1,0:T(8,128)(2,1)} fusion(bf16[960,4096]{1,0:T(8,128)(2,1)} %get-tuple-element.83, f32[960,1024]{1,0:T(8,128)} %copy-done.8, f32[1024]{0:T(1024)S(1)} %bitcast.128, f32[1024]{0:T(1024)S(1)} %bitcast.122, f32[960]{0:T(1024)S(1)} %copy-done.45, f32[960]{0:T(1024)S(1)} %copy-done.35), kind=kOutput, calls=%fused_computation.32 | convolution fusion | flops 8062173184 | bytes 20200960 | tf_op jit(solution)/shard_map/dot_general | solution.py:37
  486.7 11.8 %multiply_convert_fusion.1 = bf16[960,4096]{1,0:T(8,128)(2,1)S(1)} fusion(f32[960,4096]{1,0:T(8,128)} %get-tuple-element.84, f32[960,4096]{1,0:T(8,128)} %fusion.46, f32[4096]{0:T(1024)S(1)} %bitcast.114), kind=kLoop, calls=%fused_computation.11 | loop fusion | flops 15728640 | bytes 39337984 | tf_op jit(solution)/shard_map/convert_element_type | solution.py:211
  501.6 11.4 %convolution_convert_fusion = bf16[4096,1024]{1,0:T(8,128)(2,1)} fusion(bf16[960,4096]{1,0:T(8,128)(2,1)S(1)} %multiply_convert_fusion.1, bf16[960,1024]{1,0:T(8,128)(2,1)S(1)} %copy-done.19), kind=kOutput, calls=%fused_computation.31 | convolution fusion | flops 8057257984 | bytes 18219008 | tf_op jit(solution)/shard_map/dot_general | solution.py:37
  516.2 9.3 %all-gather.7 = bf16[8,1,128]{2,1,0:T(2,128)(2,1)S(1)} all-gather(bf16[1,1,128]{2,1,0:T(2,128)(2,1)S(1)} %bitcast.137), channel_id=1, replica_groups=mesh['group'=4,'dp'=8] {'dp'}, dimensions={0}, use_global_device_ids=true | all-gather | bytes 2304 | tf_op jit(solution)/shard_map/all_gather | solution.py:61
  527.8 12.9 %multiply_reduce_fusion.2 = (bf16[1024]{0:T(1024)(128)(2,1)S(1)}, f32[960]{0:T(1024)S(1)}, bf16[1024]{0:T(1024)(128)(2,1)S(1)}, f32[960,1024]{1,0:T(8,128)S(1)}) fusion(f32[960]{0:T(1024)S(1)} %copy-done.41, f32[960]{0:T(1024)S(1)} %copy-done.39, f32[960]{0:T(1024)S(1)} %copy-done.27, bf16[3,1,320,1024]{3,2,1,0:T(8,128)(2,1)S(1)} %copy-done.1, ...), kind=kOutput, calls=%fused_computation.43 | convolution fusion | flops 6050608128 | bytes 22043648 | tf_op jit(solution)/shard_map/dot_general | solution.py:43
  543.8 85.4 %reduce-scatter.9.cloned.1.call-done = bf16[128,4096]{1,0:T(8,128)(2,1)} async-done(((bf16[1024,4096]{1,0:T(8,128)(2,1)}), bf16[128,4096]{1,0:T(8,128)(2,1)}) %reduce-scatter.9.cloned.1.call-update) | async-done | bytes 1048592 | tf_op jit(solution)/shard_map/reduce_scatter | solution.py:91
  629.3 90.3 %reduce-scatter.11.cloned.1.call-done = bf16[512,1024]{1,0:T(8,128)(2,1)} async-done(((bf16[4096,1024]{1,0:T(8,128)(2,1)}), bf16[512,1024]{1,0:T(8,128)(2,1)}) %reduce-scatter.11.cloned.1.call-update) | async-done | bytes 1048592 | tf_op jit(solution)/shard_map/reduce_scatter | solution.py:97
  719.6 26.0 %all-reduce.8 = (bf16[1024]{0:T(1024)(128)(2,1)S(1)}, bf16[1024]{0:T(1024)(128)(2,1)S(1)}, bf16[2048]{0:T(1024)(128)(2,1)S(1)}, bf16[1024]{0:T(1024)(128)(2,1)S(...) all-reduce(bf16[1024]{0:T(1024)(128)(2,1)S(1)} %get-tuple-element.5, ...), channel_id=2, replica_groups=mesh['group'=4,'dp'=8] {'dp'}, use_global_device_ids=true, to_apply=%region_12.13.clone | all-reduce | flops 12288 | bytes 49152
  746.2 10.1 %all-reduce.9 = (bf16[128]{0:T(256)(128)(2,1)S(1)}, bf16[128]{0:T(256)(128)(2,1)S(1)}, bf16[256]{0:T(256)(128)(2,1)S(1)}, bf16[128]{0:T(256)(128)(2,1)S(1)}, bf1...) all-reduce(bf16[128]{0:T(256)(128)(2,1)S(1)} %dynamic-slice.1, ...), channel_id=1, replica_groups=mesh['group'=4,'dp'=8] {'group'}, use_global_device_ids=true, to_apply=%region_13.14 | all-reduce | flops 1536 | bytes 6144 | tf_op jit(solution)/shard_map/psum | solution.py:262
  769.4 15.0 %add_multiply_fusion.1 = f32[960,1024]{1,0:T(8,128)} fusion(f32[960,1024]{1,0:T(8,128)S(1)} %copy-done.10, f32[1024]{0:T(1024)S(1)} %bitcast.129, f32[960]{0:T(1024)S(1)} %copy-done.27, bf16[960,4096]{1,0:T(8,128)(2,1)} %copy-done.15, bf16[4096,1024]{1,0:T(8,128)(2,1)} %all-gather.19.cloned.1.call-done), kind=kOutput, calls=%fused_computation.48 | convolution fusion | flops 8056012800 | bytes 24125184 | tf_op jit(solution)/shard_map/dot_general | solution.py:33
  784.3 24.8 %all-reduce.13.cloned.1.call-done = (bf16[128,3072]{1,0:T(8,128)(2,1)}, bf16[128,1024]{1,0:T(8,128)(2,1)}, bf16[128,4096]{1,0:T(8,128)(2,1)}, bf16[512,1024]{1,0:T(8,128)(2,1)}) async-done(((bf16[128,3072]{1,0:T(8,128)(2,1)}, bf16[128,1024]{1,0:T(8,128)(2,1)}, bf16[128,4096]{1,0:T(8,128)(2,1)}, bf16[512,1024]{1,0:T(8,128)(2,1)}), (bf16[128,3072]{1,0:T(8,128)(2,1)}, bf16[128,1024]{1,0:T(8,128)(2,1)}, ...) | async-done | bytes 3145744 | tf_op jit(solution)/shard_map/psum | solution.py:262
  (218 shorter events, 138.7 us)
Async XLA Ops:
  7.2 37.0 %copy-start = (bf16[3,1,320,1024]{3,2,1,0:T(8,128)(2,1)S(1)}, bf16[3,1,320,1024]{3,2,1,0:T(8,128)(2,1)}, u32[]{:S(2)}) copy-start(bf16[3,1,320,1024]{3,2,1,0:T(8,128)(2,1)} %param.15) | copy-start | bytes 5898244
  7.2 87.7 %all-gather.13.cloned.1.call-start = ((), (), s32[]{:S(2)}) async-start(), calls=%async_computation.4 | async-start | bytes 7077888 | tf_op jit(solution)/shard_map/all_gather | solution.py:52
  7.9 181.8 %all-gather.15.cloned.1.call-start = ((), (), s32[]{:S(2)}) async-start(), calls=%async_computation.5 | async-start | bytes 2359296 | tf_op jit(solution)/shard_map/all_gather | solution.py:54
  8.7 190.2 %all-gather.17.cloned.1.call-start = ((), (), s32[]{:S(2)}) async-start(), calls=%async_computation.6 | async-start | bytes 9437184 | tf_op jit(solution)/shard_map/all_gather | solution.py:58
  9.4 262.5 %all-gather.19.cloned.1.call-start = ((), (), s32[]{:S(2)}) async-start(), calls=%async_computation.7 | async-start | bytes 9437184 | tf_op jit(solution)/shard_map/all_gather | solution.py:60
  10.0 533.8 %reduce-scatter.7.cloned.1.call-start = ((), (), s32[]{:S(2)}) async-start(), calls=%async_computation.9 | async-start | bytes 2359296 | tf_op jit(solution)/shard_map/reduce_scatter | solution.py:79
  24.2 70.7 %copy-start.30 = (f32[8,1,128]{2,1,0:T(1,128)}, f32[8,1,128]{2,1,0:T(1,128)S(1)}, u32[]{:S(2)}) copy-start(f32[8,1,128]{2,1,0:T(1,128)S(1)} %convert_element_type.281) | copy-start | bytes 12292
  44.2 127.9 %copy-start.24 = (pred[3,320]{1,0:T(4,128)(4,1)}, pred[3,320]{1,0:T(4,128)(4,1)S(1)}, u32[]{:S(2)}) copy-start(pred[3,320]{1,0:T(4,128)(4,1)S(1)} %get-tuple-element.102) | copy-start | bytes 2884
  44.2 24.4 %copy-start.55 = (bf16[128]{0:T(256)(128)(2,1)S(1)}, bf16[128]{0:T(256)(128)(2,1)}, u32[]{:S(2)}) copy-start(bf16[128]{0:T(256)(128)(2,1)} %param.24) | copy-start | bytes 772
  47.7 47.2 %copy-start.26 = (f32[960]{0:T(1024)}, f32[960]{0:T(1024)S(1)}, u32[]{:S(2)}) copy-start(f32[960]{0:T(1024)S(1)} %reshape.262) | copy-start | bytes 11524
  47.8 47.1 %copy-start.38 = (f32[960]{0:T(1024)}, f32[960]{0:T(1024)S(1)}, u32[]{:S(2)}) copy-start(f32[960]{0:T(1024)S(1)} %div.47) | copy-start | bytes 11524
  68.5 130.3 %copy-start.42 = (f32[8,1,128]{2,1,0:T(1,128)}, f32[8,1,128]{2,1,0:T(1,128)S(1)}, u32[]{:S(2)}) copy-start(f32[8,1,128]{2,1,0:T(1,128)S(1)} %convert_element_type.285) | copy-start | bytes 12292
  77.2 121.6 %copy-start.48 = (f32[8,1,128]{2,1,0:T(1,128)}, f32[8,1,128]{2,1,0:T(1,128)S(1)}, u32[]{:S(2)}) copy-start(f32[8,1,128]{2,1,0:T(1,128)S(1)} %convert_element_type.286) | copy-start | bytes 12292
  141.5 19.4 %copy-start.5 = (bf16[3,320,1,16,64]{1,4,3,0,2:T(8,128)(2,1)}, bf16[3,320,1,16,64]{1,4,3,0,2:T(8,128)(2,1)S(1)}, u32[]{:S(2)}) copy-start(bf16[3,320,1,16,64]{1,4,3,0,2:T(8,128)(2,1)S(1)} %copy.79) | copy-start | bytes 5898244
  195.7 18.9 %copy-start.34 = (f32[960]{0:T(1024)}, f32[960]{0:T(1024)S(1)}, u32[]{:S(2)}) copy-start(f32[960]{0:T(1024)S(1)} %broadcast_multiply_fusion.1) | copy-start | bytes 11524
  198.8 73.1 %copy-start.18 = (bf16[960,1024]{1,0:T(8,128)(2,1)S(1)}, bf16[960,1024]{1,0:T(8,128)(2,1)}, u32[]{:S(2)}) copy-start(bf16[960,1024]{1,0:T(8,128)(2,1)} %get-tuple-element.100) | copy-start | bytes 5898244
  272.0 49.3 %copy-start.9 = (f32[960,1024]{1,0:T(8,128)S(1)}, f32[960,1024]{1,0:T(8,128)}, u32[]{:S(2)}) copy-start(f32[960,1024]{1,0:T(8,128)} %copy-done.8) | copy-start | bytes 11796484
  272.0 49.3 %copy-start.35 = (f32[960]{0:T(1024)S(1)}, f32[960]{0:T(1024)}, u32[]{:S(2)}) copy-start(f32[960]{0:T(1024)} %copy-done.34) | copy-start | bytes 11524
  272.0 49.3 %copy-start.43 = (f32[8,1,128]{2,1,0:T(1,128)S(1)}, f32[8,1,128]{2,1,0:T(1,128)}, u32[]{:S(2)}) copy-start(f32[8,1,128]{2,1,0:T(1,128)} %copy-done.42) | copy-start | bytes 12292
  272.0 49.3 %copy-start.45 = (f32[960]{0:T(1024)S(1)}, f32[960]{0:T(1024)}, u32[]{:S(2)}) copy-start(f32[960]{0:T(1024)} %copy-done.44) | copy-start | bytes 11524
  272.0 49.3 %copy-start.57 = (bf16[1024,4096]{1,0:T(8,128)(2,1)S(1)}, bf16[1024,4096]{1,0:T(8,128)(2,1)}, u32[]{:S(2)}) copy-start(bf16[1024,4096]{1,0:T(8,128)(2,1)} %all-gather.17.cloned.1.call-done) | copy-start | bytes 25165828
  342.8 201.0 %reduce-scatter.5.cloned.1.call-start = ((), (), s32[]{:S(2)}) async-start(), calls=%async_computation.8 | async-start | bytes 7077888 | tf_op jit(solution)/shard_map/reduce_scatter | solution.py:73
  381.8 20.5 %copy-start.6 = (bf16[3,320,1,16,64]{1,4,3,0,2:T(8,128)(2,1)S(1)}, bf16[3,320,1,16,64]{1,4,3,0,2:T(8,128)(2,1)}, u32[]{:S(2)}) copy-start(bf16[3,320,1,16,64]{1,4,3,0,2:T(8,128)(2,1)} %copy-done.5) | copy-start | bytes 5898244
  470.4 158.9 %reduce-scatter.9.cloned.1.call-start = ((), (), s32[]{:S(2)}) async-start(), calls=%async_computation.10 | async-start | bytes 9437184 | tf_op jit(solution)/shard_map/reduce_scatter | solution.py:91
  486.7 232.9 %reduce-scatter.11.cloned.1.call-start = ((), (), s32[]{:S(2)}) async-start(), calls=%async_computation.11 | async-start | bytes 9437184 | tf_op jit(solution)/shard_map/reduce_scatter | solution.py:97
  513.1 296.0 %all-reduce.13.cloned.1.call-start = ((), (), s32[]{:S(2)}) async-start(), calls=%async_computation.12 | async-start | bytes 6291456 | tf_op jit(solution)/shard_map/psum | solution.py:262
  540.7 178.9 %copy-start.46 = (bf16[1024]{0:T(1024)(128)(2,1)S(1)}, bf16[1024]{0:T(1024)(128)(2,1)}, u32[]{:S(2)}) copy-start(bf16[1024]{0:T(1024)(128)(2,1)} %get-tuple-element.85) | copy-start | bytes 6148
  540.7 178.9 %copy-start.47 = (bf16[4096]{0:T(1024)(128)(2,1)S(1)}, bf16[4096]{0:T(1024)(128)(2,1)}, u32[]{:S(2)}) copy-start(bf16[4096]{0:T(1024)(128)(2,1)} %get-tuple-element.82) | copy-start | bytes 24580
  540.7 178.9 %copy-start.50 = (bf16[1024]{0:T(1024)(128)(2,1)S(1)}, bf16[1024]{0:T(1024)(128)(2,1)}, u32[]{:S(2)}) copy-start(bf16[1024]{0:T(1024)(128)(2,1)} %get-tuple-element.56) | copy-start | bytes 6148
  540.8 178.9 %copy-start.51 = (bf16[1024]{0:T(1024)(128)(2,1)S(1)}, bf16[1024]{0:T(1024)(128)(2,1)}, u32[]{:S(2)}) copy-start(bf16[1024]{0:T(1024)(128)(2,1)} %get-tuple-element.60) | copy-start | bytes 6148
  543.8 219.1 %copy-start.4 = (bf16[3,1,320,1024]{3,2,1,0:T(8,128)(2,1)S(1)}, bf16[3,1,320,1024]{3,2,1,0:T(8,128)(2,1)}, u32[]{:S(2)}) copy-start(bf16[3,1,320,1024]{3,2,1,0:T(8,128)(2,1)} %param.29) | copy-start | bytes 5898244
  543.8 219.1 %copy-start.29 = (f32[960]{0:T(1024)S(1)}, f32[960]{0:T(1024)}, u32[]{:S(2)}) copy-start(f32[960]{0:T(1024)} %copy-done.28) | copy-start | bytes 11524
  (36 other events, 313.7 us)
Sparse Core Ops, SparseCore 0:
  9.7 67.6 all-gather.12
  78.9 27.7 all-gather.14
  108.3 81.4 all-gather.16
  191.3 80.5 all-gather.18
  343.0 34.3 reduce-scatter.6
  470.5 68.4 reduce-scatter.4
  541.3 87.9 reduce-scatter.8
  631.6 87.9 reduce-scatter.10
  722.9 86.1 all-reduce.12

commit v2 on v1

v2 whole, which is shorter than its diff:
```python
import functools

import jax
import jax.numpy as jnp
from jax import lax
from jax.experimental import pallas as pl
from jax.experimental.pallas import tpu as pltpu
from jax.sharding import PartitionSpec as P

F32 = jnp.float32
BF16 = jnp.bfloat16
EPS = 1e-06
H = 16
E = 64
LANES = 128
HALF_ROOT = 2.0 ** -0.5
INV_ROOT_TAU = 0.3989422804014327
NN = (((1,), (0,)), ((), ()))
NT = (((1,), (1,)), ((), ()))
TN = (((0,), (0,)), ((), ()))


def mm(former, latter, dims=NN):
    return lax.dot_general(former, latter, dims, preferred_element_type=F32)


def params(mib):
    return pltpu.CompilerParams(vmem_limit_bytes=mib << 20, dimension_semantics=("arbitrary",))


def cost(flops, nbytes, other=0):
    return pl.CostEstimate(flops=int(flops), bytes_accessed=int(nbytes), transcendentals=int(other))


def once(shape):
    return pl.BlockSpec(shape, lambda *_: (0,) * len(shape), pipeline_mode=pl.Buffered(1))


def valid_rows(length, rows):
    return (lax.broadcasted_iota(jnp.int32, (rows, 1), 0) < length).astype(F32)


def norm_parts(values):
    centred = values - jnp.mean(values, -1, keepdims=True)
    scale = lax.rsqrt(jnp.mean(centred * centred, -1, keepdims=True) + EPS)
    return centred * scale, scale


def norm_back(unit, scale, grad, gain):
    grad_unit = grad * gain
    first = jnp.mean(grad_unit, -1, keepdims=True)
    second = jnp.mean(grad_unit * unit, -1, keepdims=True)
    return scale * (grad_unit - first - unit * second)


def column_sum(values):
    return jnp.sum(values, 0, keepdims=True)


def add_first(step, ref, value):
    @pl.when(step == 0)
    def _():
        ref[...] = value

    @pl.when(step > 0)
    def _():
        ref[...] += value


def collect(ring, pos, pieces, whole, sems):
    copies = []

    def put(source, target):
        copy = pltpu.make_async_copy(source, target, sems.at[len(copies)])
        copy.start()
        copies.append(copy)

    if not ring:
        put(pieces[0], whole)
    else:
        g, z, c = pos[0], pos[1], pos[2]
        for at in range(2):
            core = c if at == 0 else 1 - c
            own, near, far = pieces[3 * at : 3 * at + 3]
            put(own, whole.at[z, core])
            for k in range(1, Z):
                row = lax.rem(z + Z - k, Z)
                for over in range(3):
                    put(near.at[over, :, k - 1], whole.at[row, core, g ^ over])
                for part in range(2):
                    put(far.at[part, k - 1], whole.at[row, core, g ^ 3, part])
    for copy in copies:
        copy.wait()


def whole_shape(ring, pieces):
    if ring:
        return (Z, 2) + pieces[0].shape
    return pieces[0].shape


def collect_scratch(ring, pieces):
    return [
        pltpu.VMEM(whole_shape(ring, pieces), BF16),
        pltpu.SemaphoreType.DMA((32,)),
        pltpu.SemaphoreType.DMA,
    ]


def fill(ring, step, steps, pos, pieces, kept, whole, sems, sem):
    @pl.when(step == 0)
    def _():
        collect(ring, pos, pieces, whole, sems)
        pltpu.make_async_copy(whole, kept, sem).start()


def keep(step, steps, kept, whole, sem):
    @pl.when(step == steps - 1)
    def _():
        pltpu.make_async_copy(whole, kept, sem).wait()


def flat_rows(whole):
    value = whole[...]
    return value.reshape(-1, value.shape[-1])


def project_kernel(ring, count, lengths, pos, x, cot, gain, bias, weight_bias, *refs):
    pieces, (normed, packed, up, up_sum, kept, whole, sems, sem) = refs[:-8], refs[-8:]
    step = pl.program_id(0)
    fill(ring, step, count, pos, pieces, kept, whole, sems, sem)
    rows = x.shape[1]
    valid = valid_rows(lengths[step], rows)
    unit, _ = norm_parts(x[0].astype(F32) * valid)
    low = (unit * gain[...] + bias[...]).astype(BF16)
    normed[0] = low
    packed[0] = (mm(low, flat_rows(whole)) + weight_bias[...]).astype(BF16)
    upstream = cot[0].astype(F32) * valid
    up[0] = upstream.astype(BF16)
    add_first(step, up_sum, column_sum(upstream))
    keep(step, count, kept, whole, sem)


def project(ring, lengths, pos, x, cot, gain, bias, weight_bias, pieces):
    seqs, rows, width = x.shape
    wide = pieces[0].shape[-1]
    row_block = pl.BlockSpec((1, rows, width), lambda s, *_: (s, 0, 0))
    anywhere = pl.BlockSpec(memory_space=pl.ANY)
    *rest, kept = pl.pallas_call(
        functools.partial(project_kernel, ring, seqs),
        grid_spec=pltpu.PrefetchScalarGridSpec(
            num_scalar_prefetch=2,
            grid=(seqs,),
            in_specs=[
                row_block,
                row_block,
                once((1, width)),
                once((1, width)),
                once((1, wide)),
            ]
            + [anywhere] * len(pieces),
            out_specs=[
                row_block,
                pl.BlockSpec((1, rows, wide), lambda s, *_: (s, 0, 0)),
                row_block,
                pl.BlockSpec((1, width), lambda s, *_: (0, 0)),
                anywhere,
            ],
            scratch_shapes=collect_scratch(ring, pieces),
        ),
        out_shape=[
            jax.ShapeDtypeStruct(x.shape, BF16),
            jax.ShapeDtypeStruct((seqs, rows, wide), BF16),
            jax.ShapeDtypeStruct(x.shape, BF16),
            jax.ShapeDtypeStruct((1, width), F32),
            jax.ShapeDtypeStruct(whole_shape(ring, pieces), BF16),
        ],
        compiler_params=params(28),
        cost_estimate=cost(2 * seqs * rows * width * wide, seqs * rows * (4 * width + wide) * 2 + 4 * width * wide),
        name="norm_project",
    )(lengths, pos, x, cot, gain, bias, weight_bias, *pieces)
    return (*rest, kept.reshape(-1, wide))


def head_masks(rows):
    lane = lax.broadcasted_iota(jnp.int32, (rows, LANES), 1)
    return lane < E


def attend_kernel(seq, lengths, q, k, v, *refs):
    mixed, lse = refs[-2:]
    rows = q.shape[1]
    length = lengths[seq]
    key_ok = lax.broadcasted_iota(jnp.int32, (1, rows), 1) < length
    low_lane = head_masks(rows)
    for pair in range(q.shape[2] // LANES):
        at = slice(pair * LANES, (pair + 1) * LANES)
        qs, ks, vs = q[0, :, at], k[0, :, at], v[0, :, at]
        outs = []
        logs = []
        for head in range(2):
            keep = low_lane if head == 0 else ~low_lane
            qh = jnp.where(keep, qs, jnp.zeros_like(qs))
            scores = jnp.where(key_ok, mm(qh, ks, NT) * E**-0.5, -1e30)
            top = jnp.max(scores, -1, keepdims=True)
            weights = jnp.exp(scores - top)
            total = jnp.sum(weights, -1, keepdims=True)
            probs = (weights / total).astype(BF16)
            outs.append(mm(probs, vs))
            logs.append(top + jnp.log(total))
        mixed[0, :, at] = jnp.where(low_lane, outs[0], outs[1]).astype(BF16)
        lse[0, pair] = jnp.concatenate(logs, -1)


def attend(seq, lengths, packed, pairs, earlier=()):
    seqs, rows, wide = packed.shape
    width = wide // 3
    wid = pairs * LANES
    steps = width // wid
    block = lambda part: pl.BlockSpec((1, rows, wid), lambda j, *_: (seq, 0, part * steps + j))
    return pl.pallas_call(
        functools.partial(attend_kernel, seq),
        grid_spec=pltpu.PrefetchScalarGridSpec(
            num_scalar_prefetch=1,
            grid=(steps,),
            in_specs=[block(0), block(1), block(2)]
            + [pl.BlockSpec(memory_space=pl.ANY)] * len(earlier),
            out_specs=[
                pl.BlockSpec((1, rows, wid), lambda j, *_: (seq, 0, j)),
                pl.BlockSpec((1, pairs, rows, 2), lambda j, *_: (seq, j, 0, 0)),
            ],
        ),
        out_shape=[
            jax.ShapeDtypeStruct((seqs, rows, width), BF16),
            jax.ShapeDtypeStruct((seqs, width // LANES, rows, 2), F32),
        ],
        input_output_aliases={4: 0, 5: 1} if earlier else {},
        compiler_params=params(14),
        cost_estimate=cost(4 * rows * rows * width * 8, rows * wide * 3, H * rows * rows),
        name="attend",
    )(lengths, packed, packed, packed, *earlier)


def attend_back_kernel(seq, lengths, q, k, v, lse, grad, *refs):
    dq, dk, dv = refs[-3:]
    rows = q.shape[1]
    length = lengths[seq]
    key_ok = lax.broadcasted_iota(jnp.int32, (1, rows), 1) < length
    low_lane = head_masks(rows)
    for pair in range(q.shape[2] // LANES):
        at = slice(pair * LANES, (pair + 1) * LANES)
        qs, ks, vs, gs = q[0, :, at], k[0, :, at], v[0, :, at], grad[0, :, at]
        sums = []
        for head in range(2):
            keep = low_lane if head == 0 else ~low_lane
            qh = jnp.where(keep, qs, jnp.zeros_like(qs))
            gh = jnp.where(keep, gs, jnp.zeros_like(gs))
            scores = jnp.where(key_ok, mm(qh, ks, NT) * E**-0.5, -1e30)
            probs = jnp.exp(scores - lse[0, pair, :, head : head + 1])
            grad_probs = mm(gh, vs, NT)
            inner = jnp.sum(grad_probs * probs, -1, keepdims=True)
            grad_scores = (probs * (grad_probs - inner)).astype(BF16)
            sums.append(
                (
                    mm(grad_scores, ks) * E**-0.5,
                    mm(grad_scores, qs, TN) * E**-0.5,
                    mm(probs.astype(BF16), gs, TN),
                )
            )
        for ref, first, second in zip((dq, dk, dv), sums[0], sums[1]):
            ref[0, :, at] = jnp.where(low_lane, first, second).astype(BF16)


def attend_back(seq, lengths, packed, lse, grad, pairs, earlier=()):
    seqs, rows, wide = packed.shape
    width = wide // 3
    wid = pairs * LANES
    steps = width // wid
    block = lambda part: pl.BlockSpec((1, rows, wid), lambda j, *_: (seq, 0, part * steps + j))
    out = pl.BlockSpec((1, rows, wid), lambda j, *_: (seq, 0, j))
    return pl.pallas_call(
        functools.partial(attend_back_kernel, seq),
        grid_spec=pltpu.PrefetchScalarGridSpec(
            num_scalar_prefetch=1,
            grid=(steps,),
            in_specs=[
                block(0),
                block(1),
                block(2),
                pl.BlockSpec((1, pairs, rows, 2), lambda j, *_: (seq, j, 0, 0)),
                out,
            ]
            + [pl.BlockSpec(memory_space=pl.ANY)] * len(earlier),
            out_specs=[out] * 3,
        ),
        out_shape=[jax.ShapeDtypeStruct((seqs, rows, width), BF16)] * 3,
        input_output_aliases={6: 0, 7: 1, 8: 2} if earlier else {},
        compiler_params=params(16),
        cost_estimate=cost(10 * rows * rows * width * 8, rows * wide * 5, H * rows * rows),
        name="attend_back",
    )(lengths, packed, packed, packed, lse, grad, *earlier)


def branch_kernel(ring, count, lengths, pos, x, mixed, weight_bias, gain, bias, *refs):
    pieces, (resid, normed, kept, whole, sems, sem) = refs[:-6], refs[-6:]
    step = pl.program_id(0)
    fill(ring, step, count, pos, pieces, kept, whole, sems, sem)
    rows, width = x.shape[1:]
    valid = valid_rows(lengths[step], rows)
    weight = whole[..., :width].reshape(-1, width)
    total = x[0].astype(F32) * valid + mm(mixed[0], weight) + weight_bias[...]
    resid[0] = total
    unit, _ = norm_parts(total)
    normed[0] = (unit * gain[...] + bias[...]).astype(BF16)
    keep(step, count, kept, whole, sem)


def branch(ring, lengths, pos, x, mixed, weight_bias, gain, bias, pieces):
    seqs, rows, width = x.shape
    wide = pieces[0].shape[-1]
    row_block = pl.BlockSpec((1, rows, width), lambda s, *_: (s, 0, 0))
    vec = once((1, width))
    anywhere = pl.BlockSpec(memory_space=pl.ANY)
    resid, normed, kept = pl.pallas_call(
        functools.partial(branch_kernel, ring, seqs),
        grid_spec=pltpu.PrefetchScalarGridSpec(
            num_scalar_prefetch=2,
            grid=(seqs,),
            in_specs=[row_block, row_block, vec, vec, vec] + [anywhere] * len(pieces),
            out_specs=[row_block, row_block, anywhere],
            scratch_shapes=collect_scratch(ring, pieces),
        ),
        out_shape=[
            jax.ShapeDtypeStruct(x.shape, F32),
            jax.ShapeDtypeStruct(x.shape, BF16),
            jax.ShapeDtypeStruct(whole_shape(ring, pieces), BF16),
        ],
        compiler_params=params(26),
        cost_estimate=cost(2 * seqs * rows * width * width, seqs * rows * width * 10 + 4 * width * wide),
        name="branch",
    )(lengths, pos, x, mixed, weight_bias, gain, bias, *pieces)
    return resid, normed, kept.reshape(-1, wide)


def store_halves(ref, value):
    _, shards, quarters, rows, _ = ref.shape
    for shard in range(shards):
        for quarter in range(quarters):
            for half in range(2):
                at = ((shard * quarters + quarter) * 2 + half) * rows
                ref[half, shard, quarter] = value[at : at + rows]


def expand_kernel(half, seqs, order, normed, up, weight, bias, *refs):
    act, slope, grad = refs[-3:]
    rows = normed.shape[0] // seqs

    def body(s, carry):
        at = pl.ds(pl.multiple_of(s * rows, rows), rows)
        hidden = mm(normed[at, :], weight[...]) + bias[...]
        phi = 0.5 + 0.5 * lax.erf(hidden * HALF_ROOT)
        act[at, :] = (hidden * phi).astype(BF16)
        slope[at, :] = (phi + hidden * (INV_ROOT_TAU * jnp.exp(-0.5 * hidden * hidden))).astype(BF16)
        return carry

    lax.fori_loop(0, seqs, body, 0)
    store_halves(grad, mm(act[...], up[...], TN).astype(BF16))


def expand(half, seqs, order, normed, up, weight, bias, earlier=()):
    count, width = normed.shape
    hidden = bias.shape[1]
    size = hidden // 8
    column = lambda i, order: (0, order[0] * i + order[1 + half])
    skip = (weight.shape[1] - hidden) // size
    weight_column = lambda i, order: (0, skip + order[0] * i + order[1 + half])
    wide = pl.BlockSpec((count, size), column)
    shape = jax.ShapeDtypeStruct((count, hidden), BF16)
    return pl.pallas_call(
        functools.partial(expand_kernel, half, seqs),
        grid_spec=pltpu.PrefetchScalarGridSpec(
            num_scalar_prefetch=1,
            grid=(4,),
            in_specs=[
                once((count, width)),
                once((count, width)),
                pl.BlockSpec((width, size), weight_column),
                pl.BlockSpec((1, size), column),
            ]
            + [pl.BlockSpec(memory_space=pl.ANY)] * len(earlier),
            out_specs=[wide, wide, pl.BlockSpec((2, 1, 4, size // 8, width), lambda i, *_: (0, i, 0, 0, 0))],
        ),
        out_shape=[shape, shape, jax.ShapeDtypeStruct((2, 4, 4, size // 8, width), BF16)],
        input_output_aliases={5: 0, 6: 1} if earlier else {},
        compiler_params=params(24),
        cost_estimate=cost(2 * count * width * hidden, count * hidden * 2 + width * hidden * 2, count * hidden),
        name="expand_half",
    )(order, normed, up, weight, bias, *earlier)


def reduce_kernel(lengths, resid, act, weight, bias, out):
    rows = resid.shape[1]
    valid = valid_rows(lengths[pl.program_id(0)], rows)
    out[0] = (resid[0] + mm(act[0], weight[...]) + bias[...]) * valid


def reduce_out(lengths, resid, act, weight, bias):
    seqs, rows, width = resid.shape
    hidden = weight.shape[0]
    row_block = pl.BlockSpec((1, rows, width), lambda s, *_: (s, 0, 0))
    return pl.pallas_call(
        reduce_kernel,
        grid_spec=pltpu.PrefetchScalarGridSpec(
            num_scalar_prefetch=1,
            grid=(seqs,),
            in_specs=[
                row_block,
                pl.BlockSpec((1, rows, hidden), lambda s, *_: (s, 0, 0)),
                once((hidden, width)),
                once((1, width)),
            ],
            out_specs=row_block,
        ),
        out_shape=jax.ShapeDtypeStruct(resid.shape, F32),
        compiler_params=params(26),
        cost_estimate=cost(2 * seqs * rows * width * hidden, seqs * rows * (8 * width + 2 * hidden) + 2 * width * hidden),
        name="reduce_out",
    )(lengths, resid, act.reshape(seqs, rows, hidden), weight, bias)


def hidden_back_kernel(ring, seqs, pos, up, slope, *refs):
    pieces, (grad, grad_sum, kept, whole, sems, sem) = refs[:-6], refs[-6:]
    step = pl.program_id(0)
    fill(ring, step, 8, pos, pieces, kept, whole, sems, sem)
    rows = up.shape[0] // seqs
    if ring:
        block = whole[step // 2, step % 2]
    else:
        size = whole.shape[0] // 8
        block = whole[pl.ds(pl.multiple_of(step * size, size), size), :]
    weight = block.reshape(-1, block.shape[-1])

    def body(s, total):
        at = pl.ds(pl.multiple_of(s * rows, rows), rows)
        low = (mm(up[at, :], weight, NT) * slope[at, :].astype(F32)).astype(BF16)
        grad[at, :] = low
        return total + column_sum(low.astype(F32))

    grad_sum[...] = lax.fori_loop(0, seqs, body, jnp.zeros(grad_sum.shape, F32))
    keep(step, 8, kept, whole, sem)


def hidden_back(ring, seqs, pos, up, slope, pieces):
    count, width = up.shape
    hidden = slope.shape[1]
    size = hidden // 8
    wide = pl.BlockSpec((count, size), lambda i, *_: (0, i))
    anywhere = pl.BlockSpec(memory_space=pl.ANY)
    grad, grad_sum, kept = pl.pallas_call(
        functools.partial(hidden_back_kernel, ring, seqs),
        grid_spec=pltpu.PrefetchScalarGridSpec(
            num_scalar_prefetch=1,
            grid=(8,),
            in_specs=[once((count, width)), wide] + [anywhere] * len(pieces),
            out_specs=[wide, pl.BlockSpec((1, size), lambda i, *_: (0, i)), anywhere],
            scratch_shapes=collect_scratch(ring, pieces),
        ),
        out_shape=[
            jax.ShapeDtypeStruct((count, hidden), BF16),
            jax.ShapeDtypeStruct((1, hidden), F32),
            jax.ShapeDtypeStruct(whole_shape(ring, pieces), BF16),
        ],
        compiler_params=params(22),
        cost_estimate=cost(2 * count * width * hidden, count * hidden * 4 + 4 * width * hidden),
        name="hidden_back",
    )(pos, up, slope, *pieces)
    return grad, grad_sum, kept.reshape(hidden, width)


def weight_grad_kernel(half, parts, order, inputs, *refs):
    grads, (out, picked) = refs[:parts], refs[-2:]
    step = pl.program_id(0)

    @pl.when(step == 0)
    def _():
        for i in range(4):
            size = picked.shape[1] // 4
            at = pl.multiple_of((order[0] * i + order[1 + half]) * size, size)
            picked[:, i * size : (i + 1) * size] = inputs[:, pl.ds(at, size)]

    for at, grad in enumerate(grads):

        @pl.when((step == at) | (parts == 1))
        def _(grad=grad):
            store_halves(out, mm(picked[...], grad[...], TN).astype(BF16))


def weight_grad(half, order, inputs, grads, wide, first=0, earlier=()):
    count, width = inputs.shape
    size = 1024
    if len(grads) == 1:
        spec = [pl.BlockSpec((count, size), lambda j, *_: (0, j))]
    else:
        spec = [once((count, size))] * len(grads)
    here = sum(grad.shape[1] for grad in grads)
    rows = width // 64
    return pl.pallas_call(
        functools.partial(weight_grad_kernel, half, len(grads)),
        grid_spec=pltpu.PrefetchScalarGridSpec(
            num_scalar_prefetch=1,
            grid=(here // size,),
            in_specs=[once((count, width)), *spec]
            + [pl.BlockSpec(memory_space=pl.ANY)] * len(earlier),
            out_specs=pl.BlockSpec(
                (2, 4, 4, rows, size), lambda j, *_: (0, 0, 0, 0, first // size + j)
            ),
            scratch_shapes=[pltpu.VMEM((count, width // 2), BF16)],
        ),
        out_shape=jax.ShapeDtypeStruct((2, 4, 4, rows, wide), BF16),
        input_output_aliases={2 + len(grads): 0} if earlier else {},
        compiler_params=params(20),
        cost_estimate=cost(count * width * here, count * (width + here) * 2 + width * here),
        name="weight_grad",
    )(order, inputs, *grads, *earlier)


def norm_two_kernel(lengths, hidden_grad, weight, resid, cot, gain, *outs):
    grad_resid, low_ref, mixed_grad, gain_grad, bias_grad, out_bias_grad = outs
    step = pl.program_id(0)
    rows, width = resid.shape[1:]
    valid = valid_rows(lengths[step], rows)
    grad = mm(hidden_grad[0], weight[:, width:], NT)
    unit, scale = norm_parts(resid[0])
    total = cot[0].astype(F32) * valid + norm_back(unit, scale, grad, gain[...])
    grad_resid[0] = total
    low = total.astype(BF16)
    low_ref[0] = low
    mixed_grad[0] = mm(low, weight[:, :width], NT).astype(BF16)
    add_first(step, gain_grad, column_sum(grad * unit))
    add_first(step, bias_grad, column_sum(grad))
    add_first(step, out_bias_grad, column_sum(low.astype(F32)))


def norm_two_back(lengths, hidden_grad, weight, resid, cot, gain):
    seqs, rows, width = resid.shape
    hidden = hidden_grad.shape[1]
    row_block = pl.BlockSpec((1, rows, width), lambda s, *_: (s, 0, 0))
    vec = pl.BlockSpec((1, width), lambda s, *_: (0, 0))
    return pl.pallas_call(
        norm_two_kernel,
        grid_spec=pltpu.PrefetchScalarGridSpec(
            num_scalar_prefetch=1,
            grid=(seqs,),
            in_specs=[
                pl.BlockSpec((1, rows, hidden), lambda s, *_: (s, 0, 0)),
                once((width, width + hidden)),
                row_block,
                row_block,
                once((1, width)),
            ],
            out_specs=[row_block] * 3 + [vec] * 3,
        ),
        out_shape=[
            jax.ShapeDtypeStruct(resid.shape, F32),
            jax.ShapeDtypeStruct(resid.shape, BF16),
            jax.ShapeDtypeStruct(resid.shape, BF16),
        ]
        + [jax.ShapeDtypeStruct((1, width), F32)] * 3,
        compiler_params=params(40),
        cost_estimate=cost(2 * seqs * rows * width * (hidden + width), seqs * rows * (2 * hidden + 14 * width)),
        name="norm_two_back",
    )(lengths, hidden_grad.reshape(seqs, rows, hidden), weight, resid, cot, gain)


def norm_one_kernel(lengths, dq, dk, dv, weight, x, grad_resid, gain, *outs):
    input_grad, gain_grad, bias_grad, q_sum, v_sum = outs
    step = pl.program_id(0)
    rows, width = x.shape[1:]
    valid = valid_rows(lengths[step], rows)
    grad = mm(dq[0], weight[:, :width], NT)
    grad += mm(dk[0], weight[:, width : 2 * width], NT)
    grad += mm(dv[0], weight[:, 2 * width :], NT)
    unit, scale = norm_parts(x[0].astype(F32) * valid)
    input_grad[0] = (grad_resid[0] + norm_back(unit, scale, grad, gain[...])) * valid
    add_first(step, gain_grad, column_sum(grad * unit))
    add_first(step, bias_grad, column_sum(grad))
    add_first(step, q_sum, column_sum(dq[0].astype(F32)))
    add_first(step, v_sum, column_sum(dv[0].astype(F32)))


def norm_one_back(lengths, dq, dk, dv, weight, x, grad_resid, gain):
    seqs, rows, width = x.shape
    row_block = pl.BlockSpec((1, rows, width), lambda s, *_: (s, 0, 0))
    vec = pl.BlockSpec((1, width), lambda s, *_: (0, 0))
    return pl.pallas_call(
        norm_one_kernel,
        grid_spec=pltpu.PrefetchScalarGridSpec(
            num_scalar_prefetch=1,
            grid=(seqs,),
            in_specs=[row_block] * 3
            + [once((width, 3 * width)), row_block, row_block, once((1, width))],
            out_specs=[row_block] + [vec] * 4,
        ),
        out_shape=[jax.ShapeDtypeStruct(x.shape, F32)] + [jax.ShapeDtypeStruct((1, width), F32)] * 4,
        compiler_params=params(32),
        cost_estimate=cost(6 * seqs * rows * width * width, seqs * rows * width * 16 + 6 * width * width),
        name="norm_one_back",
    )(lengths, dq, dk, dv, weight, x, grad_resid, gain)

def near_kernel(pos, *refs):
    for at in range(4):
        mine, other, out = refs[at], refs[4 + at], refs[8 + at]
        total = mine[...].astype(F32) + other[...].astype(F32)
        out[...] = total.astype(BF16).reshape(out.shape)


def near_sum(pos, own, arrived):
    _, shards, _, rows, wide = own.shape
    x = lambda pos: pos[0] % 2
    y = lambda pos: pos[0] // 2
    over_x = (1, 1, 2, 1, rows, wide)
    over_y = (1, 1, 1, 2, rows, wide)
    specs = [
        pl.BlockSpec(over_x, lambda s, pos: (0, s, 0, x(pos), 0, 0)),
        pl.BlockSpec(over_y, lambda s, pos: (1, s, y(pos), 0, 0, 0)),
        pl.BlockSpec(over_x, lambda s, pos: (0, s, 0, 1 - x(pos), 0, 0)),
        pl.BlockSpec(over_y, lambda s, pos: (1, s, 1 - y(pos), 0, 0, 0)),
    ]
    shape = (2, shards, 2, 2, rows, wide)
    return pl.pallas_call(
        near_kernel,
        grid_spec=pltpu.PrefetchScalarGridSpec(
            num_scalar_prefetch=1,
            grid=(shards,),
            in_specs=specs * 2,
            out_specs=[pl.BlockSpec((1, 2, rows, wide), lambda s, pos: (s, 0, 0, 0))] * 4,
        ),
        out_shape=[jax.ShapeDtypeStruct((shards, 2, rows, wide), BF16)] * 4,
        compiler_params=params(14),
        cost_estimate=cost(own.size, own.size * 6),
        name="near_sum",
    )(pos, *[own.reshape(shape)] * 4, *[arrived.reshape(shape)] * 4)


AXES = ("group", "dp")
Z = 4


def permutation(move):
    pairs = []
    for g in range(4):
        for d in range(2 * Z):
            to_g, to_z, to_c = move(g, d // 2, d % 2)
            pairs.append((g * 2 * Z + d, (to_g * Z + to_z) * 2 + to_c))
    return pairs


CORE = permutation(lambda g, z, c: (g, z, 1 - c))
OVER_X = permutation(lambda g, z, c: (g ^ 1, z, c))
OVER_Y = permutation(lambda g, z, c: (g ^ 2, z, c))
OVER_XY = permutation(lambda g, z, c: (g ^ 3, z, c))
OVER_Z = [permutation(lambda g, z, c, k=k: (g, (z + k) % Z, c)) for k in range(Z)]
NEAR_Z = permutation(lambda g, z, c: (g, z ^ 1, c))
FAR_Z = permutation(lambda g, z, c: (g, z ^ 2, c))


def send(array, pairs):
    return lax.ppermute(array, AXES, pairs)


def tie(value, *others):
    return lax.optimization_barrier((value,) + others)[0]


def pick(array, index, axis):
    return lax.dynamic_index_in_dim(array, index, axis, keepdims=False)


def plus(former, latter):
    return (former.astype(F32) + latter.astype(F32)).astype(BF16)


def quarters(shard, g):
    rows, wide = shard.shape
    parts = shard.reshape(4, 2, rows // 8, wide)
    return parts, pick(parts, g, 0)


def send_quarter(mine):
    return [send(mine, OVER_Z[k]) for k in range(1, Z)]


def send_xy(first, second):
    return send(first, OVER_X), send(second, OVER_Y)


def scatter_core(other):
    return send(other, CORE)


def scatter_far(first, second, from_x, from_y, g):
    x, y = g % 2, g // 2
    first = plus(first, from_x)
    second = plus(second, from_y)
    return pick(first, y, 1), pick(second, x, 1), pick(first, 1 - y, 1), pick(second, 1 - x, 1)


def scatter_z(first, second, from_y, from_x, z):
    quarter = jnp.stack([plus(first, from_y), plus(second, from_x)], 1)
    return pick(quarter, z, 0), [pick(quarter, (z + k) % Z, 0) for k in range(1, Z)]


def send_z(parts):
    return [send(part, OVER_Z[k]) for k, part in enumerate(parts, 1)]


def spread(mine, arrived):
    total = mine.astype(F32)
    for part in arrived:
        total = total + part.astype(F32)
    return total.astype(BF16)


def send_near(mine):
    return [send(mine, OVER_X), send(mine, OVER_Y), send(mine, OVER_XY)]


def placed(mine, others, g):
    grid = jnp.stack([mine, *others]).reshape(2, 2, *mine.shape)
    grid = jnp.where(g % 2 == 1, grid[:, ::-1], grid)
    grid = jnp.where(g // 2 == 1, grid[::-1], grid)
    return grid.astype(F32).reshape(-1, mine.shape[-1])


VEC = (0, 1, 3, 5, 6, 7, 9, 11)


def joined(vectors):
    total = sum(v.shape[0] for v in vectors)
    at = 0
    out = None
    for v in vectors:
        wide = lax.pad(v, jnp.zeros((), v.dtype), [(at, total - at - v.shape[0], 0)])
        out = wide if out is None else out + wide
        at += v.shape[0]
    return out


def split_vectors(everyone, shards):
    full = {}
    at = 0
    for i in VEC:
        size = shards[i].shape[0]
        full[i] = everyone[:, at : at + size].reshape(1, -1).astype(F32)
        at += size
    return full


def gather_vectors(shards):
    packed = joined([shards[i] for i in VEC])
    return lax.all_gather(packed, "dp", axis=0, tiled=False)


def reduce_vectors(grads, shards, ring, after=()):
    packed = joined([grads[i].reshape(-1) for i in VEC])
    if ring:
        total = tie(packed.reshape(-1, LANES), *after)
        for pairs in (CORE, OVER_X, OVER_Y, NEAR_Z, FAR_Z):
            total = total + send(total, pairs)
        total = total.reshape(-1)
    else:
        total = lax.psum(packed, ("group", "dp"))
    d = lax.axis_index("dp")
    at = 0
    summed = {}
    for i in VEC:
        size = shards[i].shape[0]
        summed[i] = lax.dynamic_slice(total, (at + d * size,), (size,))
        at += grads[i].size
    return summed


def plain_sum(other, own):
    wide = own.shape[-1]
    low = jnp.concatenate([a.transpose(1, 2, 0, 3, 4).reshape(-1, wide) for a in (other, own)])
    part = lax.psum_scatter(low, "dp", scatter_dimension=0, tiled=True)
    return lax.psum(part, "group").astype(F32)


def local(ring, layer_input, lengths, *rest):
    shards, cot = rest[:12], rest[12]
    micro, seqs, rows, width = layer_input.shape
    count = micro * seqs
    g = lax.axis_index("group")
    d = lax.axis_index("dp")
    z, c = d // 2, d % 2
    pos = jnp.stack([g, z, c]).astype(jnp.int32)
    order = [2, 1 - c, c] if ring else [1, 0, 4]
    order = jnp.stack([jnp.asarray(v, jnp.int32) for v in order])
    lens = lengths.reshape(-1)
    x = layer_input.reshape(count, rows, width)
    cot = cot.reshape(count, rows, width)
    flat = lambda a: a.reshape(count * rows, a.shape[-1])
    wanted = (shards[2], jnp.concatenate([shards[4], shards[8]], 1), shards[10])

    everyone = gather_vectors(shards)
    if ring:
        parts_p, mine_p = quarters(wanted[0], g)
        parts_e, mine_e = quarters(wanted[1], g)
        parts_r, mine_r = quarters(wanted[2], g)
        ring_p = send_quarter(mine_p)
        core_p, core_e = send(parts_p, CORE), send(parts_e, CORE)
        stack_p = jnp.stack(tie(ring_p, core_p, core_e, everyone), 1)
        x_p, y_p = send_xy(stack_p, stack_p)
        ring_e = send_quarter(tie(mine_e, stack_p))
        b_p, a_p = send_xy(y_p[1], x_p[0])
        near_p = tie(jnp.stack([stack_p, x_p, y_p]), a_p, b_p)
        far_p = jnp.stack([a_p, b_p])
        pieces_p = [parts_p, near_p, far_p, core_p, send(near_p, CORE), send(far_p, CORE)]
        stack_e = jnp.stack(tie(ring_e, pieces_p), 1)
        lens_project, mine_r = tie((lens, mine_r), stack_e)
        x_e, y_e = send_xy(stack_e, stack_e)
        ring_r = send_quarter(mine_r)
    else:
        pieces = [lax.all_gather(w, "dp", axis=0, tiled=True) for w in wanted]
        pieces_p, pieces_e, pieces_r = [[w] for w in pieces]
        lens_project = lens
    full = split_vectors(everyone, shards)
    project_b = jnp.concatenate(
        [full[3][:, :width], jnp.zeros((1, width), F32), full[3][:, width:]], -1
    )
    normed, packed, up, up_sum, project_w = project(
        ring, lens_project, pos, x, cot, full[0], full[1], project_b, pieces_p
    )
    mixed, lse = attend(0, lens, packed, 4)
    lens_attend = lens
    if ring:
        x_e, y_e = tie((x_e, y_e), mixed)
        near_e = jnp.stack([stack_e, x_e, y_e])
        lens_attend = tie(lens, near_e)
        b_e, a_e = send_xy(y_e[1], x_e[0])
        near_core_e, core_r = send(near_e, CORE), send(parts_r, CORE)
    for seq in range(1, count):
        mixed, lse = attend(seq, lens_attend, packed, 4, (mixed, lse))
    lens_branch = lens
    if ring:
        a_e, b_e, ring_r = tie((a_e, b_e, ring_r), mixed)
        far_e = jnp.stack([a_e, b_e])
        pieces_e = [parts_e, near_e, far_e, core_e, near_core_e, send(far_e, CORE)]
        stack_r = jnp.stack(ring_r, 1)
        lens_branch = tie(lens, stack_r)
        x_r, y_r = send_xy(stack_r, stack_r)
    resid, normed_two, joint_w = branch(
        ring, lens_branch, pos, x, mixed, full[5], full[6], full[7], pieces_e
    )
    act, slope, reduce_far = expand(
        0, count, order, flat(normed_two), flat(up), joint_w, full[9]
    )
    expand_b = full[9]
    if ring:
        x_r, y_r = tie((x_r, y_r), reduce_far)
        near_r = jnp.stack([stack_r, x_r, y_r])
        expand_b = tie(expand_b, near_r)
        b_r, a_r = send_xy(y_r[1], x_r[0])
        near_core_r, arrived = send(near_r, CORE), send(tie(reduce_far, near_r), CORE)
    act, slope, reduce_near = expand(
        1, count, order, flat(normed_two), flat(up), joint_w, expand_b, (act, slope)
    )
    up_back = up
    if ring:
        a_r, b_r = tie((a_r, b_r), reduce_near)
        far_r = jnp.stack([a_r, b_r])
        pieces_r = [parts_r, near_r, far_r, core_r, near_core_r, send(far_r, CORE)]
        rs = near_sum(pos, reduce_near, arrived)
        up_back = tie(up, rs)
        from_x, from_y = send_xy(rs[2], rs[3])
    hidden_grad, hidden_sum, reduce_w = hidden_back(
        ring, count, pos, flat(up_back), slope, pieces_r
    )
    order_far = order
    if ring:
        from_x, from_y = tie((from_x, from_y), hidden_sum)
        rs = scatter_far(rs[0], rs[1], from_x, from_y, g)
        order_far = tie(order, rs)
        from_x, from_y = send_xy(rs[3], rs[2])
    joint = 5 * width
    expand_far = weight_grad(0, order_far, flat(normed_two), (hidden_grad,), joint, width)
    lens_two = lens
    if ring:
        from_x, from_y = tie((from_x, from_y), expand_far)
        mine_z, parts_z = scatter_z(rs[0], rs[1], from_y, from_x, z)
        lens_two = tie(lens, parts_z)
        arrived_r = send_z(parts_z)
    grad_resid, branch_low, mixed_grad, gain_two_grad, bias_two_grad, output_b_grad = norm_two_back(
        lens_two, hidden_grad, joint_w, resid, cot, full[6]
    )
    joint_far = weight_grad(
        0, order, flat(mixed), (flat(branch_low),), joint, 0, (expand_far,)
    )
    order_near = order
    if ring:
        order_near = tie(order, joint_far)
        arrived = send(joint_far, CORE)
    expand_near = weight_grad(1, order_near, flat(normed_two), (hidden_grad,), joint, width)
    joint_near = weight_grad(
        1, order_near, flat(mixed), (flat(branch_low),), joint, 0, (expand_near,)
    )
    lens_back = lens
    if ring:
        arrived_r = tie(arrived_r, joint_near)
        spread_r = spread(mine_z, arrived_r)
        es = near_sum(pos, joint_near, arrived)
        lens_back = tie(lens, es, spread_r)
        from_x, from_y = send_xy(es[2], es[3])
        near_r = send_near(spread_r)
    thirds = attend_back(0, lens_back, packed, lse, mixed_grad, 2)
    for seq in range(1, count - 1):
        thirds = attend_back(seq, lens_back, packed, lse, mixed_grad, 2, thirds)
    if ring:
        from_x, from_y, near_r = tie((from_x, from_y, near_r), thirds[0])
        es = scatter_far(es[0], es[1], from_x, from_y, g)
        lens_back = tie(lens, es)
        from_x, from_y = send_xy(es[3], es[2])
    for seq in range(max(1, count - 1), count):
        thirds = attend_back(seq, lens_back, packed, lse, mixed_grad, 2, thirds)
    order_p = order
    if ring:
        from_x, from_y = tie((from_x, from_y), thirds[0])
        mine_z, parts_z = scatter_z(es[0], es[1], from_y, from_x, z)
        order_p = tie(order, parts_z)
        arrived_e = send_z(parts_z)
    thirds_flat = [flat(t) for t in thirds]
    project_far = weight_grad(0, order_p, flat(normed), thirds_flat, 3 * width)
    order_near = order
    if ring:
        order_near = tie(order, project_far)
        arrived = send(project_far, CORE)
    project_near = weight_grad(1, order_near, flat(normed), thirds_flat, 3 * width)
    lens_one = lens
    if ring:
        ps = near_sum(pos, project_near, arrived)
        lens_one = tie(lens, ps)
        from_x, from_y = send_xy(ps[2], ps[3])
    input_grad, gain_one_grad, bias_one_grad, query_sum, value_sum = norm_one_back(
        lens_one, *thirds, project_w, x, grad_resid, full[0]
    )
    lens_out = lens
    if ring:
        from_x, from_y, arrived_e = tie((from_x, from_y, arrived_e), gain_one_grad)
        ps = scatter_far(ps[0], ps[1], from_x, from_y, g)
        spread_e = spread(mine_z, arrived_e)
        lens_out = tie(lens, ps, spread_e)
        from_x, from_y = send_xy(ps[3], ps[2])
        near_e = send_near(spread_e)
    layer_output = reduce_out(lens_out, resid, act, reduce_w, full[11])
    vectors = {
        0: gain_one_grad,
        1: bias_one_grad,
        3: jnp.concatenate([query_sum, value_sum], -1),
        5: output_b_grad,
        6: gain_two_grad,
        7: bias_two_grad,
        9: hidden_sum,
        11: up_sum,
    }
    sums = {}
    if ring:
        (from_x, from_y, near_e), layer_output = lax.optimization_barrier(
            ((from_x, from_y, near_e), layer_output)
        )
        mine_z, parts_z = scatter_z(ps[0], ps[1], from_y, from_x, z)
        arrived_p = send_z(parts_z)
        sums.update(reduce_vectors(vectors, shards, ring, parts_z))
        sums[10] = placed(spread_r, near_r, g)
        joint_sum = placed(spread_e, near_e, g)
        spread_p = spread(mine_z, arrived_p)
        sums[2] = placed(spread_p, send_near(spread_p), g)
    else:
        sums.update(reduce_vectors(vectors, shards, ring))
        sums[10] = plain_sum(reduce_far, reduce_near)
        joint_sum = plain_sum(joint_far, joint_near)
        sums[2] = plain_sum(project_far, project_near)
    sums[4] = joint_sum[:, :width]
    sums[8] = joint_sum[:, width:]
    return (
        layer_output.reshape(layer_input.shape),
        input_grad.reshape(layer_input.shape),
        *[sums[i] for i in range(12)],
    )


def solution(mesh):
    ring = mesh.shape["group"] == 4 and mesh.shape["dp"] == 2 * Z
    rows = P(None, ("group", "dp"), None, None)
    vec = P("dp")
    mat = P("dp", None)
    kinds = (vec, vec, mat, vec, mat, vec, vec, vec, mat, vec, mat, vec)
    return jax.shard_map(
        functools.partial(local, ring),
        mesh=mesh,
        in_specs=(rows, P(None, ("group", "dp")), *kinds, rows),
        out_specs=(rows, rows, *kinds),
        check_vma=False,
    )
```

time: 830 us -> 475 us (0.57)
  the two profiles are of different devices: /device:TPU:0 before, /device:TPU:8 now
where the time goes in v2:
time: 475 us; the launch traced here: 466 us
  Pallas kernels  213 us (45%)
  waiting for transfers between devices  94.2 us (20%)
  starting transfers between devices  67.2 us (14%)
  local copies, waits for them, and re-layouts  39.8 us (8%)
  other arithmetic  27.8 us (6%)
  blocking collectives  22.1 us (5%)
    ppermute x68, waiting for transfers between devices, send(): return lax.ppermute(array, AXES, pairs)  94.2 us
    ppermute x68, starting transfers between devices, send(): return lax.ppermute(array, AXES, pairs)  67.2 us
    pallas_call x2, Pallas kernels, expand(): pl.pallas_call(functools.partial(expand_kernel, half, seqs), grid_spec=pl...  33.8 us
    pallas_call x3, Pallas kernels, attend_back(): pl.pallas_call(functools.partial(attend_back_kernel, seq), grid_spec=pltp...  32.8 us
    unnamed x156, local copies, waits for them, and re-layouts  30.7 us
    pallas_call x6, Pallas kernels, weight_grad(): pl.pallas_call(functools.partial(weight_grad_kernel, half, len(grads)), g...  30.5 us
    pallas_call x3, Pallas kernels, attend(): pl.pallas_call(functools.partial(attend_kernel, seq), grid_spec=pltpu.Pre...  24 us
    all_gather x1, blocking collectives, gather_vectors(): return lax.all_gather(packed, 'dp', axis=0, tiled=False)  22.1 us
  transfers between devices with their start and end apart: 68, of which 23 were waited for; matrix products, arithmetic and copies ran while one was open for 5% of the time, Pallas kernels for 40%

profile of v2, /device:TPU:8, one launch (start us, length us, event | category | flops | bytes accessed | tf_op | source)
XLA Modules:
  0.0 466.2 jit_solution(12065705217965909366)
XLA Ops:
  8.4 22.1 %all-gather.1 = bf16[8,1,1536]{2,1,0:T(2,128)(2,1)S(1)} all-gather(bf16[1,1,1536]{2,1,0:T(2,128)(2,1)S(1)} %reshape.367), channel_id=2, replica_groups=mesh['group'=4,'dp'=8] {'dp'}, dimensions={0}, use_global_device_ids=true | all-gather | bytes 27648 | tf_op jit(solution)/shard_map/all_gather | solution.py:761
  33.8 12.4 %collective-permute-done.8 = bf16[2,3,16,3072]{3,2,1,0:T(8,128)(2,1)S(1)} collective-permute-done((bf16[2,3,16,3072]{3,2,1,0:T(8,128)(2,1)S(1)}, bf16[2,3,16,3072]{3,2,1,0:T(8,128)(2,1)S(1)}, u32[]{:S(2)}, u32[]{:S(2)}) %collective-permute-start.8) | collective-permute-done | bytes 589856 | tf_op jit(solution)/shard_map/ppermute | solution.py:668
  50.9 3.9 collective-permute-done.10
  63.7 5.4 %collective-permute-done.5 = bf16[2,16,5120]{2,1,0:T(8,128)(2,1)S(1)} collective-permute-done((bf16[2,16,5120]{2,1,0:T(8,128)(2,1)}, bf16[2,16,5120]{2,1,0:T(8,128)(2,1)S(1)}, u32[]{:S(2)}, u32[]{:S(2)}) %collective-permute-start.5) | collective-permute-done | bytes 327712 | tf_op jit(solution)/shard_map/ppermute | solution.py:668
  69.1 18.3 %collective-permute-done.6 = bf16[2,16,5120]{2,1,0:T(8,128)(2,1)S(1)} collective-permute-done((bf16[2,16,5120]{2,1,0:T(8,128)(2,1)}, bf16[2,16,5120]{2,1,0:T(8,128)(2,1)S(1)}, u32[]{:S(2)}, u32[]{:S(2)}) %collective-permute-start.6) | collective-permute-done | bytes 327712 | tf_op jit(solution)/shard_map/ppermute | solution.py:668
  93.1 12.3 %norm_project.1 = (bf16[3,320,1024]{2,1,0:T(8,128)(2,1)S(1)}, bf16[3,320,3072]{2,1,0:T(8,128)(2,1)S(1)}, bf16[3,320,1024]{2,1,0:T(8,128)(2,1)S(1)}, f32[1,1024]{...) custom-call(s32[3]{0:T(128)S(1)} %bitcast.266, s32[3]{0:T(128)S(1)} %add_add_fusion.pos, ...), custom_call_target="tpu_custom_call" | custom-call | flops 6039797760 | bytes 26345472 | tf_op jit(solution)/shard_map/norm_project/pallas_call | solution.py:149
  106.6 8.0 %attend.3 = (bf16[3,320,1024]{2,1,0:T(8,128)(2,1)S(1)}, f32[3,8,320,2]{3,2,1,0:T(8,128)S(1)}) custom-call(s32[3]{0:T(128)S(1)} %bitcast.267, bf16[3,320,3072]{2,1,0:T(8,128)(2,1)S(1)} %get-tuple-element.139.q.k.v, bf16[3,320,3072]{2,1,0:T(8,128)(2,1)S(1)} %get-tuple-element.139.q.k.v, bf16[3,320,3072]{2,1,0:T(8,128)(2,1)S(1)} %get-tuple-element.139.q.k.v), custom_call_target="tpu_custom_call" | custom-call | flops 3355443200 | bytes 2949120 | tf_op jit(solution)/shard_map/attend/pallas_call | solution.py:221
  118.8 8.0 %attend.4 = (bf16[3,320,1024]{2,1,0:T(8,128)(2,1)S(1)}, f32[3,8,320,2]{3,2,1,0:T(8,128)S(1)}) custom-call(s32[3]{0:T(128)S(1)} %bitcast.268, bf16[3,320,3072]{2,1,0:T(8,128)(2,1)S(1)} %get-tuple-element.139.q.k.v, bf16[3,320,3072]{2,1,0:T(8,128)(2,1)S(1)} %get-tuple-element.139.q.k.v, ...), custom_call_target="tpu_custom_call", output_to_operand_aliasing={{0}: (4, {}), {1}: (5, {})} | custom-call | flops 3355443200 | bytes 2949120 | tf_op jit(solution)/shard_map/attend/pallas_call | solution.py:221
  129.2 8.0 %attend.5 = (bf16[3,320,1024]{2,1,0:T(8,128)(2,1)S(1)}, f32[3,8,320,2]{3,2,1,0:T(8,128)S(1)}) custom-call(s32[3]{0:T(128)S(1)} %bitcast.269, bf16[3,320,3072]{2,1,0:T(8,128)(2,1)S(1)} %get-tuple-element.139.q.k.v, bf16[3,320,3072]{2,1,0:T(8,128)(2,1)S(1)} %get-tuple-element.139.q.k.v, ...), custom_call_target="tpu_custom_call", output_to_operand_aliasing={{0}: (4, {}), {1}: (5, {})} | custom-call | flops 3355443200 | bytes 2949120 | tf_op jit(solution)/shard_map/attend/pallas_call | solution.py:221
  145.1 8.1 %branch.1 = (f32[3,320,1024]{2,1,0:T(8,128)S(1)}, bf16[3,320,1024]{2,1,0:T(8,128)(2,1)S(1)}, bf16[4,2,4,2,16,5120]{5,4,3,2,1,0:T(8,128)(2,1)}) custom-call(s32[3]{0:T(128)S(1)} %bitcast.270, s32[3]{0:T(128)S(1)} %add_add_fusion.pos, bf16[3,320,1024]{2,1,0:T(8,128)(2,1)S(1)} %bitcast.254, bf16[3,320,1024]{2,1,0:T(8,128)(2,1)S(1)} %get-tuple-element.147.mixed, ...), custom_call_target="tpu_custom_call" | custom-call | flops 2013265920 | bytes 30801920 | tf_op jit(solution)/shard_map/branch/pallas_call | solution.py:324
  155.2 16.9 %expand_half.2 = (bf16[960,4096]{1,0:T(8,128)(2,1)S(1)}, bf16[960,4096]{1,0:T(8,128)(2,1)S(1)}, bf16[2,4,4,64,1024]{4,3,2,1,0:T(8,128)(2,1)S(1)}) custom-call(s32[3]{0:T(128)S(1)} %add_add_fusion.1.order, bf16[960,1024]{1,0:T(8,128)(2,1)S(1)} %bitcast.241, bf16[960,1024]{1,0:T(8,128)(2,1)S(1)} %bitcast.256, bf16[1024,5120]{1,0:T(8,128)(2,1)} %bitcast.301, ...), custom_call_target="tpu_custom_call" | custom-call | flops 8053063680 | bytes 16252928 | tf_op jit(solution)/shard_map/expand_half/pallas_call | solution.py:379
  176.6 16.8 %expand_half.3 = (bf16[960,4096]{1,0:T(8,128)(2,1)S(1)}, bf16[960,4096]{1,0:T(8,128)(2,1)S(1)}, bf16[2,4,4,64,1024]{4,3,2,1,0:T(8,128)(2,1)S(1)}) custom-call(s32[3]{0:T(128)S(1)} %add_add_fusion.1.order, bf16[960,1024]{1,0:T(8,128)(2,1)S(1)} %bitcast.242, bf16[960,1024]{1,0:T(8,128)(2,1)S(1)} %bitcast.257, ...), custom_call_target="tpu_custom_call", output_to_operand_aliasing={{0}: (5, {}), {1}: (6, {})} | custom-call | flops 8053063680 | bytes 16252928 | tf_op jit(solution)/shard_map/expand_half/pallas_call | solution.py:379
  194.5 4.8 %near_sum.3 = (bf16[4,2,64,1024]{3,2,1,0:T(8,128)(2,1)S(1)}, bf16[4,2,64,1024]{3,2,1,0:T(8,128)(2,1)S(1)}, bf16[4,2,64,1024]{3,2,1,0:T(8,128)(2,1)}, bf16[4,2,64,1024]{3,2,1,0:T(8,128)(2,1)}) custom-call(s32[3]{0:T(128)S(1)} %add_add_fusion.pos, bf16[2,4,2,2,64,1024]{5,4,3,2,1,0:T(8,128)(2,1)S(1)} %bitcast.226, ...), custom_call_target="tpu_custom_call" | custom-call | flops 2097152 | bytes 12582912 | tf_op jit(solution)/shard_map/near_sum/pallas_call | solution.py:630
  207.5 19.6 %hidden_back.1 = (bf16[960,4096]{1,0:T(8,128)(2,1)S(1)}, f32[1,4096]{1,0:T(1,128)S(1)}, bf16[4,2,4,2,64,1024]{5,4,3,2,1,0:T(8,128)(2,1)}) custom-call(s32[3]{0:T(128)S(1)} %add_add_fusion.pos, bf16[960,1024]{1,0:T(8,128)(2,1)S(1)} %bitcast.258, bf16[960,4096]{1,0:T(8,128)(2,1)S(1)} %copy-done.13, bf16[4,2,64,1024]{3,2,1,0:T(8,128)(2,1)} %bitcast.27.refs_0_, ...), custom_call_target="tpu_custom_call" | custom-call | flops 8053063680 | bytes 32505856 | tf_op jit(solution)/shard_map/hidden_back/pallas_call | solution.py:459
  241.5 7.5 %weight_grad.6.refs_1_ = bf16[2,4,4,16,5120]{4,3,2,1,0:T(8,128)(2,1)} custom-call(s32[3]{0:T(128)S(1)} %add_add_fusion.1.order, bf16[960,1024]{1,0:T(8,128)(2,1)S(1)} %bitcast.243, bf16[960,4096]{1,0:T(8,128)(2,1)S(1)} %copy-done.2), custom_call_target="tpu_custom_call" | custom-call | flops 4026531840 | bytes 14024704 | tf_op jit(solution)/shard_map/weight_grad/pallas_call | solution.py:507
  253.1 18.2 %norm_two_back.1 = (f32[3,320,1024]{2,1,0:T(8,128)S(1)}, bf16[3,320,1024]{2,1,0:T(8,128)(2,1)S(1)}, bf16[3,320,1024]{2,1,0:T(8,128)(2,1)S(1)}, f32[1,1024]{1,0:T...) custom-call(s32[3]{0:T(128)S(1)} %bitcast.271, bf16[3,320,4096]{2,1,0:T(8,128)(2,1)} %bitcast.240, ...), custom_call_target="tpu_custom_call" | custom-call | flops 10066329600 | bytes 21626880 | tf_op jit(solution)/shard_map/norm_two_back/pallas_call | solution.py:549
  271.4 3.6 weight_grad.7
  284.5 6.9 %weight_grad.8.refs_1_ = bf16[2,4,4,16,5120]{4,3,2,1,0:T(8,128)(2,1)S(1)} custom-call(s32[3]{0:T(128)S(1)} %add_add_fusion.1.order, bf16[960,1024]{1,0:T(8,128)(2,1)S(1)} %bitcast.244, bf16[960,4096]{1,0:T(8,128)(2,1)S(1)} %copy-done.3), custom_call_target="tpu_custom_call" | custom-call | flops 4026531840 | bytes 14024704 | tf_op jit(solution)/shard_map/weight_grad/pallas_call | solution.py:507
  293.4 6.2 %collective-permute-done.39 = bf16[2,64,1024]{2,1,0:T(8,128)(2,1)S(1)} collective-permute-done((bf16[2,64,1024]{2,1,0:T(8,128)(2,1)}, bf16[2,64,1024]{2,1,0:T(8,128)(2,1)S(1)}, u32[]{:S(2)}, u32[]{:S(2)}) %collective-permute-start.39) | collective-permute-done | bytes 262176 | tf_op jit(solution)/shard_map/ppermute | solution.py:668
  306.2 5.1 %near_sum.4 = (bf16[4,2,16,5120]{3,2,1,0:T(8,128)(2,1)S(1)}, bf16[4,2,16,5120]{3,2,1,0:T(8,128)(2,1)S(1)}, bf16[4,2,16,5120]{3,2,1,0:T(8,128)(2,1)S(1)}, bf16[4,2,16,5120]{3,2,1,0:T(8,128)(2,1)S(1)}) custom-call(s32[3]{0:T(128)S(1)} %add_add_fusion.pos, bf16[2,4,2,2,16,5120]{5,4,3,2,1,0:T(8,128)(2,1)S(1)} %bitcast.218, ...), custom_call_target="tpu_custom_call" | custom-call | flops 2621440 | bytes 15728640 | tf_op jit(solution)/shard_map/near_sum/pallas_call | solution.py:630
  313.1 10.9 %attend_back.3 = (bf16[3,320,1024]{2,1,0:T(8,128)(2,1)S(1)}, bf16[3,320,1024]{2,1,0:T(8,128)(2,1)S(1)}, bf16[3,320,1024]{2,1,0:T(8,128)(2,1)S(1)}) custom-call(s32[3]{0:T(128)S(1)} %bitcast.272, bf16[3,320,3072]{2,1,0:T(8,128)(2,1)S(1)} %bitcast.217, bf16[3,320,3072]{2,1,0:T(8,128)(2,1)S(1)} %bitcast.217, bf16[3,320,3072]{2,1,0:T(8,128)(2,1)S(1)} %bitcast.217, ...), custom_call_target="tpu_custom_call" | custom-call | flops 8388608000 | bytes 4915200 | tf_op jit(solution)/shard_map/attend_back/pallas_call | solution.py:281
  324.0 10.9 %attend_back.4 = (bf16[3,320,1024]{2,1,0:T(8,128)(2,1)S(1)}, bf16[3,320,1024]{2,1,0:T(8,128)(2,1)S(1)}, bf16[3,320,1024]{2,1,0:T(8,128)(2,1)S(1)}) custom-call(s32[3]{0:T(128)S(1)} %bitcast.273, bf16[3,320,3072]{2,1,0:T(8,128)(2,1)S(1)} %bitcast.217, bf16[3,320,3072]{2,1,0:T(8,128)(2,1)S(1)} %bitcast.217, ...), custom_call_target="tpu_custom_call", output_to_operand_aliasing={{0}: (6, {}), {1}: (7, {}), {2}: (8, {})} | custom-call | flops 8388608000 | bytes 4915200 | tf_op jit(solution)/shard_map/attend_back/pallas_call | solution.py:281
  335.0 9.1 %collective-permute-done.36 = bf16[4,2,16,5120]{3,2,1,0:T(8,128)(2,1)S(1)} collective-permute-done((bf16[4,2,16,5120]{3,2,1,0:T(8,128)(2,1)S(1)}, bf16[4,2,16,5120]{3,2,1,0:T(8,128)(2,1)S(1)}, u32[]{:S(2)}, u32[]{:S(2)}) %collective-permute-start.36) | collective-permute-done | bytes 1310752 | tf_op jit(solution)/shard_map/ppermute | solution.py:668
  347.5 10.9 %attend_back.5 = (bf16[3,320,1024]{2,1,0:T(8,128)(2,1)S(1)}, bf16[3,320,1024]{2,1,0:T(8,128)(2,1)S(1)}, bf16[3,320,1024]{2,1,0:T(8,128)(2,1)S(1)}) custom-call(s32[3]{0:T(128)S(1)} %bitcast.274, bf16[3,320,3072]{2,1,0:T(8,128)(2,1)S(1)} %bitcast.217, bf16[3,320,3072]{2,1,0:T(8,128)(2,1)S(1)} %bitcast.217, ...), custom_call_target="tpu_custom_call", output_to_operand_aliasing={{0}: (6, {}), {1}: (7, {}), {2}: (8, {})} | custom-call | flops 8388608000 | bytes 4915200 | tf_op jit(solution)/shard_map/attend_back/pallas_call | solution.py:281
  358.4 3.6 collective-permute-done.45
  364.8 5.8 %weight_grad.10 = bf16[2,4,4,16,3072]{4,3,2,1,0:T(8,128)(2,1)} custom-call(s32[3]{0:T(128)S(1)} %add_add_fusion.1.order, bf16[960,1024]{1,0:T(8,128)(2,1)S(1)} %bitcast.293, bf16[960,1024]{1,0:T(8,128)(2,1)S(1)} %bitcast.295, bf16[960,1024]{1,0:T(8,128)(2,1)S(1)} %bitcast.297, bf16[960,1024]{1,0:T(8,128)(2,1)S(1)} %bitcast.299), custom_call_target="tpu_custom_call" | custom-call | flops 3019898880 | bytes 11010048 | tf_op jit(solution)/shard_map/weight_grad/pallas_call | solution.py:507
  377.1 4.8 %weight_grad.11 = bf16[2,4,4,16,3072]{4,3,2,1,0:T(8,128)(2,1)S(1)} custom-call(s32[3]{0:T(128)S(1)} %add_add_fusion.1.order, bf16[960,1024]{1,0:T(8,128)(2,1)S(1)} %bitcast.294, bf16[960,1024]{1,0:T(8,128)(2,1)S(1)} %bitcast.296, bf16[960,1024]{1,0:T(8,128)(2,1)S(1)} %bitcast.298, bf16[960,1024]{1,0:T(8,128)(2,1)S(1)} %bitcast.300), custom_call_target="tpu_custom_call" | custom-call | flops 3019898880 | bytes 11010048 | tf_op jit(solution)/shard_map/weight_grad/pallas_call | solution.py:507
  386.9 11.3 %norm_one_back.1 = (f32[3,320,1024]{2,1,0:T(8,128)}, f32[1,1024]{1,0:T(1,128)S(1)}, f32[1,1024]{1,0:T(1,128)S(1)}, f32[1,1024]{1,0:T(1,128)S(1)}, f32[1,1024]{1,0:T(1,128)S(1)}) custom-call(s32[3]{0:T(128)S(1)} %bitcast.275, bf16[3,320,1024]{2,1,0:T(8,128)(2,1)S(1)} %copy-done.39, bf16[3,320,1024]{2,1,0:T(8,128)(2,1)S(1)} %copy-done.42, ...), custom_call_target="tpu_custom_call" | custom-call | flops 6039797760 | bytes 22020096 | tf_op jit(solution)/shard_map/norm_one_back/pallas_call | solution.py:595
  398.2 5.4 %collective-permute-done.50 = bf16[2,16,5120]{2,1,0:T(8,128)(2,1)} collective-permute-done((bf16[2,16,5120]{2,1,0:T(8,128)(2,1)}, bf16[2,16,5120]{2,1,0:T(8,128)(2,1)}, u32[]{:S(2)}, u32[]{:S(2)}) %collective-permute-start.50) | collective-permute-done | bytes 327712 | tf_op jit(solution)/shard_map/ppermute | solution.py:668
  412.4 3.4 copy-done.32
  415.8 10.3 %reduce_out.1 = f32[3,320,1024]{2,1,0:T(8,128)} custom-call(s32[3]{0:T(128)S(1)} %bitcast.276, f32[3,320,1024]{2,1,0:T(8,128)S(1)} %copy-done.29, bf16[3,320,4096]{2,1,0:T(8,128)(2,1)S(1)} %bitcast.249, bf16[4096,1024]{1,0:T(8,128)(2,1)S(1)} %bitcast.289, f32[1,1024]{1,0:T(1,128)S(1)} %bitcast.277), custom_call_target="tpu_custom_call" | custom-call | flops 8053063680 | bytes 24117248 | tf_op jit(solution)/shard_map/reduce_out/pallas_call | solution.py:411
  426.2 5.9 %collective-permute-done.53 = bf16[4,16,3072]{2,1,0:T(8,128)(2,1)S(1)} collective-permute-done((bf16[4,16,3072]{2,1,0:T(8,128)(2,1)S(1)}, bf16[4,16,3072]{2,1,0:T(8,128)(2,1)S(1)}, u32[]{:S(2)}, u32[]{:S(2)}) %collective-permute-start.53) | collective-permute-done | bytes 393248 | tf_op jit(solution)/shard_map/ppermute | solution.py:668
  (363 shorter events, 159.2 us)
Async XLA Ops:
  2.1 28.4 %collective-permute-start.4 = (bf16[4,2,16,5120]{3,2,1,0:T(8,128)(2,1)S(1)}, bf16[4,2,16,5120]{3,2,1,0:T(8,128)(2,1)S(1)}, u32[]{:S(2)}, u32[]{:S(2)}) collective-permute-start(bf16[4,2,16,5120]{3,2,1,0:T(8,128)(2,1)S(1)} %bitcast.250), channel_id=1, source_target_pairs={{0,1},{1,0},{2,3},{3,2},{4,5},{5,4},{6,7},{7,6},{8,9},{9,8},{10,11... | collective-permute-start | bytes 3932168 | tf_op jit(solution)/shard_map/ppermute | solution.py:668
  2.2 28.3 %collective-permute-start.3 = (bf16[4,2,16,3072]{3,2,1,0:T(8,128)(2,1)}, bf16[4,2,16,3072]{3,2,1,0:T(8,128)(2,1)}, u32[]{:S(2)}, u32[]{:S(2)}) collective-permute-start(bf16[4,2,16,3072]{3,2,1,0:T(8,128)(2,1)} %bitcast.7.refs_0_), channel_id=1, source_target_pairs={{0,1},{1,0},{2,3},{3,2},{4,5},{5,4},{6,7},{7,6},{8,9},{9,8},{10,11... | collective-permute-start | bytes 2359304 | tf_op jit(solution)/shard_map/ppermute | solution.py:668
  3.6 26.9 %collective-permute-start = (bf16[2,16,3072]{2,1,0:T(8,128)(2,1)S(1)}, bf16[2,16,3072]{2,1,0:T(8,128)(2,1)S(1)}, u32[]{:S(2)}, u32[]{:S(2)}) collective-permute-start(bf16[2,16,3072]{2,1,0:T(8,128)(2,1)S(1)} %dynamic-slice_bitcast_fusion.14), channel_id=1, source_target_pairs={{0,2},{1,3},{2,4},{3,5},{4,6},{5,7},{6,0},{7,1},{8,10},{9,11},{10,... | collective-permute-start | bytes 589832 | tf_op jit(solution)/shard_map/ppermute | solution.py:668
  5.3 25.2 %collective-permute-start.1 = (bf16[2,16,3072]{2,1,0:T(8,128)(2,1)S(1)}, bf16[2,16,3072]{2,1,0:T(8,128)(2,1)S(1)}, u32[]{:S(2)}, u32[]{:S(2)}) collective-permute-start(bf16[2,16,3072]{2,1,0:T(8,128)(2,1)S(1)} %dynamic-slice_bitcast_fusion.14), channel_id=1, source_target_pairs={{0,4},{1,5},{2,6},{3,7},{4,0},{5,1},{6,2},{7,3},{8,12},{9,13},{10,... | collective-permute-start | bytes 589832 | tf_op jit(solution)/shard_map/ppermute | solution.py:668
  6.4 24.2 %collective-permute-start.2 = (bf16[2,16,3072]{2,1,0:T(8,128)(2,1)S(1)}, bf16[2,16,3072]{2,1,0:T(8,128)(2,1)S(1)}, u32[]{:S(2)}, u32[]{:S(2)}) collective-permute-start(bf16[2,16,3072]{2,1,0:T(8,128)(2,1)S(1)} %dynamic-slice_bitcast_fusion.14), channel_id=1, source_target_pairs={{0,6},{1,7},{2,0},{3,1},{4,2},{5,3},{6,4},{7,5},{8,14},{9,15},{10,... | collective-permute-start | bytes 589832 | tf_op jit(solution)/shard_map/ppermute | solution.py:668
  56.1 34.3 %collective-permute-start.12 = (bf16[3,2,3,16,3072]{4,3,2,1,0:T(8,128)(2,1)}, bf16[3,2,3,16,3072]{4,3,2,1,0:T(8,128)(2,1)}, u32[]{:S(2)}, u32[]{:S(2)}) collective-permute-start(bf16[3,2,3,16,3072]{4,3,2,1,0:T(8,128)(2,1)} %pad_maximum_fusion.2.refs_1_), channel_id=1, source_target_pairs={{0,1},{1,0},{2,3},{3,2},{4,5},{5,4},{6,7},{7,6},{8,9},{9,8},{10,11... | collective-permute-start | bytes 5308424 | tf_op jit(solution)/shard_map/ppermute | solution.py:668
  57.0 33.4 %collective-permute-start.13 = (bf16[2,3,16,3072]{3,2,1,0:T(8,128)(2,1)}, bf16[2,3,16,3072]{3,2,1,0:T(8,128)(2,1)}, u32[]{:S(2)}, u32[]{:S(2)}) collective-permute-start(bf16[2,3,16,3072]{3,2,1,0:T(8,128)(2,1)} %pad_maximum_fusion.12.refs_2_), channel_id=1, source_target_pairs={{0,1},{1,0},{2,3},{3,2},{4,5},{5,4},{6,7},{7,6},{8,9},{9,8},{10,11... | collective-permute-start | bytes 1769480 | tf_op jit(solution)/shard_map/ppermute | solution.py:668
  58.9 28.5 %collective-permute-start.6 = (bf16[2,16,5120]{2,1,0:T(8,128)(2,1)}, bf16[2,16,5120]{2,1,0:T(8,128)(2,1)S(1)}, u32[]{:S(2)}, u32[]{:S(2)}) collective-permute-start(bf16[2,16,5120]{2,1,0:T(8,128)(2,1)} %dynamic-slice_bitcast_fusion.12), channel_id=1, source_target_pairs={{0,4},{1,5},{2,6},{3,7},{4,0},{5,1},{6,2},{7,3},{8,12},{9,13},{10,... | collective-permute-start | bytes 983048 | tf_op jit(solution)/shard_map/ppermute | solution.py:668
  62.1 28.3 %collective-permute-start.7 = (bf16[2,16,5120]{2,1,0:T(8,128)(2,1)}, bf16[2,16,5120]{2,1,0:T(8,128)(2,1)S(1)}, u32[]{:S(2)}, u32[]{:S(2)}) collective-permute-start(bf16[2,16,5120]{2,1,0:T(8,128)(2,1)} %dynamic-slice_bitcast_fusion.12), channel_id=1, source_target_pairs={{0,6},{1,7},{2,0},{3,1},{4,2},{5,3},{6,4},{7,5},{8,14},{9,15},{10,... | collective-permute-start | bytes 983048 | tf_op jit(solution)/shard_map/ppermute | solution.py:668
  90.5 24.1 %collective-permute-start.14 = (bf16[2,3,16,5120]{3,2,1,0:T(8,128)(2,1)S(1)}, bf16[2,3,16,5120]{3,2,1,0:T(8,128)(2,1)S(1)}, u32[]{:S(2)}, u32[]{:S(2)}) collective-permute-start(bf16[2,3,16,5120]{3,2,1,0:T(8,128)(2,1)S(1)} %get-tuple-element.303), channel_id=1, source_target_pairs={{0,8},{1,9},{2,10},{3,11},{4,12},{5,13},{6,14},{7,15},{8,0},{9,1},... | collective-permute-start | bytes 2949128 | tf_op jit(solution)/shard_map/ppermute | solution.py:668
  92.1 22.8 %collective-permute-start.15 = (bf16[2,3,16,5120]{3,2,1,0:T(8,128)(2,1)S(1)}, bf16[2,3,16,5120]{3,2,1,0:T(8,128)(2,1)S(1)}, u32[]{:S(2)}, u32[]{:S(2)}) collective-permute-start(bf16[2,3,16,5120]{3,2,1,0:T(8,128)(2,1)S(1)} %get-tuple-element.303), channel_id=1, source_target_pairs={{0,16},{1,17},{2,18},{3,19},{4,20},{5,21},{6,22},{7,23},{8,24},{9,... | collective-permute-start | bytes 2949128 | tf_op jit(solution)/shard_map/ppermute | solution.py:668
  92.7 34.1 %collective-permute-start.18 = (bf16[2,64,1024]{2,1,0:T(8,128)(2,1)S(1)}, bf16[2,64,1024]{2,1,0:T(8,128)(2,1)S(1)}, u32[]{:S(2)}, u32[]{:S(2)}) collective-permute-start(bf16[2,64,1024]{2,1,0:T(8,128)(2,1)S(1)} %dynamic-slice_bitcast_fusion.13), channel_id=1, source_target_pairs={{0,2},{1,3},{2,4},{3,5},{4,6},{5,7},{6,0},{7,1},{8,10},{9,11},{10,... | collective-permute-start | bytes 786440 | tf_op jit(solution)/shard_map/ppermute | solution.py:668
  92.7 46.5 %collective-permute-start.19 = (bf16[2,64,1024]{2,1,0:T(8,128)(2,1)S(1)}, bf16[2,64,1024]{2,1,0:T(8,128)(2,1)S(1)}, u32[]{:S(2)}, u32[]{:S(2)}) collective-permute-start(bf16[2,64,1024]{2,1,0:T(8,128)(2,1)S(1)} %dynamic-slice_bitcast_fusion.13), channel_id=1, source_target_pairs={{0,4},{1,5},{2,6},{3,7},{4,0},{5,1},{6,2},{7,3},{8,12},{9,13},{10,... | collective-permute-start | bytes 786440 | tf_op jit(solution)/shard_map/ppermute | solution.py:668
  116.8 27.0 %collective-permute-start.21 = (bf16[3,2,3,16,5120]{4,3,2,1,0:T(8,128)(2,1)}, bf16[3,2,3,16,5120]{4,3,2,1,0:T(8,128)(2,1)}, u32[]{:S(2)}, u32[]{:S(2)}) collective-permute-start(bf16[3,2,3,16,5120]{4,3,2,1,0:T(8,128)(2,1)} %pad_maximum_fusion.refs_1_), channel_id=1, source_target_pairs={{0,1},{1,0},{2,3},{3,2},{4,5},{5,4},{6,7},{7,6},{8,9},{9,8},{10,11... | collective-permute-start | bytes 8847368 | tf_op jit(solution)/shard_map/ppermute | solution.py:668
  116.8 22.3 %collective-permute-start.16 = (bf16[3,16,5120]{2,1,0:T(8,128)(2,1)S(1)}, bf16[3,16,5120]{2,1,0:T(8,128)(2,1)S(1)}, u32[]{:S(2)}, u32[]{:S(2)}) collective-permute-start(bf16[3,16,5120]{2,1,0:T(8,128)(2,1)S(1)} %slice_bitcast_fusion.1), channel_id=1, source_target_pairs={{0,16},{1,17},{2,18},{3,19},{4,20},{5,21},{6,22},{7,23},{8,24},{9,... | collective-permute-start | bytes 1474568 | tf_op jit(solution)/shard_map/ppermute | solution.py:668
  141.7 30.4 %collective-permute-start.23 = (bf16[2,3,64,1024]{3,2,1,0:T(8,128)(2,1)S(1)}, bf16[2,3,64,1024]{3,2,1,0:T(8,128)(2,1)S(1)}, u32[]{:S(2)}, u32[]{:S(2)}) collective-permute-start(bf16[2,3,64,1024]{3,2,1,0:T(8,128)(2,1)S(1)} %get-tuple-element.312), channel_id=1, source_target_pairs={{0,8},{1,9},{2,10},{3,11},{4,12},{5,13},{6,14},{7,15},{8,0},{9,1},... | collective-permute-start | bytes 2359304 | tf_op jit(solution)/shard_map/ppermute | solution.py:668
  143.3 28.9 %collective-permute-start.24 = (bf16[2,3,64,1024]{3,2,1,0:T(8,128)(2,1)S(1)}, bf16[2,3,64,1024]{3,2,1,0:T(8,128)(2,1)S(1)}, u32[]{:S(2)}, u32[]{:S(2)}) collective-permute-start(bf16[2,3,64,1024]{3,2,1,0:T(8,128)(2,1)S(1)} %get-tuple-element.312), channel_id=1, source_target_pairs={{0,16},{1,17},{2,18},{3,19},{4,20},{5,21},{6,22},{7,23},{8,24},{9,... | collective-permute-start | bytes 2359304 | tf_op jit(solution)/shard_map/ppermute | solution.py:668
  173.8 28.9 %collective-permute-start.31 = (bf16[3,2,3,64,1024]{4,3,2,1,0:T(8,128)(2,1)}, bf16[3,2,3,64,1024]{4,3,2,1,0:T(8,128)(2,1)}, u32[]{:S(2)}, u32[]{:S(2)}) collective-permute-start(bf16[3,2,3,64,1024]{4,3,2,1,0:T(8,128)(2,1)} %pad_maximum_fusion.1.refs_1_), channel_id=1, source_target_pairs={{0,1},{1,0},{2,3},{3,2},{4,5},{5,4},{6,7},{7,6},{8,9},{9,8},{10,11... | collective-permute-start | bytes 7077896 | tf_op jit(solution)/shard_map/ppermute | solution.py:668
  174.3 28.4 %collective-permute-start.30 = (bf16[4,2,64,1024]{3,2,1,0:T(8,128)(2,1)}, bf16[4,2,64,1024]{3,2,1,0:T(8,128)(2,1)}, u32[]{:S(2)}, u32[]{:S(2)}) collective-permute-start(bf16[4,2,64,1024]{3,2,1,0:T(8,128)(2,1)} %bitcast.27.refs_0_), channel_id=1, source_target_pairs={{0,1},{1,0},{2,3},{3,2},{4,5},{5,4},{6,7},{7,6},{8,9},{9,8},{10,11... | collective-permute-start | bytes 3145736 | tf_op jit(solution)/shard_map/ppermute | solution.py:668
  200.7 29.5 %collective-permute-start.26 = (bf16[4,2,64,1024]{3,2,1,0:T(8,128)(2,1)}, bf16[4,2,64,1024]{3,2,1,0:T(8,128)(2,1)}, u32[]{:S(2)}, u32[]{:S(2)}) collective-permute-start(bf16[4,2,64,1024]{3,2,1,0:T(8,128)(2,1)} %get-tuple-element.167), channel_id=1, source_target_pairs={{0,8},{1,9},{2,10},{3,11},{4,12},{5,13},{6,14},{7,15},{8,0},{9,1},... | collective-permute-start | bytes 3145736 | tf_op jit(solution)/shard_map/ppermute | solution.py:668
  202.2 28.1 %collective-permute-start.27 = (bf16[4,2,64,1024]{3,2,1,0:T(8,128)(2,1)}, bf16[4,2,64,1024]{3,2,1,0:T(8,128)(2,1)}, u32[]{:S(2)}, u32[]{:S(2)}) collective-permute-start(bf16[4,2,64,1024]{3,2,1,0:T(8,128)(2,1)} %get-tuple-element.168), channel_id=1, source_target_pairs={{0,16},{1,17},{2,18},{3,19},{4,20},{5,21},{6,22},{7,23},{8,24},{9,... | collective-permute-start | bytes 3145736 | tf_op jit(solution)/shard_map/ppermute | solution.py:668
  274.9 31.2 %collective-permute-start.35 = (bf16[2,4,4,16,5120]{4,3,2,1,0:T(8,128)(2,1)}, bf16[2,4,4,16,5120]{4,3,2,1,0:T(8,128)(2,1)}, u32[]{:S(2)}, u32[]{:S(2)}) collective-permute-start(bf16[2,4,4,16,5120]{4,3,2,1,0:T(8,128)(2,1)} %weight_grad.7), channel_id=1, source_target_pairs={{0,1},{1,0},{2,3},{3,2},{4,5},{5,4},{6,7},{7,6},{8,9},{9,8},{10,11... | collective-permute-start | bytes 15728648 | tf_op jit(solution)/shard_map/ppermute | solution.py:668
  276.3 23.3 %collective-permute-start.39 = (bf16[2,64,1024]{2,1,0:T(8,128)(2,1)}, bf16[2,64,1024]{2,1,0:T(8,128)(2,1)S(1)}, u32[]{:S(2)}, u32[]{:S(2)}) collective-permute-start(bf16[2,64,1024]{2,1,0:T(8,128)(2,1)} %get-tuple-element.297), channel_id=1, source_target_pairs={{0,4},{1,5},{2,6},{3,7},{4,0},{5,1},{6,2},{7,3},{8,12},{9,13},{10,... | collective-permute-start | bytes 786440 | tf_op jit(solution)/shard_map/ppermute | solution.py:668
  279.6 22.8 %collective-permute-start.40 = (bf16[2,64,1024]{2,1,0:T(8,128)(2,1)}, bf16[2,64,1024]{2,1,0:T(8,128)(2,1)S(1)}, u32[]{:S(2)}, u32[]{:S(2)}) collective-permute-start(bf16[2,64,1024]{2,1,0:T(8,128)(2,1)} %get-tuple-element.295), channel_id=1, source_target_pairs={{0,6},{1,7},{2,0},{3,1},{4,2},{5,3},{6,4},{7,5},{8,14},{9,15},{10,... | collective-permute-start | bytes 786440 | tf_op jit(solution)/shard_map/ppermute | solution.py:668
  302.6 32.4 %collective-permute-start.41 = (bf16[2,64,1024]{2,1,0:T(8,128)(2,1)S(1)}, bf16[2,64,1024]{2,1,0:T(8,128)(2,1)S(1)}, u32[]{:S(2)}, u32[]{:S(2)}) collective-permute-start(bf16[2,64,1024]{2,1,0:T(8,128)(2,1)S(1)} %fusion.9), channel_id=1, source_target_pairs={{0,8},{1,9},{2,10},{3,11},{4,12},{5,13},{6,14},{7,15},{8,0},{9,1},... | collective-permute-start | bytes 786440 | tf_op jit(solution)/shard_map/ppermute | solution.py:668
  303.6 31.4 %collective-permute-start.42 = (bf16[2,64,1024]{2,1,0:T(8,128)(2,1)S(1)}, bf16[2,64,1024]{2,1,0:T(8,128)(2,1)S(1)}, u32[]{:S(2)}, u32[]{:S(2)}) collective-permute-start(bf16[2,64,1024]{2,1,0:T(8,128)(2,1)S(1)} %fusion.9), channel_id=1, source_target_pairs={{0,16},{1,17},{2,18},{3,19},{4,20},{5,21},{6,22},{7,23},{8,24},{9,... | collective-permute-start | bytes 786440 | tf_op jit(solution)/shard_map/ppermute | solution.py:668
  304.4 30.6 %collective-permute-start.43 = (bf16[2,64,1024]{2,1,0:T(8,128)(2,1)S(1)}, bf16[2,64,1024]{2,1,0:T(8,128)(2,1)S(1)}, u32[]{:S(2)}, u32[]{:S(2)}) collective-permute-start(bf16[2,64,1024]{2,1,0:T(8,128)(2,1)S(1)} %fusion.9), channel_id=1, source_target_pairs={{0,24},{1,25},{2,26},{3,27},{4,28},{5,29},{6,30},{7,31},{8,16},{9,... | collective-permute-start | bytes 786440 | tf_op jit(solution)/shard_map/ppermute | solution.py:668
  311.2 32.9 %collective-permute-start.36 = (bf16[4,2,16,5120]{3,2,1,0:T(8,128)(2,1)S(1)}, bf16[4,2,16,5120]{3,2,1,0:T(8,128)(2,1)S(1)}, u32[]{:S(2)}, u32[]{:S(2)}) collective-permute-start(bf16[4,2,16,5120]{3,2,1,0:T(8,128)(2,1)S(1)} %get-tuple-element.186), channel_id=1, source_target_pairs={{0,8},{1,9},{2,10},{3,11},{4,12},{5,13},{6,14},{7,15},{8,0},{9,1},... | collective-permute-start | bytes 3932168 | tf_op jit(solution)/shard_map/ppermute | solution.py:668
  312.3 32.5 %collective-permute-start.37 = (bf16[4,2,16,5120]{3,2,1,0:T(8,128)(2,1)S(1)}, bf16[4,2,16,5120]{3,2,1,0:T(8,128)(2,1)S(1)}, u32[]{:S(2)}, u32[]{:S(2)}) collective-permute-start(bf16[4,2,16,5120]{3,2,1,0:T(8,128)(2,1)S(1)} %get-tuple-element.187), channel_id=1, source_target_pairs={{0,16},{1,17},{2,18},{3,19},{4,20},{5,21},{6,22},{7,23},{8,24},{9,... | collective-permute-start | bytes 3932168 | tf_op jit(solution)/shard_map/ppermute | solution.py:668
  374.3 23.9 %collective-permute-start.49 = (bf16[2,16,5120]{2,1,0:T(8,128)(2,1)}, bf16[2,16,5120]{2,1,0:T(8,128)(2,1)}, u32[]{:S(2)}, u32[]{:S(2)}) collective-permute-start(bf16[2,16,5120]{2,1,0:T(8,128)(2,1)} %get-tuple-element.289), channel_id=1, source_target_pairs={{0,2},{1,3},{2,4},{3,5},{4,6},{5,7},{6,0},{7,1},{8,10},{9,11},{10,... | collective-permute-start | bytes 983048 | tf_op jit(solution)/shard_map/ppermute | solution.py:668
  374.3 29.3 %collective-permute-start.50 = (bf16[2,16,5120]{2,1,0:T(8,128)(2,1)}, bf16[2,16,5120]{2,1,0:T(8,128)(2,1)}, u32[]{:S(2)}, u32[]{:S(2)}) collective-permute-start(bf16[2,16,5120]{2,1,0:T(8,128)(2,1)} %get-tuple-element.290), channel_id=1, source_target_pairs={{0,4},{1,5},{2,6},{3,7},{4,0},{5,1},{6,2},{7,3},{8,12},{9,13},{10,... | collective-permute-start | bytes 983048 | tf_op jit(solution)/shard_map/ppermute | solution.py:668
  375.0 29.8 %collective-permute-start.51 = (bf16[2,16,5120]{2,1,0:T(8,128)(2,1)}, bf16[2,16,5120]{2,1,0:T(8,128)(2,1)}, u32[]{:S(2)}, u32[]{:S(2)}) collective-permute-start(bf16[2,16,5120]{2,1,0:T(8,128)(2,1)} %get-tuple-element.288), channel_id=1, source_target_pairs={{0,6},{1,7},{2,0},{3,1},{4,2},{5,3},{6,4},{7,5},{8,14},{9,15},{10,... | collective-permute-start | bytes 983048 | tf_op jit(solution)/shard_map/ppermute | solution.py:668
  (112 other events, 1176.0 us)

commit v3 on v2

v3 whole, which is shorter than its diff:
```python
import functools

import jax
import jax.numpy as jnp
from jax import lax
from jax.experimental import pallas as pl
from jax.experimental.pallas import tpu as pltpu
from jax.sharding import PartitionSpec as P

F32 = jnp.float32
BF16 = jnp.bfloat16
EPS = 1e-06
H = 16
E = 64
LANES = 128
HALF_ROOT = 2.0 ** -0.5
INV_ROOT_TAU = 0.3989422804014327
NN = (((1,), (0,)), ((), ()))
NT = (((1,), (1,)), ((), ()))
TN = (((0,), (0,)), ((), ()))


def mm(former, latter, dims=NN):
    return lax.dot_general(former, latter, dims, preferred_element_type=F32)


def params(mib):
    return pltpu.CompilerParams(vmem_limit_bytes=mib << 20, dimension_semantics=("arbitrary",))


def cost(flops, nbytes, other=0):
    return pl.CostEstimate(flops=int(flops), bytes_accessed=int(nbytes), transcendentals=int(other))


def once(shape):
    return pl.BlockSpec(memory_space=pltpu.VMEM)


def valid_rows(length, rows):
    return (lax.broadcasted_iota(jnp.int32, (rows, 1), 0) < length).astype(F32)


def norm_parts(values):
    centred = values - jnp.mean(values, -1, keepdims=True)
    scale = lax.rsqrt(jnp.mean(centred * centred, -1, keepdims=True) + EPS)
    return centred * scale, scale


def norm_back(unit, scale, grad, gain):
    grad_unit = grad * gain
    first = jnp.mean(grad_unit, -1, keepdims=True)
    second = jnp.mean(grad_unit * unit, -1, keepdims=True)
    return scale * (grad_unit - first - unit * second)


def far(shape, dtype):
    return pltpu.HBM(shape, dtype)


def held(array):
    return pltpu.with_memory_space_constraint(array, pltpu.HBM)


def column_sum(values):
    return jnp.sum(values, 0, keepdims=True)


def add_first(step, ref, value):
    @pl.when(step == 0)
    def _():
        ref[...] = value

    @pl.when(step > 0)
    def _():
        ref[...] += value


def collect(ring, pos, pieces, whole, sems):
    copies = []

    def put(source, target):
        copy = pltpu.make_async_copy(source, target, sems.at[len(copies)])
        copy.start()
        copies.append(copy)

    if not ring:
        put(pieces[0], whole)
    else:
        g, z, c = pos[0], pos[1], pos[2]
        for at in range(2):
            core = c if at == 0 else 1 - c
            own, near, far = pieces[3 * at : 3 * at + 3]
            put(own, whole.at[z, core])
            for k in range(1, Z):
                row = lax.rem(z + Z - k, Z)
                for over in range(3):
                    put(near.at[over, :, k - 1], whole.at[row, core, g ^ over])
                for part in range(2):
                    put(far.at[part, k - 1], whole.at[row, core, g ^ 3, part])
    for copy in copies:
        copy.wait()


def whole_shape(ring, pieces):
    if ring:
        return (Z, 2) + pieces[0].shape
    return pieces[0].shape


def collect_scratch(ring, pieces):
    return [
        pltpu.VMEM(whole_shape(ring, pieces), BF16),
        pltpu.SemaphoreType.DMA((32,)),
        pltpu.SemaphoreType.DMA,
    ]


def fill(ring, step, steps, pos, pieces, kept, whole, sems, sem):
    @pl.when(step == 0)
    def _():
        collect(ring, pos, pieces, whole, sems)
        pltpu.make_async_copy(whole, kept, sem).start()


def keep(step, steps, kept, whole, sem):
    @pl.when(step == steps - 1)
    def _():
        pltpu.make_async_copy(whole, kept, sem).wait()


def flat_rows(whole):
    value = whole[...]
    return value.reshape(-1, value.shape[-1])


def project_kernel(ring, count, rows_each, lengths, pos, x, cot, *refs):
    normed, packed, up, up_sum, kept, table, whole, sems, sem, weight_bias = refs[-10:]
    pieces = refs[:-10] if ring else refs[:-12]
    step = pl.program_id(0)
    fill(ring, step, count, pos, pieces, kept, whole, sems, sem)
    rows, width = x.shape[1:]

    @pl.when(step == 0)
    def _():
        if ring:
            columns = whole[..., 3 * width :].reshape(width, LANES).astype(F32)
            table[...] = columns.T[: table.shape[0], :]
            weight_bias[...] = jnp.zeros(weight_bias.shape, F32)
            for shard in range(width // rows_each):
                for part in range(2):
                    at = (2 * shard + part) * rows_each
                    at += width if at >= width else 0
                    source = table[2 + part : 3 + part, shard * rows_each : (shard + 1) * rows_each]
                    weight_bias[:, at : at + rows_each] = source
        else:
            table[...] = refs[-12][...]
            weight_bias[...] = refs[-11][...]

    valid = valid_rows(lengths[step], rows)
    unit, _ = norm_parts(x[0].astype(F32) * valid)
    low = (unit * table[0:1, :] + table[1:2, :]).astype(BF16)
    normed[0] = low
    weight = whole[..., : 3 * width].reshape(width, 3 * width)
    packed[0] = (mm(low, weight) + weight_bias[...]).astype(BF16)
    upstream = cot[0].astype(F32) * valid
    up[0] = upstream.astype(BF16)
    add_first(step, up_sum, column_sum(upstream))
    keep(step, count, kept, whole, sem)


def project(ring, rows_each, lengths, pos, x, cot, pieces, vectors=()):
    seqs, rows, width = x.shape
    wide = 3 * width
    row_block = pl.BlockSpec((1, rows, width), lambda s, *_: (s, 0, 0))
    anywhere = pl.BlockSpec(memory_space=pl.ANY)
    normed, packed, up, up_sum, kept, table = pl.pallas_call(
        functools.partial(project_kernel, ring, seqs, rows_each),
        grid_spec=pltpu.PrefetchScalarGridSpec(
            num_scalar_prefetch=2,
            grid=(seqs,),
            in_specs=[row_block, row_block]
            + [anywhere] * len(pieces)
            + [once(v.shape) for v in vectors],
            out_specs=[
                row_block,
                pl.BlockSpec((1, rows, wide), lambda s, *_: (s, 0, 0)),
                row_block,
                pl.BlockSpec((1, width), lambda s, *_: (0, 0)),
                anywhere,
                pl.BlockSpec((16, width), lambda s, *_: (0, 0)),
            ],
            scratch_shapes=collect_scratch(ring, pieces) + [pltpu.VMEM((1, wide), F32)],
        ),
        out_shape=[
            jax.ShapeDtypeStruct(x.shape, BF16),
            far((seqs, rows, wide), BF16),
            jax.ShapeDtypeStruct(x.shape, BF16),
            jax.ShapeDtypeStruct((1, width), F32),
            far(whole_shape(ring, pieces), BF16),
            jax.ShapeDtypeStruct((16, width), F32),
        ],
        compiler_params=params(30),
        cost_estimate=cost(2 * seqs * rows * width * wide, seqs * rows * (4 * width + wide) * 2 + 4 * width * wide),
        name="norm_project",
    )(lengths, pos, x, cot, *pieces, *vectors)
    return normed, packed, up, up_sum, kept.reshape(width, -1), table


LEAST = 256
RATE = E**-0.5 * 1.4426950408889634


def attend_kernel(seq, lengths, q, k, v, *refs):
    mixed, lse = refs[-2:]
    rows = q.shape[1]
    length = lengths[seq]
    key_ok = lax.broadcasted_iota(jnp.int32, (1, rows - LEAST), 1) + LEAST < length
    lane = lax.broadcasted_iota(jnp.int32, (rows, LANES), 1)
    low_lane = lane < E
    logs = jnp.zeros((rows, LANES), F32)
    for pair in range(q.shape[2] // LANES):
        at = slice(pair * LANES, (pair + 1) * LANES)
        qs, ks, vs = q[0, :, at], k[0, :, at], v[0, :, at]
        outs = []
        for head in range(2):
            keep = low_lane if head == 0 else ~low_lane
            scores = mm(jnp.where(keep, qs, jnp.zeros_like(qs)), ks, NT)
            scores = jnp.concatenate(
                [scores[:, :LEAST], jnp.where(key_ok, scores[:, LEAST:], -1e30)], 1
            )
            top = jnp.max(scores, -1, keepdims=True)
            weights = jnp.exp2((scores - top) * RATE)
            total = jnp.sum(weights, -1, keepdims=True)
            outs.append(mm(weights.astype(BF16), vs) * (1.0 / total))
            logs = jnp.where(lane == 2 * pair + head, top * RATE + jnp.log2(total), logs)
        mixed[0, :, at] = jnp.where(low_lane, outs[0], outs[1]).astype(BF16)
    lse[0, 0] = logs.T[: lse.shape[2], :]


def attend(seq, lengths, packed, earlier=()):
    seqs, rows, wide = packed.shape
    width = wide // 3
    wid = 4 * LANES
    steps = width // wid
    block = lambda part: pl.BlockSpec((1, rows, wid), lambda j, *_: (seq, 0, part * steps + j))
    return pl.pallas_call(
        functools.partial(attend_kernel, seq),
        grid_spec=pltpu.PrefetchScalarGridSpec(
            num_scalar_prefetch=1,
            grid=(steps,),
            in_specs=[block(0), block(1), block(2)]
            + [pl.BlockSpec(memory_space=pl.ANY)] * len(earlier),
            out_specs=[
                pl.BlockSpec((1, rows, wid), lambda j, *_: (seq, 0, j)),
                pl.BlockSpec((1, 1, 8, rows), lambda j, *_: (seq, j, 0, 0)),
            ],
        ),
        out_shape=[
            jax.ShapeDtypeStruct((seqs, rows, width), BF16),
            jax.ShapeDtypeStruct((seqs, steps, 8, rows), F32),
        ],
        input_output_aliases={4: 0, 5: 1} if earlier else {},
        compiler_params=params(16),
        cost_estimate=cost(4 * rows * rows * width * 8, rows * wide * 3, H * rows * rows),
        name="attend",
    )(lengths, *[held(packed)] * 3, *earlier)


def attend_back_kernel(seq, lengths, q, k, v, lse, grad, *refs):
    out = refs[-1]
    rows = q.shape[1]
    length = lengths[seq + pl.program_id(0)]
    key_ok = lax.broadcasted_iota(jnp.int32, (rows - LEAST, 1), 0) + LEAST < length
    low_lane = lax.broadcasted_iota(jnp.int32, (rows, LANES), 1) < E
    for pair in range(q.shape[2] // LANES):
        at = slice(pair * LANES, (pair + 1) * LANES)
        qs, ks, vs, gs = q[0, :, at], k[0, :, at], v[0, :, at], grad[0, :, at]
        sums = []
        for head in range(2):
            keep = low_lane if head == 0 else ~low_lane
            scores = mm(jnp.where(keep, ks, jnp.zeros_like(ks)), qs, NT)
            grad_probs = mm(jnp.where(keep, vs, jnp.zeros_like(vs)), gs, NT)
            row = 2 * pair + head
            probs = jnp.exp2(scores * RATE - lse[0, 0, row : row + 1, :])
            probs = jnp.concatenate(
                [probs[:LEAST], jnp.where(key_ok, probs[LEAST:], 0.0)], 0
            )
            inner = jnp.sum(grad_probs * probs, 0, keepdims=True)
            grad_scores = (probs * (grad_probs - inner)).astype(BF16)
            sums.append(
                (
                    mm(grad_scores, ks, TN) * E**-0.5,
                    mm(grad_scores, qs) * E**-0.5,
                    mm(probs.astype(BF16), gs),
                )
            )
        for part, first, second in zip(range(3), sums[0], sums[1]):
            out[0, part, :, at] = jnp.where(low_lane, first, second).astype(BF16)


def attend_back(seq, here, lengths, packed, lse, grad, earlier=()):
    seqs, rows, wide = packed.shape
    width = wide // 3
    wid = 4 * LANES
    steps = width // wid
    block = lambda part: pl.BlockSpec(
        (1, rows, wid), lambda s, j, *_: (seq + s, 0, part * steps + j)
    )
    return pl.pallas_call(
        functools.partial(attend_back_kernel, seq),
        grid_spec=pltpu.PrefetchScalarGridSpec(
            num_scalar_prefetch=1,
            grid=(here, steps),
            in_specs=[
                block(0),
                block(1),
                block(2),
                pl.BlockSpec((1, 1, 8, rows), lambda s, j, *_: (seq + s, j, 0, 0)),
                pl.BlockSpec((1, rows, wid), lambda s, j, *_: (seq + s, 0, j)),
            ]
            + [pl.BlockSpec(memory_space=pl.ANY)] * len(earlier),
            out_specs=pl.BlockSpec((1, 3, rows, wid), lambda s, j, *_: (seq + s, 0, 0, j)),
        ),
        out_shape=far((seqs, 3, rows, width), BF16),
        input_output_aliases={6: 0} if earlier else {},
        compiler_params=pltpu.CompilerParams(
            vmem_limit_bytes=18 << 20, dimension_semantics=("arbitrary",) * 2
        ),
        cost_estimate=cost(10 * here * rows * rows * width * 8, here * rows * wide * 5, here * H * rows * rows),
        name="attend_back",
    )(lengths, *[held(packed)] * 3, lse, grad, *[held(a) for a in earlier])


def branch_kernel(ring, count, lengths, pos, x, mixed, table, *refs):
    pieces, (resid, normed, kept, whole, sems, sem) = refs[:-6], refs[-6:]
    step = pl.program_id(0)
    fill(ring, step, count, pos, pieces, kept, whole, sems, sem)
    rows, width = x.shape[1:]
    valid = valid_rows(lengths[step], rows)
    weight = whole[..., :width].reshape(-1, width)
    total = x[0].astype(F32) * valid + mm(mixed[0], weight) + table[4:5, :]
    resid[0] = total
    unit, _ = norm_parts(total)
    normed[0] = (unit * table[5:6, :] + table[6:7, :]).astype(BF16)
    keep(step, count, kept, whole, sem)


def branch(ring, lengths, pos, x, mixed, table, pieces):
    seqs, rows, width = x.shape
    wide = pieces[0].shape[-1]
    row_block = pl.BlockSpec((1, rows, width), lambda s, *_: (s, 0, 0))
    anywhere = pl.BlockSpec(memory_space=pl.ANY)
    resid, normed, kept = pl.pallas_call(
        functools.partial(branch_kernel, ring, seqs),
        grid_spec=pltpu.PrefetchScalarGridSpec(
            num_scalar_prefetch=2,
            grid=(seqs,),
            in_specs=[row_block, row_block, once(table.shape)] + [anywhere] * len(pieces),
            out_specs=[row_block, row_block, anywhere],
            scratch_shapes=collect_scratch(ring, pieces),
        ),
        out_shape=[
            far(x.shape, F32),
            jax.ShapeDtypeStruct(x.shape, BF16),
            far(whole_shape(ring, pieces), BF16),
        ],
        compiler_params=params(26),
        cost_estimate=cost(2 * seqs * rows * width * width, seqs * rows * width * 10 + 4 * width * wide),
        name="branch",
    )(lengths, pos, x, mixed, table, *pieces)
    return resid, normed, kept.reshape(-1, wide)


def store_halves(ref, value):
    _, shards, quarters, rows, _ = ref.shape
    for shard in range(shards):
        for quarter in range(quarters):
            for half in range(2):
                at = ((shard * quarters + quarter) * 2 + half) * rows
                ref[half, shard, quarter] = value[at : at + rows]


def expand_kernel(seqs, normed, up, weight, bias, act, slope, grad):
    rows = normed.shape[0] // seqs
    for s in range(seqs):
        at = slice(s * rows, (s + 1) * rows)
        hidden = mm(normed[at, :], weight[...]) + bias[...]
        phi = 0.5 + 0.5 * lax.erf(hidden * HALF_ROOT)
        act[at, :] = (hidden * phi).astype(BF16)
        slope[at, :] = (phi + hidden * (INV_ROOT_TAU * jnp.exp(-0.5 * hidden * hidden))).astype(BF16)
    grad[...] = mm(act[...], up[...], TN).astype(BF16)


def expand(seqs, normed, up, weight, bias):
    count, width = normed.shape
    hidden = bias.shape[1]
    size = hidden // 8
    skip = (weight.shape[1] - hidden) // size
    wide = pl.BlockSpec((count, size), lambda i: (0, i))
    shape = far((count, hidden), BF16)
    return pl.pallas_call(
        functools.partial(expand_kernel, seqs),
        grid=(8,),
        in_specs=[
            once((count, width)),
            once((count, width)),
            pl.BlockSpec((width, size), lambda i: (0, skip + i)),
            pl.BlockSpec((1, size), lambda i: (0, i)),
        ],
        out_specs=[wide, wide, pl.BlockSpec((size, width), lambda i: (i, 0))],
        out_shape=[shape, shape, far((hidden, width), BF16)],
        compiler_params=params(26),
        cost_estimate=cost(4 * count * width * hidden, count * hidden * 4 + width * hidden * 4, count * hidden),
        name="expand",
    )(normed, up, held(weight), bias)


def reduce_kernel(lengths, resid, act, weight, table, out):
    rows = resid.shape[1]
    valid = valid_rows(lengths[pl.program_id(0)], rows)
    out[0] = (resid[0] + mm(act[0], weight[...]) + table[11:12, :]) * valid


def reduce_out(lengths, resid, act, weight, table):
    seqs, rows, width = resid.shape
    hidden = weight.shape[0]
    row_block = pl.BlockSpec((1, rows, width), lambda s, *_: (s, 0, 0))
    return pl.pallas_call(
        reduce_kernel,
        grid_spec=pltpu.PrefetchScalarGridSpec(
            num_scalar_prefetch=1,
            grid=(seqs,),
            in_specs=[
                row_block,
                pl.BlockSpec((1, rows, hidden), lambda s, *_: (s, 0, 0)),
                once((hidden, width)),
                once(table.shape),
            ],
            out_specs=row_block,
        ),
        out_shape=far(resid.shape, F32),
        compiler_params=params(26),
        cost_estimate=cost(2 * seqs * rows * width * hidden, seqs * rows * (8 * width + 2 * hidden) + 2 * width * hidden),
        name="reduce_out",
    )(lengths, held(resid), held(act.reshape(seqs, rows, hidden)), weight, table)


def hidden_back_kernel(seqs, up, weight, slope, grad, grad_sum):
    rows = up.shape[0] // seqs
    total = None
    for s in range(seqs):
        at = slice(s * rows, (s + 1) * rows)
        low = (mm(up[at, :], weight[...], NT) * slope[at, :].astype(F32)).astype(BF16)
        grad[at, :] = low
        part = column_sum(low.astype(F32))
        total = part if s == 0 else total + part
    grad_sum[...] = total


def hidden_back(seqs, up, weight, slope):
    count, width = up.shape
    hidden = slope.shape[1]
    size = hidden // 8
    wide = pl.BlockSpec((count, size), lambda i: (0, i))
    return pl.pallas_call(
        functools.partial(hidden_back_kernel, seqs),
        grid=(8,),
        in_specs=[once((count, width)), pl.BlockSpec((size, width), lambda i: (i, 0)), wide],
        out_specs=[wide, pl.BlockSpec((1, size), lambda i: (0, i))],
        out_shape=[far((count, hidden), BF16), jax.ShapeDtypeStruct((1, hidden), F32)],
        compiler_params=params(20),
        cost_estimate=cost(2 * count * width * hidden, count * hidden * 4 + 2 * width * hidden),
        name="hidden_back",
    )(up, held(weight), held(slope))


def whole_grad_kernel(inputs, grads, *refs):
    refs[-1][...] = mm(inputs[...], grads[...], TN).astype(BF16)


def whole_grad(inputs, grads, wide, first=0, earlier=()):
    count, width = inputs.shape
    here = grads.shape[1]
    size = 512
    return pl.pallas_call(
        whole_grad_kernel,
        grid=(here // size,),
        in_specs=[once((count, width)), pl.BlockSpec((count, size), lambda j: (0, j))]
        + [pl.BlockSpec(memory_space=pl.ANY)] * len(earlier),
        out_specs=pl.BlockSpec((width, size), lambda j: (0, first // size + j)),
        out_shape=far((width, wide), BF16),
        input_output_aliases={2: 0} if earlier else {},
        compiler_params=params(20),
        cost_estimate=cost(2 * count * width * here, count * (width + here) * 2 + 2 * width * here),
        name="whole_grad",
    )(inputs, held(grads), *[held(a) for a in earlier])


def store_halves(ref, value):
    _, shards, quarters, rows, _ = ref.shape
    for shard in range(shards):
        for quarter in range(quarters):
            for half in range(2):
                at = ((shard * quarters + quarter) * 2 + half) * rows
                ref[half, shard, quarter] = value[at : at + rows]


def weight_grad_kernel(half, order, inputs, grads, *refs):
    out, picked = refs[-2:]

    @pl.when(pl.program_id(0) == 0)
    def _():
        for i in range(4):
            size = picked.shape[1] // 4
            at = pl.multiple_of((order[0] * i + order[1 + half]) * size, size)
            picked[:, i * size : (i + 1) * size] = inputs[:, pl.ds(at, size)]

    block = grads[...].reshape(inputs.shape[0], grads.shape[-1])
    store_halves(out, mm(picked[...], block, TN).astype(BF16))


def weight_grad(half, order, inputs, grads, wide, first=0, earlier=()):
    count, width = inputs.shape
    seqs, parts, each, size = grads.shape
    rows = width // 64
    return pl.pallas_call(
        functools.partial(weight_grad_kernel, half),
        grid_spec=pltpu.PrefetchScalarGridSpec(
            num_scalar_prefetch=1,
            grid=(parts,),
            in_specs=[
                once((count, width)),
                pl.BlockSpec((seqs, 1, each, size), lambda j, *_: (0, j, 0, 0)),
            ]
            + [pl.BlockSpec(memory_space=pl.ANY)] * len(earlier),
            out_specs=pl.BlockSpec(
                (2, 4, 4, rows, size), lambda j, *_: (0, 0, 0, 0, first // size + j)
            ),
            scratch_shapes=[pltpu.VMEM((count, width // 2), BF16)],
        ),
        out_shape=jax.ShapeDtypeStruct((2, 4, 4, rows, wide), BF16),
        input_output_aliases={3: 0} if earlier else {},
        compiler_params=params(20),
        cost_estimate=cost(count * width * parts * size, count * (width + parts * size) * 2 + width * parts * size),
        name="weight_grad",
    )(order, inputs, grads, *earlier)


def norm_two_kernel(lengths, hidden_grad, weight, resid, cot, table, *outs):
    grad_resid, low_ref, mixed_grad, gain_grad, bias_grad, out_bias_grad = outs
    step = pl.program_id(0)
    rows, width = resid.shape[1:]
    valid = valid_rows(lengths[step], rows)
    grad = mm(hidden_grad[0], weight[:, width:], NT)
    unit, scale = norm_parts(resid[0])
    total = cot[0].astype(F32) * valid + norm_back(unit, scale, grad, table[5:6, :])
    grad_resid[0] = total
    low = total.astype(BF16)
    low_ref[0] = low
    mixed_grad[0] = mm(low, weight[:, :width], NT).astype(BF16)
    add_first(step, gain_grad, column_sum(grad * unit))
    add_first(step, bias_grad, column_sum(grad))
    add_first(step, out_bias_grad, column_sum(low.astype(F32)))


def norm_two_back(lengths, hidden_grad, weight, resid, cot, table):
    seqs, rows, width = resid.shape
    hidden = hidden_grad.shape[1]
    row_block = pl.BlockSpec((1, rows, width), lambda s, *_: (s, 0, 0))
    vec = pl.BlockSpec((1, width), lambda s, *_: (0, 0))
    return pl.pallas_call(
        norm_two_kernel,
        grid_spec=pltpu.PrefetchScalarGridSpec(
            num_scalar_prefetch=1,
            grid=(seqs,),
            in_specs=[
                pl.BlockSpec((1, rows, hidden), lambda s, *_: (s, 0, 0)),
                once((width, width + hidden)),
                row_block,
                row_block,
                once(table.shape),
            ],
            out_specs=[row_block] * 3 + [vec] * 3,
        ),
        out_shape=[
            far(resid.shape, F32),
            jax.ShapeDtypeStruct(resid.shape, BF16),
            jax.ShapeDtypeStruct(resid.shape, BF16),
        ]
        + [jax.ShapeDtypeStruct((1, width), F32)] * 3,
        compiler_params=params(40),
        cost_estimate=cost(2 * seqs * rows * width * (hidden + width), seqs * rows * (2 * hidden + 14 * width)),
        name="norm_two_back",
    )(lengths, held(hidden_grad.reshape(seqs, rows, hidden)), weight, held(resid), cot, table)


def norm_one_kernel(lengths, thirds, weight, x, grad_resid, table, *outs):
    input_grad, gain_grad, bias_grad, q_sum, v_sum = outs
    step = pl.program_id(0)
    rows, width = x.shape[1:]
    valid = valid_rows(lengths[step], rows)
    grad = mm(thirds[0, 0], weight[:, :width], NT)
    grad += mm(thirds[0, 1], weight[:, width : 2 * width], NT)
    grad += mm(thirds[0, 2], weight[:, 2 * width : 3 * width], NT)
    unit, scale = norm_parts(x[0].astype(F32) * valid)
    input_grad[0] = (grad_resid[0] + norm_back(unit, scale, grad, table[0:1, :])) * valid
    add_first(step, gain_grad, column_sum(grad * unit))
    add_first(step, bias_grad, column_sum(grad))
    add_first(step, q_sum, column_sum(thirds[0, 0].astype(F32)))
    add_first(step, v_sum, column_sum(thirds[0, 2].astype(F32)))


def norm_one_back(lengths, thirds, weight, x, grad_resid, table):
    seqs, rows, width = x.shape
    row_block = pl.BlockSpec((1, rows, width), lambda s, *_: (s, 0, 0))
    vec = pl.BlockSpec((1, width), lambda s, *_: (0, 0))
    return pl.pallas_call(
        norm_one_kernel,
        grid_spec=pltpu.PrefetchScalarGridSpec(
            num_scalar_prefetch=1,
            grid=(seqs,),
            in_specs=[
                pl.BlockSpec((1, 3, rows, width), lambda s, *_: (s, 0, 0, 0)),
            ]
            + [once(weight.shape), row_block, row_block, once(table.shape)],
            out_specs=[row_block] + [vec] * 4,
        ),
        out_shape=[far(x.shape, F32)] + [jax.ShapeDtypeStruct((1, width), F32)] * 4,
        compiler_params=params(32),
        cost_estimate=cost(6 * seqs * rows * width * width, seqs * rows * width * 16 + 6 * width * width),
        name="norm_one_back",
    )(lengths, held(thirds), weight, x, held(grad_resid), table)

def near_kernel(pos, *refs):
    for at in range(4):
        mine, other, out = refs[at], refs[4 + at], refs[8 + at]
        total = mine[...].astype(F32) + other[...].astype(F32)
        out[...] = total.astype(BF16).reshape(out.shape)


def near_sum(pos, own, arrived):
    _, shards, _, rows, wide = own.shape
    x = lambda pos: pos[0] % 2
    y = lambda pos: pos[0] // 2
    over_x = (1, 1, 2, 1, rows, wide)
    over_y = (1, 1, 1, 2, rows, wide)
    specs = [
        pl.BlockSpec(over_x, lambda s, pos: (0, s, 0, x(pos), 0, 0)),
        pl.BlockSpec(over_y, lambda s, pos: (1, s, y(pos), 0, 0, 0)),
        pl.BlockSpec(over_x, lambda s, pos: (0, s, 0, 1 - x(pos), 0, 0)),
        pl.BlockSpec(over_y, lambda s, pos: (1, s, 1 - y(pos), 0, 0, 0)),
    ]
    shape = (2, shards, 2, 2, rows, wide)
    return pl.pallas_call(
        near_kernel,
        grid_spec=pltpu.PrefetchScalarGridSpec(
            num_scalar_prefetch=1,
            grid=(shards,),
            in_specs=specs * 2,
            out_specs=[pl.BlockSpec((1, 2, rows, wide), lambda s, pos: (s, 0, 0, 0))] * 4,
        ),
        out_shape=[jax.ShapeDtypeStruct((shards, 2, rows, wide), BF16)] * 4,
        compiler_params=params(14),
        cost_estimate=cost(own.size, own.size * 6),
        name="near_sum",
    )(pos, *[own.reshape(shape)] * 4, *[arrived.reshape(shape)] * 4)


AXES = ("group", "dp")
Z = 4


def permutation(move):
    pairs = []
    for g in range(4):
        for d in range(2 * Z):
            to_g, to_z, to_c = move(g, d // 2, d % 2)
            pairs.append((g * 2 * Z + d, (to_g * Z + to_z) * 2 + to_c))
    return pairs


CORE = permutation(lambda g, z, c: (g, z, 1 - c))
OVER_X = permutation(lambda g, z, c: (g ^ 1, z, c))
OVER_Y = permutation(lambda g, z, c: (g ^ 2, z, c))
OVER_XY = permutation(lambda g, z, c: (g ^ 3, z, c))
OVER_Z = [permutation(lambda g, z, c, k=k: (g, (z + k) % Z, c)) for k in range(Z)]
NEAR_Z = permutation(lambda g, z, c: (g, z ^ 1, c))
FAR_Z = permutation(lambda g, z, c: (g, z ^ 2, c))


def send(array, pairs):
    return lax.ppermute(array, AXES, pairs)


def tie(value, *others):
    return lax.optimization_barrier((value,) + others)[0]


def pick(array, index, axis):
    return lax.dynamic_index_in_dim(array, index, axis, keepdims=False)


def plus(former, latter):
    return (former.astype(F32) + latter.astype(F32)).astype(BF16)


def quarters(shard, g):
    rows, wide = shard.shape
    parts = shard.reshape(4, 2, rows // 8, wide)
    return parts, pick(parts, g, 0)


def send_quarter(mine):
    return [send(mine, OVER_Z[k]) for k in range(1, Z)]


def send_xy(first, second):
    return send(first, OVER_X), send(second, OVER_Y)


def scatter_core(other):
    return send(other, CORE)


def scatter_far(first, second, from_x, from_y, g):
    x, y = g % 2, g // 2
    first = plus(first, from_x)
    second = plus(second, from_y)
    return pick(first, y, 1), pick(second, x, 1), pick(first, 1 - y, 1), pick(second, 1 - x, 1)


def scatter_z(first, second, from_y, from_x, z):
    quarter = jnp.stack([plus(first, from_y), plus(second, from_x)], 1)
    return pick(quarter, z, 0), [pick(quarter, (z + k) % Z, 0) for k in range(1, Z)]


def send_z(parts):
    return [send(part, OVER_Z[k]) for k, part in enumerate(parts, 1)]


def spread(mine, arrived):
    total = mine.astype(F32)
    for part in arrived:
        total = total + part.astype(F32)
    return total.astype(BF16)


def send_near(mine):
    return [send(mine, OVER_X), send(mine, OVER_Y), send(mine, OVER_XY)]


def placed(mine, others, g):
    grid = jnp.stack([mine, *others]).reshape(2, 2, *mine.shape)
    grid = jnp.where(g % 2 == 1, grid[:, ::-1], grid)
    grid = jnp.where(g // 2 == 1, grid[::-1], grid)
    return grid.astype(F32).reshape(-1, mine.shape[-1])


def trade(shard, g):
    rows, wide = shard.shape
    parts = shard.reshape(4, rows // 4, wide)
    return pick(parts, g, 0), [pick(parts, g ^ over, 0) for over in (1, 2, 3)]


def send_trade(parts):
    return [send(part, pairs) for part, pairs in zip(parts, (OVER_X, OVER_Y, OVER_XY))]


VEC = (0, 1, 3, 5, 6, 7, 9, 11)


def joined(vectors):
    total = sum(v.shape[0] for v in vectors)
    at = 0
    out = None
    for v in vectors:
        wide = lax.pad(v, jnp.zeros((), v.dtype), [(at, total - at - v.shape[0], 0)])
        out = wide if out is None else out + wide
        at += v.shape[0]
    return out


def widened(weight, vectors):
    rows = weight.shape[0]
    columns = joined(vectors).reshape(-1, rows).T
    columns = jnp.pad(columns, ((0, 0), (0, LANES - columns.shape[1])))
    return jnp.concatenate([weight, columns], 1)


def spaced(table, first, last, rows):
    part = table[first:last].reshape(last - first, -1, rows)
    return part.transpose(1, 0, 2).reshape(1, -1)


def packed_vectors(grads):
    return joined([grads[i].reshape(-1) for i in VEC])


def own_vectors(total, grads, shards):
    d = lax.axis_index("dp")
    at = 0
    summed = {}
    for i in VEC:
        size = shards[i].shape[0]
        summed[i] = lax.dynamic_slice(total, (at + d * size,), (size,))
        at += grads[i].size
    return summed


def over_dp(array):
    return lax.psum_scatter(array, "dp", scatter_dimension=0, tiled=True)


def local(ring, layer_input, lengths, *rest):
    shards, cot = rest[:12], rest[12]
    micro, seqs, rows, width = layer_input.shape
    count = micro * seqs
    g = lax.axis_index("group")
    d = lax.axis_index("dp")
    z, c = d // 2, d % 2
    pos = jnp.stack([g, z, c]).astype(jnp.int32)
    order = [2, 1 - c, c] if ring else [1, 0, 4]
    order = jnp.stack([jnp.asarray(v, jnp.int32) for v in order])
    lens = lengths.reshape(-1)
    x = layer_input.reshape(count, rows, width)
    cot = cot.reshape(count, rows, width)
    flat = lambda a: a.reshape(count * rows, a.shape[-1])
    rows_each = shards[2].shape[0]
    wanted = (widened(shards[2], [shards[i] for i in VEC]), jnp.concatenate([shards[4], shards[8]], 1), shards[10])

    if ring:
        parts_p, mine_p = quarters(wanted[0], g)
        parts_e, mine_e = quarters(wanted[1], g)
        ring_p = send_quarter(mine_p)
        core_p, core_e = send(parts_p, CORE), send(parts_e, CORE)
        stack_p = jnp.stack(tie(ring_p, core_p, core_e), 1)
        x_p, y_p = send_xy(stack_p, stack_p)
        mine_e = tie(mine_e, stack_p)
        e_one, e_three = send(mine_e, OVER_Z[1]), send(mine_e, OVER_Z[3])
        x_p, y_p, e_one, e_three, mine_e = tie((x_p, y_p, e_one, e_three, mine_e))
        b_p, a_p = send_xy(y_p[1], x_p[0])
        e_two = send(mine_e, OVER_Z[2])
        near_p = tie(jnp.stack([stack_p, x_p, y_p]), a_p, b_p)
        far_p = jnp.stack([a_p, b_p])
        pieces_p = [parts_p, near_p, far_p, core_p, send(near_p, CORE), send(far_p, CORE)]
        vectors = ()
    else:
        pieces = [lax.all_gather(w, "dp", axis=0, tiled=True) for w in wanted]
        pieces_p, pieces_e, reduce_w = [pieces[0]], [pieces[1]], pieces[2]
        table = pieces[0][:, 3 * width : 3 * width + 16].T.astype(F32)
        pair = spaced(table, 2, 4, rows_each)
        middle = jnp.zeros((1, width), F32)
        vectors = (table, jnp.concatenate([pair[:, :width], middle, pair[:, width:]], -1))
    normed, packed, up, up_sum, project_w, table = project(
        ring, rows_each, lens, pos, x, cot, pieces_p, vectors
    )
    expand_b = spaced(table, 7, 11, rows_each)
    lens_attend = lens
    if ring:
        stack_e = jnp.stack(tie((e_one, e_two, e_three), normed), 1)
        lens_attend, shard_r = tie((lens, wanted[2]), stack_e)
        x_e, y_e = send_xy(stack_e, stack_e)
        reduce_w = lax.all_gather(shard_r, "dp", axis=0, tiled=True)
    mixed, lse = attend(0, lens_attend, packed)
    for seq in range(1, count - 1):
        mixed, lse = attend(seq, lens_attend, packed, (mixed, lse))
    if ring:
        x_e, y_e = tie((x_e, y_e), mixed)
        near_e = jnp.stack([stack_e, x_e, y_e])
        lens_attend = tie(lens, near_e)
        b_e, a_e = send_xy(y_e[1], x_e[0])
        near_core_e = send(near_e, CORE)
    for seq in range(max(1, count - 1), count):
        mixed, lse = attend(seq, lens_attend, packed, (mixed, lse))
    if ring:
        a_e, b_e = tie((a_e, b_e), mixed)
        far_e = jnp.stack([a_e, b_e])
        pieces_e = [parts_e, near_e, far_e, core_e, near_core_e, send(far_e, CORE)]
    resid, normed_two, joint_w = branch(ring, lens, pos, x, mixed, table, pieces_e)
    act, slope, reduce_grad = expand(count, flat(normed_two), flat(up), joint_w, expand_b)
    shard_r = over_dp(reduce_grad)
    hidden_grad, hidden_sum = hidden_back(count, flat(up), reduce_w, slope)
    grad_resid, branch_low, mixed_grad, gain_two_grad, bias_two_grad, output_b_grad = norm_two_back(
        lens, hidden_grad, joint_w, resid, cot, table
    )
    thirds = attend_back(0, 1, lens, packed, lse, mixed_grad)
    expand_grad = whole_grad(flat(normed_two), tie(hidden_grad, thirds), 4 * width)
    shard_e = over_dp(expand_grad)
    lens_back = tie(lens, expand_grad)
    thirds = attend_back(1, count - 1, lens_back, packed, lse, mixed_grad, (thirds,))
    branch_part = branch_low.reshape(count, 1, rows, width)
    project_far = weight_grad(0, order, flat(mixed), branch_part, 4 * width)
    order_far = order
    if ring:
        mine_r, parts_r = trade(tie(shard_r, thirds), g)
        order_far = tie(order, parts_r)
        arrived_r = send_trade(parts_r)
    project_far = weight_grad(
        0, order_far, flat(normed), thirds, 4 * width, width, (project_far,)
    )
    order_near = order
    if ring:
        order_near = tie(order, project_far)
        arrived = send(project_far, CORE)
    project_near = weight_grad(1, order_near, flat(mixed), branch_part, 4 * width)
    project_near = weight_grad(
        1, order_near, flat(normed), thirds, 4 * width, width, (project_near,)
    )
    lens_one = lens
    if ring:
        spread_r = spread(mine_r, tie(arrived_r, project_near))
        ps = near_sum(pos, project_near, arrived)
        lens_one = tie(lens, ps, spread_r)
        from_x, from_y = send_xy(ps[2], ps[3])
    input_grad, gain_one_grad, bias_one_grad, query_sum, value_sum = norm_one_back(
        lens_one, thirds, project_w, x, grad_resid, table
    )
    vectors = {
        0: gain_one_grad,
        1: bias_one_grad,
        3: jnp.concatenate([query_sum, value_sum], -1),
        5: output_b_grad,
        6: gain_two_grad,
        7: bias_two_grad,
        9: hidden_sum,
        11: up_sum,
    }
    total = packed_vectors(vectors)
    lens_out = lens
    if ring:
        total = total.reshape(-1, LANES)
        total = total + send(total, CORE)
        total = (total + send(total, OVER_XY)) + (send(total, OVER_X) + send(total, OVER_Y))
        total, from_x, from_y = tie((total, from_x, from_y))
        ps = scatter_far(ps[0], ps[1], from_x, from_y, g)
        lens_out = tie(lens, ps)
        from_x, from_y = send_xy(ps[3], ps[2])
        column = [send(total, OVER_Z[k]) for k in range(1, Z)]
    layer_output = reduce_out(lens_out, resid, act, reduce_w, table)
    sums = {}
    if ring:
        (from_x, from_y, column), layer_output = lax.optimization_barrier(
            ((from_x, from_y, column), layer_output)
        )
        mine_z, parts_z = scatter_z(ps[0], ps[1], from_y, from_x, z)
        arrived_p = send_z(parts_z)
        spread_r = tie(spread_r, parts_z)
        x_r, y_r = send_xy(spread_r, spread_r)
        half = spread_r.shape[0] // 2
        b_r, a_r = send_xy(y_r[half:], x_r[:half])
        sums[10] = placed(spread_r, [x_r, y_r, jnp.concatenate([a_r, b_r])], g)
        total = (total + column[1]) + (column[0] + column[2])
        mine_e, parts_e = trade(tie(shard_e, (x_r, y_r)), g)
        arrived_e = send_trade(parts_e)
        spread_p = spread(mine_z, tie(arrived_p, parts_e))
        near_p = send_near(spread_p)
        spread_e = spread(mine_e, tie(arrived_e, spread_p))
        near_e = send_near(spread_e)
        joint_sum = placed(spread_p, near_p, g)
        sums[8] = placed(spread_e, near_e, g)
    else:
        total = lax.psum(total, ("group", "dp"))
        sums[10] = lax.psum(shard_r, "group").astype(F32)
        sums[8] = lax.psum(shard_e, "group").astype(F32)
        parts = [a.transpose(1, 2, 0, 3, 4) for a in (project_far, project_near)]
        parts = over_dp(jnp.concatenate(parts).reshape(width, 4 * width))
        joint_sum = lax.psum(parts, "group").astype(F32)
    sums.update(own_vectors(total.reshape(-1), vectors, shards))
    sums[4] = joint_sum[:, :width]
    sums[2] = joint_sum[:, width:]
    return (
        layer_output.reshape(layer_input.shape),
        input_grad.reshape(layer_input.shape),
        *[sums[i] for i in range(12)],
    )


def solution(mesh):
    ring = mesh.shape["group"] == 4 and mesh.shape["dp"] == 2 * Z
    rows = P(None, ("group", "dp"), None, None)
    vec = P("dp")
    mat = P("dp", None)
    kinds = (vec, vec, mat, vec, mat, vec, vec, vec, mat, vec, mat, vec)
    return jax.shard_map(
        functools.partial(local, ring),
        mesh=mesh,
        in_specs=(rows, P(None, ("group", "dp")), *kinds, rows),
        out_specs=(rows, rows, *kinds),
        check_vma=False,
    )
```

time: 475 us -> 416 us (0.88)
  the two profiles are of different devices: /device:TPU:8 before, /device:TPU:0 now
where the time goes in v3:
time: 416 us; the launch traced here: 408 us
  Pallas kernels  202 us (49%)
  waiting for transfers between devices  93.8 us (23%)
  starting transfers between devices  53.8 us (13%)
  local copies, waits for them, and re-layouts  23.1 us (6%)
  other arithmetic  20.3 us (5%)
  between operations  14.9 us (4%)
    ppermute x51, waiting for transfers between devices, send(): return lax.ppermute(array, AXES, pairs)  93.7 us
    ppermute x51, starting transfers between devices, send(): return lax.ppermute(array, AXES, pairs)  53.2 us
    pallas_call x2, Pallas kernels, attend_back(): pl.pallas_call(functools.partial(attend_back_kernel, seq), grid_spec=pltp...  33.9 us
    pallas_call x1, Pallas kernels, expand(): pl.pallas_call(functools.partial(expand_kernel, seqs), grid=(8,), in_spec...  27.3 us
    pallas_call x3, Pallas kernels, attend(): pl.pallas_call(functools.partial(attend_kernel, seq), grid_spec=pltpu.Pre...  21.9 us
    pallas_call x1, Pallas kernels, norm_two_back(): pl.pallas_call(norm_two_kernel, grid_spec=pltpu.PrefetchScalarGridSpec(nu...  19.7 us
    pallas_call x4, Pallas kernels, weight_grad(): pl.pallas_call(functools.partial(weight_grad_kernel, half), grid_spec=plt...  16.3 us
    pallas_call x1, Pallas kernels, hidden_back(): pl.pallas_call(functools.partial(hidden_back_kernel, seqs), grid=(8,), in...  15.8 us
  transfers between devices with their start and end apart: 54, of which 25 were waited for; matrix products, arithmetic and copies ran while one was open for 6% of the time, Pallas kernels for 50%

profile of v3, /device:TPU:0, one launch (start us, length us, event | category | flops | bytes accessed | tf_op | source)
XLA Modules:
  0.0 408.0 jit_solution(6217749037865681383)
XLA Ops:
  12.5 5.1 %collective-permute-start.2 = (bf16[2,16,3200]{2,1,0:T(8,128)(2,1)S(1)}, bf16[2,16,3200]{2,1,0:T(8,128)(2,1)S(1)}, u32[]{:S(2)}, u32[]{:S(2)}) collective-permute-start(bf16[2,16,3200]{2,1,0:T(8,128)(2,1)S(1)} %dynamic-slice_bitcast_fusion.11), channel_id=1, source_target_pairs={{0,6},{1,7},{2,0},{3,1},{4,2},{5,3},{6,4},{7,5},{8,14},{9,15},{10,... | collective-permute-start | bytes 614408 | tf_op jit(solution)/shard_map/ppermute | solution.py:692
  18.6 4.5 %collective-permute-done.2 = bf16[2,16,3200]{2,1,0:T(8,128)(2,1)S(1)} collective-permute-done((bf16[2,16,3200]{2,1,0:T(8,128)(2,1)S(1)}, bf16[2,16,3200]{2,1,0:T(8,128)(2,1)S(1)}, u32[]{:S(2)}, u32[]{:S(2)}) %collective-permute-start.2) | collective-permute-done | bytes 204832 | tf_op jit(solution)/shard_map/ppermute | solution.py:692
  23.1 12.1 %collective-permute-done.1 = bf16[2,16,3200]{2,1,0:T(8,128)(2,1)S(1)} collective-permute-done((bf16[2,16,3200]{2,1,0:T(8,128)(2,1)S(1)}, bf16[2,16,3200]{2,1,0:T(8,128)(2,1)S(1)}, u32[]{:S(2)}, u32[]{:S(2)}) %collective-permute-start.1) | collective-permute-done | bytes 204832 | tf_op jit(solution)/shard_map/ppermute | solution.py:692
  40.5 6.3 %collective-permute-done.8 = bf16[2,16,5120]{2,1,0:T(8,128)(2,1)S(1)} collective-permute-done((bf16[2,16,5120]{2,1,0:T(8,128)(2,1)S(1)}, bf16[2,16,5120]{2,1,0:T(8,128)(2,1)S(1)}, u32[]{:S(2)}, u32[]{:S(2)}) %collective-permute-start.8) | collective-permute-done | bytes 327712 | tf_op jit(solution)/shard_map/ppermute | solution.py:692
  46.9 9.2 %collective-permute-done.7 = bf16[2,16,5120]{2,1,0:T(8,128)(2,1)S(1)} collective-permute-done((bf16[2,16,5120]{2,1,0:T(8,128)(2,1)S(1)}, bf16[2,16,5120]{2,1,0:T(8,128)(2,1)S(1)}, u32[]{:S(2)}, u32[]{:S(2)}) %collective-permute-start.7) | collective-permute-done | bytes 327712 | tf_op jit(solution)/shard_map/ppermute | solution.py:692
  58.7 4.4 %collective-permute-done.11 = bf16[3,16,3200]{2,1,0:T(8,128)(2,1)S(1)} collective-permute-done((bf16[3,16,3200]{2,1,0:T(8,128)(2,1)S(1)}, bf16[3,16,3200]{2,1,0:T(8,128)(2,1)S(1)}, u32[]{:S(2)}, u32[]{:S(2)}) %collective-permute-start.11) | collective-permute-done | bytes 307232 | tf_op jit(solution)/shard_map/ppermute | solution.py:692
  70.2 13.3 %norm_project.1 = (bf16[3,320,1024]{2,1,0:T(8,128)(2,1)S(1)}, bf16[3,320,3072]{2,1,0:T(8,128)(2,1)}, bf16[3,320,1024]{2,1,0:T(8,128)(2,1)S(1)}, f32[1,1024]{1,0:...) custom-call(s32[3]{0:T(128)S(1)} %bitcast.199, s32[3]{0:T(128)S(1)} %add_add_fusion.1.pos, ...), custom_call_target="tpu_custom_call" | custom-call | flops 6039797760 | bytes 26345472 | tf_op jit(solution)/shard_map/norm_project/pallas_call | solution.py:176
  90.0 7.3 %attend.3 = (bf16[3,320,1024]{2,1,0:T(8,128)(2,1)S(1)}, f32[3,2,8,320]{3,2,1,0:T(8,128)S(1)}) custom-call(s32[3]{0:T(128)S(1)} %bitcast.200, bf16[3,320,3072]{2,1,0:T(8,128)(2,1)} %get-tuple-element.111.q.k.v, bf16[3,320,3072]{2,1,0:T(8,128)(2,1)} %get-tuple-element.111.q.k.v, bf16[3,320,3072]{2,1,0:T(8,128)(2,1)} %get-tuple-element.111.q.k.v), custom_call_target="tpu_custom_call" | custom-call | flops 3355443200 | bytes 2949120 | tf_op jit(solution)/shard_map/attend/pallas_call | solution.py:246
  97.3 7.3 %attend.4 = (bf16[3,320,1024]{2,1,0:T(8,128)(2,1)S(1)}, f32[3,2,8,320]{3,2,1,0:T(8,128)S(1)}) custom-call(s32[3]{0:T(128)S(1)} %bitcast.201, bf16[3,320,3072]{2,1,0:T(8,128)(2,1)} %get-tuple-element.111.q.k.v, bf16[3,320,3072]{2,1,0:T(8,128)(2,1)} %get-tuple-element.111.q.k.v, ...), custom_call_target="tpu_custom_call", output_to_operand_aliasing={{0}: (4, {}), {1}: (5, {})} | custom-call | flops 3355443200 | bytes 2949120 | tf_op jit(solution)/shard_map/attend/pallas_call | solution.py:246
  104.6 7.4 %collective-permute-done.15 = bf16[2,3,16,5120]{3,2,1,0:T(8,128)(2,1)S(1)} collective-permute-done((bf16[2,3,16,5120]{3,2,1,0:T(8,128)(2,1)}, bf16[2,3,16,5120]{3,2,1,0:T(8,128)(2,1)S(1)}, u32[]{:S(2)}, u32[]{:S(2)}) %collective-permute-start.15) | collective-permute-done | bytes 983072 | tf_op jit(solution)/shard_map/ppermute | solution.py:692
  115.8 7.3 %attend.5 = (bf16[3,320,1024]{2,1,0:T(8,128)(2,1)S(1)}, f32[3,2,8,320]{3,2,1,0:T(8,128)S(1)}) custom-call(s32[3]{0:T(128)S(1)} %bitcast.202, bf16[3,320,3072]{2,1,0:T(8,128)(2,1)} %get-tuple-element.111.q.k.v, bf16[3,320,3072]{2,1,0:T(8,128)(2,1)} %get-tuple-element.111.q.k.v, ...), custom_call_target="tpu_custom_call", output_to_operand_aliasing={{0}: (4, {}), {1}: (5, {})} | custom-call | flops 3355443200 | bytes 2949120 | tf_op jit(solution)/shard_map/attend/pallas_call | solution.py:246
  123.1 3.3 collective-permute-done.17
  130.3 11.6 %branch.1 = (f32[3,320,1024]{2,1,0:T(8,128)}, bf16[3,320,1024]{2,1,0:T(8,128)(2,1)S(1)}, bf16[4,2,4,2,16,5120]{5,4,3,2,1,0:T(8,128)(2,1)}) custom-call(s32[3]{0:T(128)S(1)} %bitcast.203, s32[3]{0:T(128)S(1)} %add_add_fusion.1.pos, bf16[3,320,1024]{2,1,0:T(8,128)(2,1)S(1)} %bitcast.175, bf16[3,320,1024]{2,1,0:T(8,128)(2,1)S(1)} %get-tuple-element.119.mixed, ...), custom_call_target="tpu_custom_call" | custom-call | flops 2013265920 | bytes 30801920 | tf_op jit(solution)/shard_map/branch/pallas_call | solution.py:353
  142.0 27.3 %expand.1 = (bf16[960,4096]{1,0:T(8,128)(2,1)}, bf16[960,4096]{1,0:T(8,128)(2,1)}, bf16[4096,1024]{1,0:T(8,128)(2,1)}) custom-call(bf16[960,1024]{1,0:T(8,128)(2,1)S(1)} %bitcast.211, bf16[960,1024]{1,0:T(8,128)(2,1)S(1)} %bitcast.216, bf16[1024,5120]{1,0:T(8,128)(2,1)} %bitcast.253, f32[1,4096]{1,0:T(1,128)S(1)} %bitcast.198), custom_call_target="tpu_custom_call" | custom-call | flops 16106127360 | bytes 32505856 | tf_op jit(solution)/shard_map/expand/pallas_call | solution.py:401
  171.0 15.8 %hidden_back.1 = (bf16[960,4096]{1,0:T(8,128)(2,1)}, f32[1,4096]{1,0:T(1,128)S(1)}) custom-call(bf16[960,1024]{1,0:T(8,128)(2,1)S(1)} %bitcast.217, bf16[4096,1024]{1,0:T(8,128)(2,1)} %all-gather.2.cloned.1.call-done.weight, bf16[960,4096]{1,0:T(8,128)(2,1)} %get-tuple-element.128.slope), custom_call_target="tpu_custom_call" | custom-call | flops 8053063680 | bytes 24117248 | tf_op jit(solution)/shard_map/hidden_back/pallas_call | solution.py:465
  186.8 19.7 %norm_two_back.1 = (f32[3,320,1024]{2,1,0:T(8,128)}, bf16[3,320,1024]{2,1,0:T(8,128)(2,1)S(1)}, bf16[3,320,1024]{2,1,0:T(8,128)(2,1)S(1)}, f32[1,1024]{1,0:T(1,1...) custom-call(s32[3]{0:T(128)S(1)} %bitcast.204, bf16[3,320,4096]{2,1,0:T(8,128)(2,1)} %bitcast.256, ...), custom_call_target="tpu_custom_call" | custom-call | flops 10066329600 | bytes 21626880 | tf_op jit(solution)/shard_map/norm_two_back/pallas_call | solution.py:571
  206.5 13.1 %attend_back.2.refs_0_ = bf16[3,3,320,1024]{3,2,1,0:T(8,128)(2,1)} custom-call(s32[3]{0:T(128)S(1)} %bitcast.205, bf16[3,320,3072]{2,1,0:T(8,128)(2,1)} %get-tuple-element.111.q.k.v, bf16[3,320,3072]{2,1,0:T(8,128)(2,1)} %get-tuple-element.111.q.k.v, bf16[3,320,3072]{2,1,0:T(8,128)(2,1)} %get-tuple-element.111.q.k.v, ...), custom_call_target="tpu_custom_call" | custom-call | flops 8388608000 | bytes 4915200 | tf_op jit(solution)/shard_map/attend_back/pallas_call | solution.py:309
  219.6 13.8 %whole_grad.1 = bf16[1024,4096]{1,0:T(8,128)(2,1)} custom-call(bf16[960,1024]{1,0:T(8,128)(2,1)S(1)} %bitcast.212, bf16[960,4096]{1,0:T(8,128)(2,1)} %get-tuple-element.133.grads), custom_call_target="tpu_custom_call" | custom-call | flops 8053063680 | bytes 18219008 | tf_op jit(solution)/shard_map/whole_grad/pallas_call | solution.py:485
  235.0 3.0 weight_grad.4.refs_0_
  238.0 20.9 %attend_back.3.grads.thirds = bf16[3,3,320,1024]{3,2,1,0:T(8,128)(2,1)} custom-call(s32[3]{0:T(128)S(1)} %bitcast.206, bf16[3,320,3072]{2,1,0:T(8,128)(2,1)} %get-tuple-element.111.q.k.v, bf16[3,320,3072]{2,1,0:T(8,128)(2,1)} %get-tuple-element.111.q.k.v, bf16[3,320,3072]{2,1,0:T(8,128)(2,1)} %get-tuple-element.111.q.k.v, ...), custom_call_target="tpu_custom_call", output_to_operand_aliasing={{}: (6, {})} | custom-call | flops 16777216000 | bytes 9830400 | tf_op jit(solution)/shard_map/attend_back/pallas_call | solution.py:309
  264.3 6.1 %weight_grad.5 = bf16[2,4,4,16,4096]{4,3,2,1,0:T(8,128)(2,1)} custom-call(s32[3]{0:T(128)S(1)} %add_add_fusion.2.order, bf16[960,1024]{1,0:T(8,128)(2,1)S(1)} %bitcast.167, bf16[3,3,320,1024]{3,2,1,0:T(8,128)(2,1)S(1)} %copy-done, bf16[2,4,4,16,4096]{4,3,2,1,0:T(8,128)(2,1)} %weight_grad.4.refs_0_), custom_call_target="tpu_custom_call", output_to_operand_aliasing={{}: (3, {})} | custom-call | flops 3019898880 | bytes 11010048 | tf_op jit(solution)/shard_map/weight_grad/pallas_call | solution.py:526
  276.2 5.3 %weight_grad.7 = bf16[2,4,4,16,4096]{4,3,2,1,0:T(8,128)(2,1)S(1)} custom-call(s32[3]{0:T(128)S(1)} %add_add_fusion.2.order, bf16[960,1024]{1,0:T(8,128)(2,1)S(1)} %bitcast.168, bf16[3,3,320,1024]{3,2,1,0:T(8,128)(2,1)S(1)} %copy-done.1, bf16[2,4,4,16,4096]{4,3,2,1,0:T(8,128)(2,1)S(1)} %weight_grad.6.refs_0_), custom_call_target="tpu_custom_call", output_to_operand_aliasing={{}: (3, {})} | custom-call | flops 3019898880 | bytes 11010048 | tf_op jit(solution)/shard_map/weight_grad/pallas_call | solution.py:526
  281.5 4.1 %collective-permute-done.22 = bf16[128,1024]{1,0:T(8,128)(2,1)S(1)} collective-permute-done((bf16[128,1024]{1,0:T(8,128)(2,1)S(1)}, bf16[128,1024]{1,0:T(8,128)(2,1)S(1)}, u32[]{:S(2)}, u32[]{:S(2)}) %collective-permute-start.22) | collective-permute-done | bytes 262176 | tf_op jit(solution)/shard_map/ppermute | solution.py:692
  287.7 2.9 near_sum.1
  292.7 13.1 %norm_one_back.1 = (f32[3,320,1024]{2,1,0:T(8,128)}, f32[1,1024]{1,0:T(1,128)S(1)}, f32[1,1024]{1,0:T(1,128)S(1)}, f32[1,1024]{1,0:T(1,128)S(1)}, f32[1,1024]{1,0:T(1,128)S(1)}) custom-call(s32[3]{0:T(128)S(1)} %bitcast.207, bf16[3,3,320,1024]{3,2,1,0:T(8,128)(2,1)} %attend_back.3.grads.thirds, bf16[1024,3200]{1,0:T(8,128)(2,1)S(1)} %bitcast.215, ...), custom_call_target="tpu_custom_call" | custom-call | flops 6039797760 | bytes 22020096 | tf_op jit(solution)/shard_map/norm_one_back/pallas_call | solution.py:617
  310.7 6.7 %collective-permute-done.26 = f32[96,128]{1,0:T(8,128)S(1)} collective-permute-done((f32[96,128]{1,0:T(8,128)S(1)}, f32[96,128]{1,0:T(8,128)S(1)}, u32[]{:S(2)}, u32[]{:S(2)}) %collective-permute-start.26) | collective-permute-done | bytes 49184 | tf_op jit(solution)/shard_map/ppermute | solution.py:692
  325.5 3.4 copy-done.13
  328.9 12.4 %reduce_out.1 = f32[3,320,1024]{2,1,0:T(8,128)} custom-call(s32[3]{0:T(128)S(1)} %bitcast.208, f32[3,320,1024]{2,1,0:T(8,128)} %get-tuple-element.131.resid, bf16[3,320,4096]{2,1,0:T(8,128)(2,1)} %bitcast.255, bf16[4096,1024]{1,0:T(8,128)(2,1)S(1)} %copy-done.13, f32[16,1024]{1,0:T(8,128)S(1)} %get-tuple-element.120.table), custom_call_target="tpu_custom_call" | custom-call | flops 8053063680 | bytes 24117248 | tf_op jit(solution)/shard_map/reduce_out/pallas_call | solution.py:428
  345.1 2.7 collective-permute-start.37
  364.3 9.6 %collective-permute-done.36 = bf16[2,16,4096]{2,1,0:T(8,128)(2,1)S(1)} collective-permute-done((bf16[2,16,4096]{2,1,0:T(8,128)(2,1)S(1)}, bf16[2,16,4096]{2,1,0:T(8,128)(2,1)S(1)}, u32[]{:S(2)}, u32[]{:S(2)}) %collective-permute-start.36) | collective-permute-done | bytes 262176 | tf_op jit(solution)/shard_map/ppermute | solution.py:692
  385.7 5.5 %collective-permute-done.41 = bf16[2,16,4096]{2,1,0:T(8,128)(2,1)S(1)} collective-permute-done((bf16[2,16,4096]{2,1,0:T(8,128)(2,1)S(1)}, bf16[2,16,4096]{2,1,0:T(8,128)(2,1)S(1)}, u32[]{:S(2)}, u32[]{:S(2)}) %collective-permute-start.41) | collective-permute-done | bytes 262176 | tf_op jit(solution)/shard_map/ppermute | solution.py:692
  395.6 3.2 collective-permute-done.47
  (237 shorter events, 105.4 us)
Async XLA Ops:
  7.3 162.2 %all-gather.2.cloned.1.call-start = ((), (), s32[]{:S(2)}) async-start(), calls=%async_computation.3 | async-start | bytes 9437184 | tf_op jit(solution)/shard_map/all_gather | solution.py:863
  8.7 26.5 %collective-permute-start.4 = (bf16[4,2,16,5120]{3,2,1,0:T(8,128)(2,1)S(1)}, bf16[4,2,16,5120]{3,2,1,0:T(8,128)(2,1)S(1)}, u32[]{:S(2)}, u32[]{:S(2)}) collective-permute-start(bf16[4,2,16,5120]{3,2,1,0:T(8,128)(2,1)S(1)} %bitcast.171), channel_id=1, source_target_pairs={{0,1},{1,0},{2,3},{3,2},{4,5},{5,4},{6,7},{7,6},{8,9},{9,8},{10,11... | collective-permute-start | bytes 3932168 | tf_op jit(solution)/shard_map/ppermute | solution.py:692
  11.5 23.7 %collective-permute-start.3 = (bf16[4,2,16,3200]{3,2,1,0:T(8,128)(2,1)}, bf16[4,2,16,3200]{3,2,1,0:T(8,128)(2,1)}, u32[]{:S(2)}, u32[]{:S(2)}) collective-permute-start(bf16[4,2,16,3200]{3,2,1,0:T(8,128)(2,1)} %bitcast.8.refs_0_), channel_id=1, source_target_pairs={{0,1},{1,0},{2,3},{3,2},{4,5},{5,4},{6,7},{7,6},{8,9},{9,8},{10,11... | collective-permute-start | bytes 2457608 | tf_op jit(solution)/shard_map/ppermute | solution.py:692
  17.6 17.6 %collective-permute-start.1 = (bf16[2,16,3200]{2,1,0:T(8,128)(2,1)S(1)}, bf16[2,16,3200]{2,1,0:T(8,128)(2,1)S(1)}, u32[]{:S(2)}, u32[]{:S(2)}) collective-permute-start(bf16[2,16,3200]{2,1,0:T(8,128)(2,1)S(1)} %dynamic-slice_bitcast_fusion.11), channel_id=1, source_target_pairs={{0,4},{1,5},{2,6},{3,7},{4,0},{5,1},{6,2},{7,3},{8,12},{9,13},{10,... | collective-permute-start | bytes 614408 | tf_op jit(solution)/shard_map/ppermute | solution.py:692
  17.6 17.6 %collective-permute-start = (bf16[2,16,3200]{2,1,0:T(8,128)(2,1)S(1)}, bf16[2,16,3200]{2,1,0:T(8,128)(2,1)S(1)}, u32[]{:S(2)}, u32[]{:S(2)}) collective-permute-start(bf16[2,16,3200]{2,1,0:T(8,128)(2,1)S(1)} %dynamic-slice_bitcast_fusion.11), channel_id=1, source_target_pairs={{0,2},{1,3},{2,4},{3,5},{4,6},{5,7},{6,0},{7,1},{8,10},{9,11},{10,... | collective-permute-start | bytes 614408 | tf_op jit(solution)/shard_map/ppermute | solution.py:692
  35.3 20.7 %collective-permute-start.6 = (bf16[2,3,16,3200]{3,2,1,0:T(8,128)(2,1)S(1)}, bf16[2,3,16,3200]{3,2,1,0:T(8,128)(2,1)S(1)}, u32[]{:S(2)}, u32[]{:S(2)}) collective-permute-start(bf16[2,3,16,3200]{3,2,1,0:T(8,128)(2,1)S(1)} %get-tuple-element.222), channel_id=1, source_target_pairs={{0,16},{1,17},{2,18},{3,19},{4,20},{5,21},{6,22},{7,23},{8,24},{9,... | collective-permute-start | bytes 1843208 | tf_op jit(solution)/shard_map/ppermute | solution.py:692
  36.9 19.2 %collective-permute-start.5 = (bf16[2,3,16,3200]{3,2,1,0:T(8,128)(2,1)S(1)}, bf16[2,3,16,3200]{3,2,1,0:T(8,128)(2,1)S(1)}, u32[]{:S(2)}, u32[]{:S(2)}) collective-permute-start(bf16[2,3,16,3200]{3,2,1,0:T(8,128)(2,1)S(1)} %get-tuple-element.222), channel_id=1, source_target_pairs={{0,8},{1,9},{2,10},{3,11},{4,12},{5,13},{6,14},{7,15},{8,0},{9,1},... | collective-permute-start | bytes 1843208 | tf_op jit(solution)/shard_map/ppermute | solution.py:692
  38.6 17.4 %collective-permute-start.7 = (bf16[2,16,5120]{2,1,0:T(8,128)(2,1)S(1)}, bf16[2,16,5120]{2,1,0:T(8,128)(2,1)S(1)}, u32[]{:S(2)}, u32[]{:S(2)}) collective-permute-start(bf16[2,16,5120]{2,1,0:T(8,128)(2,1)S(1)} %dynamic-slice_bitcast_fusion.4), channel_id=1, source_target_pairs={{0,2},{1,3},{2,4},{3,5},{4,6},{5,7},{6,0},{7,1},{8,10},{9,11},{10,... | collective-permute-start | bytes 983048 | tf_op jit(solution)/shard_map/ppermute | solution.py:692
  65.0 20.9 %collective-permute-start.9 = (bf16[2,16,5120]{2,1,0:T(8,128)(2,1)}, bf16[2,16,5120]{2,1,0:T(8,128)(2,1)S(1)}, u32[]{:S(2)}, u32[]{:S(2)}) collective-permute-start(bf16[2,16,5120]{2,1,0:T(8,128)(2,1)} %copy-done.25), channel_id=1, source_target_pairs={{0,4},{1,5},{2,6},{3,7},{4,0},{5,1},{6,2},{7,3},{8,12},{9,13},{10,... | collective-permute-start | bytes 983048 | tf_op jit(solution)/shard_map/ppermute | solution.py:692
  87.4 171.5 %reduce-scatter.3.cloned.1.call-start = ((), (), s32[]{:S(2)}) async-start(), calls=%async_computation.2 | async-start | bytes 9437184 | tf_op jit(solution)/shard_map/reduce_scatter | solution.py:811
  87.9 24.1 %collective-permute-start.15 = (bf16[2,3,16,5120]{3,2,1,0:T(8,128)(2,1)}, bf16[2,3,16,5120]{3,2,1,0:T(8,128)(2,1)S(1)}, u32[]{:S(2)}, u32[]{:S(2)}) collective-permute-start(bf16[2,3,16,5120]{3,2,1,0:T(8,128)(2,1)} %get-tuple-element.220), channel_id=1, source_target_pairs={{0,16},{1,17},{2,18},{3,19},{4,20},{5,21},{6,22},{7,23},{8,24},{9,... | collective-permute-start | bytes 2949128 | tf_op jit(solution)/shard_map/ppermute | solution.py:692
  88.5 23.7 %collective-permute-start.14 = (bf16[2,3,16,5120]{3,2,1,0:T(8,128)(2,1)}, bf16[2,3,16,5120]{3,2,1,0:T(8,128)(2,1)S(1)}, u32[]{:S(2)}, u32[]{:S(2)}) collective-permute-start(bf16[2,3,16,5120]{3,2,1,0:T(8,128)(2,1)} %get-tuple-element.220), channel_id=1, source_target_pairs={{0,8},{1,9},{2,10},{3,11},{4,12},{5,13},{6,14},{7,15},{8,0},{9,1},... | collective-permute-start | bytes 2949128 | tf_op jit(solution)/shard_map/ppermute | solution.py:692
  112.5 17.8 %collective-permute-start.18 = (bf16[3,2,3,16,5120]{4,3,2,1,0:T(8,128)(2,1)S(1)}, bf16[3,2,3,16,5120]{4,3,2,1,0:T(8,128)(2,1)S(1)}, u32[]{:S(2)}, u32[]{:S(2)}) collective-permute-start(bf16[3,2,3,16,5120]{4,3,2,1,0:T(8,128)(2,1)S(1)} %pad_maximum_fusion.refs_1_), channel_id=1, source_target_pairs={{0,1},{1,0},{2,3},{3,2},{4,5},{5,4},{6,7},{7,6},{8,9},{9,8},{10,11... | collective-permute-start | bytes 8847368 | tf_op jit(solution)/shard_map/ppermute | solution.py:692
  169.4 190.2 %reduce-scatter.5.cloned.1.call-start = ((), (), s32[]{:S(2)}) async-start(), calls=%async_computation.4 | async-start | bytes 9437184 | tf_op jit(solution)/shard_map/reduce_scatter | solution.py:811
  270.4 17.2 %collective-permute-start.20 = (bf16[2,4,4,16,4096]{4,3,2,1,0:T(8,128)(2,1)}, bf16[2,4,4,16,4096]{4,3,2,1,0:T(8,128)(2,1)S(1)}, u32[]{:S(2)}, u32[]{:S(2)}) collective-permute-start(bf16[2,4,4,16,4096]{4,3,2,1,0:T(8,128)(2,1)} %weight_grad.5), channel_id=1, source_target_pairs={{0,1},{1,0},{2,3},{3,2},{4,5},{5,4},{6,7},{7,6},{8,9},{9,8},{10,11... | collective-permute-start | bytes 12582920 | tf_op jit(solution)/shard_map/ppermute | solution.py:692
  290.6 28.1 %collective-permute-start.28 = (bf16[4,2,16,4096]{3,2,1,0:T(8,128)(2,1)}, bf16[4,2,16,4096]{3,2,1,0:T(8,128)(2,1)}, u32[]{:S(2)}, u32[]{:S(2)}) collective-permute-start(bf16[4,2,16,4096]{3,2,1,0:T(8,128)(2,1)} %get-tuple-element.141), channel_id=1, source_target_pairs={{0,8},{1,9},{2,10},{3,11},{4,12},{5,13},{6,14},{7,15},{8,0},{9,1},... | collective-permute-start | bytes 3145736 | tf_op jit(solution)/shard_map/ppermute | solution.py:692
  291.7 27.0 %collective-permute-start.29 = (bf16[4,2,16,4096]{3,2,1,0:T(8,128)(2,1)S(1)}, bf16[4,2,16,4096]{3,2,1,0:T(8,128)(2,1)}, u32[]{:S(2)}, u32[]{:S(2)}) collective-permute-start(bf16[4,2,16,4096]{3,2,1,0:T(8,128)(2,1)S(1)} %get-tuple-element.142), channel_id=1, source_target_pairs={{0,16},{1,17},{2,18},{3,19},{4,20},{5,21},{6,22},{7,23},{8,24},{9,... | collective-permute-start | bytes 3145736 | tf_op jit(solution)/shard_map/ppermute | solution.py:692
  318.7 22.6 %collective-permute-start.34 = (f32[96,128]{1,0:T(8,128)S(1)}, f32[96,128]{1,0:T(8,128)S(1)}, u32[]{:S(2)}, u32[]{:S(2)}) collective-permute-start(f32[96,128]{1,0:T(8,128)S(1)} %add_add_fusion), channel_id=1, source_target_pairs={{0,6},{1,7},{2,0},{3,1},{4,2},{5,3},{6,4},{7,5},{8,14},{9,15},{10,... | collective-permute-start | bytes 147464 | tf_op jit(solution)/shard_map/ppermute | solution.py:692
  319.7 21.6 %collective-permute-start.33 = (f32[96,128]{1,0:T(8,128)S(1)}, f32[96,128]{1,0:T(8,128)S(1)}, u32[]{:S(2)}, u32[]{:S(2)}) collective-permute-start(f32[96,128]{1,0:T(8,128)S(1)} %add_add_fusion), channel_id=1, source_target_pairs={{0,4},{1,5},{2,6},{3,7},{4,0},{5,1},{6,2},{7,3},{8,12},{9,13},{10,... | collective-permute-start | bytes 147464 | tf_op jit(solution)/shard_map/ppermute | solution.py:692
  319.7 21.6 %collective-permute-start.32 = (f32[96,128]{1,0:T(8,128)S(1)}, f32[96,128]{1,0:T(8,128)S(1)}, u32[]{:S(2)}, u32[]{:S(2)}) collective-permute-start(f32[96,128]{1,0:T(8,128)S(1)} %add_add_fusion), channel_id=1, source_target_pairs={{0,2},{1,3},{2,4},{3,5},{4,6},{5,7},{6,0},{7,1},{8,10},{9,11},{10,... | collective-permute-start | bytes 147464 | tf_op jit(solution)/shard_map/ppermute | solution.py:692
  323.2 18.2 %collective-permute-start.31 = (bf16[4,16,4096]{2,1,0:T(8,128)(2,1)S(1)}, bf16[4,16,4096]{2,1,0:T(8,128)(2,1)S(1)}, u32[]{:S(2)}, u32[]{:S(2)}) collective-permute-start(bf16[4,16,4096]{2,1,0:T(8,128)(2,1)S(1)} %get-tuple-element.215), channel_id=1, source_target_pairs={{0,16},{1,17},{2,18},{3,19},{4,20},{5,21},{6,22},{7,23},{8,24},{9,... | collective-permute-start | bytes 1572872 | tf_op jit(solution)/shard_map/ppermute | solution.py:692
  324.8 16.5 %collective-permute-start.30 = (bf16[4,16,4096]{2,1,0:T(8,128)(2,1)S(1)}, bf16[4,16,4096]{2,1,0:T(8,128)(2,1)S(1)}, u32[]{:S(2)}, u32[]{:S(2)}) collective-permute-start(bf16[4,16,4096]{2,1,0:T(8,128)(2,1)S(1)} %get-tuple-element.213), channel_id=1, source_target_pairs={{0,8},{1,9},{2,10},{3,11},{4,12},{5,13},{6,14},{7,15},{8,0},{9,1},... | collective-permute-start | bytes 1572872 | tf_op jit(solution)/shard_map/ppermute | solution.py:692
  345.1 17.5 %collective-permute-start.37 = (bf16[2,16,4096]{2,1,0:T(8,128)(2,1)}, bf16[2,16,4096]{2,1,0:T(8,128)(2,1)S(1)}, u32[]{:S(2)}, u32[]{:S(2)}) collective-permute-start(bf16[2,16,4096]{2,1,0:T(8,128)(2,1)} %get-tuple-element.209), channel_id=1, source_target_pairs={{0,6},{1,7},{2,0},{3,1},{4,2},{5,3},{6,4},{7,5},{8,14},{9,15},{10,... | collective-permute-start | bytes 786440 | tf_op jit(solution)/shard_map/ppermute | solution.py:692
  347.7 16.6 %collective-permute-start.35 = (bf16[2,16,4096]{2,1,0:T(8,128)(2,1)S(1)}, bf16[2,16,4096]{2,1,0:T(8,128)(2,1)S(1)}, u32[]{:S(2)}, u32[]{:S(2)}) collective-permute-start(bf16[2,16,4096]{2,1,0:T(8,128)(2,1)S(1)} %get-tuple-element.210), channel_id=1, source_target_pairs={{0,2},{1,3},{2,4},{3,5},{4,6},{5,7},{6,0},{7,1},{8,10},{9,11},{10,... | collective-permute-start | bytes 786440 | tf_op jit(solution)/shard_map/ppermute | solution.py:692
  347.7 26.2 %collective-permute-start.36 = (bf16[2,16,4096]{2,1,0:T(8,128)(2,1)S(1)}, bf16[2,16,4096]{2,1,0:T(8,128)(2,1)S(1)}, u32[]{:S(2)}, u32[]{:S(2)}) collective-permute-start(bf16[2,16,4096]{2,1,0:T(8,128)(2,1)S(1)} %get-tuple-element.211), channel_id=1, source_target_pairs={{0,4},{1,5},{2,6},{3,7},{4,0},{5,1},{6,2},{7,3},{8,12},{9,13},{10,... | collective-permute-start | bytes 786440 | tf_op jit(solution)/shard_map/ppermute | solution.py:692
  360.8 16.3 %collective-permute-start.45 = (bf16[32,4096]{1,0:T(8,128)(2,1)S(1)}, bf16[32,4096]{1,0:T(8,128)(2,1)S(1)}, u32[]{:S(2)}, u32[]{:S(2)}) collective-permute-start(bf16[32,4096]{1,0:T(8,128)(2,1)S(1)} %get-tuple-element.206), channel_id=1, source_target_pairs={{0,24},{1,25},{2,26},{3,27},{4,28},{5,29},{6,30},{7,31},{8,16},{9,... | collective-permute-start | bytes 786440 | tf_op jit(solution)/shard_map/ppermute | solution.py:692
  362.2 15.5 %collective-permute-start.44 = (bf16[32,4096]{1,0:T(8,128)(2,1)S(1)}, bf16[32,4096]{1,0:T(8,128)(2,1)S(1)}, u32[]{:S(2)}, u32[]{:S(2)}) collective-permute-start(bf16[32,4096]{1,0:T(8,128)(2,1)S(1)} %get-tuple-element.207), channel_id=1, source_target_pairs={{0,16},{1,17},{2,18},{3,19},{4,20},{5,21},{6,22},{7,23},{8,24},{9,... | collective-permute-start | bytes 786440 | tf_op jit(solution)/shard_map/ppermute | solution.py:692
  362.5 15.1 %collective-permute-start.43 = (bf16[32,4096]{1,0:T(8,128)(2,1)S(1)}, bf16[32,4096]{1,0:T(8,128)(2,1)S(1)}, u32[]{:S(2)}, u32[]{:S(2)}) collective-permute-start(bf16[32,4096]{1,0:T(8,128)(2,1)S(1)} %get-tuple-element.208), channel_id=1, source_target_pairs={{0,8},{1,9},{2,10},{3,11},{4,12},{5,13},{6,14},{7,15},{8,0},{9,1},... | collective-permute-start | bytes 786440 | tf_op jit(solution)/shard_map/ppermute | solution.py:692
  376.5 14.7 %collective-permute-start.41 = (bf16[2,16,4096]{2,1,0:T(8,128)(2,1)S(1)}, bf16[2,16,4096]{2,1,0:T(8,128)(2,1)S(1)}, u32[]{:S(2)}, u32[]{:S(2)}) collective-permute-start(bf16[2,16,4096]{2,1,0:T(8,128)(2,1)S(1)} %fusion.9), channel_id=1, source_target_pairs={{0,16},{1,17},{2,18},{3,19},{4,20},{5,21},{6,22},{7,23},{8,24},{9,... | collective-permute-start | bytes 786440 | tf_op jit(solution)/shard_map/ppermute | solution.py:692
  378.7 16.9 %collective-permute-start.48 = (bf16[32,4096]{1,0:T(8,128)(2,1)S(1)}, bf16[32,4096]{1,0:T(8,128)(2,1)S(1)}, u32[]{:S(2)}, u32[]{:S(2)}) collective-permute-start(bf16[32,4096]{1,0:T(8,128)(2,1)S(1)} %fusion.6), channel_id=1, source_target_pairs={{0,24},{1,25},{2,26},{3,27},{4,28},{5,29},{6,30},{7,31},{8,16},{9,... | collective-permute-start | bytes 786440 | tf_op jit(solution)/shard_map/ppermute | solution.py:692
  381.2 17.7 %collective-permute-start.47 = (bf16[32,4096]{1,0:T(8,128)(2,1)S(1)}, bf16[32,4096]{1,0:T(8,128)(2,1)S(1)}, u32[]{:S(2)}, u32[]{:S(2)}) collective-permute-start(bf16[32,4096]{1,0:T(8,128)(2,1)S(1)} %fusion.6), channel_id=1, source_target_pairs={{0,16},{1,17},{2,18},{3,19},{4,20},{5,21},{6,22},{7,23},{8,24},{9,... | collective-permute-start | bytes 786440 | tf_op jit(solution)/shard_map/ppermute | solution.py:692
  384.3 14.6 %collective-permute-start.46 = (bf16[32,4096]{1,0:T(8,128)(2,1)S(1)}, bf16[32,4096]{1,0:T(8,128)(2,1)S(1)}, u32[]{:S(2)}, u32[]{:S(2)}) collective-permute-start(bf16[32,4096]{1,0:T(8,128)(2,1)S(1)} %fusion.6), channel_id=1, source_target_pairs={{0,8},{1,9},{2,10},{3,11},{4,12},{5,13},{6,14},{7,15},{8,0},{9,1},... | collective-permute-start | bytes 786440 | tf_op jit(solution)/shard_map/ppermute | solution.py:692
  (64 other events, 506.8 us)
Sparse Core Ops, SparseCore 0:
  87.5 80.5 all-gather.1
  170.4 88.1 reduce-scatter.2
  260.9 93.0 reduce-scatter.4

commit v4 on v3

--- a/solution.py
+++ b/solution.py
@@ -202,7 +202,7 @@
         compiler_params=params(30),
         cost_estimate=cost(2 * seqs * rows * width * wide, seqs * rows * (4 * width + wide) * 2 + 4 * width * wide),
         name="norm_project",
-    )(lengths, pos, x, cot, *pieces, *vectors)
+    )(lengths, pos, x, cot, *[held(piece) for piece in pieces], *vectors)
     return normed, packed, up, up_sum, kept.reshape(width, -1), table
 
 
@@ -367,7 +367,7 @@
         compiler_params=params(26),
         cost_estimate=cost(2 * seqs * rows * width * width, seqs * rows * width * 10 + 4 * width * wide),
         name="branch",
-    )(lengths, pos, x, mixed, table, *pieces)
+    )(lengths, pos, x, mixed, table, *[held(piece) for piece in pieces])
     return resid, normed, kept.reshape(-1, wide)
 
 
@@ -394,13 +394,13 @@
 def expand(seqs, normed, up, weight, bias):
     count, width = normed.shape
     hidden = bias.shape[1]
-    size = hidden // 8
+    size = hidden // 4
     skip = (weight.shape[1] - hidden) // size
     wide = pl.BlockSpec((count, size), lambda i: (0, i))
     shape = far((count, hidden), BF16)
     return pl.pallas_call(
         functools.partial(expand_kernel, seqs),
-        grid=(8,),
+        grid=(4,),
         in_specs=[
             once((count, width)),
             once((count, width)),
@@ -409,7 +409,7 @@
         ],
         out_specs=[wide, wide, pl.BlockSpec((size, width), lambda i: (i, 0))],
         out_shape=[shape, shape, far((hidden, width), BF16)],
-        compiler_params=params(26),
+        compiler_params=params(36),
         cost_estimate=cost(4 * count * width * hidden, count * hidden * 4 + width * hidden * 4, count * hidden),
         name="expand",
     )(normed, up, held(weight), bias)
@@ -460,54 +460,44 @@
 def hidden_back(seqs, up, weight, slope):
     count, width = up.shape
     hidden = slope.shape[1]
-    size = hidden // 8
+    size = hidden // 4
     wide = pl.BlockSpec((count, size), lambda i: (0, i))
     return pl.pallas_call(
         functools.partial(hidden_back_kernel, seqs),
-        grid=(8,),
+        grid=(4,),
         in_specs=[once((count, width)), pl.BlockSpec((size, width), lambda i: (i, 0)), wide],
         out_specs=[wide, pl.BlockSpec((1, size), lambda i: (0, i))],
         out_shape=[far((count, hidden), BF16), jax.ShapeDtypeStruct((1, hidden), F32)],
-        compiler_params=params(20),
+        compiler_params=params(28),
         cost_estimate=cost(2 * count * width * hidden, count * hidden * 4 + 2 * width * hidden),
         name="hidden_back",
     )(up, held(weight), held(slope))
 
 
-def whole_grad_kernel(inputs, grads, *refs):
-    refs[-1][...] = mm(inputs[...], grads[...], TN).astype(BF16)
-
-
-def whole_grad(inputs, grads, wide, first=0, earlier=()):
+def whole_grad_kernel(inputs, grads, out):
+    out[...] = mm(inputs[...], grads[...], TN).astype(BF16)
+
+
+def whole_grad(inputs, grads, first):
     count, width = inputs.shape
-    here = grads.shape[1]
-    size = 512
+    here = grads.shape[1] - first
+    size = 1024
     return pl.pallas_call(
         whole_grad_kernel,
         grid=(here // size,),
-        in_specs=[once((count, width)), pl.BlockSpec((count, size), lambda j: (0, j))]
-        + [pl.BlockSpec(memory_space=pl.ANY)] * len(earlier),
-        out_specs=pl.BlockSpec((width, size), lambda j: (0, first // size + j)),
-        out_shape=far((width, wide), BF16),
-        input_output_aliases={2: 0} if earlier else {},
-        compiler_params=params(20),
+        in_specs=[
+            once((count, width)),
+            pl.BlockSpec((count, size), lambda j: (0, first // size + j)),
+        ],
+        out_specs=pl.BlockSpec((width, size), lambda j: (0, j)),
+        out_shape=far((width, here), BF16),
+        compiler_params=params(28),
         cost_estimate=cost(2 * count * width * here, count * (width + here) * 2 + 2 * width * here),
         name="whole_grad",
-    )(inputs, held(grads), *[held(a) for a in earlier])
-
-
-def store_halves(ref, value):
-    _, shards, quarters, rows, _ = ref.shape
-    for shard in range(shards):
-        for quarter in range(quarters):
-            for half in range(2):
-                at = ((shard * quarters + quarter) * 2 + half) * rows
-                ref[half, shard, quarter] = value[at : at + rows]
-
-
-def weight_grad_kernel(half, order, inputs, grads, *refs):
-    out, picked = refs[-2:]
-
+    )(inputs, held(grads))
+
+
+def pick_columns(half, order, inputs, picked):
     @pl.when(pl.program_id(0) == 0)
     def _():
         for i in range(4):
@@ -515,23 +505,38 @@
             at = pl.multiple_of((order[0] * i + order[1 + half]) * size, size)
             picked[:, i * size : (i + 1) * size] = inputs[:, pl.ds(at, size)]
 
+
+def weight_grad_kernel(half, order, inputs, grads, *refs):
+    out, picked = refs[-2:]
+    pick_columns(half, order, inputs, picked)
     block = grads[...].reshape(inputs.shape[0], grads.shape[-1])
-    store_halves(out, mm(picked[...], block, TN).astype(BF16))
+    value = mm(picked[...], block, TN).astype(BF16)
+    _, shards, _, rows, _ = out.shape
+    for shard in range(shards):
+        for quarter in range(4):
+            for part in range(2):
+                at = ((shard * 4 + quarter) * 2 + part) * rows
+                out[part, shard, quarter ^ order[3]] = value[at : at + rows]
+
+
+def grad_spec(grads):
+    if len(grads.shape) == 2:
+        return pl.BlockSpec((grads.shape[0], 1024), lambda j, *_: (0, j)), 1
+    seqs, parts, each, size = grads.shape
+    return pl.BlockSpec((seqs, 1, each, size), lambda j, *_: (0, j, 0, 0)), parts
 
 
 def weight_grad(half, order, inputs, grads, wide, first=0, earlier=()):
     count, width = inputs.shape
-    seqs, parts, each, size = grads.shape
+    size = 1024
+    spec, parts = grad_spec(grads)
     rows = width // 64
     return pl.pallas_call(
         functools.partial(weight_grad_kernel, half),
         grid_spec=pltpu.PrefetchScalarGridSpec(
             num_scalar_prefetch=1,
             grid=(parts,),
-            in_specs=[
-                once((count, width)),
-                pl.BlockSpec((seqs, 1, each, size), lambda j, *_: (0, j, 0, 0)),
-            ]
+            in_specs=[once((count, width)), spec]
             + [pl.BlockSpec(memory_space=pl.ANY)] * len(earlier),
             out_specs=pl.BlockSpec(
                 (2, 4, 4, rows, size), lambda j, *_: (0, 0, 0, 0, first // size + j)
@@ -543,7 +548,7 @@
         compiler_params=params(20),
         cost_estimate=cost(count * width * parts * size, count * (width + parts * size) * 2 + width * parts * size),
         name="weight_grad",
-    )(order, inputs, grads, *earlier)
+    )(order, inputs, held(grads), *earlier)
 
 
 def norm_two_kernel(lengths, hidden_grad, weight, resid, cot, table, *outs):
@@ -631,39 +636,34 @@
         name="norm_one_back",
     )(lengths, held(thirds), weight, x, held(grad_resid), table)
 
-def near_kernel(pos, *refs):
+def near_kernel(*refs):
     for at in range(4):
         mine, other, out = refs[at], refs[4 + at], refs[8 + at]
         total = mine[...].astype(F32) + other[...].astype(F32)
         out[...] = total.astype(BF16).reshape(out.shape)
 
 
-def near_sum(pos, own, arrived):
+def near_sum(own, arrived):
     _, shards, _, rows, wide = own.shape
-    x = lambda pos: pos[0] % 2
-    y = lambda pos: pos[0] // 2
     over_x = (1, 1, 2, 1, rows, wide)
     over_y = (1, 1, 1, 2, rows, wide)
     specs = [
-        pl.BlockSpec(over_x, lambda s, pos: (0, s, 0, x(pos), 0, 0)),
-        pl.BlockSpec(over_y, lambda s, pos: (1, s, y(pos), 0, 0, 0)),
-        pl.BlockSpec(over_x, lambda s, pos: (0, s, 0, 1 - x(pos), 0, 0)),
-        pl.BlockSpec(over_y, lambda s, pos: (1, s, 1 - y(pos), 0, 0, 0)),
+        pl.BlockSpec(over_x, lambda s: (0, s, 0, 0, 0, 0)),
+        pl.BlockSpec(over_y, lambda s: (1, s, 0, 0, 0, 0)),
+        pl.BlockSpec(over_x, lambda s: (0, s, 0, 1, 0, 0)),
+        pl.BlockSpec(over_y, lambda s: (1, s, 1, 0, 0, 0)),
     ]
     shape = (2, shards, 2, 2, rows, wide)
     return pl.pallas_call(
         near_kernel,
-        grid_spec=pltpu.PrefetchScalarGridSpec(
-            num_scalar_prefetch=1,
-            grid=(shards,),
-            in_specs=specs * 2,
-            out_specs=[pl.BlockSpec((1, 2, rows, wide), lambda s, pos: (s, 0, 0, 0))] * 4,
-        ),
+        grid=(shards,),
+        in_specs=specs * 2,
+        out_specs=[pl.BlockSpec((1, 2, rows, wide), lambda s: (s, 0, 0, 0))] * 4,
         out_shape=[jax.ShapeDtypeStruct((shards, 2, rows, wide), BF16)] * 4,
         compiler_params=params(14),
         cost_estimate=cost(own.size, own.size * 6),
         name="near_sum",
-    )(pos, *[own.reshape(shape)] * 4, *[arrived.reshape(shape)] * 4)
+    )(*[own.reshape(shape)] * 4, *[arrived.reshape(shape)] * 4)
 
 
 AXES = ("group", "dp")
@@ -722,11 +722,10 @@
     return send(other, CORE)
 
 
-def scatter_far(first, second, from_x, from_y, g):
-    x, y = g % 2, g // 2
+def scatter_far(first, second, from_x, from_y):
     first = plus(first, from_x)
     second = plus(second, from_y)
-    return pick(first, y, 1), pick(second, x, 1), pick(first, 1 - y, 1), pick(second, 1 - x, 1)
+    return first[:, 0], second[:, 0], first[:, 1], second[:, 1]
 
 
 def scatter_z(first, second, from_y, from_x, z):
@@ -764,6 +763,13 @@
 
 def send_trade(parts):
     return [send(part, pairs) for part, pairs in zip(parts, (OVER_X, OVER_Y, OVER_XY))]
+
+
+def spread_xy(mine):
+    half = mine.shape[0] // 2
+    over_x, over_y = send_xy(mine, mine)
+    second, first = send_xy(over_y[half:], over_x[:half])
+    return [over_x, over_y, jnp.concatenate([first, second])]
 
 
 VEC = (0, 1, 3, 5, 6, 7, 9, 11)
@@ -819,7 +825,7 @@
     d = lax.axis_index("dp")
     z, c = d // 2, d % 2
     pos = jnp.stack([g, z, c]).astype(jnp.int32)
-    order = [2, 1 - c, c] if ring else [1, 0, 4]
+    order = [2, 1 - c, c, g] if ring else [1, 0, 4, 0]
     order = jnp.stack([jnp.asarray(v, jnp.int32) for v in order])
     lens = lengths.reshape(-1)
     x = layer_input.reshape(count, rows, width)
@@ -836,41 +842,41 @@
         stack_p = jnp.stack(tie(ring_p, core_p, core_e), 1)
         x_p, y_p = send_xy(stack_p, stack_p)
         mine_e = tie(mine_e, stack_p)
-        e_one, e_three = send(mine_e, OVER_Z[1]), send(mine_e, OVER_Z[3])
-        x_p, y_p, e_one, e_three, mine_e = tie((x_p, y_p, e_one, e_three, mine_e))
+        e_one, e_two = send(mine_e, OVER_Z[1]), send(mine_e, OVER_Z[2])
+        x_p, y_p, e_one, e_two, mine_e = tie((x_p, y_p, e_one, e_two, mine_e))
         b_p, a_p = send_xy(y_p[1], x_p[0])
-        e_two = send(mine_e, OVER_Z[2])
-        near_p = tie(jnp.stack([stack_p, x_p, y_p]), a_p, b_p)
+        e_three = send(mine_e, OVER_Z[3])
+        near_p = jnp.stack([stack_p, x_p, y_p])
+        near_core_p = send(near_p, CORE)
+        a_p, b_p, e_three, near_core_p = tie((a_p, b_p, e_three, near_core_p))
         far_p = jnp.stack([a_p, b_p])
-        pieces_p = [parts_p, near_p, far_p, core_p, send(near_p, CORE), send(far_p, CORE)]
+        pieces_p = [parts_p, near_p, far_p, core_p, near_core_p, send(far_p, CORE)]
+        stack_e = jnp.stack(tie((e_one, e_two, e_three), pieces_p), 1)
+        lens_project, shard_r = tie((lens, wanted[2]), stack_e)
+        x_e, y_e = send_xy(stack_e, stack_e)
+        reduce_w = lax.all_gather(shard_r, "dp", axis=0, tiled=True)
         vectors = ()
     else:
         pieces = [lax.all_gather(w, "dp", axis=0, tiled=True) for w in wanted]
         pieces_p, pieces_e, reduce_w = [pieces[0]], [pieces[1]], pieces[2]
+        lens_project = lens
         table = pieces[0][:, 3 * width : 3 * width + 16].T.astype(F32)
         pair = spaced(table, 2, 4, rows_each)
         middle = jnp.zeros((1, width), F32)
         vectors = (table, jnp.concatenate([pair[:, :width], middle, pair[:, width:]], -1))
     normed, packed, up, up_sum, project_w, table = project(
-        ring, rows_each, lens, pos, x, cot, pieces_p, vectors
+        ring, rows_each, lens_project, pos, x, cot, pieces_p, vectors
     )
     expand_b = spaced(table, 7, 11, rows_each)
+    mixed, lse = attend(0, lens, packed)
     lens_attend = lens
-    if ring:
-        stack_e = jnp.stack(tie((e_one, e_two, e_three), normed), 1)
-        lens_attend, shard_r = tie((lens, wanted[2]), stack_e)
-        x_e, y_e = send_xy(stack_e, stack_e)
-        reduce_w = lax.all_gather(shard_r, "dp", axis=0, tiled=True)
-    mixed, lse = attend(0, lens_attend, packed)
-    for seq in range(1, count - 1):
-        mixed, lse = attend(seq, lens_attend, packed, (mixed, lse))
     if ring:
         x_e, y_e = tie((x_e, y_e), mixed)
         near_e = jnp.stack([stack_e, x_e, y_e])
         lens_attend = tie(lens, near_e)
         b_e, a_e = send_xy(y_e[1], x_e[0])
         near_core_e = send(near_e, CORE)
-    for seq in range(max(1, count - 1), count):
+    for seq in range(1, count):
         mixed, lse = attend(seq, lens_attend, packed, (mixed, lse))
     if ring:
         a_e, b_e = tie((a_e, b_e), mixed)
@@ -883,16 +889,15 @@
     grad_resid, branch_low, mixed_grad, gain_two_grad, bias_two_grad, output_b_grad = norm_two_back(
         lens, hidden_grad, joint_w, resid, cot, table
     )
-    thirds = attend_back(0, 1, lens, packed, lse, mixed_grad)
-    expand_grad = whole_grad(flat(normed_two), tie(hidden_grad, thirds), 4 * width)
+    thirds = attend_back(0, count, lens, packed, lse, mixed_grad)
+    expand_grad = whole_grad(flat(normed_two), tie(hidden_grad, thirds), 0)
     shard_e = over_dp(expand_grad)
-    lens_back = tie(lens, expand_grad)
-    thirds = attend_back(1, count - 1, lens_back, packed, lse, mixed_grad, (thirds,))
-    branch_part = branch_low.reshape(count, 1, rows, width)
+    branch_part = flat(branch_low)
     project_far = weight_grad(0, order, flat(mixed), branch_part, 4 * width)
+    project_near = weight_grad(1, order, flat(mixed), branch_part, 4 * width)
     order_far = order
     if ring:
-        mine_r, parts_r = trade(tie(shard_r, thirds), g)
+        mine_r, parts_r = trade(tie(shard_r, (project_far, project_near)), g)
         order_far = tie(order, parts_r)
         arrived_r = send_trade(parts_r)
     project_far = weight_grad(
@@ -902,14 +907,13 @@
     if ring:
         order_near = tie(order, project_far)
         arrived = send(project_far, CORE)
-    project_near = weight_grad(1, order_near, flat(mixed), branch_part, 4 * width)
     project_near = weight_grad(
         1, order_near, flat(normed), thirds, 4 * width, width, (project_near,)
     )
     lens_one = lens
     if ring:
         spread_r = spread(mine_r, tie(arrived_r, project_near))
-        ps = near_sum(pos, project_near, arrived)
+        ps = near_sum(project_near, arrived)
         lens_one = tie(lens, ps, spread_r)
         from_x, from_y = send_xy(ps[2], ps[3])
     input_grad, gain_one_grad, bias_one_grad, query_sum, value_sum = norm_one_back(
@@ -932,7 +936,7 @@
         total = total + send(total, CORE)
         total = (total + send(total, OVER_XY)) + (send(total, OVER_X) + send(total, OVER_Y))
         total, from_x, from_y = tie((total, from_x, from_y))
-        ps = scatter_far(ps[0], ps[1], from_x, from_y, g)
+        ps = scatter_far(ps[0], ps[1], from_x, from_y)
         lens_out = tie(lens, ps)
         from_x, from_y = send_xy(ps[3], ps[2])
         column = [send(total, OVER_Z[k]) for k in range(1, Z)]

time: 416 us -> 405 us (0.974); the launches traced: 408 us -> 402 us
  waiting for transfers between devices: 93.8 us -> 86.2 us
  local copies, waits for them, and re-layouts: 23.1 us -> 27.6 us
    ppermute x51, waiting for transfers between devices: 93.7 us -> 86.1 us  [send(): return lax.ppermute(array, AXES, pairs)]
    pallas_call x4, Pallas kernels: 16.3 us -> 21.8 us  [weight_grad(): pl.pallas_call(functools.partial(weight_grad_kernel, half), grid_spec=plt...]
    unnamed x85 -> x89, local copies, waits for them, and re-layouts: 15.5 us -> 19.9 us
    pallas_call x2 -> x1, Pallas kernels: 33.9 us -> 30.4 us  [attend_back(): pl.pallas_call(functools.partial(attend_back_kernel, seq), grid_spec=pltp...]
  transfers between devices with their start and end apart: 54 -> 54, of which waited for: 25 -> 19; matrix products, arithmetic and copies ran while one was open for 6% -> 5% of each run, Pallas kernels for 50% -> 50%
where the time goes in v4:
time: 405 us; the launch traced here: 402 us
  Pallas kernels  201 us (50%)
  waiting for transfers between devices  86.2 us (21%)
  starting transfers between devices  54.4 us (13%)
  local copies, waits for them, and re-layouts  27.6 us (7%)
  other arithmetic  17.8 us (4%)
  between operations  14.9 us (4%)
    ppermute x51, waiting for transfers between devices, send(): return lax.ppermute(array, AXES, pairs)  86.1 us
    ppermute x51, starting transfers between devices, send(): return lax.ppermute(array, AXES, pairs)  54.3 us
    pallas_call x1, Pallas kernels, attend_back(): pl.pallas_call(functools.partial(attend_back_kernel, seq), grid_spec=pltp...  30.4 us
    pallas_call x1, Pallas kernels, expand(): pl.pallas_call(functools.partial(expand_kernel, seqs), grid=(4,), in_spec...  26.8 us
    pallas_call x3, Pallas kernels, attend(): pl.pallas_call(functools.partial(attend_kernel, seq), grid_spec=pltpu.Pre...  22.7 us
    pallas_call x4, Pallas kernels, weight_grad(): pl.pallas_call(functools.partial(weight_grad_kernel, half), grid_spec=plt...  21.8 us
    unnamed x89, local copies, waits for them, and re-layouts  19.9 us
    pallas_call x1, Pallas kernels, norm_two_back(): pl.pallas_call(norm_two_kernel, grid_spec=pltpu.PrefetchScalarGridSpec(nu...  19.6 us
  transfers between devices with their start and end apart: 54, of which 19 were waited for; matrix products, arithmetic and copies ran while one was open for 5% of the time, Pallas kernels for 50%

profile of v4, /device:TPU:0, one launch (start us, length us, event | category | flops | bytes accessed | tf_op | source)
XLA Modules:
  0.0 401.5 jit_solution(6801229723698792349)
XLA Ops:
  10.9 5.0 %collective-permute-start.2 = (bf16[2,16,3200]{2,1,0:T(8,128)(2,1)S(1)}, bf16[2,16,3200]{2,1,0:T(8,128)(2,1)S(1)}, u32[]{:S(2)}, u32[]{:S(2)}) collective-permute-start(bf16[2,16,3200]{2,1,0:T(8,128)(2,1)S(1)} %dynamic-slice_bitcast_fusion.7), channel_id=1, source_target_pairs={{0,6},{1,7},{2,0},{3,1},{4,2},{5,3},{6,4},{7,5},{8,14},{9,15},{10,... | collective-permute-start | bytes 614408 | tf_op jit(solution)/shard_map/ppermute | solution.py:692
  16.9 4.5 %collective-permute-done.2 = bf16[2,16,3200]{2,1,0:T(8,128)(2,1)S(1)} collective-permute-done((bf16[2,16,3200]{2,1,0:T(8,128)(2,1)S(1)}, bf16[2,16,3200]{2,1,0:T(8,128)(2,1)S(1)}, u32[]{:S(2)}, u32[]{:S(2)}) %collective-permute-start.2) | collective-permute-done | bytes 204832 | tf_op jit(solution)/shard_map/ppermute | solution.py:692
  21.4 12.2 %collective-permute-done.1 = bf16[2,16,3200]{2,1,0:T(8,128)(2,1)S(1)} collective-permute-done((bf16[2,16,3200]{2,1,0:T(8,128)(2,1)S(1)}, bf16[2,16,3200]{2,1,0:T(8,128)(2,1)S(1)}, u32[]{:S(2)}, u32[]{:S(2)}) %collective-permute-start.1) | collective-permute-done | bytes 204832 | tf_op jit(solution)/shard_map/ppermute | solution.py:692
  36.8 2.9 collective-permute-start.8
  39.7 20.6 %collective-permute-done.8 = bf16[2,16,5120]{2,1,0:T(8,128)(2,1)S(1)} collective-permute-done((bf16[2,16,5120]{2,1,0:T(8,128)(2,1)S(1)}, bf16[2,16,5120]{2,1,0:T(8,128)(2,1)S(1)}, u32[]{:S(2)}, u32[]{:S(2)}) %collective-permute-start.8) | collective-permute-done | bytes 327712 | tf_op jit(solution)/shard_map/ppermute | solution.py:692
  61.9 8.6 %collective-permute-done.10 = bf16[3,16,3200]{2,1,0:T(8,128)(2,1)S(1)} collective-permute-done((bf16[3,16,3200]{2,1,0:T(8,128)(2,1)S(1)}, bf16[3,16,3200]{2,1,0:T(8,128)(2,1)S(1)}, u32[]{:S(2)}, u32[]{:S(2)}) %collective-permute-start.10) | collective-permute-done | bytes 307232 | tf_op jit(solution)/shard_map/ppermute | solution.py:692
  80.0 14.1 %norm_project.1 = (bf16[3,320,1024]{2,1,0:T(8,128)(2,1)S(1)}, bf16[3,320,3072]{2,1,0:T(8,128)(2,1)}, bf16[3,320,1024]{2,1,0:T(8,128)(2,1)S(1)}, f32[1,1024]{1,0:...) custom-call(s32[3]{0:T(128)S(1)} %bitcast.202, s32[3]{0:T(128)S(1)} %pad_add_fusion.1.pos, ...), custom_call_target="tpu_custom_call" | custom-call | flops 6039797760 | bytes 26345472 | tf_op jit(solution)/shard_map/norm_project/pallas_call | solution.py:176
  94.1 8.1 %attend.3 = (bf16[3,320,1024]{2,1,0:T(8,128)(2,1)S(1)}, f32[3,2,8,320]{3,2,1,0:T(8,128)S(1)}) custom-call(s32[3]{0:T(128)S(1)} %bitcast.203, bf16[3,320,3072]{2,1,0:T(8,128)(2,1)} %get-tuple-element.115.q.k.v, bf16[3,320,3072]{2,1,0:T(8,128)(2,1)} %get-tuple-element.115.q.k.v, bf16[3,320,3072]{2,1,0:T(8,128)(2,1)} %get-tuple-element.115.q.k.v), custom_call_target="tpu_custom_call" | custom-call | flops 3355443200 | bytes 2949120 | tf_op jit(solution)/shard_map/attend/pallas_call | solution.py:246
  104.6 7.3 %attend.4 = (bf16[3,320,1024]{2,1,0:T(8,128)(2,1)S(1)}, f32[3,2,8,320]{3,2,1,0:T(8,128)S(1)}) custom-call(s32[3]{0:T(128)S(1)} %bitcast.204, bf16[3,320,3072]{2,1,0:T(8,128)(2,1)} %get-tuple-element.115.q.k.v, bf16[3,320,3072]{2,1,0:T(8,128)(2,1)} %get-tuple-element.115.q.k.v, ...), custom_call_target="tpu_custom_call", output_to_operand_aliasing={{0}: (4, {}), {1}: (5, {})} | custom-call | flops 3355443200 | bytes 2949120 | tf_op jit(solution)/shard_map/attend/pallas_call | solution.py:246
  111.9 7.3 %attend.5 = (bf16[3,320,1024]{2,1,0:T(8,128)(2,1)S(1)}, f32[3,2,8,320]{3,2,1,0:T(8,128)S(1)}) custom-call(s32[3]{0:T(128)S(1)} %bitcast.205, bf16[3,320,3072]{2,1,0:T(8,128)(2,1)} %get-tuple-element.115.q.k.v, bf16[3,320,3072]{2,1,0:T(8,128)(2,1)} %get-tuple-element.115.q.k.v, ...), custom_call_target="tpu_custom_call", output_to_operand_aliasing={{0}: (4, {}), {1}: (5, {})} | custom-call | flops 3355443200 | bytes 2949120 | tf_op jit(solution)/shard_map/attend/pallas_call | solution.py:246
  119.5 2.5 collective-permute-done.19.refs_5_
  124.6 11.9 %branch.1 = (f32[3,320,1024]{2,1,0:T(8,128)}, bf16[3,320,1024]{2,1,0:T(8,128)(2,1)S(1)}, bf16[4,2,4,2,16,5120]{5,4,3,2,1,0:T(8,128)(2,1)}) custom-call(s32[3]{0:T(128)S(1)} %bitcast.206, s32[3]{0:T(128)S(1)} %pad_add_fusion.1.pos, bf16[3,320,1024]{2,1,0:T(8,128)(2,1)S(1)} %bitcast.178, bf16[3,320,1024]{2,1,0:T(8,128)(2,1)S(1)} %get-tuple-element.123.mixed, ...), custom_call_target="tpu_custom_call" | custom-call | flops 2013265920 | bytes 30801920 | tf_op jit(solution)/shard_map/branch/pallas_call | solution.py:353
  136.5 26.8 %expand.1 = (bf16[960,4096]{1,0:T(8,128)(2,1)}, bf16[960,4096]{1,0:T(8,128)(2,1)}, bf16[4096,1024]{1,0:T(8,128)(2,1)}) custom-call(bf16[960,1024]{1,0:T(8,128)(2,1)S(1)} %bitcast.213, bf16[960,1024]{1,0:T(8,128)(2,1)S(1)} %bitcast.218, bf16[1024,5120]{1,0:T(8,128)(2,1)} %bitcast.261, f32[1,4096]{1,0:T(1,128)S(1)} %bitcast.201), custom_call_target="tpu_custom_call" | custom-call | flops 16106127360 | bytes 32505856 | tf_op jit(solution)/shard_map/expand/pallas_call | solution.py:401
  165.0 13.9 %hidden_back.1 = (bf16[960,4096]{1,0:T(8,128)(2,1)}, f32[1,4096]{1,0:T(1,128)S(1)}) custom-call(bf16[960,1024]{1,0:T(8,128)(2,1)S(1)} %bitcast.219, bf16[4096,1024]{1,0:T(8,128)(2,1)} %all-gather.2.cloned.1.call-done.weight, bf16[960,4096]{1,0:T(8,128)(2,1)} %get-tuple-element.132.slope), custom_call_target="tpu_custom_call" | custom-call | flops 8053063680 | bytes 24117248 | tf_op jit(solution)/shard_map/hidden_back/pallas_call | solution.py:465
  178.9 19.6 %norm_two_back.1 = (f32[3,320,1024]{2,1,0:T(8,128)}, bf16[3,320,1024]{2,1,0:T(8,128)(2,1)S(1)}, bf16[3,320,1024]{2,1,0:T(8,128)(2,1)S(1)}, f32[1,1024]{1,0:T(1,1...) custom-call(s32[3]{0:T(128)S(1)} %bitcast.207, bf16[3,320,4096]{2,1,0:T(8,128)(2,1)} %bitcast.264, ...), custom_call_target="tpu_custom_call" | custom-call | flops 10066329600 | bytes 21626880 | tf_op jit(solution)/shard_map/norm_two_back/pallas_call | solution.py:576
  198.5 30.4 %attend_back.1.grads.thirds = bf16[3,3,320,1024]{3,2,1,0:T(8,128)(2,1)} custom-call(s32[3]{0:T(128)S(1)} %bitcast.208, bf16[3,320,3072]{2,1,0:T(8,128)(2,1)} %get-tuple-element.115.q.k.v, bf16[3,320,3072]{2,1,0:T(8,128)(2,1)} %get-tuple-element.115.q.k.v, bf16[3,320,3072]{2,1,0:T(8,128)(2,1)} %get-tuple-element.115.q.k.v, ...), custom_call_target="tpu_custom_call" | custom-call | flops 25165824000 | bytes 14745600 | tf_op jit(solution)/shard_map/attend_back/pallas_call | solution.py:309
  228.9 12.7 %whole_grad.1 = bf16[1024,4096]{1,0:T(8,128)(2,1)} custom-call(bf16[960,1024]{1,0:T(8,128)(2,1)S(1)} %bitcast.214, bf16[960,4096]{1,0:T(8,128)(2,1)} %get-tuple-element.173.grads), custom_call_target="tpu_custom_call" | custom-call | flops 8053063680 | bytes 18219008 | tf_op jit(solution)/shard_map/whole_grad/pallas_call | solution.py:485
  241.7 3.6 weight_grad.5.refs_0_
  247.3 3.6 weight_grad.4.refs_0_
  257.8 7.7 %weight_grad.6 = bf16[2,4,4,16,4096]{4,3,2,1,0:T(8,128)(2,1)S(1)} custom-call(s32[4]{0:T(128)S(1)} %pad_add_fusion.order, bf16[960,1024]{1,0:T(8,128)(2,1)S(1)} %bitcast.173, bf16[3,3,320,1024]{3,2,1,0:T(8,128)(2,1)} %attend_back.1.grads.thirds, bf16[2,4,4,16,4096]{4,3,2,1,0:T(8,128)(2,1)S(1)} %copy-done.3), custom_call_target="tpu_custom_call", output_to_operand_aliasing={{}: (3, {})} | custom-call | flops 3019898880 | bytes 11010048 | tf_op jit(solution)/shard_map/weight_grad/pallas_call | solution.py:534
  269.2 6.9 %weight_grad.7 = bf16[2,4,4,16,4096]{4,3,2,1,0:T(8,128)(2,1)S(1)} custom-call(s32[4]{0:T(128)S(1)} %pad_add_fusion.order, bf16[960,1024]{1,0:T(8,128)(2,1)S(1)} %bitcast.174, bf16[3,3,320,1024]{3,2,1,0:T(8,128)(2,1)} %attend_back.1.grads.thirds, bf16[2,4,4,16,4096]{4,3,2,1,0:T(8,128)(2,1)S(1)} %copy-done.1), custom_call_target="tpu_custom_call", output_to_operand_aliasing={{}: (3, {})} | custom-call | flops 3019898880 | bytes 11010048 | tf_op jit(solution)/shard_map/weight_grad/pallas_call | solution.py:534
  276.2 4.6 %collective-permute-done.22 = bf16[128,1024]{1,0:T(8,128)(2,1)S(1)} collective-permute-done((bf16[128,1024]{1,0:T(8,128)(2,1)S(1)}, bf16[128,1024]{1,0:T(8,128)(2,1)S(1)}, u32[]{:S(2)}, u32[]{:S(2)}) %collective-permute-start.22) | collective-permute-done | bytes 262176 | tf_op jit(solution)/shard_map/ppermute | solution.py:692
  286.8 12.7 %norm_one_back.1 = (f32[3,320,1024]{2,1,0:T(8,128)}, f32[1,1024]{1,0:T(1,128)S(1)}, f32[1,1024]{1,0:T(1,128)S(1)}, f32[1,1024]{1,0:T(1,128)S(1)}, f32[1,1024]{1,0:T(1,128)S(1)}) custom-call(s32[3]{0:T(128)S(1)} %bitcast.209, bf16[3,3,320,1024]{3,2,1,0:T(8,128)(2,1)} %attend_back.1.grads.thirds, bf16[1024,3200]{1,0:T(8,128)(2,1)S(1)} %bitcast.217, ...), custom_call_target="tpu_custom_call" | custom-call | flops 6039797760 | bytes 22020096 | tf_op jit(solution)/shard_map/norm_one_back/pallas_call | solution.py:622
  305.6 6.2 %collective-permute-done.26 = f32[96,128]{1,0:T(8,128)} collective-permute-done((f32[96,128]{1,0:T(8,128)}, f32[96,128]{1,0:T(8,128)}, u32[]{:S(2)}, u32[]{:S(2)}) %collective-permute-start.26) | collective-permute-done | bytes 49184 | tf_op jit(solution)/shard_map/ppermute | solution.py:692
  315.0 2.6 collective-permute-start.33
  323.0 3.4 copy-done.11
  326.4 12.7 %reduce_out.1 = f32[3,320,1024]{2,1,0:T(8,128)} custom-call(s32[3]{0:T(128)S(1)} %bitcast.210, f32[3,320,1024]{2,1,0:T(8,128)} %get-tuple-element.134.resid, bf16[3,320,4096]{2,1,0:T(8,128)(2,1)} %bitcast.263, bf16[4096,1024]{1,0:T(8,128)(2,1)S(1)} %copy-done.11, f32[16,1024]{1,0:T(8,128)S(1)} %get-tuple-element.124.table), custom_call_target="tpu_custom_call" | custom-call | flops 8053063680 | bytes 24117248 | tf_op jit(solution)/shard_map/reduce_out/pallas_call | solution.py:428
  341.6 3.9 collective-permute-start.37
  359.8 7.7 %collective-permute-done.36 = bf16[2,16,4096]{2,1,0:T(8,128)(2,1)S(1)} collective-permute-done((bf16[2,16,4096]{2,1,0:T(8,128)(2,1)S(1)}, bf16[2,16,4096]{2,1,0:T(8,128)(2,1)S(1)}, u32[]{:S(2)}, u32[]{:S(2)}) %collective-permute-start.36) | collective-permute-done | bytes 262176 | tf_op jit(solution)/shard_map/ppermute | solution.py:692
  375.3 2.6 collective-permute-done.42
  379.3 5.5 %collective-permute-done.41 = bf16[2,16,4096]{2,1,0:T(8,128)(2,1)S(1)} collective-permute-done((bf16[2,16,4096]{2,1,0:T(8,128)(2,1)S(1)}, bf16[2,16,4096]{2,1,0:T(8,128)(2,1)S(1)}, u32[]{:S(2)}, u32[]{:S(2)}) %collective-permute-start.41) | collective-permute-done | bytes 262176 | tf_op jit(solution)/shard_map/ppermute | solution.py:692
  389.1 3.2 collective-permute-done.47
  (241 shorter events, 91.2 us)
Async XLA Ops:
  7.3 156.1 %all-gather.2.cloned.1.call-start = ((), (), s32[]{:S(2)}) async-start(), calls=%async_computation.3 | async-start | bytes 9437184 | tf_op jit(solution)/shard_map/all_gather | solution.py:857
  8.7 24.9 %collective-permute-start.4 = (bf16[4,2,16,5120]{3,2,1,0:T(8,128)(2,1)S(1)}, bf16[4,2,16,5120]{3,2,1,0:T(8,128)(2,1)S(1)}, u32[]{:S(2)}, u32[]{:S(2)}) collective-permute-start(bf16[4,2,16,5120]{3,2,1,0:T(8,128)(2,1)S(1)} %bitcast.220), channel_id=1, source_target_pairs={{0,1},{1,0},{2,3},{3,2},{4,5},{5,4},{6,7},{7,6},{8,9},{9,8},{10,11... | collective-permute-start | bytes 3932168 | tf_op jit(solution)/shard_map/ppermute | solution.py:692
  10.6 23.0 %collective-permute-start.3 = (bf16[4,2,16,3200]{3,2,1,0:T(8,128)(2,1)S(1)}, bf16[4,2,16,3200]{3,2,1,0:T(8,128)(2,1)}, u32[]{:S(2)}, u32[]{:S(2)}) collective-permute-start(bf16[4,2,16,3200]{3,2,1,0:T(8,128)(2,1)S(1)} %bitcast.230), channel_id=1, source_target_pairs={{0,1},{1,0},{2,3},{3,2},{4,5},{5,4},{6,7},{7,6},{8,9},{9,8},{10,11... | collective-permute-start | bytes 2457608 | tf_op jit(solution)/shard_map/ppermute | solution.py:692
  15.9 17.7 %collective-permute-start.1 = (bf16[2,16,3200]{2,1,0:T(8,128)(2,1)S(1)}, bf16[2,16,3200]{2,1,0:T(8,128)(2,1)S(1)}, u32[]{:S(2)}, u32[]{:S(2)}) collective-permute-start(bf16[2,16,3200]{2,1,0:T(8,128)(2,1)S(1)} %dynamic-slice_bitcast_fusion.7), channel_id=1, source_target_pairs={{0,4},{1,5},{2,6},{3,7},{4,0},{5,1},{6,2},{7,3},{8,12},{9,13},{10,... | collective-permute-start | bytes 614408 | tf_op jit(solution)/shard_map/ppermute | solution.py:692
  15.9 17.7 %collective-permute-start = (bf16[2,16,3200]{2,1,0:T(8,128)(2,1)S(1)}, bf16[2,16,3200]{2,1,0:T(8,128)(2,1)S(1)}, u32[]{:S(2)}, u32[]{:S(2)}) collective-permute-start(bf16[2,16,3200]{2,1,0:T(8,128)(2,1)S(1)} %dynamic-slice_bitcast_fusion.7), channel_id=1, source_target_pairs={{0,2},{1,3},{2,4},{3,5},{4,6},{5,7},{6,0},{7,1},{8,10},{9,11},{10,... | collective-permute-start | bytes 614408 | tf_op jit(solution)/shard_map/ppermute | solution.py:692
  33.7 26.6 %collective-permute-start.6 = (bf16[2,3,16,3200]{3,2,1,0:T(8,128)(2,1)S(1)}, bf16[2,3,16,3200]{3,2,1,0:T(8,128)(2,1)S(1)}, u32[]{:S(2)}, u32[]{:S(2)}) collective-permute-start(bf16[2,3,16,3200]{3,2,1,0:T(8,128)(2,1)S(1)} %get-tuple-element.222), channel_id=1, source_target_pairs={{0,16},{1,17},{2,18},{3,19},{4,20},{5,21},{6,22},{7,23},{8,24},{9,... | collective-permute-start | bytes 1843208 | tf_op jit(solution)/shard_map/ppermute | solution.py:692
  35.3 25.0 %collective-permute-start.5 = (bf16[2,3,16,3200]{3,2,1,0:T(8,128)(2,1)S(1)}, bf16[2,3,16,3200]{3,2,1,0:T(8,128)(2,1)S(1)}, u32[]{:S(2)}, u32[]{:S(2)}) collective-permute-start(bf16[2,3,16,3200]{3,2,1,0:T(8,128)(2,1)S(1)} %get-tuple-element.222), channel_id=1, source_target_pairs={{0,8},{1,9},{2,10},{3,11},{4,12},{5,13},{6,14},{7,15},{8,0},{9,1},... | collective-permute-start | bytes 1843208 | tf_op jit(solution)/shard_map/ppermute | solution.py:692
  36.8 23.5 %collective-permute-start.8 = (bf16[2,16,5120]{2,1,0:T(8,128)(2,1)S(1)}, bf16[2,16,5120]{2,1,0:T(8,128)(2,1)S(1)}, u32[]{:S(2)}, u32[]{:S(2)}) collective-permute-start(bf16[2,16,5120]{2,1,0:T(8,128)(2,1)S(1)} %dynamic-slice_bitcast_fusion), channel_id=1, source_target_pairs={{0,4},{1,5},{2,6},{3,7},{4,0},{5,1},{6,2},{7,3},{8,12},{9,13},{10,... | collective-permute-start | bytes 983048 | tf_op jit(solution)/shard_map/ppermute | solution.py:692
  39.7 20.6 %collective-permute-start.7 = (bf16[2,16,5120]{2,1,0:T(8,128)(2,1)S(1)}, bf16[2,16,5120]{2,1,0:T(8,128)(2,1)S(1)}, u32[]{:S(2)}, u32[]{:S(2)}) collective-permute-start(bf16[2,16,5120]{2,1,0:T(8,128)(2,1)S(1)} %dynamic-slice_bitcast_fusion), channel_id=1, source_target_pairs={{0,2},{1,3},{2,4},{3,5},{4,6},{5,7},{6,0},{7,1},{8,10},{9,11},{10,... | collective-permute-start | bytes 983048 | tf_op jit(solution)/shard_map/ppermute | solution.py:692
  76.2 176.7 %reduce-scatter.3.cloned.1.call-start = ((), (), s32[]{:S(2)}) async-start(), calls=%async_computation.2 | async-start | bytes 9437184 | tf_op jit(solution)/shard_map/reduce_scatter | solution.py:817
  76.3 25.9 %collective-permute-start.15 = (bf16[2,3,16,5120]{3,2,1,0:T(8,128)(2,1)}, bf16[2,3,16,5120]{3,2,1,0:T(8,128)(2,1)S(1)}, u32[]{:S(2)}, u32[]{:S(2)}) collective-permute-start(bf16[2,3,16,5120]{3,2,1,0:T(8,128)(2,1)} %get-tuple-element.220), channel_id=1, source_target_pairs={{0,16},{1,17},{2,18},{3,19},{4,20},{5,21},{6,22},{7,23},{8,24},{9,... | collective-permute-start | bytes 2949128 | tf_op jit(solution)/shard_map/ppermute | solution.py:692
  76.8 25.4 %collective-permute-start.14 = (bf16[2,3,16,5120]{3,2,1,0:T(8,128)(2,1)}, bf16[2,3,16,5120]{3,2,1,0:T(8,128)(2,1)S(1)}, u32[]{:S(2)}, u32[]{:S(2)}) collective-permute-start(bf16[2,3,16,5120]{3,2,1,0:T(8,128)(2,1)} %get-tuple-element.220), channel_id=1, source_target_pairs={{0,8},{1,9},{2,10},{3,11},{4,12},{5,13},{6,14},{7,15},{8,0},{9,1},... | collective-permute-start | bytes 2949128 | tf_op jit(solution)/shard_map/ppermute | solution.py:692
  102.6 19.5 %collective-permute-start.18 = (bf16[3,2,3,16,5120]{4,3,2,1,0:T(8,128)(2,1)S(1)}, bf16[3,2,3,16,5120]{4,3,2,1,0:T(8,128)(2,1)S(1)}, u32[]{:S(2)}, u32[]{:S(2)}) collective-permute-start(bf16[3,2,3,16,5120]{4,3,2,1,0:T(8,128)(2,1)S(1)} %pad_maximum_fusion.refs_1_), channel_id=1, source_target_pairs={{0,1},{1,0},{2,3},{3,2},{4,5},{5,4},{6,7},{7,6},{8,9},{9,8},{10,11... | collective-permute-start | bytes 8847368 | tf_op jit(solution)/shard_map/ppermute | solution.py:692
  102.7 16.6 %collective-permute-start.17 = (bf16[3,16,5120]{2,1,0:T(8,128)(2,1)S(1)}, bf16[3,16,5120]{2,1,0:T(8,128)(2,1)S(1)}, u32[]{:S(2)}, u32[]{:S(2)}) collective-permute-start(bf16[3,16,5120]{2,1,0:T(8,128)(2,1)S(1)} %slice_bitcast_fusion.4), channel_id=1, source_target_pairs={{0,8},{1,9},{2,10},{3,11},{4,12},{5,13},{6,14},{7,15},{8,0},{9,1},... | collective-permute-start | bytes 1474568 | tf_op jit(solution)/shard_map/ppermute | solution.py:692
  103.0 16.3 %collective-permute-start.16 = (bf16[3,16,5120]{2,1,0:T(8,128)(2,1)S(1)}, bf16[3,16,5120]{2,1,0:T(8,128)(2,1)S(1)}, u32[]{:S(2)}, u32[]{:S(2)}) collective-permute-start(bf16[3,16,5120]{2,1,0:T(8,128)(2,1)S(1)} %slice_bitcast_fusion.5), channel_id=1, source_target_pairs={{0,16},{1,17},{2,18},{3,19},{4,20},{5,21},{6,22},{7,23},{8,24},{9,... | collective-permute-start | bytes 1474568 | tf_op jit(solution)/shard_map/ppermute | solution.py:692
  163.3 191.8 %reduce-scatter.5.cloned.1.call-start = ((), (), s32[]{:S(2)}) async-start(), calls=%async_computation.4 | async-start | bytes 9437184 | tf_op jit(solution)/shard_map/reduce_scatter | solution.py:817
  265.4 16.4 %collective-permute-start.20 = (bf16[2,4,4,16,4096]{4,3,2,1,0:T(8,128)(2,1)S(1)}, bf16[2,4,4,16,4096]{4,3,2,1,0:T(8,128)(2,1)S(1)}, u32[]{:S(2)}, u32[]{:S(2)}) collective-permute-start(bf16[2,4,4,16,4096]{4,3,2,1,0:T(8,128)(2,1)S(1)} %weight_grad.6), channel_id=1, source_target_pairs={{0,1},{1,0},{2,3},{3,2},{4,5},{5,4},{6,7},{7,6},{8,9},{9,8},{10,11... | collective-permute-start | bytes 12582920 | tf_op jit(solution)/shard_map/ppermute | solution.py:692
  284.3 29.7 %collective-permute-start.29 = (bf16[4,2,16,4096]{3,2,1,0:T(8,128)(2,1)S(1)}, bf16[4,2,16,4096]{3,2,1,0:T(8,128)(2,1)}, u32[]{:S(2)}, u32[]{:S(2)}) collective-permute-start(bf16[4,2,16,4096]{3,2,1,0:T(8,128)(2,1)S(1)} %get-tuple-element.145), channel_id=1, source_target_pairs={{0,16},{1,17},{2,18},{3,19},{4,20},{5,21},{6,22},{7,23},{8,24},{9,... | collective-permute-start | bytes 3145736 | tf_op jit(solution)/shard_map/ppermute | solution.py:692
  285.0 29.0 %collective-permute-start.28 = (bf16[4,2,16,4096]{3,2,0,1:T(8,128)(2,1)}, bf16[4,2,16,4096]{3,2,0,1:T(8,128)(2,1)}, u32[]{:S(2)}, u32[]{:S(2)}) collective-permute-start(bf16[4,2,16,4096]{3,2,0,1:T(8,128)(2,1)} %copy.51), channel_id=1, source_target_pairs={{0,8},{1,9},{2,10},{3,11},{4,12},{5,13},{6,14},{7,15},{8,0},{9,1},... | collective-permute-start | bytes 3145736 | tf_op jit(solution)/shard_map/ppermute | solution.py:692
  314.1 25.0 %collective-permute-start.34 = (f32[96,128]{1,0:T(8,128)S(1)}, f32[96,128]{1,0:T(8,128)S(1)}, u32[]{:S(2)}, u32[]{:S(2)}) collective-permute-start(f32[96,128]{1,0:T(8,128)S(1)} %add_add_fusion), channel_id=1, source_target_pairs={{0,6},{1,7},{2,0},{3,1},{4,2},{5,3},{6,4},{7,5},{8,14},{9,15},{10,... | collective-permute-start | bytes 147464 | tf_op jit(solution)/shard_map/ppermute | solution.py:692
  315.0 24.1 %collective-permute-start.33 = (f32[96,128]{1,0:T(8,128)S(1)}, f32[96,128]{1,0:T(8,128)S(1)}, u32[]{:S(2)}, u32[]{:S(2)}) collective-permute-start(f32[96,128]{1,0:T(8,128)S(1)} %add_add_fusion), channel_id=1, source_target_pairs={{0,4},{1,5},{2,6},{3,7},{4,0},{5,1},{6,2},{7,3},{8,12},{9,13},{10,... | collective-permute-start | bytes 147464 | tf_op jit(solution)/shard_map/ppermute | solution.py:692
  317.6 21.5 %collective-permute-start.32 = (f32[96,128]{1,0:T(8,128)S(1)}, f32[96,128]{1,0:T(8,128)S(1)}, u32[]{:S(2)}, u32[]{:S(2)}) collective-permute-start(f32[96,128]{1,0:T(8,128)S(1)} %add_add_fusion), channel_id=1, source_target_pairs={{0,2},{1,3},{2,4},{3,5},{4,6},{5,7},{6,0},{7,1},{8,10},{9,11},{10,... | collective-permute-start | bytes 147464 | tf_op jit(solution)/shard_map/ppermute | solution.py:692
  319.2 20.0 %collective-permute-start.30 = (bf16[4,16,4096]{2,1,0:T(8,128)(2,1)S(1)}, bf16[4,16,4096]{2,1,0:T(8,128)(2,1)S(1)}, u32[]{:S(2)}, u32[]{:S(2)}) collective-permute-start(bf16[4,16,4096]{2,1,0:T(8,128)(2,1)S(1)} %slice_bitcast_fusion.3), channel_id=1, source_target_pairs={{0,8},{1,9},{2,10},{3,11},{4,12},{5,13},{6,14},{7,15},{8,0},{9,1},... | collective-permute-start | bytes 1572872 | tf_op jit(solution)/shard_map/ppermute | solution.py:692
  321.4 17.7 %collective-permute-start.31 = (bf16[4,16,4096]{2,1,0:T(8,128)(2,1)S(1)}, bf16[4,16,4096]{2,1,0:T(8,128)(2,1)S(1)}, u32[]{:S(2)}, u32[]{:S(2)}) collective-permute-start(bf16[4,16,4096]{2,1,0:T(8,128)(2,1)S(1)} %slice_bitcast_fusion.2), channel_id=1, source_target_pairs={{0,16},{1,17},{2,18},{3,19},{4,20},{5,21},{6,22},{7,23},{8,24},{9,... | collective-permute-start | bytes 1572872 | tf_op jit(solution)/shard_map/ppermute | solution.py:692
  341.6 17.9 %collective-permute-start.37 = (bf16[2,16,4096]{2,1,0:T(8,128)(2,1)S(1)}, bf16[2,16,4096]{2,1,0:T(8,128)(2,1)S(1)}, u32[]{:S(2)}, u32[]{:S(2)}) collective-permute-start(bf16[2,16,4096]{2,1,0:T(8,128)(2,1)S(1)} %get-tuple-element.213), channel_id=1, source_target_pairs={{0,6},{1,7},{2,0},{3,1},{4,2},{5,3},{6,4},{7,5},{8,14},{9,15},{10,... | collective-permute-start | bytes 786440 | tf_op jit(solution)/shard_map/ppermute | solution.py:692
  345.5 14.3 %collective-permute-start.35 = (bf16[2,16,4096]{2,1,0:T(8,128)(2,1)S(1)}, bf16[2,16,4096]{2,1,0:T(8,128)(2,1)S(1)}, u32[]{:S(2)}, u32[]{:S(2)}) collective-permute-start(bf16[2,16,4096]{2,1,0:T(8,128)(2,1)S(1)} %get-tuple-element.214), channel_id=1, source_target_pairs={{0,2},{1,3},{2,4},{3,5},{4,6},{5,7},{6,0},{7,1},{8,10},{9,11},{10,... | collective-permute-start | bytes 786440 | tf_op jit(solution)/shard_map/ppermute | solution.py:692
  345.5 21.9 %collective-permute-start.36 = (bf16[2,16,4096]{2,1,0:T(8,128)(2,1)S(1)}, bf16[2,16,4096]{2,1,0:T(8,128)(2,1)S(1)}, u32[]{:S(2)}, u32[]{:S(2)}) collective-permute-start(bf16[2,16,4096]{2,1,0:T(8,128)(2,1)S(1)} %get-tuple-element.215), channel_id=1, source_target_pairs={{0,4},{1,5},{2,6},{3,7},{4,0},{5,1},{6,2},{7,3},{8,12},{9,13},{10,... | collective-permute-start | bytes 786440 | tf_op jit(solution)/shard_map/ppermute | solution.py:692
  356.3 14.4 %collective-permute-start.45 = (bf16[32,4096]{1,0:T(8,128)(2,1)S(1)}, bf16[32,4096]{1,0:T(8,128)(2,1)S(1)}, u32[]{:S(2)}, u32[]{:S(2)}) collective-permute-start(bf16[32,4096]{1,0:T(8,128)(2,1)S(1)} %get-tuple-element.210), channel_id=1, source_target_pairs={{0,24},{1,25},{2,26},{3,27},{4,28},{5,29},{6,30},{7,31},{8,16},{9,... | collective-permute-start | bytes 786440 | tf_op jit(solution)/shard_map/ppermute | solution.py:692
  370.1 14.8 %collective-permute-start.41 = (bf16[2,16,4096]{2,1,0:T(8,128)(2,1)S(1)}, bf16[2,16,4096]{2,1,0:T(8,128)(2,1)S(1)}, u32[]{:S(2)}, u32[]{:S(2)}) collective-permute-start(bf16[2,16,4096]{2,1,0:T(8,128)(2,1)S(1)} %fusion.9), channel_id=1, source_target_pairs={{0,16},{1,17},{2,18},{3,19},{4,20},{5,21},{6,22},{7,23},{8,24},{9,... | collective-permute-start | bytes 786440 | tf_op jit(solution)/shard_map/ppermute | solution.py:692
  372.3 16.8 %collective-permute-start.48 = (bf16[32,4096]{1,0:T(8,128)(2,1)S(1)}, bf16[32,4096]{1,0:T(8,128)(2,1)S(1)}, u32[]{:S(2)}, u32[]{:S(2)}) collective-permute-start(bf16[32,4096]{1,0:T(8,128)(2,1)S(1)} %fusion.6), channel_id=1, source_target_pairs={{0,24},{1,25},{2,26},{3,27},{4,28},{5,29},{6,30},{7,31},{8,16},{9,... | collective-permute-start | bytes 786440 | tf_op jit(solution)/shard_map/ppermute | solution.py:692
  374.7 17.6 %collective-permute-start.47 = (bf16[32,4096]{1,0:T(8,128)(2,1)S(1)}, bf16[32,4096]{1,0:T(8,128)(2,1)S(1)}, u32[]{:S(2)}, u32[]{:S(2)}) collective-permute-start(bf16[32,4096]{1,0:T(8,128)(2,1)S(1)} %fusion.6), channel_id=1, source_target_pairs={{0,16},{1,17},{2,18},{3,19},{4,20},{5,21},{6,22},{7,23},{8,24},{9,... | collective-permute-start | bytes 786440 | tf_op jit(solution)/shard_map/ppermute | solution.py:692
  377.9 14.8 %collective-permute-start.46 = (bf16[32,4096]{1,0:T(8,128)(2,1)S(1)}, bf16[32,4096]{1,0:T(8,128)(2,1)S(1)}, u32[]{:S(2)}, u32[]{:S(2)}) collective-permute-start(bf16[32,4096]{1,0:T(8,128)(2,1)S(1)} %fusion.6), channel_id=1, source_target_pairs={{0,8},{1,9},{2,10},{3,11},{4,12},{5,13},{6,14},{7,15},{8,0},{9,1},... | collective-permute-start | bytes 786440 | tf_op jit(solution)/shard_map/ppermute | solution.py:692
  (66 other events, 590.2 us)
Sparse Core Ops, SparseCore 0:
  76.3 80.7 all-gather.1
  163.4 88.6 reduce-scatter.2
  254.5 91.5 reduce-scatter.4

commit v5 on v4

--- a/solution.py
+++ b/solution.py
@@ -202,7 +202,7 @@
         compiler_params=params(30),
         cost_estimate=cost(2 * seqs * rows * width * wide, seqs * rows * (4 * width + wide) * 2 + 4 * width * wide),
         name="norm_project",
-    )(lengths, pos, x, cot, *[held(piece) for piece in pieces], *vectors)
+    )(lengths, pos, held(x), held(cot), *[held(piece) for piece in pieces], *vectors)
     return normed, packed, up, up_sum, kept.reshape(width, -1), table
 
 
@@ -213,7 +213,7 @@
 def attend_kernel(seq, lengths, q, k, v, *refs):
     mixed, lse = refs[-2:]
     rows = q.shape[1]
-    length = lengths[seq]
+    length = lengths[seq + pl.program_id(0)]
     key_ok = lax.broadcasted_iota(jnp.int32, (1, rows - LEAST), 1) + LEAST < length
     lane = lax.broadcasted_iota(jnp.int32, (rows, LANES), 1)
     low_lane = lane < E
@@ -237,22 +237,22 @@
     lse[0, 0] = logs.T[: lse.shape[2], :]
 
 
-def attend(seq, lengths, packed, earlier=()):
+def attend(seq, here, lengths, packed, earlier=()):
     seqs, rows, wide = packed.shape
     width = wide // 3
     wid = 4 * LANES
     steps = width // wid
-    block = lambda part: pl.BlockSpec((1, rows, wid), lambda j, *_: (seq, 0, part * steps + j))
+    block = lambda part: pl.BlockSpec((1, rows, wid), lambda s, j, *_: (seq + s, 0, part * steps + j))
     return pl.pallas_call(
         functools.partial(attend_kernel, seq),
         grid_spec=pltpu.PrefetchScalarGridSpec(
             num_scalar_prefetch=1,
-            grid=(steps,),
+            grid=(here, steps),
             in_specs=[block(0), block(1), block(2)]
             + [pl.BlockSpec(memory_space=pl.ANY)] * len(earlier),
             out_specs=[
-                pl.BlockSpec((1, rows, wid), lambda j, *_: (seq, 0, j)),
-                pl.BlockSpec((1, 1, 8, rows), lambda j, *_: (seq, j, 0, 0)),
+                pl.BlockSpec((1, rows, wid), lambda s, j, *_: (seq + s, 0, j)),
+                pl.BlockSpec((1, 1, 8, rows), lambda s, j, *_: (seq + s, j, 0, 0)),
             ],
         ),
         out_shape=[
@@ -260,8 +260,10 @@
             jax.ShapeDtypeStruct((seqs, steps, 8, rows), F32),
         ],
         input_output_aliases={4: 0, 5: 1} if earlier else {},
-        compiler_params=params(16),
-        cost_estimate=cost(4 * rows * rows * width * 8, rows * wide * 3, H * rows * rows),
+        compiler_params=pltpu.CompilerParams(
+            vmem_limit_bytes=16 << 20, dimension_semantics=("arbitrary",) * 2
+        ),
+        cost_estimate=cost(4 * here * rows * rows * width * 8, here * rows * wide * 3, here * H * rows * rows),
         name="attend",
     )(lengths, *[held(packed)] * 3, *earlier)
 
@@ -367,7 +369,7 @@
         compiler_params=params(26),
         cost_estimate=cost(2 * seqs * rows * width * width, seqs * rows * width * 10 + 4 * width * wide),
         name="branch",
-    )(lengths, pos, x, mixed, table, *[held(piece) for piece in pieces])
+    )(lengths, pos, held(x), mixed, table, *pieces)
     return resid, normed, kept.reshape(-1, wide)
 
 
@@ -442,7 +444,7 @@
         compiler_params=params(26),
         cost_estimate=cost(2 * seqs * rows * width * hidden, seqs * rows * (8 * width + 2 * hidden) + 2 * width * hidden),
         name="reduce_out",
-    )(lengths, held(resid), held(act.reshape(seqs, rows, hidden)), weight, table)
+    )(lengths, held(resid), held(act.reshape(seqs, rows, hidden)), held(weight), table)
 
 
 def hidden_back_kernel(seqs, up, weight, slope, grad, grad_sum):
@@ -543,12 +545,12 @@
             ),
             scratch_shapes=[pltpu.VMEM((count, width // 2), BF16)],
         ),
-        out_shape=jax.ShapeDtypeStruct((2, 4, 4, rows, wide), BF16),
+        out_shape=far((2, 4, 4, rows, wide), BF16),
         input_output_aliases={3: 0} if earlier else {},
         compiler_params=params(20),
         cost_estimate=cost(count * width * parts * size, count * (width + parts * size) * 2 + width * parts * size),
         name="weight_grad",
-    )(order, inputs, held(grads), *earlier)
+    )(order, inputs, held(grads), *[held(a) for a in earlier])
 
 
 def norm_two_kernel(lengths, hidden_grad, weight, resid, cot, table, *outs):
@@ -596,7 +598,7 @@
         compiler_params=params(40),
         cost_estimate=cost(2 * seqs * rows * width * (hidden + width), seqs * rows * (2 * hidden + 14 * width)),
         name="norm_two_back",
-    )(lengths, held(hidden_grad.reshape(seqs, rows, hidden)), weight, held(resid), cot, table)
+    )(lengths, held(hidden_grad.reshape(seqs, rows, hidden)), held(weight), held(resid), held(cot), table)
 
 
 def norm_one_kernel(lengths, thirds, weight, x, grad_resid, table, *outs):
@@ -634,7 +636,7 @@
         compiler_params=params(32),
         cost_estimate=cost(6 * seqs * rows * width * width, seqs * rows * width * 16 + 6 * width * width),
         name="norm_one_back",
-    )(lengths, held(thirds), weight, x, held(grad_resid), table)
+    )(lengths, held(thirds), held(weight), held(x), held(grad_resid), table)
 
 def near_kernel(*refs):
     for at in range(4):
@@ -868,7 +870,7 @@
         ring, rows_each, lens_project, pos, x, cot, pieces_p, vectors
     )
     expand_b = spaced(table, 7, 11, rows_each)
-    mixed, lse = attend(0, lens, packed)
+    mixed, lse = attend(0, 1, lens, packed)
     lens_attend = lens
     if ring:
         x_e, y_e = tie((x_e, y_e), mixed)
@@ -876,8 +878,7 @@
         lens_attend = tie(lens, near_e)
         b_e, a_e = send_xy(y_e[1], x_e[0])
         near_core_e = send(near_e, CORE)
-    for seq in range(1, count):
-        mixed, lse = attend(seq, lens_attend, packed, (mixed, lse))
+    mixed, lse = attend(1, count - 1, lens_attend, packed, (mixed, lse))
     if ring:
         a_e, b_e = tie((a_e, b_e), mixed)
         far_e = jnp.stack([a_e, b_e])

time: 405 us -> 401 us (level)
  local copies, waits for them, and re-layouts: 27.6 us -> 14.7 us
  Pallas kernels: 201 us -> 211 us
    unnamed x89 -> x57, local copies, waits for them, and re-layouts: 19.9 us -> 7.17 us
    pallas_call x3 -> x2, Pallas kernels: 22.7 us -> 21.3 us  [attend(): pl.pallas_call(functools.partial(attend_kernel, seq), grid_spec=pltpu.Pre...]
  transfers between devices with their start and end apart: 54 -> 54, of which waited for: 19 -> 21; matrix products, arithmetic and copies ran while one was open for 5% -> 6% of each run, Pallas kernels for 50% -> 53%
where the time goes in v5:
time: 401 us; the launch traced here: 397 us
  Pallas kernels  211 us (53%)
  waiting for transfers between devices  83.6 us (21%)
  starting transfers between devices  53.9 us (13%)
  other arithmetic  19.9 us (5%)
  between operations  14.8 us (4%)
  local copies, waits for them, and re-layouts  14.7 us (4%)
    ppermute x51, waiting for transfers between devices, send(): return lax.ppermute(array, AXES, pairs)  82.8 us
    ppermute x51, starting transfers between devices, send(): return lax.ppermute(array, AXES, pairs)  53.6 us
    pallas_call x1, Pallas kernels, attend_back(): pl.pallas_call(functools.partial(attend_back_kernel, seq), grid_spec=pltp...  30.4 us
    pallas_call x1, Pallas kernels, expand(): pl.pallas_call(functools.partial(expand_kernel, seqs), grid=(4,), in_spec...  26.9 us
    pallas_call x4, Pallas kernels, weight_grad(): pl.pallas_call(functools.partial(weight_grad_kernel, half), grid_spec=plt...  24.9 us
    pallas_call x2, Pallas kernels, attend(): pl.pallas_call(functools.partial(attend_kernel, seq), grid_spec=pltpu.Pre...  21.3 us
    pallas_call x1, Pallas kernels, norm_two_back(): pl.pallas_call(norm_two_kernel, grid_spec=pltpu.PrefetchScalarGridSpec(nu...  20.3 us
    pallas_call x1, Pallas kernels, reduce_out(): pl.pallas_call(reduce_kernel, grid_spec=pltpu.PrefetchScalarGridSpec(num_...  15.6 us
  transfers between devices with their start and end apart: 54, of which 21 were waited for; matrix products, arithmetic and copies ran while one was open for 6% of the time, Pallas kernels for 53%

profile of v5, /device:TPU:0, one launch (start us, length us, event | category | flops | bytes accessed | tf_op | source)
XLA Modules:
  0.0 397.4 jit_solution(5406735836710240143)
XLA Ops:
  10.7 5.1 %collective-permute-start.2 = (bf16[2,16,3200]{2,1,0:T(8,128)(2,1)S(1)}, bf16[2,16,3200]{2,1,0:T(8,128)(2,1)S(1)}, u32[]{:S(2)}, u32[]{:S(2)}) collective-permute-start(bf16[2,16,3200]{2,1,0:T(8,128)(2,1)S(1)} %dynamic-slice_bitcast_fusion.7), channel_id=1, source_target_pairs={{0,6},{1,7},{2,0},{3,1},{4,2},{5,3},{6,4},{7,5},{8,14},{9,15},{10,... | collective-permute-start | bytes 614408 | tf_op jit(solution)/shard_map/ppermute | solution.py:694
  16.9 4.5 %collective-permute-done.2 = bf16[2,16,3200]{2,1,0:T(8,128)(2,1)S(1)} collective-permute-done((bf16[2,16,3200]{2,1,0:T(8,128)(2,1)S(1)}, bf16[2,16,3200]{2,1,0:T(8,128)(2,1)S(1)}, u32[]{:S(2)}, u32[]{:S(2)}) %collective-permute-start.2) | collective-permute-done | bytes 204832 | tf_op jit(solution)/shard_map/ppermute | solution.py:694
  21.4 12.1 %collective-permute-done.1 = bf16[2,16,3200]{2,1,0:T(8,128)(2,1)S(1)} collective-permute-done((bf16[2,16,3200]{2,1,0:T(8,128)(2,1)S(1)}, bf16[2,16,3200]{2,1,0:T(8,128)(2,1)S(1)}, u32[]{:S(2)}, u32[]{:S(2)}) %collective-permute-start.1) | collective-permute-done | bytes 204832 | tf_op jit(solution)/shard_map/ppermute | solution.py:694
  36.7 2.9 collective-permute-start.8
  39.5 20.6 %collective-permute-done.8 = bf16[2,16,5120]{2,1,0:T(8,128)(2,1)S(1)} collective-permute-done((bf16[2,16,5120]{2,1,0:T(8,128)(2,1)S(1)}, bf16[2,16,5120]{2,1,0:T(8,128)(2,1)S(1)}, u32[]{:S(2)}, u32[]{:S(2)}) %collective-permute-start.8) | collective-permute-done | bytes 327712 | tf_op jit(solution)/shard_map/ppermute | solution.py:694
  61.8 8.6 %collective-permute-done.10 = bf16[3,16,3200]{2,1,0:T(8,128)(2,1)S(1)} collective-permute-done((bf16[3,16,3200]{2,1,0:T(8,128)(2,1)S(1)}, bf16[3,16,3200]{2,1,0:T(8,128)(2,1)S(1)}, u32[]{:S(2)}, u32[]{:S(2)}) %collective-permute-start.10) | collective-permute-done | bytes 307232 | tf_op jit(solution)/shard_map/ppermute | solution.py:694
  78.0 15.2 %norm_project.1 = (bf16[3,320,1024]{2,1,0:T(8,128)(2,1)S(1)}, bf16[3,320,3072]{2,1,0:T(8,128)(2,1)}, bf16[3,320,1024]{2,1,0:T(8,128)(2,1)S(1)}, f32[1,1024]{1,0:...) custom-call(s32[3]{0:T(128)S(1)} %bitcast.202, s32[3]{0:T(128)S(1)} %pad_add_fusion.1.pos, ...), custom_call_target="tpu_custom_call" | custom-call | flops 6039797760 | bytes 26345472 | tf_op jit(solution)/shard_map/norm_project/pallas_call | solution.py:176
  93.2 8.5 %attend.2 = (bf16[3,320,1024]{2,1,0:T(8,128)(2,1)S(1)}, f32[3,2,8,320]{3,2,1,0:T(8,128)S(1)}) custom-call(s32[3]{0:T(128)S(1)} %bitcast.203, bf16[3,320,3072]{2,1,0:T(8,128)(2,1)} %get-tuple-element.113.q.k.v, bf16[3,320,3072]{2,1,0:T(8,128)(2,1)} %get-tuple-element.113.q.k.v, bf16[3,320,3072]{2,1,0:T(8,128)(2,1)} %get-tuple-element.113.q.k.v), custom_call_target="tpu_custom_call" | custom-call | flops 3355443200 | bytes 2949120 | tf_op jit(solution)/shard_map/attend/pallas_call | solution.py:246
  104.0 12.9 %attend.3 = (bf16[3,320,1024]{2,1,0:T(8,128)(2,1)S(1)}, f32[3,2,8,320]{3,2,1,0:T(8,128)S(1)}) custom-call(s32[3]{0:T(128)S(1)} %bitcast.204, bf16[3,320,3072]{2,1,0:T(8,128)(2,1)} %get-tuple-element.113.q.k.v, bf16[3,320,3072]{2,1,0:T(8,128)(2,1)} %get-tuple-element.113.q.k.v, ...), custom_call_target="tpu_custom_call", output_to_operand_aliasing={{0}: (4, {}), {1}: (5, {})} | custom-call | flops 6710886400 | bytes 5898240 | tf_op jit(solution)/shard_map/attend/pallas_call | solution.py:246
  117.1 2.5 collective-permute-done.19.refs_5_
  119.6 12.9 %branch.1 = (f32[3,320,1024]{2,1,0:T(8,128)}, bf16[3,320,1024]{2,1,0:T(8,128)(2,1)S(1)}, bf16[4,2,4,2,16,5120]{5,4,3,2,1,0:T(8,128)(2,1)}) custom-call(s32[3]{0:T(128)S(1)} %bitcast.205, s32[3]{0:T(128)S(1)} %pad_add_fusion.1.pos, bf16[3,320,1024]{2,1,0:T(8,128)(2,1)} %bitcast.220, bf16[3,320,1024]{2,1,0:T(8,128)(2,1)S(1)} %get-tuple-element.119.mixed, ...), custom_call_target="tpu_custom_call" | custom-call | flops 2013265920 | bytes 30801920 | tf_op jit(solution)/shard_map/branch/pallas_call | solution.py:355
  132.6 26.9 %expand.1 = (bf16[960,4096]{1,0:T(8,128)(2,1)}, bf16[960,4096]{1,0:T(8,128)(2,1)}, bf16[4096,1024]{1,0:T(8,128)(2,1)}) custom-call(bf16[960,1024]{1,0:T(8,128)(2,1)S(1)} %bitcast.210, bf16[960,1024]{1,0:T(8,128)(2,1)S(1)} %bitcast.212, bf16[1024,5120]{1,0:T(8,128)(2,1)} %bitcast.255, f32[1,4096]{1,0:T(1,128)S(1)} %bitcast.201), custom_call_target="tpu_custom_call" | custom-call | flops 16106127360 | bytes 32505856 | tf_op jit(solution)/shard_map/expand/pallas_call | solution.py:403
  161.1 13.8 %hidden_back.1 = (bf16[960,4096]{1,0:T(8,128)(2,1)}, f32[1,4096]{1,0:T(1,128)S(1)}) custom-call(bf16[960,1024]{1,0:T(8,128)(2,1)S(1)} %bitcast.213, bf16[4096,1024]{1,0:T(8,128)(2,1)} %all-gather.2.cloned.1.call-done.weight, bf16[960,4096]{1,0:T(8,128)(2,1)} %get-tuple-element.128.slope), custom_call_target="tpu_custom_call" | custom-call | flops 8053063680 | bytes 24117248 | tf_op jit(solution)/shard_map/hidden_back/pallas_call | solution.py:467
  174.9 20.3 %norm_two_back.1 = (f32[3,320,1024]{2,1,0:T(8,128)}, bf16[3,320,1024]{2,1,0:T(8,128)(2,1)S(1)}, bf16[3,320,1024]{2,1,0:T(8,128)(2,1)S(1)}, f32[1,1024]{1,0:T(1,1...) custom-call(s32[3]{0:T(128)S(1)} %bitcast.206, bf16[3,320,4096]{2,1,0:T(8,128)(2,1)} %bitcast.260, ...), custom_call_target="tpu_custom_call" | custom-call | flops 10066329600 | bytes 21626880 | tf_op jit(solution)/shard_map/norm_two_back/pallas_call | solution.py:578
  195.2 30.4 %attend_back.1.grads.thirds = bf16[3,3,320,1024]{3,2,1,0:T(8,128)(2,1)} custom-call(s32[3]{0:T(128)S(1)} %bitcast.207, bf16[3,320,3072]{2,1,0:T(8,128)(2,1)} %get-tuple-element.113.q.k.v, bf16[3,320,3072]{2,1,0:T(8,128)(2,1)} %get-tuple-element.113.q.k.v, bf16[3,320,3072]{2,1,0:T(8,128)(2,1)} %get-tuple-element.113.q.k.v, ...), custom_call_target="tpu_custom_call" | custom-call | flops 25165824000 | bytes 14745600 | tf_op jit(solution)/shard_map/attend_back/pallas_call | solution.py:311
  225.6 12.7 %whole_grad.1 = bf16[1024,4096]{1,0:T(8,128)(2,1)} custom-call(bf16[960,1024]{1,0:T(8,128)(2,1)S(1)} %bitcast.211, bf16[960,4096]{1,0:T(8,128)(2,1)} %get-tuple-element.169.grads), custom_call_target="tpu_custom_call" | custom-call | flops 8053063680 | bytes 18219008 | tf_op jit(solution)/shard_map/whole_grad/pallas_call | solution.py:487
  238.4 4.5 %weight_grad.5.refs_0_ = bf16[2,4,4,16,4096]{4,3,2,1,0:T(8,128)(2,1)} custom-call(s32[4]{0:T(128)S(1)} %pad_add_fusion.order, bf16[960,1024]{1,0:T(8,128)(2,1)S(1)} %bitcast.171, bf16[960,1024]{1,0:T(8,128)(2,1)} %bitcast.175), custom_call_target="tpu_custom_call" | custom-call | flops 1006632960 | bytes 4980736 | tf_op jit(solution)/shard_map/weight_grad/pallas_call | solution.py:536
  243.0 4.5 %weight_grad.4.refs_0_ = bf16[2,4,4,16,4096]{4,3,2,1,0:T(8,128)(2,1)} custom-call(s32[4]{0:T(128)S(1)} %pad_add_fusion.order, bf16[960,1024]{1,0:T(8,128)(2,1)S(1)} %bitcast.172, bf16[960,1024]{1,0:T(8,128)(2,1)} %bitcast.176), custom_call_target="tpu_custom_call" | custom-call | flops 1006632960 | bytes 4980736 | tf_op jit(solution)/shard_map/weight_grad/pallas_call | solution.py:536
  251.0 8.0 %weight_grad.6 = bf16[2,4,4,16,4096]{4,3,2,1,0:T(8,128)(2,1)} custom-call(s32[4]{0:T(128)S(1)} %pad_add_fusion.order, bf16[960,1024]{1,0:T(8,128)(2,1)S(1)} %bitcast.173, bf16[3,3,320,1024]{3,2,1,0:T(8,128)(2,1)} %attend_back.1.grads.thirds, bf16[2,4,4,16,4096]{4,3,2,1,0:T(8,128)(2,1)} %weight_grad.4.refs_0_), custom_call_target="tpu_custom_call", output_to_operand_aliasing={{}: (3, {})} | custom-call | flops 3019898880 | bytes 11010048 | tf_op jit(solution)/shard_map/weight_grad/pallas_call | solution.py:536
  259.0 2.5 collective-permute-start.23
  262.5 7.9 %weight_grad.7 = bf16[2,4,4,16,4096]{4,3,2,1,0:T(8,128)(2,1)} custom-call(s32[4]{0:T(128)S(1)} %pad_add_fusion.order, bf16[960,1024]{1,0:T(8,128)(2,1)S(1)} %bitcast.174, bf16[3,3,320,1024]{3,2,1,0:T(8,128)(2,1)} %attend_back.1.grads.thirds, bf16[2,4,4,16,4096]{4,3,2,1,0:T(8,128)(2,1)} %weight_grad.5.refs_0_), custom_call_target="tpu_custom_call", output_to_operand_aliasing={{}: (3, {})} | custom-call | flops 3019898880 | bytes 11010048 | tf_op jit(solution)/shard_map/weight_grad/pallas_call | solution.py:536
  270.3 3.9 collective-permute-done.22
  282.2 15.2 %norm_one_back.1 = (f32[3,320,1024]{2,1,0:T(8,128)}, f32[1,1024]{1,0:T(1,128)S(1)}, f32[1,1024]{1,0:T(1,128)S(1)}, f32[1,1024]{1,0:T(1,128)S(1)}, f32[1,1024]{1,0:T(1,128)S(1)}) custom-call(s32[3]{0:T(128)S(1)} %bitcast.208, bf16[3,3,320,1024]{3,2,1,0:T(8,128)(2,1)} %attend_back.1.grads.thirds, bf16[1024,3200]{1,0:T(8,128)(2,1)} %bitcast.261, ...), custom_call_target="tpu_custom_call" | custom-call | flops 6039797760 | bytes 22020096 | tf_op jit(solution)/shard_map/norm_one_back/pallas_call | solution.py:624
  303.8 4.5 %collective-permute-done.26 = f32[96,128]{1,0:T(8,128)} collective-permute-done((f32[96,128]{1,0:T(8,128)}, f32[96,128]{1,0:T(8,128)}, u32[]{:S(2)}, u32[]{:S(2)}) %collective-permute-start.26) | collective-permute-done | bytes 49184 | tf_op jit(solution)/shard_map/ppermute | solution.py:694
  310.3 2.5 collective-permute-start.33
  318.5 15.6 %reduce_out.1 = f32[3,320,1024]{2,1,0:T(8,128)} custom-call(s32[3]{0:T(128)S(1)} %bitcast.209, f32[3,320,1024]{2,1,0:T(8,128)} %get-tuple-element.130.resid, bf16[3,320,4096]{2,1,0:T(8,128)(2,1)} %bitcast.259, bf16[4096,1024]{1,0:T(8,128)(2,1)} %all-gather.2.cloned.1.call-done.weight, f32[16,1024]{1,0:T(8,128)S(1)} %get-tuple-element.120.table), custom_call_target="tpu_custom_call" | custom-call | flops 8053063680 | bytes 24117248 | tf_op jit(solution)/shard_map/reduce_out/pallas_call | solution.py:430
  337.3 3.7 collective-permute-start.37
  342.9 2.5 collective-permute-start.49
  355.4 8.2 %collective-permute-done.36 = bf16[2,16,4096]{2,1,0:T(8,128)(2,1)S(1)} collective-permute-done((bf16[2,16,4096]{2,1,0:T(8,128)(2,1)S(1)}, bf16[2,16,4096]{2,1,0:T(8,128)(2,1)S(1)}, u32[]{:S(2)}, u32[]{:S(2)}) %collective-permute-start.36) | collective-permute-done | bytes 262176 | tf_op jit(solution)/shard_map/ppermute | solution.py:694
  371.4 2.6 collective-permute-done.42
  375.4 5.5 %collective-permute-done.41 = bf16[2,16,4096]{2,1,0:T(8,128)(2,1)S(1)} collective-permute-done((bf16[2,16,4096]{2,1,0:T(8,128)(2,1)S(1)}, bf16[2,16,4096]{2,1,0:T(8,128)(2,1)S(1)}, u32[]{:S(2)}, u32[]{:S(2)}) %collective-permute-start.41) | collective-permute-done | bytes 262176 | tf_op jit(solution)/shard_map/ppermute | solution.py:694
  385.2 3.2 collective-permute-done.47
  (207 shorter events, 78.0 us)
Async XLA Ops:
  7.3 152.3 %all-gather.2.cloned.1.call-start = ((), (), s32[]{:S(2)}) async-start(), calls=%async_computation.3 | async-start | bytes 9437184 | tf_op jit(solution)/shard_map/all_gather | solution.py:859
  8.7 24.8 %collective-permute-start.4 = (bf16[4,2,16,5120]{3,2,1,0:T(8,128)(2,1)S(1)}, bf16[4,2,16,5120]{3,2,1,0:T(8,128)(2,1)S(1)}, u32[]{:S(2)}, u32[]{:S(2)}) collective-permute-start(bf16[4,2,16,5120]{3,2,1,0:T(8,128)(2,1)S(1)} %bitcast.177), channel_id=1, source_target_pairs={{0,1},{1,0},{2,3},{3,2},{4,5},{5,4},{6,7},{7,6},{8,9},{9,8},{10,11... | collective-permute-start | bytes 3932168 | tf_op jit(solution)/shard_map/ppermute | solution.py:694
  10.6 22.8 %collective-permute-start.3 = (bf16[4,2,16,3200]{3,2,1,0:T(8,128)(2,1)S(1)}, bf16[4,2,16,3200]{3,2,1,0:T(8,128)(2,1)}, u32[]{:S(2)}, u32[]{:S(2)}) collective-permute-start(bf16[4,2,16,3200]{3,2,1,0:T(8,128)(2,1)S(1)} %bitcast.224), channel_id=1, source_target_pairs={{0,1},{1,0},{2,3},{3,2},{4,5},{5,4},{6,7},{7,6},{8,9},{9,8},{10,11... | collective-permute-start | bytes 2457608 | tf_op jit(solution)/shard_map/ppermute | solution.py:694
  15.8 17.6 %collective-permute-start.1 = (bf16[2,16,3200]{2,1,0:T(8,128)(2,1)S(1)}, bf16[2,16,3200]{2,1,0:T(8,128)(2,1)S(1)}, u32[]{:S(2)}, u32[]{:S(2)}) collective-permute-start(bf16[2,16,3200]{2,1,0:T(8,128)(2,1)S(1)} %dynamic-slice_bitcast_fusion.7), channel_id=1, source_target_pairs={{0,4},{1,5},{2,6},{3,7},{4,0},{5,1},{6,2},{7,3},{8,12},{9,13},{10,... | collective-permute-start | bytes 614408 | tf_op jit(solution)/shard_map/ppermute | solution.py:694
  15.8 17.6 %collective-permute-start = (bf16[2,16,3200]{2,1,0:T(8,128)(2,1)S(1)}, bf16[2,16,3200]{2,1,0:T(8,128)(2,1)S(1)}, u32[]{:S(2)}, u32[]{:S(2)}) collective-permute-start(bf16[2,16,3200]{2,1,0:T(8,128)(2,1)S(1)} %dynamic-slice_bitcast_fusion.7), channel_id=1, source_target_pairs={{0,2},{1,3},{2,4},{3,5},{4,6},{5,7},{6,0},{7,1},{8,10},{9,11},{10,... | collective-permute-start | bytes 614408 | tf_op jit(solution)/shard_map/ppermute | solution.py:694
  33.6 26.6 %collective-permute-start.6 = (bf16[2,3,16,3200]{3,2,1,0:T(8,128)(2,1)S(1)}, bf16[2,3,16,3200]{3,2,1,0:T(8,128)(2,1)S(1)}, u32[]{:S(2)}, u32[]{:S(2)}) collective-permute-start(bf16[2,3,16,3200]{3,2,1,0:T(8,128)(2,1)S(1)} %get-tuple-element.218), channel_id=1, source_target_pairs={{0,16},{1,17},{2,18},{3,19},{4,20},{5,21},{6,22},{7,23},{8,24},{9,... | collective-permute-start | bytes 1843208 | tf_op jit(solution)/shard_map/ppermute | solution.py:694
  35.2 25.0 %collective-permute-start.5 = (bf16[2,3,16,3200]{3,2,1,0:T(8,128)(2,1)S(1)}, bf16[2,3,16,3200]{3,2,1,0:T(8,128)(2,1)S(1)}, u32[]{:S(2)}, u32[]{:S(2)}) collective-permute-start(bf16[2,3,16,3200]{3,2,1,0:T(8,128)(2,1)S(1)} %get-tuple-element.218), channel_id=1, source_target_pairs={{0,8},{1,9},{2,10},{3,11},{4,12},{5,13},{6,14},{7,15},{8,0},{9,1},... | collective-permute-start | bytes 1843208 | tf_op jit(solution)/shard_map/ppermute | solution.py:694
  36.7 23.5 %collective-permute-start.8 = (bf16[2,16,5120]{2,1,0:T(8,128)(2,1)S(1)}, bf16[2,16,5120]{2,1,0:T(8,128)(2,1)S(1)}, u32[]{:S(2)}, u32[]{:S(2)}) collective-permute-start(bf16[2,16,5120]{2,1,0:T(8,128)(2,1)S(1)} %dynamic-slice_bitcast_fusion), channel_id=1, source_target_pairs={{0,4},{1,5},{2,6},{3,7},{4,0},{5,1},{6,2},{7,3},{8,12},{9,13},{10,... | collective-permute-start | bytes 983048 | tf_op jit(solution)/shard_map/ppermute | solution.py:694
  39.5 20.6 %collective-permute-start.7 = (bf16[2,16,5120]{2,1,0:T(8,128)(2,1)S(1)}, bf16[2,16,5120]{2,1,0:T(8,128)(2,1)S(1)}, u32[]{:S(2)}, u32[]{:S(2)}) collective-permute-start(bf16[2,16,5120]{2,1,0:T(8,128)(2,1)S(1)} %dynamic-slice_bitcast_fusion), channel_id=1, source_target_pairs={{0,2},{1,3},{2,4},{3,5},{4,6},{5,7},{6,0},{7,1},{8,10},{9,11},{10,... | collective-permute-start | bytes 983048 | tf_op jit(solution)/shard_map/ppermute | solution.py:694
  75.6 172.7 %reduce-scatter.3.cloned.1.call-start = ((), (), s32[]{:S(2)}) async-start(), calls=%async_computation.2 | async-start | bytes 9437184 | tf_op jit(solution)/shard_map/reduce_scatter | solution.py:819
  75.8 25.9 %collective-permute-start.15 = (bf16[2,3,16,5120]{3,2,1,0:T(8,128)(2,1)}, bf16[2,3,16,5120]{3,2,1,0:T(8,128)(2,1)S(1)}, u32[]{:S(2)}, u32[]{:S(2)}) collective-permute-start(bf16[2,3,16,5120]{3,2,1,0:T(8,128)(2,1)} %get-tuple-element.216), channel_id=1, source_target_pairs={{0,16},{1,17},{2,18},{3,19},{4,20},{5,21},{6,22},{7,23},{8,24},{9,... | collective-permute-start | bytes 2949128 | tf_op jit(solution)/shard_map/ppermute | solution.py:694
  76.4 25.3 %collective-permute-start.14 = (bf16[2,3,16,5120]{3,2,1,0:T(8,128)(2,1)}, bf16[2,3,16,5120]{3,2,1,0:T(8,128)(2,1)S(1)}, u32[]{:S(2)}, u32[]{:S(2)}) collective-permute-start(bf16[2,3,16,5120]{3,2,1,0:T(8,128)(2,1)} %get-tuple-element.216), channel_id=1, source_target_pairs={{0,8},{1,9},{2,10},{3,11},{4,12},{5,13},{6,14},{7,15},{8,0},{9,1},... | collective-permute-start | bytes 2949128 | tf_op jit(solution)/shard_map/ppermute | solution.py:694
  102.1 17.5 %collective-permute-start.18 = (bf16[3,2,3,16,5120]{4,3,2,1,0:T(8,128)(2,1)S(1)}, bf16[3,2,3,16,5120]{4,3,2,1,0:T(8,128)(2,1)S(1)}, u32[]{:S(2)}, u32[]{:S(2)}) collective-permute-start(bf16[3,2,3,16,5120]{4,3,2,1,0:T(8,128)(2,1)S(1)} %pad_maximum_fusion.refs_1_), channel_id=1, source_target_pairs={{0,1},{1,0},{2,3},{3,2},{4,5},{5,4},{6,7},{7,6},{8,9},{9,8},{10,11... | collective-permute-start | bytes 8847368 | tf_op jit(solution)/shard_map/ppermute | solution.py:694
  102.2 14.7 %collective-permute-start.17 = (bf16[3,16,5120]{2,1,0:T(8,128)(2,1)S(1)}, bf16[3,16,5120]{2,1,0:T(8,128)(2,1)S(1)}, u32[]{:S(2)}, u32[]{:S(2)}) collective-permute-start(bf16[3,16,5120]{2,1,0:T(8,128)(2,1)S(1)} %slice_bitcast_fusion.4), channel_id=1, source_target_pairs={{0,8},{1,9},{2,10},{3,11},{4,12},{5,13},{6,14},{7,15},{8,0},{9,1},... | collective-permute-start | bytes 1474568 | tf_op jit(solution)/shard_map/ppermute | solution.py:694
  102.4 14.5 %collective-permute-start.16 = (bf16[3,16,5120]{2,1,0:T(8,128)(2,1)S(1)}, bf16[3,16,5120]{2,1,0:T(8,128)(2,1)S(1)}, u32[]{:S(2)}, u32[]{:S(2)}) collective-permute-start(bf16[3,16,5120]{2,1,0:T(8,128)(2,1)S(1)} %slice_bitcast_fusion.5), channel_id=1, source_target_pairs={{0,16},{1,17},{2,18},{3,19},{4,20},{5,21},{6,22},{7,23},{8,24},{9,... | collective-permute-start | bytes 1474568 | tf_op jit(solution)/shard_map/ppermute | solution.py:694
  159.5 191.1 %reduce-scatter.5.cloned.1.call-start = ((), (), s32[]{:S(2)}) async-start(), calls=%async_computation.4 | async-start | bytes 9437184 | tf_op jit(solution)/shard_map/reduce_scatter | solution.py:819
  259.0 16.5 %collective-permute-start.20 = (bf16[2,4,4,16,4096]{4,3,2,1,0:T(8,128)(2,1)}, bf16[2,4,4,16,4096]{4,3,2,1,0:T(8,128)(2,1)S(1)}, u32[]{:S(2)}, u32[]{:S(2)}) collective-permute-start(bf16[2,4,4,16,4096]{4,3,2,1,0:T(8,128)(2,1)} %weight_grad.6), channel_id=1, source_target_pairs={{0,1},{1,0},{2,3},{3,2},{4,5},{5,4},{6,7},{7,6},{8,9},{9,8},{10,11... | collective-permute-start | bytes 12582920 | tf_op jit(solution)/shard_map/ppermute | solution.py:694
  280.1 29.5 %collective-permute-start.29 = (bf16[4,2,16,4096]{3,2,1,0:T(8,128)(2,1)S(1)}, bf16[4,2,16,4096]{3,2,1,0:T(8,128)(2,1)}, u32[]{:S(2)}, u32[]{:S(2)}) collective-permute-start(bf16[4,2,16,4096]{3,2,1,0:T(8,128)(2,1)S(1)} %get-tuple-element.141), channel_id=1, source_target_pairs={{0,16},{1,17},{2,18},{3,19},{4,20},{5,21},{6,22},{7,23},{8,24},{9,... | collective-permute-start | bytes 3145736 | tf_op jit(solution)/shard_map/ppermute | solution.py:694
  281.6 28.1 %collective-permute-start.28 = (bf16[4,2,16,4096]{3,2,0,1:T(8,128)(2,1)}, bf16[4,2,16,4096]{3,2,0,1:T(8,128)(2,1)}, u32[]{:S(2)}, u32[]{:S(2)}) collective-permute-start(bf16[4,2,16,4096]{3,2,0,1:T(8,128)(2,1)} %copy.49), channel_id=1, source_target_pairs={{0,8},{1,9},{2,10},{3,11},{4,12},{5,13},{6,14},{7,15},{8,0},{9,1},... | collective-permute-start | bytes 3145736 | tf_op jit(solution)/shard_map/ppermute | solution.py:694
  309.6 24.4 %collective-permute-start.34 = (f32[96,128]{1,0:T(8,128)S(1)}, f32[96,128]{1,0:T(8,128)S(1)}, u32[]{:S(2)}, u32[]{:S(2)}) collective-permute-start(f32[96,128]{1,0:T(8,128)S(1)} %add_add_fusion), channel_id=1, source_target_pairs={{0,6},{1,7},{2,0},{3,1},{4,2},{5,3},{6,4},{7,5},{8,14},{9,15},{10,... | collective-permute-start | bytes 147464 | tf_op jit(solution)/shard_map/ppermute | solution.py:694
  310.3 23.7 %collective-permute-start.33 = (f32[96,128]{1,0:T(8,128)S(1)}, f32[96,128]{1,0:T(8,128)S(1)}, u32[]{:S(2)}, u32[]{:S(2)}) collective-permute-start(f32[96,128]{1,0:T(8,128)S(1)} %add_add_fusion), channel_id=1, source_target_pairs={{0,4},{1,5},{2,6},{3,7},{4,0},{5,1},{6,2},{7,3},{8,12},{9,13},{10,... | collective-permute-start | bytes 147464 | tf_op jit(solution)/shard_map/ppermute | solution.py:694
  312.8 21.3 %collective-permute-start.32 = (f32[96,128]{1,0:T(8,128)S(1)}, f32[96,128]{1,0:T(8,128)S(1)}, u32[]{:S(2)}, u32[]{:S(2)}) collective-permute-start(f32[96,128]{1,0:T(8,128)S(1)} %add_add_fusion), channel_id=1, source_target_pairs={{0,2},{1,3},{2,4},{3,5},{4,6},{5,7},{6,0},{7,1},{8,10},{9,11},{10,... | collective-permute-start | bytes 147464 | tf_op jit(solution)/shard_map/ppermute | solution.py:694
  314.5 19.6 %collective-permute-start.30 = (bf16[4,16,4096]{2,1,0:T(8,128)(2,1)S(1)}, bf16[4,16,4096]{2,1,0:T(8,128)(2,1)S(1)}, u32[]{:S(2)}, u32[]{:S(2)}) collective-permute-start(bf16[4,16,4096]{2,1,0:T(8,128)(2,1)S(1)} %slice_bitcast_fusion.3), channel_id=1, source_target_pairs={{0,8},{1,9},{2,10},{3,11},{4,12},{5,13},{6,14},{7,15},{8,0},{9,1},... | collective-permute-start | bytes 1572872 | tf_op jit(solution)/shard_map/ppermute | solution.py:694
  316.7 17.4 %collective-permute-start.31 = (bf16[4,16,4096]{2,1,0:T(8,128)(2,1)S(1)}, bf16[4,16,4096]{2,1,0:T(8,128)(2,1)S(1)}, u32[]{:S(2)}, u32[]{:S(2)}) collective-permute-start(bf16[4,16,4096]{2,1,0:T(8,128)(2,1)S(1)} %slice_bitcast_fusion.2), channel_id=1, source_target_pairs={{0,16},{1,17},{2,18},{3,19},{4,20},{5,21},{6,22},{7,23},{8,24},{9,... | collective-permute-start | bytes 1572872 | tf_op jit(solution)/shard_map/ppermute | solution.py:694
  337.3 17.9 %collective-permute-start.37 = (bf16[2,16,4096]{2,1,0:T(8,128)(2,1)}, bf16[2,16,4096]{2,1,0:T(8,128)(2,1)S(1)}, u32[]{:S(2)}, u32[]{:S(2)}) collective-permute-start(bf16[2,16,4096]{2,1,0:T(8,128)(2,1)} %get-tuple-element.209), channel_id=1, source_target_pairs={{0,6},{1,7},{2,0},{3,1},{4,2},{5,3},{6,4},{7,5},{8,14},{9,15},{10,... | collective-permute-start | bytes 786440 | tf_op jit(solution)/shard_map/ppermute | solution.py:694
  341.1 14.3 %collective-permute-start.35 = (bf16[2,16,4096]{2,1,0:T(8,128)(2,1)S(1)}, bf16[2,16,4096]{2,1,0:T(8,128)(2,1)S(1)}, u32[]{:S(2)}, u32[]{:S(2)}) collective-permute-start(bf16[2,16,4096]{2,1,0:T(8,128)(2,1)S(1)} %get-tuple-element.210), channel_id=1, source_target_pairs={{0,2},{1,3},{2,4},{3,5},{4,6},{5,7},{6,0},{7,1},{8,10},{9,11},{10,... | collective-permute-start | bytes 786440 | tf_op jit(solution)/shard_map/ppermute | solution.py:694
  341.1 22.5 %collective-permute-start.36 = (bf16[2,16,4096]{2,1,0:T(8,128)(2,1)S(1)}, bf16[2,16,4096]{2,1,0:T(8,128)(2,1)S(1)}, u32[]{:S(2)}, u32[]{:S(2)}) collective-permute-start(bf16[2,16,4096]{2,1,0:T(8,128)(2,1)S(1)} %get-tuple-element.211), channel_id=1, source_target_pairs={{0,4},{1,5},{2,6},{3,7},{4,0},{5,1},{6,2},{7,3},{8,12},{9,13},{10,... | collective-permute-start | bytes 786440 | tf_op jit(solution)/shard_map/ppermute | solution.py:694
  351.8 14.9 %collective-permute-start.45 = (bf16[32,4096]{1,0:T(8,128)(2,1)S(1)}, bf16[32,4096]{1,0:T(8,128)(2,1)S(1)}, u32[]{:S(2)}, u32[]{:S(2)}) collective-permute-start(bf16[32,4096]{1,0:T(8,128)(2,1)S(1)} %get-tuple-element.206), channel_id=1, source_target_pairs={{0,24},{1,25},{2,26},{3,27},{4,28},{5,29},{6,30},{7,31},{8,16},{9,... | collective-permute-start | bytes 786440 | tf_op jit(solution)/shard_map/ppermute | solution.py:694
  366.2 14.7 %collective-permute-start.41 = (bf16[2,16,4096]{2,1,0:T(8,128)(2,1)S(1)}, bf16[2,16,4096]{2,1,0:T(8,128)(2,1)S(1)}, u32[]{:S(2)}, u32[]{:S(2)}) collective-permute-start(bf16[2,16,4096]{2,1,0:T(8,128)(2,1)S(1)} %fusion.9), channel_id=1, source_target_pairs={{0,16},{1,17},{2,18},{3,19},{4,20},{5,21},{6,22},{7,23},{8,24},{9,... | collective-permute-start | bytes 786440 | tf_op jit(solution)/shard_map/ppermute | solution.py:694
  368.4 16.9 %collective-permute-start.48 = (bf16[32,4096]{1,0:T(8,128)(2,1)S(1)}, bf16[32,4096]{1,0:T(8,128)(2,1)S(1)}, u32[]{:S(2)}, u32[]{:S(2)}) collective-permute-start(bf16[32,4096]{1,0:T(8,128)(2,1)S(1)} %fusion.6), channel_id=1, source_target_pairs={{0,24},{1,25},{2,26},{3,27},{4,28},{5,29},{6,30},{7,31},{8,16},{9,... | collective-permute-start | bytes 786440 | tf_op jit(solution)/shard_map/ppermute | solution.py:694
  370.8 17.6 %collective-permute-start.47 = (bf16[32,4096]{1,0:T(8,128)(2,1)S(1)}, bf16[32,4096]{1,0:T(8,128)(2,1)S(1)}, u32[]{:S(2)}, u32[]{:S(2)}) collective-permute-start(bf16[32,4096]{1,0:T(8,128)(2,1)S(1)} %fusion.6), channel_id=1, source_target_pairs={{0,16},{1,17},{2,18},{3,19},{4,20},{5,21},{6,22},{7,23},{8,24},{9,... | collective-permute-start | bytes 786440 | tf_op jit(solution)/shard_map/ppermute | solution.py:694
  374.0 14.6 %collective-permute-start.46 = (bf16[32,4096]{1,0:T(8,128)(2,1)S(1)}, bf16[32,4096]{1,0:T(8,128)(2,1)S(1)}, u32[]{:S(2)}, u32[]{:S(2)}) collective-permute-start(bf16[32,4096]{1,0:T(8,128)(2,1)S(1)} %fusion.6), channel_id=1, source_target_pairs={{0,8},{1,9},{2,10},{3,11},{4,12},{5,13},{6,14},{7,15},{8,0},{9,1},... | collective-permute-start | bytes 786440 | tf_op jit(solution)/shard_map/ppermute | solution.py:694
  (50 other events, 483.5 us)
Sparse Core Ops, SparseCore 0:
  75.7 80.7 all-gather.1
  159.6 88.5 reduce-scatter.2
  250.6 91.7 reduce-scatter.4

commit v6 on v5

--- a/solution.py
+++ b/solution.py
@@ -636,7 +636,7 @@
         compiler_params=params(32),
         cost_estimate=cost(6 * seqs * rows * width * width, seqs * rows * width * 16 + 6 * width * width),
         name="norm_one_back",
-    )(lengths, held(thirds), held(weight), held(x), held(grad_resid), table)
+    )(lengths, held(thirds), weight, x, held(grad_resid), table)
 
 def near_kernel(*refs):
     for at in range(4):
@@ -665,7 +665,7 @@
         compiler_params=params(14),
         cost_estimate=cost(own.size, own.size * 6),
         name="near_sum",
-    )(*[own.reshape(shape)] * 4, *[arrived.reshape(shape)] * 4)
+    )(*[held(own.reshape(shape))] * 4, *[held(arrived.reshape(shape))] * 4)
 
 
 AXES = ("group", "dp")
@@ -940,27 +940,25 @@
         ps = scatter_far(ps[0], ps[1], from_x, from_y)
         lens_out = tie(lens, ps)
         from_x, from_y = send_xy(ps[3], ps[2])
-        column = [send(total, OVER_Z[k]) for k in range(1, Z)]
+        near_r = send_near(spread_r)
     layer_output = reduce_out(lens_out, resid, act, reduce_w, table)
     sums = {}
     if ring:
-        (from_x, from_y, column), layer_output = lax.optimization_barrier(
-            ((from_x, from_y, column), layer_output)
+        (from_x, from_y, near_r), layer_output = lax.optimization_barrier(
+            ((from_x, from_y, near_r), layer_output)
         )
         mine_z, parts_z = scatter_z(ps[0], ps[1], from_y, from_x, z)
         arrived_p = send_z(parts_z)
-        spread_r = tie(spread_r, parts_z)
-        x_r, y_r = send_xy(spread_r, spread_r)
-        half = spread_r.shape[0] // 2
-        b_r, a_r = send_xy(y_r[half:], x_r[:half])
-        sums[10] = placed(spread_r, [x_r, y_r, jnp.concatenate([a_r, b_r])], g)
-        total = (total + column[1]) + (column[0] + column[2])
-        mine_e, parts_e = trade(tie(shard_e, (x_r, y_r)), g)
+        mine_e, parts_e = trade(tie(shard_e, parts_z), g)
         arrived_e = send_trade(parts_e)
-        spread_p = spread(mine_z, tie(arrived_p, parts_e))
+        sums[10] = placed(spread_r, near_r, g)
+        spread_e = spread(mine_e, arrived_e)
+        near_e = send_near(spread_e)
+        total = tie(total, spread_e)
+        total = total + send(total, NEAR_Z)
+        total = total + send(total, FAR_Z)
+        spread_p = spread(mine_z, tie(arrived_p, spread_e))
         near_p = send_near(spread_p)
-        spread_e = spread(mine_e, tie(arrived_e, spread_p))
-        near_e = send_near(spread_e)
         joint_sum = placed(spread_p, near_p, g)
         sums[8] = placed(spread_e, near_e, g)
     else:

time: 401 us -> 398 us (level)
  starting transfers between devices: 53.9 us -> 47.3 us
  waiting for transfers between devices: 83.6 us -> 88.5 us
    ppermute x51 -> x49, starting transfers between devices: 53.6 us -> 47.1 us  [send(): return lax.ppermute(array, AXES, pairs)]
    ppermute x51 -> x49, waiting for transfers between devices: 82.8 us -> 87.7 us  [send(): return lax.ppermute(array, AXES, pairs)]
  transfers between devices with their start and end apart: 54 -> 52, of which waited for: 21 -> 22; matrix products, arithmetic and copies ran while one was open for 6% -> 5% of each run, Pallas kernels for 53% -> 54%
where the time goes in v6:
time: 398 us; the launch traced here: 395 us
  Pallas kernels  212 us (53%)
  waiting for transfers between devices  88.5 us (22%)
  starting transfers between devices  47.3 us (12%)
  other arithmetic  18.7 us (5%)
  between operations  14.8 us (4%)
  local copies, waits for them, and re-layouts  13.5 us (3%)
    ppermute x49, waiting for transfers between devices, send(): return lax.ppermute(array, AXES, pairs)  87.7 us
    ppermute x49, starting transfers between devices, send(): return lax.ppermute(array, AXES, pairs)  47.1 us
    pallas_call x1, Pallas kernels, attend_back(): pl.pallas_call(functools.partial(attend_back_kernel, seq), grid_spec=pltp...  30.4 us
    pallas_call x1, Pallas kernels, expand(): pl.pallas_call(functools.partial(expand_kernel, seqs), grid=(4,), in_spec...  26.9 us
    pallas_call x4, Pallas kernels, weight_grad(): pl.pallas_call(functools.partial(weight_grad_kernel, half), grid_spec=plt...  25.5 us
    pallas_call x2, Pallas kernels, attend(): pl.pallas_call(functools.partial(attend_kernel, seq), grid_spec=pltpu.Pre...  21.3 us
    pallas_call x1, Pallas kernels, norm_two_back(): pl.pallas_call(norm_two_kernel, grid_spec=pltpu.PrefetchScalarGridSpec(nu...  20.2 us
    pallas_call x1, Pallas kernels, reduce_out(): pl.pallas_call(reduce_kernel, grid_spec=pltpu.PrefetchScalarGridSpec(num_...  15.5 us
  transfers between devices with their start and end apart: 52, of which 22 were waited for; matrix products, arithmetic and copies ran while one was open for 5% of the time, Pallas kernels for 54%

profile of v6, /device:TPU:0, one launch (start us, length us, event | category | flops | bytes accessed | tf_op | source)
XLA Modules:
  0.0 394.9 jit_solution(12688770932660727469)
XLA Ops:
  10.7 5.1 %collective-permute-start.2 = (bf16[2,16,3200]{2,1,0:T(8,128)(2,1)S(1)}, bf16[2,16,3200]{2,1,0:T(8,128)(2,1)S(1)}, u32[]{:S(2)}, u32[]{:S(2)}) collective-permute-start(bf16[2,16,3200]{2,1,0:T(8,128)(2,1)S(1)} %dynamic-slice_bitcast_fusion.7), channel_id=1, source_target_pairs={{0,6},{1,7},{2,0},{3,1},{4,2},{5,3},{6,4},{7,5},{8,14},{9,15},{10,... | collective-permute-start | bytes 614408 | tf_op jit(solution)/shard_map/ppermute | solution.py:694
  16.9 4.5 %collective-permute-done.2 = bf16[2,16,3200]{2,1,0:T(8,128)(2,1)S(1)} collective-permute-done((bf16[2,16,3200]{2,1,0:T(8,128)(2,1)S(1)}, bf16[2,16,3200]{2,1,0:T(8,128)(2,1)S(1)}, u32[]{:S(2)}, u32[]{:S(2)}) %collective-permute-start.2) | collective-permute-done | bytes 204832 | tf_op jit(solution)/shard_map/ppermute | solution.py:694
  21.4 12.1 %collective-permute-done.1 = bf16[2,16,3200]{2,1,0:T(8,128)(2,1)S(1)} collective-permute-done((bf16[2,16,3200]{2,1,0:T(8,128)(2,1)S(1)}, bf16[2,16,3200]{2,1,0:T(8,128)(2,1)S(1)}, u32[]{:S(2)}, u32[]{:S(2)}) %collective-permute-start.1) | collective-permute-done | bytes 204832 | tf_op jit(solution)/shard_map/ppermute | solution.py:694
  36.7 2.9 collective-permute-start.8
  39.5 20.6 %collective-permute-done.8 = bf16[2,16,5120]{2,1,0:T(8,128)(2,1)S(1)} collective-permute-done((bf16[2,16,5120]{2,1,0:T(8,128)(2,1)S(1)}, bf16[2,16,5120]{2,1,0:T(8,128)(2,1)S(1)}, u32[]{:S(2)}, u32[]{:S(2)}) %collective-permute-start.8) | collective-permute-done | bytes 327712 | tf_op jit(solution)/shard_map/ppermute | solution.py:694
  61.8 8.6 %collective-permute-done.10 = bf16[3,16,3200]{2,1,0:T(8,128)(2,1)S(1)} collective-permute-done((bf16[3,16,3200]{2,1,0:T(8,128)(2,1)S(1)}, bf16[3,16,3200]{2,1,0:T(8,128)(2,1)S(1)}, u32[]{:S(2)}, u32[]{:S(2)}) %collective-permute-start.10) | collective-permute-done | bytes 307232 | tf_op jit(solution)/shard_map/ppermute | solution.py:694
  76.8 15.3 %norm_project.1 = (bf16[3,320,1024]{2,1,0:T(8,128)(2,1)S(1)}, bf16[3,320,3072]{2,1,0:T(8,128)(2,1)}, bf16[3,320,1024]{2,1,0:T(8,128)(2,1)S(1)}, f32[1,1024]{1,0:...) custom-call(s32[3]{0:T(128)S(1)} %bitcast.196, s32[3]{0:T(128)S(1)} %pad_add_fusion.1.pos, ...), custom_call_target="tpu_custom_call" | custom-call | flops 6039797760 | bytes 26345472 | tf_op jit(solution)/shard_map/norm_project/pallas_call | solution.py:176
  92.1 8.4 %attend.2 = (bf16[3,320,1024]{2,1,0:T(8,128)(2,1)S(1)}, f32[3,2,8,320]{3,2,1,0:T(8,128)S(1)}) custom-call(s32[3]{0:T(128)S(1)} %bitcast.197, bf16[3,320,3072]{2,1,0:T(8,128)(2,1)} %get-tuple-element.110.q.k.v, bf16[3,320,3072]{2,1,0:T(8,128)(2,1)} %get-tuple-element.110.q.k.v, bf16[3,320,3072]{2,1,0:T(8,128)(2,1)} %get-tuple-element.110.q.k.v), custom_call_target="tpu_custom_call" | custom-call | flops 3355443200 | bytes 2949120 | tf_op jit(solution)/shard_map/attend/pallas_call | solution.py:246
  102.8 12.9 %attend.3 = (bf16[3,320,1024]{2,1,0:T(8,128)(2,1)S(1)}, f32[3,2,8,320]{3,2,1,0:T(8,128)S(1)}) custom-call(s32[3]{0:T(128)S(1)} %bitcast.198, bf16[3,320,3072]{2,1,0:T(8,128)(2,1)} %get-tuple-element.110.q.k.v, bf16[3,320,3072]{2,1,0:T(8,128)(2,1)} %get-tuple-element.110.q.k.v, ...), custom_call_target="tpu_custom_call", output_to_operand_aliasing={{0}: (4, {}), {1}: (5, {})} | custom-call | flops 6710886400 | bytes 5898240 | tf_op jit(solution)/shard_map/attend/pallas_call | solution.py:246
  115.9 2.5 collective-permute-done.19.refs_5_
  118.5 12.9 %branch.1 = (f32[3,320,1024]{2,1,0:T(8,128)}, bf16[3,320,1024]{2,1,0:T(8,128)(2,1)S(1)}, bf16[4,2,4,2,16,5120]{5,4,3,2,1,0:T(8,128)(2,1)}) custom-call(s32[3]{0:T(128)S(1)} %bitcast.199, s32[3]{0:T(128)S(1)} %pad_add_fusion.1.pos, bf16[3,320,1024]{2,1,0:T(8,128)(2,1)} %bitcast.172, bf16[3,320,1024]{2,1,0:T(8,128)(2,1)S(1)} %get-tuple-element.116.mixed, ...), custom_call_target="tpu_custom_call" | custom-call | flops 2013265920 | bytes 30801920 | tf_op jit(solution)/shard_map/branch/pallas_call | solution.py:355
  131.4 26.9 %expand.1 = (bf16[960,4096]{1,0:T(8,128)(2,1)}, bf16[960,4096]{1,0:T(8,128)(2,1)}, bf16[4096,1024]{1,0:T(8,128)(2,1)}) custom-call(bf16[960,1024]{1,0:T(8,128)(2,1)S(1)} %bitcast.204, bf16[960,1024]{1,0:T(8,128)(2,1)S(1)} %bitcast.209, bf16[1024,5120]{1,0:T(8,128)(2,1)} %bitcast.258, f32[1,4096]{1,0:T(1,128)S(1)} %bitcast.195), custom_call_target="tpu_custom_call" | custom-call | flops 16106127360 | bytes 32505856 | tf_op jit(solution)/shard_map/expand/pallas_call | solution.py:403
  159.9 13.9 %hidden_back.1 = (bf16[960,4096]{1,0:T(8,128)(2,1)}, f32[1,4096]{1,0:T(1,128)S(1)}) custom-call(bf16[960,1024]{1,0:T(8,128)(2,1)S(1)} %bitcast.210, bf16[4096,1024]{1,0:T(8,128)(2,1)} %all-gather.2.cloned.1.call-done.weight, bf16[960,4096]{1,0:T(8,128)(2,1)} %get-tuple-element.125.slope), custom_call_target="tpu_custom_call" | custom-call | flops 8053063680 | bytes 24117248 | tf_op jit(solution)/shard_map/hidden_back/pallas_call | solution.py:467
  173.8 20.2 %norm_two_back.1 = (f32[3,320,1024]{2,1,0:T(8,128)}, bf16[3,320,1024]{2,1,0:T(8,128)(2,1)S(1)}, bf16[3,320,1024]{2,1,0:T(8,128)(2,1)S(1)}, f32[1,1024]{1,0:T(1,1...) custom-call(s32[3]{0:T(128)S(1)} %bitcast.200, bf16[3,320,4096]{2,1,0:T(8,128)(2,1)} %bitcast.263, ...), custom_call_target="tpu_custom_call" | custom-call | flops 10066329600 | bytes 21626880 | tf_op jit(solution)/shard_map/norm_two_back/pallas_call | solution.py:578
  194.0 30.4 %attend_back.1.grads.thirds = bf16[3,3,320,1024]{3,2,1,0:T(8,128)(2,1)} custom-call(s32[3]{0:T(128)S(1)} %bitcast.201, bf16[3,320,3072]{2,1,0:T(8,128)(2,1)} %get-tuple-element.110.q.k.v, bf16[3,320,3072]{2,1,0:T(8,128)(2,1)} %get-tuple-element.110.q.k.v, bf16[3,320,3072]{2,1,0:T(8,128)(2,1)} %get-tuple-element.110.q.k.v, ...), custom_call_target="tpu_custom_call" | custom-call | flops 25165824000 | bytes 14745600 | tf_op jit(solution)/shard_map/attend_back/pallas_call | solution.py:311
  224.4 12.7 %whole_grad.1 = bf16[1024,4096]{1,0:T(8,128)(2,1)} custom-call(bf16[960,1024]{1,0:T(8,128)(2,1)S(1)} %bitcast.205, bf16[960,4096]{1,0:T(8,128)(2,1)} %get-tuple-element.161.grads), custom_call_target="tpu_custom_call" | custom-call | flops 8053063680 | bytes 18219008 | tf_op jit(solution)/shard_map/whole_grad/pallas_call | solution.py:487
  237.3 4.6 %weight_grad.5.refs_0_ = bf16[2,4,4,16,4096]{4,3,2,1,0:T(8,128)(2,1)} custom-call(s32[4]{0:T(128)S(1)} %pad_add_fusion.order, bf16[960,1024]{1,0:T(8,128)(2,1)S(1)} %bitcast.162, bf16[960,1024]{1,0:T(8,128)(2,1)} %bitcast.166), custom_call_target="tpu_custom_call" | custom-call | flops 1006632960 | bytes 4980736 | tf_op jit(solution)/shard_map/weight_grad/pallas_call | solution.py:536
  241.9 4.6 %weight_grad.4.refs_0_ = bf16[2,4,4,16,4096]{4,3,2,1,0:T(8,128)(2,1)} custom-call(s32[4]{0:T(128)S(1)} %pad_add_fusion.order, bf16[960,1024]{1,0:T(8,128)(2,1)S(1)} %bitcast.163, bf16[960,1024]{1,0:T(8,128)(2,1)} %bitcast.167), custom_call_target="tpu_custom_call" | custom-call | flops 1006632960 | bytes 4980736 | tf_op jit(solution)/shard_map/weight_grad/pallas_call | solution.py:536
  249.9 8.1 %weight_grad.6 = bf16[2,4,4,16,4096]{4,3,2,1,0:T(8,128)(2,1)} custom-call(s32[4]{0:T(128)S(1)} %pad_add_fusion.order, bf16[960,1024]{1,0:T(8,128)(2,1)S(1)} %bitcast.164, bf16[3,3,320,1024]{3,2,1,0:T(8,128)(2,1)} %attend_back.1.grads.thirds, bf16[2,4,4,16,4096]{4,3,2,1,0:T(8,128)(2,1)} %weight_grad.4.refs_0_), custom_call_target="tpu_custom_call", output_to_operand_aliasing={{}: (3, {})} | custom-call | flops 3019898880 | bytes 11010048 | tf_op jit(solution)/shard_map/weight_grad/pallas_call | solution.py:536
  257.9 2.5 collective-permute-start.23
  261.4 8.2 %weight_grad.7 = bf16[2,4,4,16,4096]{4,3,2,1,0:T(8,128)(2,1)} custom-call(s32[4]{0:T(128)S(1)} %pad_add_fusion.order, bf16[960,1024]{1,0:T(8,128)(2,1)S(1)} %bitcast.165, bf16[3,3,320,1024]{3,2,1,0:T(8,128)(2,1)} %attend_back.1.grads.thirds, bf16[2,4,4,16,4096]{4,3,2,1,0:T(8,128)(2,1)} %weight_grad.5.refs_0_), custom_call_target="tpu_custom_call", output_to_operand_aliasing={{}: (3, {})} | custom-call | flops 3019898880 | bytes 11010048 | tf_op jit(solution)/shard_map/weight_grad/pallas_call | solution.py:536
  269.7 3.5 collective-permute-done.22
  276.4 4.6 %near_sum.1 = (bf16[4,2,16,4096]{3,2,1,0:T(8,128)(2,1)S(1)}, bf16[4,2,16,4096]{3,2,1,0:T(8,128)(2,1)S(1)}, bf16[4,2,16,4096]{3,2,1,0:T(8,128)(2,1)S(1)}, bf16[4,2,16,4096]{3,2,1,0:T(8,128)(2,1)S(1)}) custom-call(bf16[2,4,2,2,16,4096]{5,4,3,2,1,0:T(8,128)(2,1)} %bitcast.211, bf16[2,4,2,2,16,4096]{5,4,3,2,1,0:T(8,128)(2,1)} %bitcast.212, ...), custom_call_target="tpu_custom_call" | custom-call | flops 2097152 | bytes 12582912 | tf_op jit(solution)/shard_map/near_sum/pallas_call | solution.py:659
  284.2 12.9 %norm_one_back.1 = (f32[3,320,1024]{2,1,0:T(8,128)}, f32[1,1024]{1,0:T(1,128)S(1)}, f32[1,1024]{1,0:T(1,128)S(1)}, f32[1,1024]{1,0:T(1,128)S(1)}, f32[1,1024]{1,0:T(1,128)S(1)}) custom-call(s32[3]{0:T(128)S(1)} %bitcast.202, bf16[3,3,320,1024]{3,2,1,0:T(8,128)(2,1)} %attend_back.1.grads.thirds, bf16[1024,3200]{1,0:T(8,128)(2,1)S(1)} %bitcast.208, ...), custom_call_target="tpu_custom_call" | custom-call | flops 6039797760 | bytes 22020096 | tf_op jit(solution)/shard_map/norm_one_back/pallas_call | solution.py:624
  303.2 7.1 %collective-permute-done.26 = f32[96,128]{1,0:T(8,128)} collective-permute-done((f32[96,128]{1,0:T(8,128)}, f32[96,128]{1,0:T(8,128)}, u32[]{:S(2)}, u32[]{:S(2)}) %collective-permute-start.26) | collective-permute-done | bytes 49184 | tf_op jit(solution)/shard_map/ppermute | solution.py:694
  320.7 15.5 %reduce_out.1 = f32[3,320,1024]{2,1,0:T(8,128)} custom-call(s32[3]{0:T(128)S(1)} %bitcast.203, f32[3,320,1024]{2,1,0:T(8,128)} %get-tuple-element.127.resid, bf16[3,320,4096]{2,1,0:T(8,128)(2,1)} %bitcast.262, bf16[4096,1024]{1,0:T(8,128)(2,1)} %all-gather.2.cloned.1.call-done.weight, f32[16,1024]{1,0:T(8,128)S(1)} %get-tuple-element.117.table), custom_call_target="tpu_custom_call" | custom-call | flops 8053063680 | bytes 24117248 | tf_op jit(solution)/shard_map/reduce_out/pallas_call | solution.py:430
  344.7 5.4 %collective-permute-done.35 = bf16[32,4096]{1,0:T(8,128)(2,1)S(1)} collective-permute-done((bf16[32,4096]{1,0:T(8,128)(2,1)S(1)}, bf16[32,4096]{1,0:T(8,128)(2,1)S(1)}, u32[]{:S(2)}, u32[]{:S(2)}) %collective-permute-start.35) | collective-permute-done | bytes 262176 | tf_op jit(solution)/shard_map/ppermute | solution.py:694
  350.3 2.5 collective-permute-done.37
  358.4 2.5 collective-permute-done.41
  369.9 2.6 collective-permute-done.45
  373.1 5.2 %collective-permute-done.44 = bf16[2,16,4096]{2,1,0:T(8,128)(2,1)S(1)} collective-permute-done((bf16[2,16,4096]{2,1,0:T(8,128)(2,1)S(1)}, bf16[2,16,4096]{2,1,0:T(8,128)(2,1)S(1)}, u32[]{:S(2)}, u32[]{:S(2)}) %collective-permute-start.44) | collective-permute-done | bytes 262176 | tf_op jit(solution)/shard_map/ppermute | solution.py:694
  382.4 2.6 collective-permute-done.47
  (206 shorter events, 77.8 us)
Async XLA Ops:
  7.3 151.1 %all-gather.2.cloned.1.call-start = ((), (), s32[]{:S(2)}) async-start(), calls=%async_computation.3 | async-start | bytes 9437184 | tf_op jit(solution)/shard_map/all_gather | solution.py:859
  8.7 24.8 %collective-permute-start.4 = (bf16[4,2,16,5120]{3,2,1,0:T(8,128)(2,1)S(1)}, bf16[4,2,16,5120]{3,2,1,0:T(8,128)(2,1)S(1)}, u32[]{:S(2)}, u32[]{:S(2)}) collective-permute-start(bf16[4,2,16,5120]{3,2,1,0:T(8,128)(2,1)S(1)} %bitcast.168), channel_id=1, source_target_pairs={{0,1},{1,0},{2,3},{3,2},{4,5},{5,4},{6,7},{7,6},{8,9},{9,8},{10,11... | collective-permute-start | bytes 3932168 | tf_op jit(solution)/shard_map/ppermute | solution.py:694
  10.6 22.8 %collective-permute-start.3 = (bf16[4,2,16,3200]{3,2,1,0:T(8,128)(2,1)S(1)}, bf16[4,2,16,3200]{3,2,1,0:T(8,128)(2,1)}, u32[]{:S(2)}, u32[]{:S(2)}) collective-permute-start(bf16[4,2,16,3200]{3,2,1,0:T(8,128)(2,1)S(1)} %bitcast.226), channel_id=1, source_target_pairs={{0,1},{1,0},{2,3},{3,2},{4,5},{5,4},{6,7},{7,6},{8,9},{9,8},{10,11... | collective-permute-start | bytes 2457608 | tf_op jit(solution)/shard_map/ppermute | solution.py:694
  15.8 17.6 %collective-permute-start.1 = (bf16[2,16,3200]{2,1,0:T(8,128)(2,1)S(1)}, bf16[2,16,3200]{2,1,0:T(8,128)(2,1)S(1)}, u32[]{:S(2)}, u32[]{:S(2)}) collective-permute-start(bf16[2,16,3200]{2,1,0:T(8,128)(2,1)S(1)} %dynamic-slice_bitcast_fusion.7), channel_id=1, source_target_pairs={{0,4},{1,5},{2,6},{3,7},{4,0},{5,1},{6,2},{7,3},{8,12},{9,13},{10,... | collective-permute-start | bytes 614408 | tf_op jit(solution)/shard_map/ppermute | solution.py:694
  15.8 17.6 %collective-permute-start = (bf16[2,16,3200]{2,1,0:T(8,128)(2,1)S(1)}, bf16[2,16,3200]{2,1,0:T(8,128)(2,1)S(1)}, u32[]{:S(2)}, u32[]{:S(2)}) collective-permute-start(bf16[2,16,3200]{2,1,0:T(8,128)(2,1)S(1)} %dynamic-slice_bitcast_fusion.7), channel_id=1, source_target_pairs={{0,2},{1,3},{2,4},{3,5},{4,6},{5,7},{6,0},{7,1},{8,10},{9,11},{10,... | collective-permute-start | bytes 614408 | tf_op jit(solution)/shard_map/ppermute | solution.py:694
  33.6 26.6 %collective-permute-start.6 = (bf16[2,3,16,3200]{3,2,1,0:T(8,128)(2,1)S(1)}, bf16[2,3,16,3200]{3,2,1,0:T(8,128)(2,1)S(1)}, u32[]{:S(2)}, u32[]{:S(2)}) collective-permute-start(bf16[2,3,16,3200]{3,2,1,0:T(8,128)(2,1)S(1)} %get-tuple-element.212), channel_id=1, source_target_pairs={{0,16},{1,17},{2,18},{3,19},{4,20},{5,21},{6,22},{7,23},{8,24},{9,... | collective-permute-start | bytes 1843208 | tf_op jit(solution)/shard_map/ppermute | solution.py:694
  35.2 25.0 %collective-permute-start.5 = (bf16[2,3,16,3200]{3,2,1,0:T(8,128)(2,1)S(1)}, bf16[2,3,16,3200]{3,2,1,0:T(8,128)(2,1)S(1)}, u32[]{:S(2)}, u32[]{:S(2)}) collective-permute-start(bf16[2,3,16,3200]{3,2,1,0:T(8,128)(2,1)S(1)} %get-tuple-element.212), channel_id=1, source_target_pairs={{0,8},{1,9},{2,10},{3,11},{4,12},{5,13},{6,14},{7,15},{8,0},{9,1},... | collective-permute-start | bytes 1843208 | tf_op jit(solution)/shard_map/ppermute | solution.py:694
  36.7 23.5 %collective-permute-start.8 = (bf16[2,16,5120]{2,1,0:T(8,128)(2,1)S(1)}, bf16[2,16,5120]{2,1,0:T(8,128)(2,1)S(1)}, u32[]{:S(2)}, u32[]{:S(2)}) collective-permute-start(bf16[2,16,5120]{2,1,0:T(8,128)(2,1)S(1)} %dynamic-slice_bitcast_fusion), channel_id=1, source_target_pairs={{0,4},{1,5},{2,6},{3,7},{4,0},{5,1},{6,2},{7,3},{8,12},{9,13},{10,... | collective-permute-start | bytes 983048 | tf_op jit(solution)/shard_map/ppermute | solution.py:694
  39.5 20.6 %collective-permute-start.7 = (bf16[2,16,5120]{2,1,0:T(8,128)(2,1)S(1)}, bf16[2,16,5120]{2,1,0:T(8,128)(2,1)S(1)}, u32[]{:S(2)}, u32[]{:S(2)}) collective-permute-start(bf16[2,16,5120]{2,1,0:T(8,128)(2,1)S(1)} %dynamic-slice_bitcast_fusion), channel_id=1, source_target_pairs={{0,2},{1,3},{2,4},{3,5},{4,6},{5,7},{6,0},{7,1},{8,10},{9,11},{10,... | collective-permute-start | bytes 983048 | tf_op jit(solution)/shard_map/ppermute | solution.py:694
  74.4 172.8 %reduce-scatter.3.cloned.1.call-start = ((), (), s32[]{:S(2)}) async-start(), calls=%async_computation.2 | async-start | bytes 9437184 | tf_op jit(solution)/shard_map/reduce_scatter | solution.py:819
  74.6 25.9 %collective-permute-start.15 = (bf16[2,3,16,5120]{3,2,1,0:T(8,128)(2,1)}, bf16[2,3,16,5120]{3,2,1,0:T(8,128)(2,1)S(1)}, u32[]{:S(2)}, u32[]{:S(2)}) collective-permute-start(bf16[2,3,16,5120]{3,2,1,0:T(8,128)(2,1)} %get-tuple-element.210), channel_id=1, source_target_pairs={{0,16},{1,17},{2,18},{3,19},{4,20},{5,21},{6,22},{7,23},{8,24},{9,... | collective-permute-start | bytes 2949128 | tf_op jit(solution)/shard_map/ppermute | solution.py:694
  75.2 25.4 %collective-permute-start.14 = (bf16[2,3,16,5120]{3,2,1,0:T(8,128)(2,1)}, bf16[2,3,16,5120]{3,2,1,0:T(8,128)(2,1)S(1)}, u32[]{:S(2)}, u32[]{:S(2)}) collective-permute-start(bf16[2,3,16,5120]{3,2,1,0:T(8,128)(2,1)} %get-tuple-element.210), channel_id=1, source_target_pairs={{0,8},{1,9},{2,10},{3,11},{4,12},{5,13},{6,14},{7,15},{8,0},{9,1},... | collective-permute-start | bytes 2949128 | tf_op jit(solution)/shard_map/ppermute | solution.py:694
  100.9 17.6 %collective-permute-start.18 = (bf16[3,2,3,16,5120]{4,3,2,1,0:T(8,128)(2,1)S(1)}, bf16[3,2,3,16,5120]{4,3,2,1,0:T(8,128)(2,1)S(1)}, u32[]{:S(2)}, u32[]{:S(2)}) collective-permute-start(bf16[3,2,3,16,5120]{4,3,2,1,0:T(8,128)(2,1)S(1)} %pad_maximum_fusion.refs_1_), channel_id=1, source_target_pairs={{0,1},{1,0},{2,3},{3,2},{4,5},{5,4},{6,7},{7,6},{8,9},{9,8},{10,11... | collective-permute-start | bytes 8847368 | tf_op jit(solution)/shard_map/ppermute | solution.py:694
  101.0 14.7 %collective-permute-start.17 = (bf16[3,16,5120]{2,1,0:T(8,128)(2,1)S(1)}, bf16[3,16,5120]{2,1,0:T(8,128)(2,1)S(1)}, u32[]{:S(2)}, u32[]{:S(2)}) collective-permute-start(bf16[3,16,5120]{2,1,0:T(8,128)(2,1)S(1)} %slice_bitcast_fusion.4), channel_id=1, source_target_pairs={{0,8},{1,9},{2,10},{3,11},{4,12},{5,13},{6,14},{7,15},{8,0},{9,1},... | collective-permute-start | bytes 1474568 | tf_op jit(solution)/shard_map/ppermute | solution.py:694
  101.2 14.5 %collective-permute-start.16 = (bf16[3,16,5120]{2,1,0:T(8,128)(2,1)S(1)}, bf16[3,16,5120]{2,1,0:T(8,128)(2,1)S(1)}, u32[]{:S(2)}, u32[]{:S(2)}) collective-permute-start(bf16[3,16,5120]{2,1,0:T(8,128)(2,1)S(1)} %slice_bitcast_fusion.5), channel_id=1, source_target_pairs={{0,16},{1,17},{2,18},{3,19},{4,20},{5,21},{6,22},{7,23},{8,24},{9,... | collective-permute-start | bytes 1474568 | tf_op jit(solution)/shard_map/ppermute | solution.py:694
  158.3 181.5 %reduce-scatter.5.cloned.1.call-start = ((), (), s32[]{:S(2)}) async-start(), calls=%async_computation.4 | async-start | bytes 9437184 | tf_op jit(solution)/shard_map/reduce_scatter | solution.py:819
  257.9 16.5 %collective-permute-start.20 = (bf16[2,4,4,16,4096]{4,3,2,1,0:T(8,128)(2,1)}, bf16[2,4,4,16,4096]{4,3,2,1,0:T(8,128)(2,1)S(1)}, u32[]{:S(2)}, u32[]{:S(2)}) collective-permute-start(bf16[2,4,4,16,4096]{4,3,2,1,0:T(8,128)(2,1)} %weight_grad.6), channel_id=1, source_target_pairs={{0,1},{1,0},{2,3},{3,2},{4,5},{5,4},{6,7},{7,6},{8,9},{9,8},{10,11... | collective-permute-start | bytes 12582920 | tf_op jit(solution)/shard_map/ppermute | solution.py:694
  260.4 12.7 %collective-permute-start.22 = (bf16[128,1024]{1,0:T(8,128)(2,1)S(1)}, bf16[128,1024]{1,0:T(8,128)(2,1)S(1)}, u32[]{:S(2)}, u32[]{:S(2)}) collective-permute-start(bf16[128,1024]{1,0:T(8,128)(2,1)S(1)} %get-tuple-element.207), channel_id=1, source_target_pairs={{0,16},{1,17},{2,18},{3,19},{4,20},{5,21},{6,22},{7,23},{8,24},{9,... | collective-permute-start | bytes 786440 | tf_op jit(solution)/shard_map/ppermute | solution.py:694
  282.0 33.3 %collective-permute-start.29 = (bf16[4,2,16,4096]{3,2,1,0:T(8,128)(2,1)S(1)}, bf16[4,2,16,4096]{3,2,1,0:T(8,128)(2,1)}, u32[]{:S(2)}, u32[]{:S(2)}) collective-permute-start(bf16[4,2,16,4096]{3,2,1,0:T(8,128)(2,1)S(1)} %get-tuple-element.138), channel_id=1, source_target_pairs={{0,16},{1,17},{2,18},{3,19},{4,20},{5,21},{6,22},{7,23},{8,24},{9,... | collective-permute-start | bytes 3145736 | tf_op jit(solution)/shard_map/ppermute | solution.py:694
  283.5 31.9 %collective-permute-start.28 = (bf16[4,2,16,4096]{3,2,0,1:T(8,128)(2,1)}, bf16[4,2,16,4096]{3,2,0,1:T(8,128)(2,1)}, u32[]{:S(2)}, u32[]{:S(2)}) collective-permute-start(bf16[4,2,16,4096]{3,2,0,1:T(8,128)(2,1)} %copy.49), channel_id=1, source_target_pairs={{0,8},{1,9},{2,10},{3,11},{4,12},{5,13},{6,14},{7,15},{8,0},{9,1},... | collective-permute-start | bytes 3145736 | tf_op jit(solution)/shard_map/ppermute | solution.py:694
  310.4 25.8 %collective-permute-start.34 = (bf16[128,1024]{1,0:T(8,128)(2,1)S(1)}, bf16[128,1024]{1,0:T(8,128)(2,1)S(1)}, u32[]{:S(2)}, u32[]{:S(2)}) collective-permute-start(bf16[128,1024]{1,0:T(8,128)(2,1)S(1)} %fusion.12), channel_id=1, source_target_pairs={{0,24},{1,25},{2,26},{3,27},{4,28},{5,29},{6,30},{7,31},{8,16},{9,... | collective-permute-start | bytes 786440 | tf_op jit(solution)/shard_map/ppermute | solution.py:694
  311.8 24.4 %collective-permute-start.33 = (bf16[128,1024]{1,0:T(8,128)(2,1)S(1)}, bf16[128,1024]{1,0:T(8,128)(2,1)S(1)}, u32[]{:S(2)}, u32[]{:S(2)}) collective-permute-start(bf16[128,1024]{1,0:T(8,128)(2,1)S(1)} %fusion.12), channel_id=1, source_target_pairs={{0,16},{1,17},{2,18},{3,19},{4,20},{5,21},{6,22},{7,23},{8,24},{9,... | collective-permute-start | bytes 786440 | tf_op jit(solution)/shard_map/ppermute | solution.py:694
  312.1 24.1 %collective-permute-start.32 = (bf16[128,1024]{1,0:T(8,128)(2,1)S(1)}, bf16[128,1024]{1,0:T(8,128)(2,1)S(1)}, u32[]{:S(2)}, u32[]{:S(2)}) collective-permute-start(bf16[128,1024]{1,0:T(8,128)(2,1)S(1)} %fusion.12), channel_id=1, source_target_pairs={{0,8},{1,9},{2,10},{3,11},{4,12},{5,13},{6,14},{7,15},{8,0},{9,1},... | collective-permute-start | bytes 786440 | tf_op jit(solution)/shard_map/ppermute | solution.py:694
  316.9 19.3 %collective-permute-start.30 = (bf16[4,16,4096]{2,1,0:T(8,128)(2,1)S(1)}, bf16[4,16,4096]{2,1,0:T(8,128)(2,1)S(1)}, u32[]{:S(2)}, u32[]{:S(2)}) collective-permute-start(bf16[4,16,4096]{2,1,0:T(8,128)(2,1)S(1)} %slice_bitcast_fusion.3), channel_id=1, source_target_pairs={{0,8},{1,9},{2,10},{3,11},{4,12},{5,13},{6,14},{7,15},{8,0},{9,1},... | collective-permute-start | bytes 1572872 | tf_op jit(solution)/shard_map/ppermute | solution.py:694
  318.8 17.4 %collective-permute-start.31 = (bf16[4,16,4096]{2,1,0:T(8,128)(2,1)S(1)}, bf16[4,16,4096]{2,1,0:T(8,128)(2,1)S(1)}, u32[]{:S(2)}, u32[]{:S(2)}) collective-permute-start(bf16[4,16,4096]{2,1,0:T(8,128)(2,1)S(1)} %slice_bitcast_fusion.2), channel_id=1, source_target_pairs={{0,16},{1,17},{2,18},{3,19},{4,20},{5,21},{6,22},{7,23},{8,24},{9,... | collective-permute-start | bytes 1572872 | tf_op jit(solution)/shard_map/ppermute | solution.py:694
  337.3 21.1 %collective-permute-start.42 = (bf16[2,16,4096]{2,1,0:T(8,128)(2,1)}, bf16[2,16,4096]{2,1,0:T(8,128)(2,1)S(1)}, u32[]{:S(2)}, u32[]{:S(2)}) collective-permute-start(bf16[2,16,4096]{2,1,0:T(8,128)(2,1)} %get-tuple-element.203), channel_id=1, source_target_pairs={{0,6},{1,7},{2,0},{3,1},{4,2},{5,3},{6,4},{7,5},{8,14},{9,15},{10,... | collective-permute-start | bytes 786440 | tf_op jit(solution)/shard_map/ppermute | solution.py:694
  338.0 20.4 %collective-permute-start.40 = (bf16[2,16,4096]{2,1,0:T(8,128)(2,1)S(1)}, bf16[2,16,4096]{2,1,0:T(8,128)(2,1)S(1)}, u32[]{:S(2)}, u32[]{:S(2)}) collective-permute-start(bf16[2,16,4096]{2,1,0:T(8,128)(2,1)S(1)} %get-tuple-element.204), channel_id=1, source_target_pairs={{0,2},{1,3},{2,4},{3,5},{4,6},{5,7},{6,0},{7,1},{8,10},{9,11},{10,... | collective-permute-start | bytes 786440 | tf_op jit(solution)/shard_map/ppermute | solution.py:694
  363.3 14.9 %collective-permute-start.44 = (bf16[2,16,4096]{2,1,0:T(8,128)(2,1)S(1)}, bf16[2,16,4096]{2,1,0:T(8,128)(2,1)S(1)}, u32[]{:S(2)}, u32[]{:S(2)}) collective-permute-start(bf16[2,16,4096]{2,1,0:T(8,128)(2,1)S(1)} %fusion.6), channel_id=1, source_target_pairs={{0,16},{1,17},{2,18},{3,19},{4,20},{5,21},{6,22},{7,23},{8,24},{9,... | collective-permute-start | bytes 786440 | tf_op jit(solution)/shard_map/ppermute | solution.py:694
  364.3 13.9 %collective-permute-start.43 = (bf16[2,16,4096]{2,1,0:T(8,128)(2,1)S(1)}, bf16[2,16,4096]{2,1,0:T(8,128)(2,1)S(1)}, u32[]{:S(2)}, u32[]{:S(2)}) collective-permute-start(bf16[2,16,4096]{2,1,0:T(8,128)(2,1)S(1)} %fusion.6), channel_id=1, source_target_pairs={{0,8},{1,9},{2,10},{3,11},{4,12},{5,13},{6,14},{7,15},{8,0},{9,1},... | collective-permute-start | bytes 786440 | tf_op jit(solution)/shard_map/ppermute | solution.py:694
  365.8 16.6 %collective-permute-start.48 = (bf16[32,4096]{1,0:T(8,128)(2,1)S(1)}, bf16[32,4096]{1,0:T(8,128)(2,1)S(1)}, u32[]{:S(2)}, u32[]{:S(2)}) collective-permute-start(bf16[32,4096]{1,0:T(8,128)(2,1)S(1)} %fusion.9), channel_id=1, source_target_pairs={{0,24},{1,25},{2,26},{3,27},{4,28},{5,29},{6,30},{7,31},{8,16},{9,... | collective-permute-start | bytes 786440 | tf_op jit(solution)/shard_map/ppermute | solution.py:694
  366.8 18.2 %collective-permute-start.47 = (bf16[32,4096]{1,0:T(8,128)(2,1)S(1)}, bf16[32,4096]{1,0:T(8,128)(2,1)S(1)}, u32[]{:S(2)}, u32[]{:S(2)}) collective-permute-start(bf16[32,4096]{1,0:T(8,128)(2,1)S(1)} %fusion.9), channel_id=1, source_target_pairs={{0,16},{1,17},{2,18},{3,19},{4,20},{5,21},{6,22},{7,23},{8,24},{9,... | collective-permute-start | bytes 786440 | tf_op jit(solution)/shard_map/ppermute | solution.py:694
  372.5 13.5 %collective-permute-start.46 = (bf16[32,4096]{1,0:T(8,128)(2,1)S(1)}, bf16[32,4096]{1,0:T(8,128)(2,1)S(1)}, u32[]{:S(2)}, u32[]{:S(2)}) collective-permute-start(bf16[32,4096]{1,0:T(8,128)(2,1)S(1)} %fusion.9), channel_id=1, source_target_pairs={{0,8},{1,9},{2,10},{3,11},{4,12},{5,13},{6,14},{7,15},{8,0},{9,1},... | collective-permute-start | bytes 786440 | tf_op jit(solution)/shard_map/ppermute | solution.py:694
  (50 other events, 502.4 us)
Sparse Core Ops, SparseCore 0:
  74.5 80.7 all-gather.1
  158.4 88.7 reduce-scatter.2
  249.5 87.9 reduce-scatter.4

commit v7 on v6

--- a/solution.py
+++ b/solution.py
@@ -369,7 +369,7 @@
         compiler_params=params(26),
         cost_estimate=cost(2 * seqs * rows * width * width, seqs * rows * width * 10 + 4 * width * wide),
         name="branch",
-    )(lengths, pos, held(x), mixed, table, *pieces)
+    )(lengths, pos, x, mixed, table, *pieces)
     return resid, normed, kept.reshape(-1, wide)
 
 

time: 398 us -> 398 us (level)
  no operation moved by 1% of the time
where the time goes in v7:
time: 398 us; the launch traced here: 394 us
  Pallas kernels  211 us (53%)
  waiting for transfers between devices  87.8 us (22%)
  starting transfers between devices  48.2 us (12%)
  other arithmetic  18.7 us (5%)
  between operations  14.8 us (4%)
  local copies, waits for them, and re-layouts  13.5 us (3%)
    ppermute x49, waiting for transfers between devices, send(): return lax.ppermute(array, AXES, pairs)  87 us
    ppermute x49, starting transfers between devices, send(): return lax.ppermute(array, AXES, pairs)  47.9 us
    pallas_call x1, Pallas kernels, attend_back(): pl.pallas_call(functools.partial(attend_back_kernel, seq), grid_spec=pltp...  30.4 us
    pallas_call x1, Pallas kernels, expand(): pl.pallas_call(functools.partial(expand_kernel, seqs), grid=(4,), in_spec...  26.8 us
    pallas_call x4, Pallas kernels, weight_grad(): pl.pallas_call(functools.partial(weight_grad_kernel, half), grid_spec=plt...  25.4 us
    pallas_call x2, Pallas kernels, attend(): pl.pallas_call(functools.partial(attend_kernel, seq), grid_spec=pltpu.Pre...  21.3 us
    pallas_call x1, Pallas kernels, norm_two_back(): pl.pallas_call(norm_two_kernel, grid_spec=pltpu.PrefetchScalarGridSpec(nu...  20.2 us
    pallas_call x1, Pallas kernels, reduce_out(): pl.pallas_call(reduce_kernel, grid_spec=pltpu.PrefetchScalarGridSpec(num_...  15.5 us
  transfers between devices with their start and end apart: 52, of which 22 were waited for; matrix products, arithmetic and copies ran while one was open for 5% of the time, Pallas kernels for 54%

profile of v7, /device:TPU:0, one launch (start us, length us, event | category | flops | bytes accessed | tf_op | source)
XLA Modules:
  0.0 393.8 jit_solution(1783042821927645593)
XLA Ops:
  10.7 5.1 %collective-permute-start.2 = (bf16[2,16,3200]{2,1,0:T(8,128)(2,1)S(1)}, bf16[2,16,3200]{2,1,0:T(8,128)(2,1)S(1)}, u32[]{:S(2)}, u32[]{:S(2)}) collective-permute-start(bf16[2,16,3200]{2,1,0:T(8,128)(2,1)S(1)} %dynamic-slice_bitcast_fusion.7), channel_id=1, source_target_pairs={{0,6},{1,7},{2,0},{3,1},{4,2},{5,3},{6,4},{7,5},{8,14},{9,15},{10,... | collective-permute-start | bytes 614408 | tf_op jit(solution)/shard_map/ppermute | solution.py:694
  16.9 4.5 %collective-permute-done.2 = bf16[2,16,3200]{2,1,0:T(8,128)(2,1)S(1)} collective-permute-done((bf16[2,16,3200]{2,1,0:T(8,128)(2,1)S(1)}, bf16[2,16,3200]{2,1,0:T(8,128)(2,1)S(1)}, u32[]{:S(2)}, u32[]{:S(2)}) %collective-permute-start.2) | collective-permute-done | bytes 204832 | tf_op jit(solution)/shard_map/ppermute | solution.py:694
  21.4 12.1 %collective-permute-done.1 = bf16[2,16,3200]{2,1,0:T(8,128)(2,1)S(1)} collective-permute-done((bf16[2,16,3200]{2,1,0:T(8,128)(2,1)S(1)}, bf16[2,16,3200]{2,1,0:T(8,128)(2,1)S(1)}, u32[]{:S(2)}, u32[]{:S(2)}) %collective-permute-start.1) | collective-permute-done | bytes 204832 | tf_op jit(solution)/shard_map/ppermute | solution.py:694
  36.7 2.9 collective-permute-start.8
  39.5 20.6 %collective-permute-done.8 = bf16[2,16,5120]{2,1,0:T(8,128)(2,1)S(1)} collective-permute-done((bf16[2,16,5120]{2,1,0:T(8,128)(2,1)S(1)}, bf16[2,16,5120]{2,1,0:T(8,128)(2,1)S(1)}, u32[]{:S(2)}, u32[]{:S(2)}) %collective-permute-start.8) | collective-permute-done | bytes 327712 | tf_op jit(solution)/shard_map/ppermute | solution.py:694
  61.8 8.6 %collective-permute-done.10 = bf16[3,16,3200]{2,1,0:T(8,128)(2,1)S(1)} collective-permute-done((bf16[3,16,3200]{2,1,0:T(8,128)(2,1)S(1)}, bf16[3,16,3200]{2,1,0:T(8,128)(2,1)S(1)}, u32[]{:S(2)}, u32[]{:S(2)}) %collective-permute-start.10) | collective-permute-done | bytes 307232 | tf_op jit(solution)/shard_map/ppermute | solution.py:694
  76.8 15.3 %norm_project.1 = (bf16[3,320,1024]{2,1,0:T(8,128)(2,1)S(1)}, bf16[3,320,3072]{2,1,0:T(8,128)(2,1)}, bf16[3,320,1024]{2,1,0:T(8,128)(2,1)S(1)}, f32[1,1024]{1,0:...) custom-call(s32[3]{0:T(128)S(1)} %bitcast.196, s32[3]{0:T(128)S(1)} %pad_add_fusion.1.pos, ...), custom_call_target="tpu_custom_call" | custom-call | flops 6039797760 | bytes 26345472 | tf_op jit(solution)/shard_map/norm_project/pallas_call | solution.py:176
  92.1 8.4 %attend.2 = (bf16[3,320,1024]{2,1,0:T(8,128)(2,1)S(1)}, f32[3,2,8,320]{3,2,1,0:T(8,128)S(1)}) custom-call(s32[3]{0:T(128)S(1)} %bitcast.197, bf16[3,320,3072]{2,1,0:T(8,128)(2,1)} %get-tuple-element.110.q.k.v, bf16[3,320,3072]{2,1,0:T(8,128)(2,1)} %get-tuple-element.110.q.k.v, bf16[3,320,3072]{2,1,0:T(8,128)(2,1)} %get-tuple-element.110.q.k.v), custom_call_target="tpu_custom_call" | custom-call | flops 3355443200 | bytes 2949120 | tf_op jit(solution)/shard_map/attend/pallas_call | solution.py:246
  102.8 12.9 %attend.3 = (bf16[3,320,1024]{2,1,0:T(8,128)(2,1)S(1)}, f32[3,2,8,320]{3,2,1,0:T(8,128)S(1)}) custom-call(s32[3]{0:T(128)S(1)} %bitcast.198, bf16[3,320,3072]{2,1,0:T(8,128)(2,1)} %get-tuple-element.110.q.k.v, bf16[3,320,3072]{2,1,0:T(8,128)(2,1)} %get-tuple-element.110.q.k.v, ...), custom_call_target="tpu_custom_call", output_to_operand_aliasing={{0}: (4, {}), {1}: (5, {})} | custom-call | flops 6710886400 | bytes 5898240 | tf_op jit(solution)/shard_map/attend/pallas_call | solution.py:246
  115.9 2.5 collective-permute-done.19.refs_5_
  118.5 11.8 %branch.1 = (f32[3,320,1024]{2,1,0:T(8,128)}, bf16[3,320,1024]{2,1,0:T(8,128)(2,1)S(1)}, bf16[4,2,4,2,16,5120]{5,4,3,2,1,0:T(8,128)(2,1)}) custom-call(s32[3]{0:T(128)S(1)} %bitcast.199, s32[3]{0:T(128)S(1)} %pad_add_fusion.1.pos, bf16[3,320,1024]{2,1,0:T(8,128)(2,1)S(1)} %bitcast.172, bf16[3,320,1024]{2,1,0:T(8,128)(2,1)S(1)} %get-tuple-element.116.mixed, ...), custom_call_target="tpu_custom_call" | custom-call | flops 2013265920 | bytes 30801920 | tf_op jit(solution)/shard_map/branch/pallas_call | solution.py:355
  130.3 26.8 %expand.1 = (bf16[960,4096]{1,0:T(8,128)(2,1)}, bf16[960,4096]{1,0:T(8,128)(2,1)}, bf16[4096,1024]{1,0:T(8,128)(2,1)}) custom-call(bf16[960,1024]{1,0:T(8,128)(2,1)S(1)} %bitcast.204, bf16[960,1024]{1,0:T(8,128)(2,1)S(1)} %bitcast.209, bf16[1024,5120]{1,0:T(8,128)(2,1)} %bitcast.258, f32[1,4096]{1,0:T(1,128)S(1)} %bitcast.195), custom_call_target="tpu_custom_call" | custom-call | flops 16106127360 | bytes 32505856 | tf_op jit(solution)/shard_map/expand/pallas_call | solution.py:403
  158.8 13.8 %hidden_back.1 = (bf16[960,4096]{1,0:T(8,128)(2,1)}, f32[1,4096]{1,0:T(1,128)S(1)}) custom-call(bf16[960,1024]{1,0:T(8,128)(2,1)S(1)} %bitcast.210, bf16[4096,1024]{1,0:T(8,128)(2,1)} %all-gather.2.cloned.1.call-done.weight, bf16[960,4096]{1,0:T(8,128)(2,1)} %get-tuple-element.125.slope), custom_call_target="tpu_custom_call" | custom-call | flops 8053063680 | bytes 24117248 | tf_op jit(solution)/shard_map/hidden_back/pallas_call | solution.py:467
  172.6 20.2 %norm_two_back.1 = (f32[3,320,1024]{2,1,0:T(8,128)}, bf16[3,320,1024]{2,1,0:T(8,128)(2,1)S(1)}, bf16[3,320,1024]{2,1,0:T(8,128)(2,1)S(1)}, f32[1,1024]{1,0:T(1,1...) custom-call(s32[3]{0:T(128)S(1)} %bitcast.200, bf16[3,320,4096]{2,1,0:T(8,128)(2,1)} %bitcast.263, ...), custom_call_target="tpu_custom_call" | custom-call | flops 10066329600 | bytes 21626880 | tf_op jit(solution)/shard_map/norm_two_back/pallas_call | solution.py:578
  192.8 30.4 %attend_back.1.grads.thirds = bf16[3,3,320,1024]{3,2,1,0:T(8,128)(2,1)} custom-call(s32[3]{0:T(128)S(1)} %bitcast.201, bf16[3,320,3072]{2,1,0:T(8,128)(2,1)} %get-tuple-element.110.q.k.v, bf16[3,320,3072]{2,1,0:T(8,128)(2,1)} %get-tuple-element.110.q.k.v, bf16[3,320,3072]{2,1,0:T(8,128)(2,1)} %get-tuple-element.110.q.k.v, ...), custom_call_target="tpu_custom_call" | custom-call | flops 25165824000 | bytes 14745600 | tf_op jit(solution)/shard_map/attend_back/pallas_call | solution.py:311
  223.2 12.8 %whole_grad.1 = bf16[1024,4096]{1,0:T(8,128)(2,1)} custom-call(bf16[960,1024]{1,0:T(8,128)(2,1)S(1)} %bitcast.205, bf16[960,4096]{1,0:T(8,128)(2,1)} %get-tuple-element.161.grads), custom_call_target="tpu_custom_call" | custom-call | flops 8053063680 | bytes 18219008 | tf_op jit(solution)/shard_map/whole_grad/pallas_call | solution.py:487
  236.1 4.6 %weight_grad.5.refs_0_ = bf16[2,4,4,16,4096]{4,3,2,1,0:T(8,128)(2,1)} custom-call(s32[4]{0:T(128)S(1)} %pad_add_fusion.order, bf16[960,1024]{1,0:T(8,128)(2,1)S(1)} %bitcast.162, bf16[960,1024]{1,0:T(8,128)(2,1)} %bitcast.166), custom_call_target="tpu_custom_call" | custom-call | flops 1006632960 | bytes 4980736 | tf_op jit(solution)/shard_map/weight_grad/pallas_call | solution.py:536
  240.7 4.5 %weight_grad.4.refs_0_ = bf16[2,4,4,16,4096]{4,3,2,1,0:T(8,128)(2,1)} custom-call(s32[4]{0:T(128)S(1)} %pad_add_fusion.order, bf16[960,1024]{1,0:T(8,128)(2,1)S(1)} %bitcast.163, bf16[960,1024]{1,0:T(8,128)(2,1)} %bitcast.167), custom_call_target="tpu_custom_call" | custom-call | flops 1006632960 | bytes 4980736 | tf_op jit(solution)/shard_map/weight_grad/pallas_call | solution.py:536
  248.6 8.1 %weight_grad.6 = bf16[2,4,4,16,4096]{4,3,2,1,0:T(8,128)(2,1)} custom-call(s32[4]{0:T(128)S(1)} %pad_add_fusion.order, bf16[960,1024]{1,0:T(8,128)(2,1)S(1)} %bitcast.164, bf16[3,3,320,1024]{3,2,1,0:T(8,128)(2,1)} %attend_back.1.grads.thirds, bf16[2,4,4,16,4096]{4,3,2,1,0:T(8,128)(2,1)} %weight_grad.4.refs_0_), custom_call_target="tpu_custom_call", output_to_operand_aliasing={{}: (3, {})} | custom-call | flops 3019898880 | bytes 11010048 | tf_op jit(solution)/shard_map/weight_grad/pallas_call | solution.py:536
  256.8 2.4 collective-permute-start.23
  260.3 8.2 %weight_grad.7 = bf16[2,4,4,16,4096]{4,3,2,1,0:T(8,128)(2,1)} custom-call(s32[4]{0:T(128)S(1)} %pad_add_fusion.order, bf16[960,1024]{1,0:T(8,128)(2,1)S(1)} %bitcast.165, bf16[3,3,320,1024]{3,2,1,0:T(8,128)(2,1)} %attend_back.1.grads.thirds, bf16[2,4,4,16,4096]{4,3,2,1,0:T(8,128)(2,1)} %weight_grad.5.refs_0_), custom_call_target="tpu_custom_call", output_to_operand_aliasing={{}: (3, {})} | custom-call | flops 3019898880 | bytes 11010048 | tf_op jit(solution)/shard_map/weight_grad/pallas_call | solution.py:536
  268.5 3.5 collective-permute-done.22
  275.2 4.6 %near_sum.1 = (bf16[4,2,16,4096]{3,2,1,0:T(8,128)(2,1)S(1)}, bf16[4,2,16,4096]{3,2,1,0:T(8,128)(2,1)S(1)}, bf16[4,2,16,4096]{3,2,1,0:T(8,128)(2,1)S(1)}, bf16[4,2,16,4096]{3,2,1,0:T(8,128)(2,1)S(1)}) custom-call(bf16[2,4,2,2,16,4096]{5,4,3,2,1,0:T(8,128)(2,1)} %bitcast.211, bf16[2,4,2,2,16,4096]{5,4,3,2,1,0:T(8,128)(2,1)} %bitcast.212, ...), custom_call_target="tpu_custom_call" | custom-call | flops 2097152 | bytes 12582912 | tf_op jit(solution)/shard_map/near_sum/pallas_call | solution.py:659
  283.0 12.9 %norm_one_back.1 = (f32[3,320,1024]{2,1,0:T(8,128)}, f32[1,1024]{1,0:T(1,128)S(1)}, f32[1,1024]{1,0:T(1,128)S(1)}, f32[1,1024]{1,0:T(1,128)S(1)}, f32[1,1024]{1,0:T(1,128)S(1)}) custom-call(s32[3]{0:T(128)S(1)} %bitcast.202, bf16[3,3,320,1024]{3,2,1,0:T(8,128)(2,1)} %attend_back.1.grads.thirds, bf16[1024,3200]{1,0:T(8,128)(2,1)S(1)} %bitcast.208, ...), custom_call_target="tpu_custom_call" | custom-call | flops 6039797760 | bytes 22020096 | tf_op jit(solution)/shard_map/norm_one_back/pallas_call | solution.py:624
  302.0 7.1 %collective-permute-done.26 = f32[96,128]{1,0:T(8,128)} collective-permute-done((f32[96,128]{1,0:T(8,128)}, f32[96,128]{1,0:T(8,128)}, u32[]{:S(2)}, u32[]{:S(2)}) %collective-permute-start.26) | collective-permute-done | bytes 49184 | tf_op jit(solution)/shard_map/ppermute | solution.py:694
  319.5 15.5 %reduce_out.1 = f32[3,320,1024]{2,1,0:T(8,128)} custom-call(s32[3]{0:T(128)S(1)} %bitcast.203, f32[3,320,1024]{2,1,0:T(8,128)} %get-tuple-element.127.resid, bf16[3,320,4096]{2,1,0:T(8,128)(2,1)} %bitcast.262, bf16[4096,1024]{1,0:T(8,128)(2,1)} %all-gather.2.cloned.1.call-done.weight, f32[16,1024]{1,0:T(8,128)S(1)} %get-tuple-element.117.table), custom_call_target="tpu_custom_call" | custom-call | flops 8053063680 | bytes 24117248 | tf_op jit(solution)/shard_map/reduce_out/pallas_call | solution.py:430
  343.6 5.4 %collective-permute-done.35 = bf16[32,4096]{1,0:T(8,128)(2,1)S(1)} collective-permute-done((bf16[32,4096]{1,0:T(8,128)(2,1)S(1)}, bf16[32,4096]{1,0:T(8,128)(2,1)S(1)}, u32[]{:S(2)}, u32[]{:S(2)}) %collective-permute-start.35) | collective-permute-done | bytes 262176 | tf_op jit(solution)/shard_map/ppermute | solution.py:694
  349.1 2.5 collective-permute-done.37
  357.5 2.2 collective-permute-done.41
  369.0 2.3 collective-permute-done.45
  372.1 5.3 %collective-permute-done.44 = bf16[2,16,4096]{2,1,0:T(8,128)(2,1)S(1)} collective-permute-done((bf16[2,16,4096]{2,1,0:T(8,128)(2,1)S(1)}, bf16[2,16,4096]{2,1,0:T(8,128)(2,1)S(1)}, u32[]{:S(2)}, u32[]{:S(2)}) %collective-permute-start.44) | collective-permute-done | bytes 262176 | tf_op jit(solution)/shard_map/ppermute | solution.py:694
  381.3 2.6 collective-permute-done.47
  (208 shorter events, 78.4 us)
Async XLA Ops:
  7.3 149.9 %all-gather.2.cloned.1.call-start = ((), (), s32[]{:S(2)}) async-start(), calls=%async_computation.3 | async-start | bytes 9437184 | tf_op jit(solution)/shard_map/all_gather | solution.py:859
  8.7 24.8 %collective-permute-start.4 = (bf16[4,2,16,5120]{3,2,1,0:T(8,128)(2,1)S(1)}, bf16[4,2,16,5120]{3,2,1,0:T(8,128)(2,1)S(1)}, u32[]{:S(2)}, u32[]{:S(2)}) collective-permute-start(bf16[4,2,16,5120]{3,2,1,0:T(8,128)(2,1)S(1)} %bitcast.168), channel_id=1, source_target_pairs={{0,1},{1,0},{2,3},{3,2},{4,5},{5,4},{6,7},{7,6},{8,9},{9,8},{10,11... | collective-permute-start | bytes 3932168 | tf_op jit(solution)/shard_map/ppermute | solution.py:694
  10.6 22.8 %collective-permute-start.3 = (bf16[4,2,16,3200]{3,2,1,0:T(8,128)(2,1)S(1)}, bf16[4,2,16,3200]{3,2,1,0:T(8,128)(2,1)}, u32[]{:S(2)}, u32[]{:S(2)}) collective-permute-start(bf16[4,2,16,3200]{3,2,1,0:T(8,128)(2,1)S(1)} %bitcast.226), channel_id=1, source_target_pairs={{0,1},{1,0},{2,3},{3,2},{4,5},{5,4},{6,7},{7,6},{8,9},{9,8},{10,11... | collective-permute-start | bytes 2457608 | tf_op jit(solution)/shard_map/ppermute | solution.py:694
  15.8 17.6 %collective-permute-start.1 = (bf16[2,16,3200]{2,1,0:T(8,128)(2,1)S(1)}, bf16[2,16,3200]{2,1,0:T(8,128)(2,1)S(1)}, u32[]{:S(2)}, u32[]{:S(2)}) collective-permute-start(bf16[2,16,3200]{2,1,0:T(8,128)(2,1)S(1)} %dynamic-slice_bitcast_fusion.7), channel_id=1, source_target_pairs={{0,4},{1,5},{2,6},{3,7},{4,0},{5,1},{6,2},{7,3},{8,12},{9,13},{10,... | collective-permute-start | bytes 614408 | tf_op jit(solution)/shard_map/ppermute | solution.py:694
  15.8 17.6 %collective-permute-start = (bf16[2,16,3200]{2,1,0:T(8,128)(2,1)S(1)}, bf16[2,16,3200]{2,1,0:T(8,128)(2,1)S(1)}, u32[]{:S(2)}, u32[]{:S(2)}) collective-permute-start(bf16[2,16,3200]{2,1,0:T(8,128)(2,1)S(1)} %dynamic-slice_bitcast_fusion.7), channel_id=1, source_target_pairs={{0,2},{1,3},{2,4},{3,5},{4,6},{5,7},{6,0},{7,1},{8,10},{9,11},{10,... | collective-permute-start | bytes 614408 | tf_op jit(solution)/shard_map/ppermute | solution.py:694
  33.6 26.6 %collective-permute-start.6 = (bf16[2,3,16,3200]{3,2,1,0:T(8,128)(2,1)S(1)}, bf16[2,3,16,3200]{3,2,1,0:T(8,128)(2,1)S(1)}, u32[]{:S(2)}, u32[]{:S(2)}) collective-permute-start(bf16[2,3,16,3200]{3,2,1,0:T(8,128)(2,1)S(1)} %get-tuple-element.212), channel_id=1, source_target_pairs={{0,16},{1,17},{2,18},{3,19},{4,20},{5,21},{6,22},{7,23},{8,24},{9,... | collective-permute-start | bytes 1843208 | tf_op jit(solution)/shard_map/ppermute | solution.py:694
  35.2 25.0 %collective-permute-start.5 = (bf16[2,3,16,3200]{3,2,1,0:T(8,128)(2,1)S(1)}, bf16[2,3,16,3200]{3,2,1,0:T(8,128)(2,1)S(1)}, u32[]{:S(2)}, u32[]{:S(2)}) collective-permute-start(bf16[2,3,16,3200]{3,2,1,0:T(8,128)(2,1)S(1)} %get-tuple-element.212), channel_id=1, source_target_pairs={{0,8},{1,9},{2,10},{3,11},{4,12},{5,13},{6,14},{7,15},{8,0},{9,1},... | collective-permute-start | bytes 1843208 | tf_op jit(solution)/shard_map/ppermute | solution.py:694
  36.7 23.5 %collective-permute-start.8 = (bf16[2,16,5120]{2,1,0:T(8,128)(2,1)S(1)}, bf16[2,16,5120]{2,1,0:T(8,128)(2,1)S(1)}, u32[]{:S(2)}, u32[]{:S(2)}) collective-permute-start(bf16[2,16,5120]{2,1,0:T(8,128)(2,1)S(1)} %dynamic-slice_bitcast_fusion), channel_id=1, source_target_pairs={{0,4},{1,5},{2,6},{3,7},{4,0},{5,1},{6,2},{7,3},{8,12},{9,13},{10,... | collective-permute-start | bytes 983048 | tf_op jit(solution)/shard_map/ppermute | solution.py:694
  39.5 20.6 %collective-permute-start.7 = (bf16[2,16,5120]{2,1,0:T(8,128)(2,1)S(1)}, bf16[2,16,5120]{2,1,0:T(8,128)(2,1)S(1)}, u32[]{:S(2)}, u32[]{:S(2)}) collective-permute-start(bf16[2,16,5120]{2,1,0:T(8,128)(2,1)S(1)} %dynamic-slice_bitcast_fusion), channel_id=1, source_target_pairs={{0,2},{1,3},{2,4},{3,5},{4,6},{5,7},{6,0},{7,1},{8,10},{9,11},{10,... | collective-permute-start | bytes 983048 | tf_op jit(solution)/shard_map/ppermute | solution.py:694
  74.4 171.5 %reduce-scatter.3.cloned.1.call-start = ((), (), s32[]{:S(2)}) async-start(), calls=%async_computation.2 | async-start | bytes 9437184 | tf_op jit(solution)/shard_map/reduce_scatter | solution.py:819
  74.6 25.9 %collective-permute-start.15 = (bf16[2,3,16,5120]{3,2,1,0:T(8,128)(2,1)}, bf16[2,3,16,5120]{3,2,1,0:T(8,128)(2,1)S(1)}, u32[]{:S(2)}, u32[]{:S(2)}) collective-permute-start(bf16[2,3,16,5120]{3,2,1,0:T(8,128)(2,1)} %get-tuple-element.210), channel_id=1, source_target_pairs={{0,16},{1,17},{2,18},{3,19},{4,20},{5,21},{6,22},{7,23},{8,24},{9,... | collective-permute-start | bytes 2949128 | tf_op jit(solution)/shard_map/ppermute | solution.py:694
  75.2 25.4 %collective-permute-start.14 = (bf16[2,3,16,5120]{3,2,1,0:T(8,128)(2,1)}, bf16[2,3,16,5120]{3,2,1,0:T(8,128)(2,1)S(1)}, u32[]{:S(2)}, u32[]{:S(2)}) collective-permute-start(bf16[2,3,16,5120]{3,2,1,0:T(8,128)(2,1)} %get-tuple-element.210), channel_id=1, source_target_pairs={{0,8},{1,9},{2,10},{3,11},{4,12},{5,13},{6,14},{7,15},{8,0},{9,1},... | collective-permute-start | bytes 2949128 | tf_op jit(solution)/shard_map/ppermute | solution.py:694
  100.9 17.6 %collective-permute-start.18 = (bf16[3,2,3,16,5120]{4,3,2,1,0:T(8,128)(2,1)S(1)}, bf16[3,2,3,16,5120]{4,3,2,1,0:T(8,128)(2,1)S(1)}, u32[]{:S(2)}, u32[]{:S(2)}) collective-permute-start(bf16[3,2,3,16,5120]{4,3,2,1,0:T(8,128)(2,1)S(1)} %pad_maximum_fusion.refs_1_), channel_id=1, source_target_pairs={{0,1},{1,0},{2,3},{3,2},{4,5},{5,4},{6,7},{7,6},{8,9},{9,8},{10,11... | collective-permute-start | bytes 8847368 | tf_op jit(solution)/shard_map/ppermute | solution.py:694
  101.0 14.7 %collective-permute-start.17 = (bf16[3,16,5120]{2,1,0:T(8,128)(2,1)S(1)}, bf16[3,16,5120]{2,1,0:T(8,128)(2,1)S(1)}, u32[]{:S(2)}, u32[]{:S(2)}) collective-permute-start(bf16[3,16,5120]{2,1,0:T(8,128)(2,1)S(1)} %slice_bitcast_fusion.4), channel_id=1, source_target_pairs={{0,8},{1,9},{2,10},{3,11},{4,12},{5,13},{6,14},{7,15},{8,0},{9,1},... | collective-permute-start | bytes 1474568 | tf_op jit(solution)/shard_map/ppermute | solution.py:694
  101.2 14.5 %collective-permute-start.16 = (bf16[3,16,5120]{2,1,0:T(8,128)(2,1)S(1)}, bf16[3,16,5120]{2,1,0:T(8,128)(2,1)S(1)}, u32[]{:S(2)}, u32[]{:S(2)}) collective-permute-start(bf16[3,16,5120]{2,1,0:T(8,128)(2,1)S(1)} %slice_bitcast_fusion.5), channel_id=1, source_target_pairs={{0,16},{1,17},{2,18},{3,19},{4,20},{5,21},{6,22},{7,23},{8,24},{9,... | collective-permute-start | bytes 1474568 | tf_op jit(solution)/shard_map/ppermute | solution.py:694
  157.1 181.4 %reduce-scatter.5.cloned.1.call-start = ((), (), s32[]{:S(2)}) async-start(), calls=%async_computation.4 | async-start | bytes 9437184 | tf_op jit(solution)/shard_map/reduce_scatter | solution.py:819
  256.7 16.5 %collective-permute-start.20 = (bf16[2,4,4,16,4096]{4,3,2,1,0:T(8,128)(2,1)}, bf16[2,4,4,16,4096]{4,3,2,1,0:T(8,128)(2,1)S(1)}, u32[]{:S(2)}, u32[]{:S(2)}) collective-permute-start(bf16[2,4,4,16,4096]{4,3,2,1,0:T(8,128)(2,1)} %weight_grad.6), channel_id=1, source_target_pairs={{0,1},{1,0},{2,3},{3,2},{4,5},{5,4},{6,7},{7,6},{8,9},{9,8},{10,11... | collective-permute-start | bytes 12582920 | tf_op jit(solution)/shard_map/ppermute | solution.py:694
  259.2 12.7 %collective-permute-start.22 = (bf16[128,1024]{1,0:T(8,128)(2,1)S(1)}, bf16[128,1024]{1,0:T(8,128)(2,1)S(1)}, u32[]{:S(2)}, u32[]{:S(2)}) collective-permute-start(bf16[128,1024]{1,0:T(8,128)(2,1)S(1)} %get-tuple-element.207), channel_id=1, source_target_pairs={{0,16},{1,17},{2,18},{3,19},{4,20},{5,21},{6,22},{7,23},{8,24},{9,... | collective-permute-start | bytes 786440 | tf_op jit(solution)/shard_map/ppermute | solution.py:694
  280.9 33.3 %collective-permute-start.29 = (bf16[4,2,16,4096]{3,2,1,0:T(8,128)(2,1)S(1)}, bf16[4,2,16,4096]{3,2,1,0:T(8,128)(2,1)}, u32[]{:S(2)}, u32[]{:S(2)}) collective-permute-start(bf16[4,2,16,4096]{3,2,1,0:T(8,128)(2,1)S(1)} %get-tuple-element.138), channel_id=1, source_target_pairs={{0,16},{1,17},{2,18},{3,19},{4,20},{5,21},{6,22},{7,23},{8,24},{9,... | collective-permute-start | bytes 3145736 | tf_op jit(solution)/shard_map/ppermute | solution.py:694
  282.3 31.9 %collective-permute-start.28 = (bf16[4,2,16,4096]{3,2,0,1:T(8,128)(2,1)}, bf16[4,2,16,4096]{3,2,0,1:T(8,128)(2,1)}, u32[]{:S(2)}, u32[]{:S(2)}) collective-permute-start(bf16[4,2,16,4096]{3,2,0,1:T(8,128)(2,1)} %copy.49), channel_id=1, source_target_pairs={{0,8},{1,9},{2,10},{3,11},{4,12},{5,13},{6,14},{7,15},{8,0},{9,1},... | collective-permute-start | bytes 3145736 | tf_op jit(solution)/shard_map/ppermute | solution.py:694
  309.2 25.8 %collective-permute-start.34 = (bf16[128,1024]{1,0:T(8,128)(2,1)S(1)}, bf16[128,1024]{1,0:T(8,128)(2,1)S(1)}, u32[]{:S(2)}, u32[]{:S(2)}) collective-permute-start(bf16[128,1024]{1,0:T(8,128)(2,1)S(1)} %fusion.12), channel_id=1, source_target_pairs={{0,24},{1,25},{2,26},{3,27},{4,28},{5,29},{6,30},{7,31},{8,16},{9,... | collective-permute-start | bytes 786440 | tf_op jit(solution)/shard_map/ppermute | solution.py:694
  310.6 24.4 %collective-permute-start.33 = (bf16[128,1024]{1,0:T(8,128)(2,1)S(1)}, bf16[128,1024]{1,0:T(8,128)(2,1)S(1)}, u32[]{:S(2)}, u32[]{:S(2)}) collective-permute-start(bf16[128,1024]{1,0:T(8,128)(2,1)S(1)} %fusion.12), channel_id=1, source_target_pairs={{0,16},{1,17},{2,18},{3,19},{4,20},{5,21},{6,22},{7,23},{8,24},{9,... | collective-permute-start | bytes 786440 | tf_op jit(solution)/shard_map/ppermute | solution.py:694
  310.9 24.1 %collective-permute-start.32 = (bf16[128,1024]{1,0:T(8,128)(2,1)S(1)}, bf16[128,1024]{1,0:T(8,128)(2,1)S(1)}, u32[]{:S(2)}, u32[]{:S(2)}) collective-permute-start(bf16[128,1024]{1,0:T(8,128)(2,1)S(1)} %fusion.12), channel_id=1, source_target_pairs={{0,8},{1,9},{2,10},{3,11},{4,12},{5,13},{6,14},{7,15},{8,0},{9,1},... | collective-permute-start | bytes 786440 | tf_op jit(solution)/shard_map/ppermute | solution.py:694
  315.7 19.3 %collective-permute-start.30 = (bf16[4,16,4096]{2,1,0:T(8,128)(2,1)S(1)}, bf16[4,16,4096]{2,1,0:T(8,128)(2,1)S(1)}, u32[]{:S(2)}, u32[]{:S(2)}) collective-permute-start(bf16[4,16,4096]{2,1,0:T(8,128)(2,1)S(1)} %slice_bitcast_fusion.3), channel_id=1, source_target_pairs={{0,8},{1,9},{2,10},{3,11},{4,12},{5,13},{6,14},{7,15},{8,0},{9,1},... | collective-permute-start | bytes 1572872 | tf_op jit(solution)/shard_map/ppermute | solution.py:694
  317.7 17.4 %collective-permute-start.31 = (bf16[4,16,4096]{2,1,0:T(8,128)(2,1)S(1)}, bf16[4,16,4096]{2,1,0:T(8,128)(2,1)S(1)}, u32[]{:S(2)}, u32[]{:S(2)}) collective-permute-start(bf16[4,16,4096]{2,1,0:T(8,128)(2,1)S(1)} %slice_bitcast_fusion.2), channel_id=1, source_target_pairs={{0,16},{1,17},{2,18},{3,19},{4,20},{5,21},{6,22},{7,23},{8,24},{9,... | collective-permute-start | bytes 1572872 | tf_op jit(solution)/shard_map/ppermute | solution.py:694
  336.1 21.4 %collective-permute-start.42 = (bf16[2,16,4096]{2,1,0:T(8,128)(2,1)}, bf16[2,16,4096]{2,1,0:T(8,128)(2,1)S(1)}, u32[]{:S(2)}, u32[]{:S(2)}) collective-permute-start(bf16[2,16,4096]{2,1,0:T(8,128)(2,1)} %get-tuple-element.203), channel_id=1, source_target_pairs={{0,6},{1,7},{2,0},{3,1},{4,2},{5,3},{6,4},{7,5},{8,14},{9,15},{10,... | collective-permute-start | bytes 786440 | tf_op jit(solution)/shard_map/ppermute | solution.py:694
  336.9 20.7 %collective-permute-start.40 = (bf16[2,16,4096]{2,1,0:T(8,128)(2,1)S(1)}, bf16[2,16,4096]{2,1,0:T(8,128)(2,1)S(1)}, u32[]{:S(2)}, u32[]{:S(2)}) collective-permute-start(bf16[2,16,4096]{2,1,0:T(8,128)(2,1)S(1)} %get-tuple-element.204), channel_id=1, source_target_pairs={{0,2},{1,3},{2,4},{3,5},{4,6},{5,7},{6,0},{7,1},{8,10},{9,11},{10,... | collective-permute-start | bytes 786440 | tf_op jit(solution)/shard_map/ppermute | solution.py:694
  362.6 14.9 %collective-permute-start.44 = (bf16[2,16,4096]{2,1,0:T(8,128)(2,1)S(1)}, bf16[2,16,4096]{2,1,0:T(8,128)(2,1)S(1)}, u32[]{:S(2)}, u32[]{:S(2)}) collective-permute-start(bf16[2,16,4096]{2,1,0:T(8,128)(2,1)S(1)} %fusion.6), channel_id=1, source_target_pairs={{0,16},{1,17},{2,18},{3,19},{4,20},{5,21},{6,22},{7,23},{8,24},{9,... | collective-permute-start | bytes 786440 | tf_op jit(solution)/shard_map/ppermute | solution.py:694
  363.4 14.0 %collective-permute-start.43 = (bf16[2,16,4096]{2,1,0:T(8,128)(2,1)S(1)}, bf16[2,16,4096]{2,1,0:T(8,128)(2,1)S(1)}, u32[]{:S(2)}, u32[]{:S(2)}) collective-permute-start(bf16[2,16,4096]{2,1,0:T(8,128)(2,1)S(1)} %fusion.6), channel_id=1, source_target_pairs={{0,8},{1,9},{2,10},{3,11},{4,12},{5,13},{6,14},{7,15},{8,0},{9,1},... | collective-permute-start | bytes 786440 | tf_op jit(solution)/shard_map/ppermute | solution.py:694
  364.6 16.7 %collective-permute-start.48 = (bf16[32,4096]{1,0:T(8,128)(2,1)S(1)}, bf16[32,4096]{1,0:T(8,128)(2,1)S(1)}, u32[]{:S(2)}, u32[]{:S(2)}) collective-permute-start(bf16[32,4096]{1,0:T(8,128)(2,1)S(1)} %fusion.9), channel_id=1, source_target_pairs={{0,24},{1,25},{2,26},{3,27},{4,28},{5,29},{6,30},{7,31},{8,16},{9,... | collective-permute-start | bytes 786440 | tf_op jit(solution)/shard_map/ppermute | solution.py:694
  366.0 17.9 %collective-permute-start.47 = (bf16[32,4096]{1,0:T(8,128)(2,1)S(1)}, bf16[32,4096]{1,0:T(8,128)(2,1)S(1)}, u32[]{:S(2)}, u32[]{:S(2)}) collective-permute-start(bf16[32,4096]{1,0:T(8,128)(2,1)S(1)} %fusion.9), channel_id=1, source_target_pairs={{0,16},{1,17},{2,18},{3,19},{4,20},{5,21},{6,22},{7,23},{8,24},{9,... | collective-permute-start | bytes 786440 | tf_op jit(solution)/shard_map/ppermute | solution.py:694
  371.4 13.5 %collective-permute-start.46 = (bf16[32,4096]{1,0:T(8,128)(2,1)S(1)}, bf16[32,4096]{1,0:T(8,128)(2,1)S(1)}, u32[]{:S(2)}, u32[]{:S(2)}) collective-permute-start(bf16[32,4096]{1,0:T(8,128)(2,1)S(1)} %fusion.9), channel_id=1, source_target_pairs={{0,8},{1,9},{2,10},{3,11},{4,12},{5,13},{6,14},{7,15},{8,0},{9,1},... | collective-permute-start | bytes 786440 | tf_op jit(solution)/shard_map/ppermute | solution.py:694
  (51 other events, 517.3 us)
Sparse Core Ops, SparseCore 0:
  74.5 80.7 all-gather.1
  157.6 88.2 reduce-scatter.2
  248.2 87.9 reduce-scatter.4
